TPU v7x, 32 devices: a whole 2x2x4 slice. The times are simulated.
32 devices in a mesh: tm: 8 (over z, x), rows: 4 (over y, core).
Axes of the slice: x: 2, y: 2, z: 4, core: 2. Of those that a mesh axis runs over, the one named last changes fastest.
Arguments:
- x_in: bfloat16 [8, 1024, 512], P('rows', 'tm'), may hold values from -24 to 24
- lengths: int32 [8, 16], P('rows'), may hold values from 1 to 512, 1024 in all within a row
- bn_gain: float32 [2, 512], replicated, may hold values from 0.25 to 1.75
- bn_bias: float32 [2, 512], replicated, may hold values from -3 to 3
- w_in: bfloat16 [2, 512, 512], replicated, may hold values from -0.25 to 0.25
- decay_rate: float32 [2, 256], replicated, may hold values from 0.00012207031 to 0.033
- phase: float32 [2, 256], replicated, may hold values from -3.140625 to 3.140625
- w_out: bfloat16 [2, 512, 512], replicated, may hold values from -0.25 to 0.25
- skip_gain: float32 [2, 512], replicated, may hold values from -4 to 4
- w_glu: bfloat16 [2, 512, 1024], replicated, may hold values from -0.5 to 0.5
- b_glu: float32 [2, 1024], replicated, may hold values from -2 to 2
- grad_out: bfloat16 [8, 1024, 512], P('rows', 'tm'), may hold values from -5 to 5
Outputs:
- out: bfloat16 [8, 1024, 512], P('rows', 'tm')
- grad_x: float32 [8, 1024, 512], P('rows', 'tm')
- g_bn_gain: float32 [2, 512], replicated
- g_bn_bias: float32 [2, 512], replicated
- g_w_in: float32 [2, 512, 512], replicated
- g_decay_rate: float32 [2, 256], replicated
- g_phase: float32 [2, 256], replicated
- g_w_out: float32 [2, 512, 512], replicated
- g_skip_gain: float32 [2, 512], replicated
- g_w_glu: float32 [2, 512, 1024], replicated
- g_b_glu: float32 [2, 1024], replicated
All inputs are finite; a program needn't handle non-finite values.
Results may differ from a plain program's by a relative error of at most 0.015.
Values sent between devices are 32-bit elements; how exact they have to be, the bound alone decides.
No kernel may reach another device: no remote copies, remote signals or barrier semaphores. Data moves between devices by JAX's collectives and lax.ppermute only.
A program may use at most 128 MiB of HBM per device.

v0:
```python
import jax
import jax.numpy as jnp
from jax import lax
from jax.sharding import PartitionSpec as P

norm_eps = 1e-05


def prefix(part, axis, combine, identity, reverse):
    count = lax.axis_size(axis)
    place = lax.axis_index(axis)
    ahead = count - 1 - place if reverse else place
    gathered = jax.tree.map(lambda a: lax.all_gather(a, axis), part)
    state = jax.tree.map(lambda a, e: jnp.zeros_like(a) + jnp.asarray(e, a.dtype), part, identity)

    def one(hop, state):
        source = count - 1 - hop if reverse else hop
        return combine(
            state, jax.tree.map(lambda a: lax.dynamic_index_in_dim(a, source, 0, False), gathered)
        )

    return lax.fori_loop(0, ahead, one, state)


def lam_terms(rate_vec, angle_vec):
    magnitude = jnp.exp(-rate_vec)
    return (
        magnitude * jnp.cos(angle_vec),
        magnitude * jnp.sin(angle_vec),
        jnp.sqrt(1.0 - jnp.exp(-2.0 * rate_vec)),
    )


def glu_gate(pre_act):
    half_width = pre_act.shape[-1] // 2
    return pre_act[..., :half_width] * jax.nn.sigmoid(pre_act[..., half_width:])


def gelu_exact(values):
    return jax.nn.gelu(values, approximate=False)


def times_weight(left_side, right_side):
    return jnp.dot(left_side, right_side, preferred_element_type=jnp.float32)


def times_transposed(left_side, right_side):
    return lax.dot_general(
        left_side, right_side, (((1,), (1,)), ((), ())), preferred_element_type=jnp.float32
    )


def outer_sum(left_side, right_side):
    return lax.dot_general(
        left_side, right_side, (((0,), (0,)), ((), ())), preferred_element_type=jnp.float32
    )


def combine_pairs(earlier, latter):
    prior_re, prior_im, state_re, state_im = earlier
    factor_re, factor_im, drive_re, drive_im = latter
    return (
        factor_re * prior_re - factor_im * prior_im,
        factor_re * prior_im + factor_im * prior_re,
        factor_re * state_re - factor_im * state_im + drive_re,
        factor_re * state_im + factor_im * state_re + drive_im,
    )


def linear_scan(coef_re, coef_im, drive_re, drive_im, backward_time):
    running = lax.associative_scan(
        combine_pairs, (coef_re, coef_im, drive_re, drive_im), reverse=backward_time, axis=1
    )
    edge_index = 0 if backward_time else -1
    total_re = running[0][:, edge_index]
    total_im = running[1][:, edge_index]
    final_re = running[2][:, edge_index]
    final_im = running[3][:, edge_index]
    ones_part = jnp.ones_like(total_re)
    zero_part = jnp.zeros_like(total_re)
    if backward_time:
        entering = prefix(
            (total_re, total_im, final_re, final_im),
            "tm",
            combine_pairs,
            (ones_part, zero_part, zero_part, zero_part),
            True,
        )
    else:
        entering = prefix(
            (total_re, total_im, final_re, final_im),
            "tm",
            combine_pairs,
            (ones_part, zero_part, zero_part, zero_part),
            False,
        )
    carry_re = entering[2]
    carry_im = entering[3]
    product_re, product_im, local_re, local_im = running
    state_re = local_re + product_re * carry_re[:, None] - product_im * carry_im[:, None]
    state_im = local_im + product_re * carry_im[:, None] + product_im * carry_re[:, None]
    return (state_re, state_im, carry_re, carry_im)


def body(
    x_in,
    lengths,
    bn_gain,
    bn_bias,
    w_in,
    decay_rate,
    phase,
    w_out,
    skip_gain,
    w_glu,
    b_glu,
    grad_out,
):
    row_count, steps_dev, width = x_in.shape
    states = w_in.shape[2] // 2
    tokens_all = row_count * steps_dev * lax.axis_size("tm") * lax.axis_size("rows")
    positions = lax.axis_index("tm") * steps_dev + jnp.arange(steps_dev, dtype=jnp.int32)
    seq_ends = jnp.cumsum(lengths, axis=1)
    seq_starts = seq_ends - lengths
    seq_lasts = seq_ends - 1

    def kept_where(table, offset):
        matched = jnp.any((positions + offset)[None, :, None] == table[:, None, :], axis=2)
        return (1.0 - matched.astype(jnp.float32))[:, :, None]

    keep_forward = (kept_where(seq_starts, 0), kept_where(seq_lasts, 0))
    keep_adjoint = (kept_where(seq_starts, 1), kept_where(seq_lasts, -1))
    current = x_in.astype(jnp.float32)
    saved_all = []
    for block_index in range(2):
        flat_in = current.reshape(-1, width)
        total_sum, square_sum = lax.psum(
            (jnp.sum(flat_in, axis=0), jnp.sum(flat_in * flat_in, axis=0)), ("tm", "rows")
        )
        mean_vec = total_sum / tokens_all
        inv_std = lax.rsqrt(square_sum / tokens_all - mean_vec * mean_vec + norm_eps)
        normed = (flat_in - mean_vec) * inv_std
        scaled = bn_gain[block_index] * normed + bn_bias[block_index]
        scaled_low = scaled.astype(jnp.bfloat16)
        projected = times_weight(scaled_low, w_in[block_index])
        lam_re, lam_im, norm_factor = lam_terms(decay_rate[block_index], phase[block_index])
        keep_mask = keep_forward[block_index]
        drive_re = (norm_factor * projected[:, :states]).reshape(row_count, steps_dev, states)
        drive_im = (norm_factor * projected[:, states:]).reshape(row_count, steps_dev, states)
        state_re, state_im, carry_re, carry_im = linear_scan(
            keep_mask * lam_re, keep_mask * lam_im, drive_re, drive_im, block_index == 1
        )
        states_low = (
            jnp.concatenate([state_re, state_im], axis=2)
            .reshape(-1, 2 * states)
            .astype(jnp.bfloat16)
        )
        mixed = times_weight(states_low, w_out[block_index]) + skip_gain[block_index] * scaled
        active_low = gelu_exact(mixed).astype(jnp.bfloat16)
        gate_pre = times_weight(active_low, w_glu[block_index]) + b_glu[block_index]
        current = current + glu_gate(gate_pre).reshape(row_count, steps_dev, width)
        saved_all.append(
            (
                normed,
                inv_std,
                scaled_low,
                projected,
                state_re,
                state_im,
                carry_re,
                carry_im,
                states_low,
                mixed,
                active_low,
                gate_pre,
            )
        )
    result = current.astype(jnp.bfloat16)
    upstream = grad_out.astype(jnp.float32).reshape(-1, width)
    weight_grads = [None, None]
    gain_grads = [None, None]
    bias_grads = [None, None]
    for block_index in (1, 0):
        (
            normed,
            inv_std,
            scaled_low,
            projected,
            state_re,
            state_im,
            carry_re,
            carry_im,
            states_low,
            mixed,
            active_low,
            gate_pre,
        ) = saved_all[block_index]
        gain_vec = bn_gain[block_index]
        _, glu_pull = jax.vjp(glu_gate, gate_pre)
        gate_grad = glu_pull(upstream)[0]
        grad_bglu = jnp.sum(gate_grad, axis=0)
        gate_low = gate_grad.astype(jnp.bfloat16)
        grad_wglu = outer_sum(active_low, gate_low)
        active_grad = times_transposed(gate_low, w_glu[block_index])
        _, gelu_pull = jax.vjp(gelu_exact, mixed)
        mixed_grad = gelu_pull(active_grad)[0]
        scaled = gain_vec * normed + bn_bias[block_index]
        grad_skip = jnp.sum(mixed_grad * scaled, axis=0)
        mixed_low = mixed_grad.astype(jnp.bfloat16)
        grad_wout = outer_sum(states_low, mixed_low)
        state_grad = times_transposed(mixed_low, w_out[block_index])
        lam_re, lam_im, norm_factor = lam_terms(decay_rate[block_index], phase[block_index])
        adjoint_mask = keep_adjoint[block_index]
        adjoint_re, adjoint_im, _, _ = linear_scan(
            adjoint_mask * lam_re,
            adjoint_mask * -lam_im,
            state_grad[:, :states].reshape(row_count, steps_dev, states),
            state_grad[:, states:].reshape(row_count, steps_dev, states),
            block_index == 0,
        )
        proj_re = projected[:, :states].reshape(row_count, steps_dev, states)
        proj_im = projected[:, states:].reshape(row_count, steps_dev, states)
        factor_grad = jnp.sum(adjoint_re * proj_re + adjoint_im * proj_im, axis=(0, 1))
        if block_index == 0:
            near_re = jnp.concatenate([carry_re[:, None], state_re[:, :-1]], axis=1)
            near_im = jnp.concatenate([carry_im[:, None], state_im[:, :-1]], axis=1)
        else:
            near_re = jnp.concatenate([state_re[:, 1:], carry_re[:, None]], axis=1)
            near_im = jnp.concatenate([state_im[:, 1:], carry_im[:, None]], axis=1)
        keep_mask = keep_forward[block_index]
        lam_grad_re = jnp.sum(
            keep_mask * (adjoint_re * near_re + adjoint_im * near_im), axis=(0, 1)
        )
        lam_grad_im = jnp.sum(
            keep_mask * (adjoint_im * near_re - adjoint_re * near_im), axis=(0, 1)
        )
        _, lam_pull = jax.vjp(lam_terms, decay_rate[block_index], phase[block_index])
        grad_rate, grad_phase = lam_pull((lam_grad_re, lam_grad_im, factor_grad))
        both_factor = jnp.concatenate([norm_factor, norm_factor])
        proj_low = (
            (jnp.concatenate([adjoint_re, adjoint_im], axis=2) * both_factor)
            .reshape(-1, 2 * states)
            .astype(jnp.bfloat16)
        )
        grad_win = outer_sum(scaled_low, proj_low)
        scaled_grad = (
            times_transposed(proj_low, w_in[block_index]) + skip_gain[block_index] * mixed_grad
        )
        bias_term = jnp.sum(scaled_grad, axis=0)
        gain_term = jnp.sum(scaled_grad * normed, axis=0)
        summed = lax.psum(
            (
                bias_term,
                gain_term,
                grad_win,
                grad_rate,
                grad_phase,
                grad_wout,
                grad_skip,
                grad_wglu,
                grad_bglu,
            ),
            ("tm", "rows"),
        )
        bias_total = summed[0]
        gain_total = summed[1]
        weight_grads[block_index] = summed[2:]
        bias_grads[block_index] = bias_total
        gain_grads[block_index] = gain_total
        upstream = (
            inv_std
            * (
                gain_vec * scaled_grad
                - gain_vec * bias_total / tokens_all
                - normed * gain_vec * gain_total / tokens_all
            )
            + upstream
        )
    stacked = [
        jnp.stack([weight_grads[0][member_index], weight_grads[1][member_index]])
        for member_index in range(7)
    ]
    grad_input = upstream.reshape(row_count, steps_dev, width)
    return (
        result,
        grad_input,
        jnp.stack(gain_grads),
        jnp.stack(bias_grads),
        stacked[0],
        stacked[1],
        stacked[2],
        stacked[3],
        stacked[4],
        stacked[5],
        stacked[6],
    )


def solution(mesh):
    placed = (
        P("rows", "tm", None),
        P("rows", None),
        P(),
        P(),
        P(),
        P(),
        P(),
        P(),
        P(),
        P(),
        P(),
        P("rows", "tm", None),
    )
    return jax.shard_map(
        body,
        mesh=mesh,
        in_specs=placed,
        out_specs=(
            P("rows", "tm", None),
            P("rows", "tm", None),
            P(),
            P(),
            P(),
            P(),
            P(),
            P(),
            P(),
            P(),
            P(),
        ),
        check_vma=False,
    )
```

profile of v0, /device:TPU:0, one launch (start us, length us, event | category | flops | bytes accessed | tf_op | source)
XLA Modules:
  0.0 1275.1 jit_solution(7595005419896533725)
XLA Ops:
  12.3 42.0 %all-reduce.231 = (f32[512]{0:T(512)S(1)}, f32[512]{0:T(512)S(1)}) all-reduce(f32[512]{0:T(512)S(1)} %get-tuple-element.436, f32[512]{0:T(512)S(1)} %get-tuple-element.435), channel_id=1, replica_groups=mesh['tm'=8,'rows'=4] {'tm','rows'}, use_global_device_ids=true, to_apply=%region_3.4 | all-reduce | flops 1024 | bytes 8192 | tf_op jit(solution)/shard_map/psum | solution.py:137
  90.0 26.0 %all-gather = f32[16,1,256]{2,1,0:T(1,128)S(1)} all-gather(f32[2,1,256]{2,1,0:T(1,128)S(1)} %slice_add_fusion.107), channel_id=2, replica_groups=mesh['tm'=8,'rows'=4] {'tm'}, dimensions={0}, use_global_device_ids=true | all-gather | bytes 18432 | tf_op jit(solution)/shard_map/all_gather | solution.py:13
  117.7 26.0 %all-gather.1 = f32[16,1,256]{2,1,0:T(1,128)S(1)} all-gather(f32[2,1,256]{2,1,0:T(1,128)S(1)} %slice_add_fusion.106), channel_id=3, replica_groups=mesh['tm'=8,'rows'=4] {'tm'}, dimensions={0}, use_global_device_ids=true | all-gather | bytes 18432 | tf_op jit(solution)/shard_map/all_gather | solution.py:13
  162.5 26.0 %all-gather.2 = f32[16,1,256]{2,1,0:T(1,128)S(1)} all-gather(f32[2,1,256]{2,1,0:T(1,128)S(1)} %slice_add_fusion.105), channel_id=4, replica_groups=mesh['tm'=8,'rows'=4] {'tm'}, dimensions={0}, use_global_device_ids=true | all-gather | bytes 18432 | tf_op jit(solution)/shard_map/all_gather | solution.py:13
  191.7 2.3 pad.755
  194.6 26.0 %all-gather.3 = f32[16,1,256]{2,1,0:T(1,128)S(1)} all-gather(f32[2,1,256]{2,1,0:T(1,128)S(1)} %slice_add_fusion.104), channel_id=5, replica_groups=mesh['tm'=8,'rows'=4] {'tm'}, dimensions={0}, use_global_device_ids=true | all-gather | bytes 18432 | tf_op jit(solution)/shard_map/all_gather | solution.py:13
  223.2 2.0 fusion.128
  231.9 3.5 multiply_convert_fusion.1
  236.1 41.1 %all-reduce.230 = (f32[512]{0:T(512)}, f32[512]{0:T(512)}) all-reduce(f32[512]{0:T(512)S(1)} %get-tuple-element.433, f32[512]{0:T(512)S(1)} %get-tuple-element.432), channel_id=1, replica_groups=mesh['tm'=8,'rows'=4] {'tm','rows'}, use_global_device_ids=true, to_apply=%region_11.12 | all-reduce | flops 1024 | bytes 8192 | tf_op jit(solution)/shard_map/psum | solution.py:137
  339.7 26.0 %all-gather.4 = f32[16,1,256]{2,1,0:T(1,128)S(1)} all-gather(f32[2,1,256]{2,1,0:T(1,128)S(1)} %copy-done.144), channel_id=6, replica_groups=mesh['tm'=8,'rows'=4] {'tm'}, dimensions={0}, use_global_device_ids=true | all-gather | bytes 18432 | tf_op jit(solution)/shard_map/all_gather | solution.py:13
  368.1 27.0 %all-gather.5 = f32[16,1,256]{2,1,0:T(1,128)} all-gather(f32[2,1,256]{2,1,0:T(1,128)} %slice_add_fusion.98), channel_id=7, replica_groups=mesh['tm'=8,'rows'=4] {'tm'}, dimensions={0}, use_global_device_ids=true | all-gather | bytes 18432 | tf_op jit(solution)/shard_map/all_gather | solution.py:13
  397.8 3.0 rev.32
  400.8 27.0 %all-gather.6 = f32[16,1,256]{2,1,0:T(1,128)} all-gather(f32[2,1,256]{2,1,0:T(1,128)} %slice_add_fusion.97), channel_id=8, replica_groups=mesh['tm'=8,'rows'=4] {'tm'}, dimensions={0}, use_global_device_ids=true | all-gather | bytes 18432 | tf_op jit(solution)/shard_map/all_gather | solution.py:13
  430.5 3.0 rev.35
  433.4 26.8 %all-gather.7 = f32[16,1,256]{2,1,0:T(1,128)} all-gather(f32[2,1,256]{2,1,0:T(1,128)S(1)} %copy-done.145), channel_id=9, replica_groups=mesh['tm'=8,'rows'=4] {'tm'}, dimensions={0}, use_global_device_ids=true | all-gather | bytes 18432 | tf_op jit(solution)/shard_map/all_gather | solution.py:13
  462.9 5.1 while.65
  469.2 1.9 fusion.126
  471.8 2.2 multiply_convert_fusion
  491.1 2.1 add_add_fusion.3
  609.3 1.9 pad.844
  613.1 1.9 pad.845
  620.9 1.9 pad.848
  622.8 1.9 pad.850
  634.6 1.9 pad.852
  636.5 1.9 pad.854
  638.4 1.9 pad.853
  640.4 1.9 pad.855
  648.5 2.0 pad.856
  650.5 2.0 pad.858
  652.4 2.0 pad.857
  654.4 2.0 pad.859
  663.0 2.1 pad.860
  665.1 2.1 pad.862
  667.2 2.1 pad.861
  669.3 2.1 pad.863
  678.6 2.3 pad.865
  681.6 26.0 %all-gather.8 = f32[16,1,256]{2,1,0:T(1,128)S(1)} all-gather(f32[2,1,256]{2,1,0:T(1,128)S(1)} %slice_add_fusion.91), channel_id=10, replica_groups=mesh['tm'=8,'rows'=4] {'tm'}, dimensions={0}, use_global_device_ids=true | all-gather | bytes 18432 | tf_op jit(solution)/shard_map/all_gather | solution.py:13
  710.6 2.3 pad.867
  713.7 26.0 %all-gather.9 = f32[16,1,256]{2,1,0:T(1,128)S(1)} all-gather(f32[2,1,256]{2,1,0:T(1,128)S(1)} %slice_add_fusion.90), channel_id=11, replica_groups=mesh['tm'=8,'rows'=4] {'tm'}, dimensions={0}, use_global_device_ids=true | all-gather | bytes 18432 | tf_op jit(solution)/shard_map/all_gather | solution.py:13
  753.6 2.0 pad.831
  755.6 2.0 pad.833
  763.6 2.1 pad.836
  765.7 2.1 pad.835
  767.8 2.1 pad.837
  773.1 1.9 add_add_fusion.2
  776.5 2.3 pad.839
  779.5 26.0 %all-gather.10 = f32[16,1,256]{2,1,0:T(1,128)S(1)} all-gather(f32[2,1,256]{2,1,0:T(1,128)S(1)} %slice_add_fusion.89), channel_id=12, replica_groups=mesh['tm'=8,'rows'=4] {'tm'}, dimensions={0}, use_global_device_ids=true | all-gather | bytes 18432 | tf_op jit(solution)/shard_map/all_gather | solution.py:13
  807.9 2.3 pad.869
  811.0 26.0 %all-gather.11 = f32[16,1,256]{2,1,0:T(1,128)S(1)} all-gather(f32[2,1,256]{2,1,0:T(1,128)S(1)} %slice_add_fusion.88), channel_id=13, replica_groups=mesh['tm'=8,'rows'=4] {'tm'}, dimensions={0}, use_global_device_ids=true | all-gather | bytes 18432 | tf_op jit(solution)/shard_map/all_gather | solution.py:13
  837.1 2.2 multiply_reduce_fusion.7
  843.1 41.2 %all-reduce.229 = (f32[512]{0:T(512)S(1)}, f32[512]{0:T(512)S(1)}) all-reduce(f32[512]{0:T(512)S(1)} %get-tuple-element.426, f32[512]{0:T(512)S(1)} %get-tuple-element.427), channel_id=1, replica_groups=mesh['tm'=8,'rows'=4] {'tm','rows'}, use_global_device_ids=true, to_apply=%region_21.22 | all-reduce | flops 1024 | bytes 8192 | tf_op jit(solution)/shard_map/psum | solution.py:251
  952.2 2.9 convolution_bitcast_fusion.1
  958.2 2.9 rev.37
  961.2 26.0 %all-gather.12 = f32[16,1,256]{2,1,0:T(1,128)S(1)} all-gather(f32[2,1,256]{2,1,0:T(1,128)S(1)} %copy-done.142), channel_id=14, replica_groups=mesh['tm'=8,'rows'=4] {'tm'}, dimensions={0}, use_global_device_ids=true | all-gather | bytes 18432 | tf_op jit(solution)/shard_map/all_gather | solution.py:13
  987.2 3.0 rev.38
  990.2 26.0 %all-gather.13 = f32[16,1,256]{2,1,0:T(1,128)S(1)} all-gather(f32[2,1,256]{2,1,0:T(1,128)S(1)} %copy-done.143), channel_id=15, replica_groups=mesh['tm'=8,'rows'=4] {'tm'}, dimensions={0}, use_global_device_ids=true | all-gather | bytes 18432 | tf_op jit(solution)/shard_map/all_gather | solution.py:13
  1016.3 3.0 rev.36
  1019.3 26.0 %all-gather.14 = f32[16,1,256]{2,1,0:T(1,128)S(1)} all-gather(f32[2,1,256]{2,1,0:T(1,128)S(1)} %slice_add_fusion.81), channel_id=16, replica_groups=mesh['tm'=8,'rows'=4] {'tm'}, dimensions={0}, use_global_device_ids=true | all-gather | bytes 18432 | tf_op jit(solution)/shard_map/all_gather | solution.py:13
  1045.4 3.0 rev.39
  1048.3 26.0 %all-gather.15 = f32[16,1,256]{2,1,0:T(1,128)S(1)} all-gather(f32[2,1,256]{2,1,0:T(1,128)S(1)} %slice_add_fusion.80), channel_id=17, replica_groups=mesh['tm'=8,'rows'=4] {'tm'}, dimensions={0}, use_global_device_ids=true | all-gather | bytes 18432 | tf_op jit(solution)/shard_map/all_gather | solution.py:13
  1081.3 40.4 %all-reduce.228 = (f32[512]{0:T(512)S(1)}, f32[512]{0:T(512)S(1)}, f32[1,256]{1,0:T(1,128)S(1)}, f32[1,256]{1,0:T(1,128)S(1)}, f32[1,256]{1,0:T(1,128)S(1)}, /*i...) all-reduce(f32[512]{0:T(512)S(1)} %get-tuple-element.431, ...), channel_id=1, replica_groups=mesh['tm'=8,'rows'=4] {'tm','rows'}, use_global_device_ids=true, to_apply=%region_28.29 | all-reduce | flops 5120 | bytes 40960 | tf_op jit(solution)/shard_map/psum | solution.py:251
  1127.1 132.3 %all-reduce.235.cloned.1.call-done = (f32[1,512,512]{2,1,0:T(8,128)}, f32[1,512,512]{2,1,0:T(8,128)}, f32[1,512,512]{2,1,0:T(8,128)}, f32[1,512,512]{2,1,0:T(8,1...) async-done(((f32[1,512,512]{2,1,0:T(8,128)}, f32[1,512,512]{2,1,0:T(8,128)}, f32[1,512,512]{2,1,0:T(8,128)}, f32[1,512,512]{2,1,0:T(8,128)}, ...) | async-done | bytes 8388624 | tf_op jit(solution)/shard_map/psum | solution.py:251
  1259.3 3.2 pad_maximum_fusion.1
  1265.5 2.3 pad_maximum_fusion
  (1306 shorter events, 445.1 us)
Async XLA Ops:
  7.2 1252.1 %all-reduce.235.cloned.1.call-start = ((), (), s32[]{:S(2)}) async-start(), calls=%async_computation | async-start | bytes 16777216 | tf_op jit(solution)/shard_map/psum | solution.py:251
  8.6 50.9 %copy-start.91 = (f32[1,512]{1,0:T(1,128)}, f32[1,512]{1,0:T(1,128)S(1)}, u32[]{:S(2)}) copy-start(f32[1,512]{1,0:T(1,128)S(1)} %get-tuple-element.857) | copy-start | bytes 6148
  9.9 49.6 %copy-start.106 = (f32[1,512]{1,0:T(1,128)}, f32[1,512]{1,0:T(1,128)S(1)}, u32[]{:S(2)}) copy-start(f32[1,512]{1,0:T(1,128)S(1)} %get-tuple-element.859) | copy-start | bytes 6148
  12.3 47.8 %copy-start.119 = (f32[1,256]{1,0:T(1,128)}, f32[1,256]{1,0:T(1,128)S(1)}, u32[]{:S(2)}) copy-start(f32[1,256]{1,0:T(1,128)S(1)} %get-tuple-element.862) | copy-start | bytes 3076
  12.3 58.0 %copy-start.117 = (f32[1,256]{1,0:T(1,128)}, f32[1,256]{1,0:T(1,128)S(1)}, u32[]{:S(2)}) copy-start(f32[1,256]{1,0:T(1,128)S(1)} %get-tuple-element.861) | copy-start | bytes 3076
  59.7 172.3 %copy-start.15 = (f32[256,512]{1,0:T(8,128)}, f32[256,512]{1,0:T(8,128)S(1)}, u32[]{:S(2)}) copy-start(f32[256,512]{1,0:T(8,128)S(1)} %fusion.63) | copy-start | bytes 1572868
  61.0 613.6 %copy-start.25 = (f32[2,63,256]{2,1,0:T(8,128)}, f32[2,63,256]{2,1,0:T(8,128)S(1)}, u32[]{:S(2)}) copy-start(f32[2,63,256]{2,1,0:T(8,128)S(1)} %slice.2170) | copy-start | bytes 387076
  75.1 13.6 %copy-start.47 = (f32[2,31,256]{2,1,0:T(8,128)}, f32[2,31,256]{2,1,0:T(8,128)S(1)}, u32[]{:S(2)}) copy-start(f32[2,31,256]{2,1,0:T(8,128)S(1)} %slice.1962) | copy-start | bytes 190468
  75.2 13.6 %copy-start.49 = (f32[2,31,256]{2,1,0:T(8,128)}, f32[2,31,256]{2,1,0:T(8,128)S(1)}, u32[]{:S(2)}) copy-start(f32[2,31,256]{2,1,0:T(8,128)S(1)} %slice.1883) | copy-start | bytes 190468
  88.8 27.9 %copy-start.136 = (f32[2,1,256]{2,1,0:T(1,128)S(1)}, f32[2,1,256]{2,1,0:T(1,128)}, u32[]{:S(2)}) copy-start(f32[2,1,256]{2,1,0:T(1,128)} %slice.2538) | copy-start | bytes 6148
  89.8 62.5 %copy-start.68 = (f32[2,15,256]{2,1,0:T(8,128)S(1)}, f32[2,15,256]{2,1,0:T(8,128)}, u32[]{:S(2)}) copy-start(f32[2,15,256]{2,1,0:T(8,128)} %copy-done.67) | copy-start | bytes 92164
  89.8 62.5 %copy-start.70 = (f32[2,15,256]{2,1,0:T(8,128)S(1)}, f32[2,15,256]{2,1,0:T(8,128)}, u32[]{:S(2)}) copy-start(f32[2,15,256]{2,1,0:T(8,128)} %copy-done.69) | copy-start | bytes 92164
  89.8 62.5 %copy-start.79 = (f32[2,15,256]{2,1,0:T(8,128)S(1)}, f32[2,15,256]{2,1,0:T(8,128)}, u32[]{:S(2)}) copy-start(f32[2,15,256]{2,1,0:T(8,128)} %slice.1964) | copy-start | bytes 92164
  89.8 62.5 %copy-start.80 = (f32[2,15,256]{2,1,0:T(8,128)S(1)}, f32[2,15,256]{2,1,0:T(8,128)}, u32[]{:S(2)}) copy-start(f32[2,15,256]{2,1,0:T(8,128)} %slice.1960) | copy-start | bytes 92164
  89.9 65.3 %copy-start.48 = (f32[2,31,256]{2,1,0:T(8,128)S(1)}, f32[2,31,256]{2,1,0:T(8,128)}, u32[]{:S(2)}) copy-start(f32[2,31,256]{2,1,0:T(8,128)} %copy-done.47) | copy-start | bytes 190468
  89.9 65.3 %copy-start.50 = (f32[2,31,256]{2,1,0:T(8,128)S(1)}, f32[2,31,256]{2,1,0:T(8,128)}, u32[]{:S(2)}) copy-start(f32[2,31,256]{2,1,0:T(8,128)} %copy-done.49) | copy-start | bytes 190468
  156.8 32.4 %copy-start.123 = (f32[2,1,256]{2,1,0:T(1,128)S(1)}, f32[2,1,256]{2,1,0:T(1,128)}, u32[]{:S(2)}) copy-start(f32[2,1,256]{2,1,0:T(1,128)} %slice.2543) | copy-start | bytes 6148
  235.4 42.6 %copy-start.88 = (f32[1,512]{1,0:T(1,128)S(1)}, f32[1,512]{1,0:T(1,128)}, u32[]{:S(2)}) copy-start(f32[1,512]{1,0:T(1,128)} %get-tuple-element.856) | copy-start | bytes 6148
  235.4 42.6 %copy-start.103 = (f32[1,512]{1,0:T(1,128)S(1)}, f32[1,512]{1,0:T(1,128)}, u32[]{:S(2)}) copy-start(f32[1,512]{1,0:T(1,128)} %get-tuple-element.858) | copy-start | bytes 6148
  235.4 43.1 %copy-start.10 = (bf16[2,512,512]{2,1,0:T(8,128)(2,1)S(1)}, bf16[2,512,512]{2,1,0:T(8,128)(2,1)}, u32[]{:S(2)}) copy-start(bf16[2,512,512]{2,1,0:T(8,128)(2,1)} %param.24) | copy-start | bytes 3145732
  293.0 17.8 %copy-start.43 = (f32[2,31,256]{2,1,0:T(8,128)}, f32[2,31,256]{2,1,0:T(8,128)S(1)}, u32[]{:S(2)}) copy-start(f32[2,31,256]{2,1,0:T(8,128)S(1)} %slice.2116) | copy-start | bytes 190468
  293.7 17.2 %copy-start.45 = (f32[2,31,256]{2,1,0:T(8,128)}, f32[2,31,256]{2,1,0:T(8,128)S(1)}, u32[]{:S(2)}) copy-start(f32[2,31,256]{2,1,0:T(8,128)S(1)} %slice.2036) | copy-start | bytes 190468
  296.2 13.6 %copy-start.54 = (f32[2,63,256]{2,1,0:T(8,128)S(1)}, f32[2,63,256]{2,1,0:T(8,128)}, u32[]{:S(2)}) copy-start(f32[2,63,256]{2,1,0:T(8,128)} %slice.2018) | copy-start | bytes 387076
  316.4 14.7 %copy-start.44 = (f32[2,31,256]{2,1,0:T(8,128)S(1)}, f32[2,31,256]{2,1,0:T(8,128)}, u32[]{:S(2)}) copy-start(f32[2,31,256]{2,1,0:T(8,128)} %copy-done.43) | copy-start | bytes 190468
  316.4 14.7 %copy-start.46 = (f32[2,31,256]{2,1,0:T(8,128)S(1)}, f32[2,31,256]{2,1,0:T(8,128)}, u32[]{:S(2)}) copy-start(f32[2,31,256]{2,1,0:T(8,128)} %copy-done.45) | copy-start | bytes 190468
  317.8 13.4 %copy-start.71 = (f32[2,31,256]{2,1,0:T(8,128)S(1)}, f32[2,31,256]{2,1,0:T(8,128)}, u32[]{:S(2)}) copy-start(f32[2,31,256]{2,1,0:T(8,128)} %slice.2125) | copy-start | bytes 190468
  317.8 13.4 %copy-start.73 = (f32[2,31,256]{2,1,0:T(8,128)S(1)}, f32[2,31,256]{2,1,0:T(8,128)}, u32[]{:S(2)}) copy-start(f32[2,31,256]{2,1,0:T(8,128)} %slice.2120) | copy-start | bytes 190468
  317.8 13.4 %copy-start.132 = (f32[2,1,256]{2,1,0:T(1,128)S(1)}, f32[2,1,256]{2,1,0:T(1,128)}, u32[]{:S(2)}) copy-start(f32[2,1,256]{2,1,0:T(1,128)} %slice.2592) | copy-start | bytes 6148
  317.8 13.5 %copy-start.134 = (f32[2,1,256]{2,1,0:T(1,128)S(1)}, f32[2,1,256]{2,1,0:T(1,128)}, u32[]{:S(2)}) copy-start(f32[2,1,256]{2,1,0:T(1,128)} %slice.2551) | copy-start | bytes 6148
  338.0 95.5 %copy-start.145 = (f32[2,1,256]{2,1,0:T(1,128)S(1)}, f32[2,1,256]{2,1,0:T(1,128)}, u32[]{:S(2)}) copy-start(f32[2,1,256]{2,1,0:T(1,128)} %slice_add_fusion.96) | copy-start | bytes 6148
  368.1 103.7 %copy-start.89 = (f32[1,512]{1,0:T(1,128)S(1)}, f32[1,512]{1,0:T(1,128)}, u32[]{:S(2)}) copy-start(f32[1,512]{1,0:T(1,128)} %get-tuple-element.856) | copy-start | bytes 6148
  368.1 103.7 %copy-start.104 = (f32[1,512]{1,0:T(1,128)S(1)}, f32[1,512]{1,0:T(1,128)}, u32[]{:S(2)}) copy-start(f32[1,512]{1,0:T(1,128)} %get-tuple-element.858) | copy-start | bytes 6148
  746.7 14.8 %copy-start.130 = (f32[2,1,256]{2,1,0:T(1,128)S(1)}, f32[2,1,256]{2,1,0:T(1,128)}, u32[]{:S(2)}) copy-start(f32[2,1,256]{2,1,0:T(1,128)} %slice.2688) | copy-start | bytes 6148
  746.7 15.4 %copy-start.131 = (f32[2,1,256]{2,1,0:T(1,128)S(1)}, f32[2,1,256]{2,1,0:T(1,128)}, u32[]{:S(2)}) copy-start(f32[2,1,256]{2,1,0:T(1,128)} %slice.2647) | copy-start | bytes 6148
  757.6 17.5 %copy-start.129 = (f32[2,1,256]{2,1,0:T(1,128)S(1)}, f32[2,1,256]{2,1,0:T(1,128)}, u32[]{:S(2)}) copy-start(f32[2,1,256]{2,1,0:T(1,128)} %slice.2645) | copy-start | bytes 6148
  810.2 29.1 %copy-start.114 = (f32[1,256]{1,0:T(1,128)S(1)}, f32[1,256]{1,0:T(1,128)}, u32[]{:S(2)}) copy-start(f32[1,256]{1,0:T(1,128)} %copy-done.113) | copy-start | bytes 3076
  810.2 29.1 %copy-start.116 = (f32[1,256]{1,0:T(1,128)S(1)}, f32[1,256]{1,0:T(1,128)}, u32[]{:S(2)}) copy-start(f32[1,256]{1,0:T(1,128)} %copy-done.115) | copy-start | bytes 3076
  810.2 29.1 %copy-start.120 = (f32[1,256]{1,0:T(1,128)S(1)}, f32[1,256]{1,0:T(1,128)}, u32[]{:S(2)}) copy-start(f32[1,256]{1,0:T(1,128)} %copy-done.119) | copy-start | bytes 3076
  810.2 29.1 %copy-start.158 = (f32[1,256]{1,0:T(1,128)S(1)}, f32[1,256]{1,0:T(1,128)}, u32[]{:S(2)}) copy-start(f32[1,256]{1,0:T(1,128)} %get-tuple-element.542) | copy-start | bytes 3076
  810.2 29.7 %copy-start.90 = (f32[1,512]{1,0:T(1,128)S(1)}, f32[1,512]{1,0:T(1,128)}, u32[]{:S(2)}) copy-start(f32[1,512]{1,0:T(1,128)} %get-tuple-element.856) | copy-start | bytes 6148
  810.2 29.7 %copy-start.105 = (f32[1,512]{1,0:T(1,128)S(1)}, f32[1,512]{1,0:T(1,128)}, u32[]{:S(2)}) copy-start(f32[1,512]{1,0:T(1,128)} %get-tuple-element.858) | copy-start | bytes 6148
  810.3 29.7 %copy-start.150 = (f32[1,512]{1,0:T(1,128)S(1)}, f32[1,512]{1,0:T(1,128)}, u32[]{:S(2)}) copy-start(f32[1,512]{1,0:T(1,128)} %get-tuple-element.853) | copy-start | bytes 6148
  840.0 44.3 %copy-start.95 = (f32[512]{0:T(512)S(1)}, f32[512]{0:T(512)}, u32[]{:S(2)}) copy-start(f32[512]{0:T(512)} %copy-done.93) | copy-start | bytes 6148
  840.0 44.3 %copy-start.98 = (f32[512]{0:T(512)S(1)}, f32[512]{0:T(512)}, u32[]{:S(2)}) copy-start(f32[512]{0:T(512)} %copy-done.96) | copy-start | bytes 6148
  887.8 13.4 %copy-start.13 = (f32[256,512]{1,0:T(8,128)}, f32[256,512]{1,0:T(8,128)S(1)}, u32[]{:S(2)}) copy-start(f32[256,512]{1,0:T(8,128)S(1)} %multiply_add_fusion.1) | copy-start | bytes 1572868
  887.8 14.2 %copy-start.52 = (f32[2,64,256]{2,1,0:T(8,128)S(1)}, f32[2,64,256]{2,1,0:T(8,128)}, u32[]{:S(2)}) copy-start(f32[2,64,256]{2,1,0:T(8,128)} %slice.2306) | copy-start | bytes 393220
  912.9 13.6 %copy-start.51 = (f32[2,63,256]{2,1,0:T(8,128)S(1)}, f32[2,63,256]{2,1,0:T(8,128)}, u32[]{:S(2)}) copy-start(f32[2,63,256]{2,1,0:T(8,128)} %slice.2304) | copy-start | bytes 387076
  931.9 13.8 %copy-start.72 = (f32[2,31,256]{2,1,0:T(8,128)S(1)}, f32[2,31,256]{2,1,0:T(8,128)}, u32[]{:S(2)}) copy-start(f32[2,31,256]{2,1,0:T(8,128)} %slice.2411) | copy-start | bytes 190468
  933.2 12.5 copy-start.74
  933.2 12.5 copy-start.133
  933.2 12.5 copy-start.135
  956.9 33.3 %copy-start.143 = (f32[2,1,256]{2,1,0:T(1,128)S(1)}, f32[2,1,256]{2,1,0:T(1,128)}, u32[]{:S(2)}) copy-start(f32[2,1,256]{2,1,0:T(1,128)} %slice_add_fusion.82) | copy-start | bytes 6148
  956.9 117.8 %copy-start.121 = (f32[2,1,256]{2,1,0:T(1,128)S(1)}, f32[2,1,256]{2,1,0:T(1,128)}, u32[]{:S(2)}) copy-start(f32[2,1,256]{2,1,0:T(1,128)} %broadcast_in_dim.14) | copy-start | bytes 6148
  956.9 117.8 %copy-start.122 = (f32[2,1,256]{2,1,0:T(1,128)S(1)}, f32[2,1,256]{2,1,0:T(1,128)}, u32[]{:S(2)}) copy-start(f32[2,1,256]{2,1,0:T(1,128)} %broadcast_in_dim.15) | copy-start | bytes 6148
  956.9 117.8 %copy-start.152 = (f32[2,128]{1,0:T(2,128)S(1)}, f32[2,128]{1,0:T(2,128)}, u32[]{:S(2)}) copy-start(f32[2,128]{1,0:T(2,128)} %copy-done.151) | copy-start | bytes 3076
  1016.2 60.2 %copy-start.110 = (f32[1,256]{1,0:T(1,128)S(1)}, f32[1,256]{1,0:T(1,128)}, u32[]{:S(2)}) copy-start(f32[1,256]{1,0:T(1,128)} %copy-done.109) | copy-start | bytes 3076
  1016.2 60.2 %copy-start.112 = (f32[1,256]{1,0:T(1,128)S(1)}, f32[1,256]{1,0:T(1,128)}, u32[]{:S(2)}) copy-start(f32[1,256]{1,0:T(1,128)} %copy-done.111) | copy-start | bytes 3076
  1016.3 60.2 %copy-start.118 = (f32[1,256]{1,0:T(1,128)S(1)}, f32[1,256]{1,0:T(1,128)}, u32[]{:S(2)}) copy-start(f32[1,256]{1,0:T(1,128)} %copy-done.117) | copy-start | bytes 3076
  1016.3 60.2 %copy-start.157 = (f32[1,256]{1,0:T(1,128)S(1)}, f32[1,256]{1,0:T(1,128)}, u32[]{:S(2)}) copy-start(f32[1,256]{1,0:T(1,128)} %get-tuple-element.864) | copy-start | bytes 3076
  1016.3 60.2 %copy-start.14 = (f32[256,512]{1,0:T(8,128)S(1)}, f32[256,512]{1,0:T(8,128)}, u32[]{:S(2)}) copy-start(f32[256,512]{1,0:T(8,128)} %copy-done.13) | copy-start | bytes 1572868
  1080.3 42.5 %copy-start.148 = (f32[512]{0:T(512)S(1)}, f32[512]{0:T(512)}, u32[]{:S(2)}) copy-start(f32[512]{0:T(512)} %copy-done.147) | copy-start | bytes 6148
  1080.3 43.1 %copy-start.141 = (f32[512]{0:T(512)S(1)}, f32[512]{0:T(512)}, u32[]{:S(2)}) copy-start(f32[512]{0:T(512)} %copy-done.140) | copy-start | bytes 6148
  1080.4 44.9 %copy-start.20 = (f32[256,512]{1,0:T(8,128)S(1)}, f32[256,512]{1,0:T(8,128)}, u32[]{:S(2)}) copy-start(f32[256,512]{1,0:T(8,128)} %get-tuple-element.562) | copy-start | bytes 1572868
  1080.8 45.2 %copy-start.3 = (f32[256,512]{1,0:T(8,128)S(1)}, f32[256,512]{1,0:T(8,128)}, u32[]{:S(2)}) copy-start(f32[256,512]{1,0:T(8,128)} %copy-done.2) | copy-start | bytes 1572868
  (100 other events, 423.6 us)
Sparse Core Ops, SparseCore 0:
  1079.4 179.8 all-reduce.234
where the time goes:
time: 1300 us; the launch traced here: 1280 us
  blocking collectives  583 us (45%)
  local copies, waits for them, and re-layouts  339 us (26%)
  other arithmetic  177 us (14%)
  waiting for transfers between devices  132 us (10%)
  matrix products  24.1 us (2%)
  between operations  19.2 us (1%)
    all_gather x16, blocking collectives, prefix(): gathered = jax.tree.map(lambda a: lax.all_gather(a, axis), part)  419 us
    slice x388, local copies, waits for them, and re-layouts, linear_scan(): lax.associative_scan(combine_pairs, (coef_re, coef_im, drive_re, drive_im...  200 us
    psum x1, waiting for transfers between devices, body(): lax.psum((bias_term, gain_term, grad_win, grad_rate, grad_phase, grad_wou...  132 us
    pad x192, local copies, waits for them, and re-layouts, linear_scan(): lax.associative_scan(combine_pairs, (coef_re, coef_im, drive_re, drive_im...  85.4 us
    psum x2, blocking collectives, body(): lax.psum((jnp.sum(flat_in, axis=0), jnp.sum(flat_in * flat_in, axis=0)),...  83.1 us
    psum x2, blocking collectives, body(): lax.psum((bias_term, gain_term, grad_win, grad_rate, grad_phase, grad_wou...  81.6 us
    add x120, other arithmetic, linear_scan(): lax.associative_scan(combine_pairs, (coef_re, coef_im, drive_re, drive_im...  48.4 us
    concatenate x96, other arithmetic, linear_scan(): lax.associative_scan(combine_pairs, (coef_re, coef_im, drive_re, drive_im...  45.2 us
  transfers between devices with their start and end apart: 1, of which 1 were waited for; matrix products, arithmetic and copies ran while one was open for 0% of the time, Pallas kernels for 0%

commit v1 on v0

v1 whole, which is shorter than its diff:
```python
import functools

import jax
import jax.numpy as jnp
from jax import lax
from jax.experimental import pallas as pl
from jax.experimental.pallas import tpu as pltpu
from jax.sharding import PartitionSpec as P

EPS = 1e-05
LANES = 128
CHUNKS = 8
TILE = 32
F32 = jnp.float32
BF16 = jnp.bfloat16
ROOT_HALF = 0.7071067811865476
ROOT_TWO_PI_INV = 0.3989422804014327


class Sizes:
    def __init__(self, rows, steps, width, states, count_tm, count_rows, per_row):
        self.R, self.S, self.D, self.N = rows, steps, width, states
        self.T = rows * steps
        self.L = steps // CHUNKS
        self.tm, self.rows = count_tm, count_rows
        self.all = count_tm * count_rows
        self.seqs = per_row
        self.half = states // LANES
        self.packed = rows * 2 * self.half
        self.stat = 2 * width // LANES
        self.tokens = self.T * self.all


def dot(a, b):
    return jnp.dot(a, b, preferred_element_type=F32)


def dot_t(a, b):
    return lax.dot_general(a, b, (((1,), (1,)), ((), ())), preferred_element_type=F32)


def dot_0(a, b):
    return lax.dot_general(a, b, (((0,), (0,)), ((), ())), preferred_element_type=F32)


def fold(a):
    return a.reshape(a.shape[0] // 8, 8, a.shape[1]).sum(0)


def wide(a, z):
    return jnp.concatenate([a] * z.half, axis=1)


def tiles(z, body, carry):
    def one(i, c):
        return body(pl.ds(pl.multiple_of(i * TILE, TILE), TILE), c)

    return lax.fori_loop(0, z.T // TILE, one, carry)


def pack(ref, rows):
    k = 0
    for row in rows:
        for i in range(row.shape[1] // LANES):
            ref[k : k + 1, :] = row[:, i * LANES : (i + 1) * LANES]
            k += 1


def unpack(ref, first, count):
    return jnp.concatenate([ref[first + i : first + i + 1, :] for i in range(count)], axis=1)


def spread(out_ref, tile_ref):
    value = tile_ref[...]
    for j in range(out_ref.shape[0]):
        out_ref[j] = value


def two_sums(recv_ref, tile_ref, z):
    tile_ref[...] = jnp.sum(recv_ref[...], axis=0)
    n = z.D // LANES
    return unpack(tile_ref, 0, n), unpack(tile_ref, n, n)


def step_rows(z, r, s):
    first = r * z.S + s * CHUNKS
    return slice(first, first + CHUNKS)


def to_steps(z, source, out_ref, natural_ref):
    lanes = z.D // LANES

    def split(rows, c):
        value = source(rows)
        for k in range(lanes):
            natural_ref[k, rows, :] = value[:, k * LANES : (k + 1) * LANES]
        return c

    tiles(z, split, 0)
    for r in range(z.R):
        for s in range(z.L):
            for k in range(lanes):
                out_ref[step_rows(z, r, s), k * LANES : (k + 1) * LANES] = natural_ref[k, pl.ds(r * z.S + s, CHUNKS, stride=z.L), :]


def to_time(z, source_ref, out_ref, natural_ref):
    lanes = z.D // LANES
    for r in range(z.R):
        for s in range(z.L):
            for k in range(lanes):
                natural_ref[k, pl.ds(r * z.S + s, CHUNKS, stride=z.L), :] = source_ref[step_rows(z, r, s), k * LANES : (k + 1) * LANES]

    def join(rows, c):
        value = jnp.concatenate([natural_ref[k, rows, :] for k in range(lanes)], axis=1)
        out_ref[rows, :] = value.astype(out_ref.dtype)
        return c

    tiles(z, join, 0)


def pair_store(z, ref):
    held = {}

    def put(r, s, re, im):
        if (r, s ^ 1) not in held:
            held[r, s] = (re, im)
            return
        other = held.pop((r, s ^ 1))
        low, high = (other, (re, im)) if s & 1 else ((re, im), other)
        rows = slice(r * z.S + (s & ~1) * CHUNKS, r * z.S + ((s & ~1) + 2) * CHUNKS)
        ref[rows, 0 : z.N] = jnp.concatenate([low[0], high[0]], axis=0).astype(ref.dtype)
        ref[rows, z.N : 2 * z.N] = jnp.concatenate([low[1], high[1]], axis=0).astype(ref.dtype)

    return put


def scan(z, drive_ref, gain, lr, li, keep_ref, state, reverse, visit=None):
    for step in range(z.L):
        s = z.L - 1 - step if reverse else step
        for r in range(z.R):
            rows = step_rows(z, r, s)
            keep = wide(keep_ref[rows, :], z)
            ur = drive_ref[rows, 0 : z.N]
            ui = drive_ref[rows, z.N : 2 * z.N]
            if gain is not None:
                ur, ui = ur * gain, ui * gain
            hr, hi = keep * state[r][0], keep * state[r][1]
            state[r] = (lr * hr - li * hi + ur, lr * hi + li * hr + ui)
            if visit is not None:
                visit(r, s, rows, *state[r])
    return state


def zeros_state(z):
    return [(jnp.zeros((CHUNKS, z.N), F32), jnp.zeros((CHUNKS, z.N), F32)) for _ in range(z.R)]


def chunk_order(reverse):
    return range(CHUNKS - 1, -1, -1) if reverse else range(CHUNKS)


def end_state(z, state, ends_ref, chunk_keep_ref, pr, pi, reverse):
    rows = []
    for r in range(z.R):
        ends_ref[r * CHUNKS : (r + 1) * CHUNKS, 0 : z.N] = state[r][0]
        ends_ref[r * CHUNKS : (r + 1) * CHUNKS, z.N : 2 * z.N] = state[r][1]
    for r in range(z.R):
        cr = ci = None
        for c in chunk_order(reverse):
            k = r * CHUNKS + c
            er, ei = ends_ref[k : k + 1, 0 : z.N], ends_ref[k : k + 1, z.N : 2 * z.N]
            if cr is None:
                cr, ci = er, ei
            else:
                keep = wide(chunk_keep_ref[k : k + 1, :], z)
                cr, ci = keep * cr, keep * ci
                cr, ci = pr * cr - pi * ci + er, pr * ci + pi * cr + ei
        rows += [cr, ci]
    return rows


def carries(z, recv_ref, device_keep_ref, power_ref, b, sign, ends_ref, chunk_keep_ref, pr, pi, tile_ref, carry_ref, reverse):
    place = lax.axis_index("tm")
    pow_re = power_ref[2 * b]
    pow_im = sign * power_ref[2 * b + 1]
    is_re = (lax.broadcasted_iota(jnp.int32, (z.packed, LANES), 0) // z.half) % 2 == 0

    def hop(i, c):
        j = z.tm - 1 - i if reverse else i
        other = jnp.where(is_re, pltpu.roll(c, z.packed - z.half, 0), pltpu.roll(c, z.half, 0))
        return device_keep_ref[j] * (pow_re * c + pow_im * other) + recv_ref[j]

    ahead = z.tm - 1 - place if reverse else place
    tile_ref[...] = lax.fori_loop(0, ahead, hop, jnp.zeros((z.packed, LANES), F32))
    for r in range(z.R):
        cr = unpack(tile_ref, r * 2 * z.half, z.half)
        ci = unpack(tile_ref, r * 2 * z.half + z.half, z.half)
        order = list(chunk_order(reverse))
        for c in order:
            k = r * CHUNKS + c
            carry_ref[k : k + 1, 0 : z.N] = cr
            carry_ref[k : k + 1, z.N : 2 * z.N] = ci
            if c != order[-1]:
                keep = wide(chunk_keep_ref[k : k + 1, :], z)
                er, ei = ends_ref[k : k + 1, 0 : z.N], ends_ref[k : k + 1, z.N : 2 * z.N]
                cr, ci = keep * cr, keep * ci
                cr, ci = pr * cr - pi * ci + er, pr * ci + pi * cr + ei
    state = []
    for r in range(z.R):
        span = slice(r * CHUNKS, (r + 1) * CHUNKS)
        state.append((carry_ref[span, 0 : z.N], carry_ref[span, z.N : 2 * z.N]))
    return state


def lam_rows(z, tab_ref, b):
    def row(i):
        return tab_ref[b * 8 + i : b * 8 + i + 1, :]

    def full(i):
        return jnp.broadcast_to(row(i), (CHUNKS, z.N))

    return full(0), full(1), full(2), row(3), row(4)


def prepare(z, len_ref, x_ref, gout_ref, rate_ref, phase_ref, v_ref, up_ref, stat_ref, keep_f, keep_r, chunk_f, chunk_r, dev_f, dev_r, tab_ref, power_ref, tile_ref, natural_ref):
    to_steps(z, lambda rows: x_ref[rows, :].astype(F32), v_ref, natural_ref)
    to_steps(z, lambda rows: gout_ref[rows, :].astype(F32), up_ref, natural_ref)

    def body(rows, c):
        v = v_ref[rows, :]
        return c[0] + fold(v), c[1] + fold(v * v)

    zero = jnp.zeros((8, z.D), F32)
    s0, s1 = tiles(z, body, (zero, zero))
    pack(tile_ref, [jnp.sum(s0, 0, keepdims=True), jnp.sum(s1, 0, keepdims=True)])
    spread(stat_ref, tile_ref)
    base = lax.axis_index("tm") * z.S
    place = lax.broadcasted_iota(jnp.int32, (z.S, LANES), 0)
    at = base + (place % CHUNKS) * z.L + place // CHUNKS
    chunk_at = base + z.L * lax.broadcasted_iota(jnp.int32, (CHUNKS, LANES), 0)
    dev_at = z.S * lax.broadcasted_iota(jnp.int32, (z.tm, LANES), 0)
    for r in range(z.R):
        end = jnp.int32(0)
        hit = [jnp.zeros(a.shape, jnp.bool_) for a in (at, at, chunk_at, chunk_at, dev_at, dev_at)]
        for q in range(z.seqs):
            start = end
            end = end + len_ref[r, q]
            last = end - 1
            hit[0] = hit[0] | (at == start)
            hit[1] = hit[1] | (at == last)
            for i, mark in ((2, start), (3, last)):
                hit[i] = hit[i] | ((chunk_at <= mark) & (mark < chunk_at + z.L))
            for i, mark in ((4, start), (5, last)):
                hit[i] = hit[i] | ((dev_at <= mark) & (mark < dev_at + z.S))
        keep = [1.0 - h.astype(F32) for h in hit]
        keep_f[r * z.S : (r + 1) * z.S, :] = keep[0]
        keep_r[r * z.S : (r + 1) * z.S, :] = keep[1]
        chunk_f[r * CHUNKS : (r + 1) * CHUNKS, :] = keep[2]
        chunk_r[r * CHUNKS : (r + 1) * CHUNKS, :] = keep[3]
        each = 2 * z.half
        for j in range(z.tm):
            for ref, k in ((dev_f, keep[4]), (dev_r, keep[5])):
                ref[j, r * each : (r + 1) * each, :] = jnp.broadcast_to(k[j : j + 1, :], (each, LANES))
    for b in range(2):
        rate, angle = rate_ref[b : b + 1, :], phase_ref[b : b + 1, :]
        size = jnp.exp(-rate)
        lr, li = size * jnp.cos(angle), size * jnp.sin(angle)
        gamma = jnp.sqrt(1.0 - jnp.exp(-2.0 * rate))

        def power(n):
            out, br, bi = None, lr, li
            while n:
                if n & 1:
                    out = (br, bi) if out is None else (out[0] * br - out[1] * bi, out[0] * bi + out[1] * br)
                br, bi = br * br - bi * bi, 2.0 * br * bi
                n >>= 1
            return out

        chunk_power, device_power = power(z.L), power(z.S)
        rows = [lr, li, gamma, chunk_power[0], chunk_power[1], jnp.exp(-2.0 * rate) / gamma]
        for i, row in enumerate(rows):
            tab_ref[b * 8 + i : b * 8 + i + 1, :] = row
        for i in range(6, 8):
            tab_ref[b * 8 + i : b * 8 + i + 1, :] = jnp.zeros_like(lr)
        pack(power_ref.at[2 * b], [device_power[0], device_power[0]] * z.R)
        pack(power_ref.at[2 * b + 1], [-device_power[1], device_power[1]] * z.R)


def enter(z, b, stat_ref, v_ref, gain_ref, bias_ref, win_ref, keep_ref, chunk_ref, tab_ref,
          norm_ref, low_ref, proj_ref, ends_ref, send_ref, stat_tile, tile_ref):
    total, square = two_sums(stat_ref, stat_tile, z)
    mean = total / z.tokens
    rstd = lax.rsqrt(square / z.tokens - mean * mean + EPS)
    norm_ref[0:1, :] = mean
    norm_ref[1:2, :] = rstd
    gain, bias = gain_ref[b : b + 1, :], bias_ref[b : b + 1, :]

    def body(rows, c):
        xhat = (v_ref[rows, :] - mean) * rstd
        low_ref[rows, :] = (gain * xhat + bias).astype(BF16)
        return c

    tiles(z, body, 0)
    proj_ref[...] = dot(low_ref[...], win_ref[b])
    lr, li, gamma, pr, pi = lam_rows(z, tab_ref, b)
    state = scan(z, proj_ref, gamma, lr, li, keep_ref, zeros_state(z), b == 1)
    pack(tile_ref, end_state(z, state, ends_ref, chunk_ref, pr, pi, b == 1))
    spread(send_ref, tile_ref)


def gelu_pair(y):
    cdf = 0.5 + 0.5 * lax.erf(y * ROOT_HALF)
    return y * cdf, cdf + y * (ROOT_TWO_PI_INV * jnp.exp(-0.5 * y * y))


def mix(z, b, recv_ref, dev_ref, power_ref, ends_ref, chunk_ref, proj_ref, keep_ref, tab_ref, v_ref, norm_ref, gain_ref,
        bias_ref, skip_ref, wout_ref, wglu_ref, h_ref, hlow_ref, carry_ref, slope_ref, act_ref, tile_ref, wide_ref):
    lr, li, gamma, pr, pi = lam_rows(z, tab_ref, b)
    state = carries(z, recv_ref, dev_ref, power_ref, b, 1.0, ends_ref, chunk_ref, pr, pi, tile_ref, carry_ref, b == 1)

    put = pair_store(z, hlow_ref)

    def visit(r, s, rows, hr, hi):
        h_ref[rows, 0 : z.N] = hr
        h_ref[rows, z.N : 2 * z.N] = hi
        put(r, s, hr, hi)

    scan(z, proj_ref, gamma, lr, li, keep_ref, state, b == 1, visit)
    slope_ref[...] = dot(hlow_ref[...], wout_ref[b])
    mean, rstd = norm_ref[0:1, :], norm_ref[1:2, :]
    gain, bias, skip = gain_ref[b : b + 1, :], bias_ref[b : b + 1, :], skip_ref[b : b + 1, :]

    def body(rows, c):
        xn = gain * ((v_ref[rows, :] - mean) * rstd) + bias
        act, slope = gelu_pair(slope_ref[rows, :] + skip * xn)
        act_ref[rows, :] = act.astype(BF16)
        slope_ref[rows, :] = slope
        return c

    tiles(z, body, 0)
    wide_ref[...] = dot(act_ref[...], wglu_ref[b])


def middle(z, recv_ref, dev_ref, power_ref, ends_ref, chunk_ref, proj_ref, keep_ref, tab_ref, v_ref, norm_ref, gain_ref,
           bias_ref, skip_ref, wout_ref, wglu_ref, bglu_ref,
           h_ref, hlow_ref, carry_ref, slope_ref, act_ref, sig_ref, gate_ref, next_ref, stat_ref, tile_ref, wide_ref, stat_tile):
    mix(z, 0, recv_ref, dev_ref, power_ref, ends_ref, chunk_ref, proj_ref, keep_ref, tab_ref, v_ref, norm_ref, gain_ref,
        bias_ref, skip_ref, wout_ref, wglu_ref, h_ref, hlow_ref, carry_ref, slope_ref, act_ref, tile_ref, wide_ref)
    d = z.D
    b1, b2 = bglu_ref[0:1, 0:d], bglu_ref[0:1, d : 2 * d]

    def body(rows, c):
        z1 = wide_ref[rows, 0:d] + b1
        sig = jax.nn.sigmoid(wide_ref[rows, d : 2 * d] + b2)
        prod = z1 * sig
        sig_ref[rows, :] = sig
        gate_ref[rows, :] = prod * (1.0 - sig)
        v = v_ref[rows, :] + prod
        next_ref[rows, :] = v
        return c[0] + fold(v), c[1] + fold(v * v)

    zero = jnp.zeros((8, d), F32)
    s0, s1 = tiles(z, body, (zero, zero))
    pack(stat_tile, [jnp.sum(s0, 0, keepdims=True), jnp.sum(s1, 0, keepdims=True)])
    spread(stat_ref, stat_tile)


def descend(z, b, grad_bglu, dz_ref, slope_ref, v_ref, norm_ref, gain_ref, bias_ref, wglu_ref, wout_ref, keep_ref, chunk_ref, tab_ref,
            dy_ref, dylow_ref, dh_ref, ends_ref, send_ref, small_ref, tile_ref):
    dy_ref[...] = dot_t(dz_ref[...], wglu_ref[b])
    mean, rstd = norm_ref[0:1, :], norm_ref[1:2, :]
    gain, bias = gain_ref[b : b + 1, :], bias_ref[b : b + 1, :]

    def body(rows, c):
        xn = gain * ((v_ref[rows, :] - mean) * rstd) + bias
        dy = dy_ref[rows, :] * slope_ref[rows, :]
        dy_ref[rows, :] = dy
        dylow_ref[rows, :] = dy.astype(BF16)
        return c + fold(dy * xn)

    grad_skip = tiles(z, body, jnp.zeros((8, z.D), F32))
    small_ref[0:1, :] = jnp.sum(grad_skip, 0, keepdims=True)
    total = jnp.sum(grad_bglu, 0, keepdims=True)
    small_ref[1:2, :] = total[:, 0 : z.D]
    small_ref[2:3, :] = total[:, z.D : 2 * z.D]
    dh_ref[...] = dot_t(dylow_ref[...], wout_ref[b])
    lr, li, _, pr, pi = lam_rows(z, tab_ref, b)
    state = scan(z, dh_ref, None, lr, -li, keep_ref, zeros_state(z), b == 0)
    pack(tile_ref, end_state(z, state, ends_ref, chunk_ref, pr, -pi, b == 0))
    spread(send_ref, tile_ref)


def turn(z, recv_ref, dev_ref, power_ref, ends_ref, chunk_ref, proj_ref, keep_ref, tab_ref, v_ref, norm_ref, gain_ref,
         bias_ref, skip_ref, wout_ref, wglu_ref, bglu_ref, gout_ref, adj_keep_ref, adj_chunk_ref,
         h_ref, hlow_ref, carry_ref, act_ref, out_ref, dz_ref, dy_ref, dylow_ref, dh_ref, adj_ends_ref, send_ref, small_ref,
         tile_ref, wide_ref, slope_ref, natural_ref):
    mix(z, 1, recv_ref, dev_ref, power_ref, ends_ref, chunk_ref, proj_ref, keep_ref, tab_ref, v_ref, norm_ref, gain_ref,
        bias_ref, skip_ref, wout_ref, wglu_ref, h_ref, hlow_ref, carry_ref, slope_ref, act_ref, tile_ref, wide_ref)
    d = z.D
    b1, b2 = bglu_ref[1:2, 0:d], bglu_ref[1:2, d : 2 * d]

    def body(rows, c):
        z1 = wide_ref[rows, 0:d] + b1
        sig = jax.nn.sigmoid(wide_ref[rows, d : 2 * d] + b2)
        prod = z1 * sig
        dy_ref[rows, :] = v_ref[rows, :] + prod
        e = gout_ref[rows, :]
        d1, d2 = e * sig, e * (prod * (1.0 - sig))
        dz_ref[rows, 0:d] = d1.astype(BF16)
        dz_ref[rows, d : 2 * d] = d2.astype(BF16)
        return c[0] + fold(d1), c[1] + fold(d2)

    zero = jnp.zeros((8, d), F32)
    s0, s1 = tiles(z, body, (zero, zero))
    to_time(z, dy_ref, out_ref, natural_ref)
    descend(z, 1, jnp.concatenate([s0, s1], axis=1), dz_ref, slope_ref, v_ref, norm_ref, gain_ref, bias_ref, wglu_ref, wout_ref,
            adj_keep_ref, adj_chunk_ref, tab_ref, dy_ref, dylow_ref, dh_ref, adj_ends_ref, send_ref, small_ref, tile_ref)


def finish(z, b, recv_ref, dev_ref, power_ref, ends_ref, chunk_ref, dh_ref, keep_ref, tab_ref, proj_ref, h_ref, carry_ref,
           fwd_keep_ref, dy_ref, v_ref, norm_ref, skip_ref, win_ref,
           dplow_ref, dxn_ref, stat_ref, lam_ref, tile_ref, adj_carry_ref, stat_tile):
    lr, li, gamma, pr, pi = lam_rows(z, tab_ref, b)
    reverse = b == 0
    state = carries(z, recv_ref, dev_ref, power_ref, b, -1.0, ends_ref, chunk_ref, pr, -pi, tile_ref, adj_carry_ref, reverse)
    zero = jnp.zeros((CHUNKS, z.N), F32)
    sums = [zero, zero, zero]
    put = pair_store(z, dplow_ref)

    def visit(r, s, rows, gr, gi):
        put(r, s, gamma * gr, gamma * gi)
        sums[2] = sums[2] + gr * proj_ref[rows, 0 : z.N] + gi * proj_ref[rows, z.N : 2 * z.N]
        if s == (0 if b == 0 else z.L - 1):
            span = slice(r * CHUNKS, (r + 1) * CHUNKS)
            nr, ni = carry_ref[span, 0 : z.N], carry_ref[span, z.N : 2 * z.N]
        else:
            near = step_rows(z, r, s - 1 if b == 0 else s + 1)
            nr, ni = h_ref[near, 0 : z.N], h_ref[near, z.N : 2 * z.N]
        keep = wide(fwd_keep_ref[rows, :], z)
        nr, ni = keep * nr, keep * ni
        sums[0] = sums[0] + (gr * nr + gi * ni)
        sums[1] = sums[1] + (gi * nr - gr * ni)

    scan(z, dh_ref, None, lr, -li, keep_ref, state, reverse, visit)
    dr, di, dg = (jnp.sum(s, 0, keepdims=True) for s in sums)
    r0, i0 = lr[0:1, :], li[0:1, :]
    lam_ref[0:1, :] = dg * tab_ref[b * 8 + 5 : b * 8 + 6, :] - (dr * r0 + di * i0)
    lam_ref[1:2, :] = di * r0 - dr * i0

    dxn_ref[...] = dot_t(dplow_ref[...], win_ref[b])
    mean, rstd = norm_ref[0:1, :], norm_ref[1:2, :]
    skip = skip_ref[b : b + 1, :]

    def body(rows, c):
        xhat = (v_ref[rows, :] - mean) * rstd
        dxn = dxn_ref[rows, :] + skip * dy_ref[rows, :]
        dxn_ref[rows, :] = dxn
        return c[0] + fold(dxn), c[1] + fold(dxn * xhat)

    zero = jnp.zeros((8, z.D), F32)
    s0, s1 = tiles(z, body, (zero, zero))
    pack(stat_tile, [jnp.sum(s0, 0, keepdims=True), jnp.sum(s1, 0, keepdims=True)])
    spread(stat_ref, stat_tile)


def norm_grad(z, b, stat_ref, stat_tile, norm_ref, gain_ref, total_ref):
    bias_sum, gain_sum = two_sums(stat_ref, stat_tile, z)
    total_ref[0:1, :] = bias_sum
    total_ref[1:2, :] = gain_sum
    mean, rstd = norm_ref[0:1, :], norm_ref[1:2, :]
    gain = gain_ref[b : b + 1, :]
    scale, shift, slope = rstd * gain, rstd * gain * bias_sum / z.tokens, rstd * gain * gain_sum / z.tokens

    def grad(dxn, v, up):
        return scale * dxn - shift - ((v - mean) * rstd) * slope + up

    return grad


def lower_block(z, stat_ref, dxn_ref, v1_ref, norm1_ref, gout_ref, sig_ref, gate_ref, slope_ref, v_ref, norm_ref, gain_ref, bias_ref,
                wglu_ref, wout_ref, keep_ref, chunk_ref, tab_ref,
                total_ref, e_ref, dz_ref, dy_ref, dylow_ref, dh_ref, ends_ref, send_ref, small_ref, tile_ref, stat_tile):
    grad = norm_grad(z, 1, stat_ref, stat_tile, norm1_ref, gain_ref, total_ref)
    d = z.D

    def body(rows, c):
        e = grad(dxn_ref[rows, :], v1_ref[rows, :], gout_ref[rows, :])
        e_ref[rows, :] = e
        d1, d2 = e * sig_ref[rows, :], e * gate_ref[rows, :]
        dz_ref[rows, 0:d] = d1.astype(BF16)
        dz_ref[rows, d : 2 * d] = d2.astype(BF16)
        return c[0] + fold(d1), c[1] + fold(d2)

    zero = jnp.zeros((8, d), F32)
    s0, s1 = tiles(z, body, (zero, zero))
    descend(z, 0, jnp.concatenate([s0, s1], axis=1), dz_ref, slope_ref, v_ref, norm_ref, gain_ref, bias_ref, wglu_ref, wout_ref,
            keep_ref, chunk_ref, tab_ref, dy_ref, dylow_ref, dh_ref, ends_ref, send_ref, small_ref, tile_ref)


def last(z, stat_ref, dxn_ref, v_ref, norm_ref, gain_ref, e_ref, total_ref, grad_ref, stat_tile, natural_ref, work_ref):
    grad = norm_grad(z, 0, stat_ref, stat_tile, norm_ref, gain_ref, total_ref)

    def body(rows, c):
        work_ref[rows, :] = grad(dxn_ref[rows, :], v_ref[rows, :], e_ref[rows, :])
        return c

    tiles(z, body, 0)
    to_time(z, work_ref, grad_ref, natural_ref)


def outer(z, act_ref, dz_ref, hlow_ref, dylow_ref, wglu_ref, wout_ref):
    wglu_ref[...] = dot_0(act_ref[...], dz_ref[...])
    wout_ref[...] = dot_0(hlow_ref[...], dylow_ref[...])


def outer_in(z, low_ref, dplow_ref, win_ref):
    win_ref[...] = dot_0(low_ref[...], dplow_ref[...])


def run(kernel, name, outs, args, scratch=(), smem=0):
    spaces = [pltpu.SMEM] * smem + [pltpu.VMEM] * (len(args) - smem)
    return pl.pallas_call(
        kernel,
        out_shape=[jax.ShapeDtypeStruct(s, t) for s, t in outs],
        in_specs=[pl.BlockSpec(memory_space=m) for m in spaces],
        out_specs=[pl.BlockSpec(memory_space=pltpu.VMEM)] * len(outs),
        scratch_shapes=[pltpu.VMEM(s, t) for s, t in scratch],
        compiler_params=pltpu.CompilerParams(vmem_limit_bytes=24 << 20),
        name=name,
    )(*args)


def body(x_in, lengths, bn_gain, bn_bias, w_in, decay_rate, phase, w_out, skip_gain, w_glu, b_glu, grad_out):
    rows, steps, width = x_in.shape
    z = Sizes(rows, steps, width, w_in.shape[2] // 2, lax.axis_size("tm"), lax.axis_size("rows"), lengths.shape[1])
    T, D, N = z.T, z.D, z.N
    everyone = ("tm", "rows")

    def swap(a, axis):
        return lax.all_to_all(a, axis, 0, 0)

    stat_shape = ((z.all, z.stat, LANES), F32)
    send_shape = ((z.tm, z.packed, LANES), F32)
    tile = ((z.packed, LANES), F32)
    stat_tile = ((z.stat, LANES), F32)
    full, low = ((T, D), F32), ((T, D), BF16)
    full_n, low_n = ((T, 2 * N), F32), ((T, 2 * N), BF16)
    chunk = ((z.R * CHUNKS, 2 * N), F32)
    mask = ((T, LANES), F32)
    chunk_mask = ((z.R * CHUNKS, LANES), F32)
    norm_shape = ((8, D), F32)
    small_shape = ((8, D), F32)
    lam_shape = ((8, N), F32)
    wide_f, wide_b = ((T, 2 * D), F32), ((T, 2 * D), BF16)
    bind = functools.partial

    natural = ((D // LANES, T, LANES), F32)
    x, gout, stat0, keep_f, keep_r, chunk_f, chunk_r, dev_f, dev_r, tab, power = run(
        bind(prepare, z), "prepare",
        [full, full, stat_shape, mask, mask, chunk_mask, chunk_mask, send_shape, send_shape, ((16, N), F32), ((4, z.packed, LANES), F32)],
        (lengths, x_in.reshape(T, D), grad_out.reshape(T, D), decay_rate, phase), [stat_tile, natural], smem=1)
    stat0 = swap(stat0, everyone)
    norm0, low0, proj0, ends0, send0 = run(
        bind(enter, z, 0), "enter0", [norm_shape, low, full_n, chunk, send_shape],
        (stat0, x, bn_gain, bn_bias, w_in, keep_f, chunk_f, tab), [stat_tile, tile])
    send0 = swap(send0, "tm")
    h0, hlow0, carry0, slope0, act0, sig0, gate0, v1, stat1 = run(
        bind(middle, z), "middle", [full_n, low_n, chunk, full, low, full, full, full, stat_shape],
        (send0, dev_f, power, ends0, chunk_f, proj0, keep_f, tab, x, norm0, bn_gain, bn_bias, skip_gain, w_out, w_glu, b_glu),
        [tile, wide_f, stat_tile])
    stat1 = swap(stat1, everyone)
    norm1, low1, proj1, ends1, send1 = run(
        bind(enter, z, 1), "enter1", [norm_shape, low, full_n, chunk, send_shape],
        (stat1, v1, bn_gain, bn_bias, w_in, keep_r, chunk_r, tab), [stat_tile, tile])
    send1 = swap(send1, "tm")
    h1, hlow1, carry1, act1, out, dz1, dy1, dylow1, dh1, adj_ends1, adj1, small1 = run(
        bind(turn, z), "turn",
        [full_n, low_n, chunk, low, low, wide_b, full, low, full_n, chunk, send_shape, small_shape],
        (send1, dev_r, power, ends1, chunk_r, proj1, keep_r, tab, v1, norm1, bn_gain, bn_bias, skip_gain, w_out, w_glu, b_glu, gout,
         keep_f, chunk_f), [tile, wide_f, full, natural])
    adj1 = swap(adj1, "tm")
    gwglu1, gwout1 = run(bind(outer, z), "outer1", [((D, 2 * D), F32), ((2 * N, D), F32)], (act1, dz1, hlow1, dylow1))
    dplow1, dxn1, sum1, lam1 = run(
        bind(finish, z, 1), "finish1", [low_n, full, stat_shape, lam_shape],
        (adj1, dev_f, power, adj_ends1, chunk_f, dh1, keep_f, tab, proj1, h1, carry1, keep_r, dy1, v1, norm1, skip_gain, w_in),
        [tile, chunk, stat_tile])
    sum1 = swap(sum1, everyone)
    (gwin1,) = run(bind(outer_in, z), "outer_in1", [((D, 2 * N), F32)], (low1, dplow1))
    total1, e1, dz0, dy0, dylow0, dh0, adj_ends0, adj0, small0 = run(
        bind(lower_block, z), "lower_block",
        [norm_shape, full, wide_b, full, low, full_n, chunk, send_shape, small_shape],
        (sum1, dxn1, v1, norm1, gout, sig0, gate0, slope0, x, norm0, bn_gain, bn_bias, w_glu, w_out, keep_r, chunk_r, tab),
        [tile, stat_tile])
    adj0 = swap(adj0, "tm")
    gwglu0, gwout0 = run(bind(outer, z), "outer0", [((D, 2 * D), F32), ((2 * N, D), F32)], (act0, dz0, hlow0, dylow0))
    dplow0, dxn0, sum0, lam0 = run(
        bind(finish, z, 0), "finish0", [low_n, full, stat_shape, lam_shape],
        (adj0, dev_r, power, adj_ends0, chunk_r, dh0, keep_r, tab, proj0, h0, carry0, keep_f, dy0, x, norm0, skip_gain, w_in),
        [tile, chunk, stat_tile])
    sum0 = swap(sum0, everyone)
    (gwin0,) = run(bind(outer_in, z), "outer_in0", [((D, 2 * N), F32)], (low0, dplow0))
    total0, grad_x = run(
        bind(last, z), "last", [norm_shape, full], (sum0, dxn0, x, norm0, bn_gain, e1), [stat_tile, natural, full])
    summed = lax.psum(
        (jnp.stack([gwin0, gwin1]), jnp.stack([gwout0, gwout1]), jnp.stack([gwglu0, gwglu1]),
         jnp.stack([small0, small1]), jnp.stack([lam0, lam1])), everyone)
    gwin, gwout, gwglu, small, lam = summed
    totals = jnp.stack([total0, total1])
    return (
        out.reshape(rows, steps, width),
        grad_x.reshape(rows, steps, width),
        totals[:, 1],
        totals[:, 0],
        gwin,
        lam[:, 0],
        lam[:, 1],
        gwout,
        small[:, 0],
        gwglu,
        small[:, 1:3].reshape(2, 2 * D),
    )


def solution(mesh):
    split, rep = P("rows", "tm", None), P()
    return jax.shard_map(
        body,
        mesh=mesh,
        in_specs=(split, P("rows", None)) + (rep,) * 9 + (split,),
        out_specs=(split, split) + (rep,) * 9,
        check_vma=False,
    )
```

time: 1300 us -> 347 us (0.27); the launches traced: 1280 us -> 345 us
  blocking collectives: 583 us -> 95.6 us
  local copies, waits for them, and re-layouts: 339 us -> 67.2 us
  other arithmetic: 177 us -> 6.87 us
  matrix products: 24.1 us -> 0 us
  Pallas kernels: 0 us -> 15.3 us
  starting transfers between devices: 0.04 us -> 14.3 us
    all_gather x16 -> x0, blocking collectives: 419 us -> none  [prefix(): gathered = jax.tree.map(lambda a: lax.all_gather(a, axis), part)]
    slice x396 -> x2, local copies, waits for them, and re-layouts: 210 us -> 0.01 us  [the longest x1 0.01 us: body(): lam[:, 1]]
    psum x4 -> x1, blocking collectives: 165 us -> 42.7 us  [body(): lax.psum((jnp.stack([gwin0, gwin1]), jnp.stack([gwout0, gwout1]), jnp.sta...]
    add x212 -> x0, other arithmetic: 94.1 us -> none  [the longest x120 48.4 us: linear_scan(): lax.associative_scan(combine_pairs, (coef_re, coef_im, drive_re, drive_im...]
    pad x192 -> x0, local copies, waits for them, and re-layouts: 85.4 us -> none  [linear_scan(): lax.associative_scan(combine_pairs, (coef_re, coef_im, drive_re, drive_im...]
    unnamed x326 -> x220, local copies, waits for them, and re-layouts: 10.8 us -> 67.2 us
    all_to_all x0 -> x5, blocking collectives: none -> 52.9 us  [swap(): return lax.all_to_all(a, axis, 0, 0)]
    concatenate x100 -> x0, other arithmetic: 47.6 us -> none  [the longest x96 45.2 us: linear_scan(): lax.associative_scan(combine_pairs, (coef_re, coef_im, drive_re, drive_im...]
  transfers between devices with their start and end apart: 1 -> 4, of which waited for: 1 -> 1; matrix products, arithmetic and copies ran while one was open for 0% -> 2% of each run, Pallas kernels for 0% -> 1%
where the time goes in v1:
time: 347 us; the launch traced here: 345 us
  waiting for transfers between devices  131 us (38%)
  blocking collectives  95.6 us (28%)
  local copies, waits for them, and re-layouts  67.2 us (19%)
  Pallas kernels  15.3 us (4%)
  between operations  14.6 us (4%)
  starting transfers between devices  14.3 us (4%)
  other arithmetic  6.87 us (2%)
    psum x1, waiting for transfers between devices, body(): lax.psum((jnp.stack([gwin0, gwin1]), jnp.stack([gwout0, gwout1]), jnp.sta...  131 us
    unnamed x220, local copies, waits for them, and re-layouts  67.2 us
    all_to_all x5, blocking collectives, swap(): return lax.all_to_all(a, axis, 0, 0)  52.9 us
    psum x1, blocking collectives, body(): lax.psum((jnp.stack([gwin0, gwin1]), jnp.stack([gwout0, gwout1]), jnp.sta...  42.7 us
    pallas_call x13, Pallas kernels, run(): pl.pallas_call(kernel, out_shape=[jax.ShapeDtypeStruct(s, t) for s, t in...  15.3 us
    all_to_all x3, starting transfers between devices, swap(): return lax.all_to_all(a, axis, 0, 0)  14.3 us
  transfers between devices with their start and end apart: 4, of which 1 were waited for; matrix products, arithmetic and copies ran while one was open for 2% of the time, Pallas kernels for 1%

profile of v1, /device:TPU:0, one launch (start us, length us, event | category | flops | bytes accessed | tf_op | source)
XLA Modules:
  0.0 344.9 jit_solution(17504289384219164684)
XLA Ops:
  7.2 1.1 copy-done.61
  8.3 0.9 copy-done.62
  11.3 1.9 prepare.1
  13.2 15.3 %all_to_all.40.stat_ref = f32[32,8,128]{2,1,0:T(8,128)S(1)} all-to-all(f32[32,8,128]{2,1,0:T(8,128)S(1)} %get-tuple-element.76), channel_id=1, replica_groups=mesh['tm'=8,'rows'=4] {'tm','rows'}, dimensions={0} | all-to-all | bytes 262144 | tf_op jit(solution)/shard_map/all_to_all | solution.py:540
  28.5 1.2 copy-done.1
  31.7 0.7 copy-done.63
  32.5 9.2 %all_to_all.41.recv_ref = f32[8,8,128]{2,1,0:T(8,128)S(1)} all-to-all(f32[8,8,128]{2,1,0:T(8,128)S(1)} %get-tuple-element.81), channel_id=1, replica_groups=mesh['tm'=8,'rows'=4] {'tm'}, dimensions={0} | all-to-all | bytes 65536 | tf_op jit(solution)/shard_map/all_to_all | solution.py:540
  41.7 1.2 copy-done.6
  45.6 1.6 middle.1
  47.3 0.8 copy-done.28
  49.5 10.2 %all_to_all.42.stat_ref = f32[32,8,128]{2,1,0:T(8,128)S(1)} all-to-all(f32[32,8,128]{2,1,0:T(8,128)S(1)} %get-tuple-element.87), channel_id=1, replica_groups=mesh['tm'=8,'rows'=4] {'tm','rows'}, dimensions={0} | all-to-all | bytes 262144 | tf_op jit(solution)/shard_map/all_to_all | solution.py:540
  61.1 9.1 %all_to_all.43.recv_ref = f32[8,8,128]{2,1,0:T(8,128)S(1)} all-to-all(f32[8,8,128]{2,1,0:T(8,128)S(1)} %get-tuple-element.91), channel_id=1, replica_groups=mesh['tm'=8,'rows'=4] {'tm'}, dimensions={0} | all-to-all | bytes 65536 | tf_op jit(solution)/shard_map/all_to_all | solution.py:540
  70.2 3.8 %turn.1 = (f32[256,512]{1,0:T(8,128)S(1)}, bf16[256,512]{1,0:T(8,128)(2,1)S(1)}, f32[16,512]{1,0:T(8,128)S(1)}, bf16[256,512]{1,0:T(8,128)(2,1)S(1)}, bf16[256,5...) custom-call(f32[8,8,128]{2,1,0:T(8,128)S(1)} %all_to_all.43.recv_ref, ...), custom_call_target="tpu_custom_call" | custom-call | tf_op jit(solution)/shard_map/turn/pallas_call | solution.py:522
  74.0 0.8 copy-done.40
  74.8 9.1 %all_to_all.44.recv_ref = f32[8,8,128]{2,1,0:T(8,128)S(1)} all-to-all(f32[8,8,128]{2,1,0:T(8,128)S(1)} %get-tuple-element.98), channel_id=1, replica_groups=mesh['tm'=8,'rows'=4] {'tm'}, dimensions={0} | all-to-all | bytes 65536 | tf_op jit(solution)/shard_map/all_to_all | solution.py:540
  83.9 0.8 finish1.1
  84.7 0.8 copy-done.34
  87.4 2.6 all-to-all-start.5
  90.0 1.0 copy-done.41
  91.1 0.9 copy-done.54
  92.0 0.9 copy-done.56
  93.0 0.9 copy-done.58
  94.5 1.0 copy-done.18
  95.5 1.3 copy-done.17
  96.8 0.9 copy-done.66
  97.8 0.9 copy-done.68
  99.1 1.0 copy-done.11
  100.0 1.0 copy-done.4
  101.1 1.2 copy-done.8
  102.3 1.0 copy-done.10
  103.3 1.0 copy-done.16
  104.4 1.0 copy-done.25
  105.4 1.0 copy-done.27
  106.5 1.0 copy-done.29
  107.5 1.0 copy-done.35
  112.0 1.5 lower_block.1
  113.5 0.8 copy-done.30
  114.3 0.8 copy-done.32
  115.1 0.8 copy-done.36
  116.0 0.8 copy-done.42
  116.8 0.7 copy-done.59
  119.9 5.8 %all-to-all-start.6 = ((f32[8,8,128]{2,1,0:T(8,128)}), f32[8,8,128]{2,1,0:T(8,128)S(1)}, u32[]{:S(2)}, u32[]{:S(2)}) async-start(f32[8,8,128]{2,1,0:T(8,128)} %copy-done.92), calls=%async_computation.6 | async-start | bytes 65536 | tf_op jit(solution)/shard_map/all_to_all | solution.py:540
  125.8 1.0 copy-done.43
  126.8 0.9 copy-done.50
  127.7 0.9 copy-done.52
  128.7 0.9 copy-done.60
  130.2 1.0 copy-done.20
  131.3 4.3 %pad_maximum_fusion = f32[2,512,1024]{2,1,0:T(8,128)} fusion(f32[1,512,1024]{2,1,0:T(8,128)} %bitcast.32, f32[1,512,1024]{2,1,0:T(8,128)S(1)} %bitcast.33), kind=kLoop, calls=%fused_computation | loop fusion | flops 1048576 | bytes 8388608 | tf_op jit(solution)/shard_map/stack | solution.py:605
  135.6 1.0 copy-done.23
  136.6 1.0 copy-done.31
  137.7 1.0 copy-done.33
  138.7 0.8 copy-done.87
  139.5 0.8 copy-done.89
  140.3 1.5 finish0.1
  141.7 1.1 copy-done.64
  143.2 2.6 pad_maximum_fusion.1
  146.5 5.9 %all-to-all-start.7 = ((f32[32,8,128]{2,1,0:T(8,128)}), f32[32,8,128]{2,1,0:T(8,128)S(1)}, u32[]{:S(2)}, u32[]{:S(2)}) async-start(f32[32,8,128]{2,1,0:T(8,128)} %get-tuple-element.115), calls=%async_computation.7 | async-start | bytes 262144 | tf_op jit(solution)/shard_map/all_to_all | solution.py:540
  152.5 42.7 %all-reduce = (f32[2,8,256]{2,1,0:T(8,128)S(1)}, f32[2,8,512]{2,1,0:T(8,128)S(1)}) all-reduce(f32[2,8,256]{2,1,0:T(8,128)S(1)} %pad_maximum_fusion.4, f32[2,8,512]{2,1,0:T(8,128)S(1)} %pad_maximum_fusion.3), channel_id=1, replica_groups=mesh['tm'=8,'rows'=4] {'tm','rows'}, use_global_device_ids=true, to_apply=%region_1.0 | all-reduce | flops 12288 | bytes 98304 | tf_op jit(solution)/shard_map/psum | solution.py:604
  197.0 1.3 last.1
  198.9 130.9 %all-reduce.4.cloned.1.call-done = (f32[2,512,512]{2,1,0:T(8,128)}, f32[2,512,512]{2,1,0:T(8,128)}, f32[2,512,1024]{2,1,0:T(8,128)}) async-done(((f32[2,512,512]{2,1,0:T(8,128)}, f32[2,512,512]{2,1,0:T(8,128)}, f32[2,512,1024]{2,1,0:T(8,128)}), (f32[2,512,512]{2,1,0:T(8,128)}, f32[2,512,512]{2,1,0:T(8,128)}, f32[2,512,1024]{2,1,0:T(8,128)})) %all-reduce.4.cloned.1.call-update) | async-done | bytes 8388624 | tf_op jit(solution)/shard_map/psum | solution.py:604
  329.9 3.2 copy.38
  333.1 1.3 copy.39
  334.4 1.6 copy-done.104
  336.1 2.0 copy.40
  (191 shorter events, 22.6 us)
Async XLA Ops:
  7.2 34.5 %copy-start = (bf16[2,512,1024]{2,1,0:T(8,128)(2,1)S(1)}, bf16[2,512,1024]{2,1,0:T(8,128)(2,1)}, u32[]{:S(2)}) copy-start(bf16[2,512,1024]{2,1,0:T(8,128)(2,1)} %wglu_ref.5) | copy-start | bytes 6291460
  7.2 1.1 copy-start.61
  13.1 34.1 %copy-start.3 = (f32[256,512]{1,0:T(8,128)}, f32[256,512]{1,0:T(8,128)S(1)}, u32[]{:S(2)}) copy-start(f32[256,512]{1,0:T(8,128)S(1)} %get-tuple-element.77.v_ref) | copy-start | bytes 1572868
  13.1 57.1 %copy-start.15 = (f32[256,512]{1,0:T(8,128)}, f32[256,512]{1,0:T(8,128)S(1)}, u32[]{:S(2)}) copy-start(f32[256,512]{1,0:T(8,128)S(1)} %get-tuple-element.96.gout_ref) | copy-start | bytes 1572868
  13.2 57.1 %copy-start.75 = (f32[8,8,128]{2,1,0:T(8,128)}, f32[8,8,128]{2,1,0:T(8,128)S(1)}, u32[]{:S(2)}) copy-start(f32[8,8,128]{2,1,0:T(8,128)S(1)} %get-tuple-element.92.dev_ref) | copy-start | bytes 98308
  13.2 57.1 %copy-start.77 = (f32[16,128]{1,0:T(8,128)}, f32[16,128]{1,0:T(8,128)S(1)}, u32[]{:S(2)}) copy-start(f32[16,128]{1,0:T(8,128)S(1)} %get-tuple-element.90.chunk_ref) | copy-start | bytes 24580
  13.2 70.7 %copy-start.47 = (f32[4,8,128]{2,1,0:T(8,128)}, f32[4,8,128]{2,1,0:T(8,128)S(1)}, u32[]{:S(2)}) copy-start(f32[4,8,128]{2,1,0:T(8,128)S(1)} %get-tuple-element.83.power_ref) | copy-start | bytes 49156
  28.5 1.2 copy-start.1
  32.5 14.8 %copy-start.13 = (f32[256,512]{1,0:T(8,128)}, f32[256,512]{1,0:T(8,128)S(1)}, u32[]{:S(2)}) copy-start(f32[256,512]{1,0:T(8,128)S(1)} %get-tuple-element.85.proj_ref) | copy-start | bytes 1572868
  32.5 14.8 %copy-start.44 = (f32[8,512]{1,0:T(8,128)}, f32[8,512]{1,0:T(8,128)S(1)}, u32[]{:S(2)}) copy-start(f32[8,512]{1,0:T(8,128)S(1)} %get-tuple-element.86.norm_ref) | copy-start | bytes 49156
  41.7 1.2 copy-start.6
  45.6 14.1 %copy-start.2 = (bf16[2,512,512]{2,1,0:T(8,128)(2,1)S(1)}, bf16[2,512,512]{2,1,0:T(8,128)(2,1)}, u32[]{:S(2)}) copy-start(bf16[2,512,512]{2,1,0:T(8,128)(2,1)} %win_ref.7) | copy-start | bytes 3145732
  49.5 10.9 %copy-start.22 = (f32[256,512]{1,0:T(8,128)}, f32[256,512]{1,0:T(8,128)S(1)}, u32[]{:S(2)}) copy-start(f32[256,512]{1,0:T(8,128)S(1)} %get-tuple-element.112.h_ref) | copy-start | bytes 1572868
  49.5 11.6 %copy-start.24 = (f32[256,512]{1,0:T(8,128)}, f32[256,512]{1,0:T(8,128)S(1)}, u32[]{:S(2)}) copy-start(f32[256,512]{1,0:T(8,128)S(1)} %get-tuple-element.108.slope_ref) | copy-start | bytes 1572868
  49.5 20.7 %copy-start.26 = (f32[256,512]{1,0:T(8,128)}, f32[256,512]{1,0:T(8,128)S(1)}, u32[]{:S(2)}) copy-start(f32[256,512]{1,0:T(8,128)S(1)} %get-tuple-element.106.sig_ref) | copy-start | bytes 1572868
  49.5 20.7 %copy-start.86 = (f32[16,512]{1,0:T(8,128)}, f32[16,512]{1,0:T(8,128)S(1)}, u32[]{:S(2)}) copy-start(f32[16,512]{1,0:T(8,128)S(1)} %get-tuple-element.113.carry_ref) | copy-start | bytes 98308
  49.5 34.4 %copy-start.9 = (f32[256,512]{1,0:T(8,128)}, f32[256,512]{1,0:T(8,128)S(1)}, u32[]{:S(2)}) copy-start(f32[256,512]{1,0:T(8,128)S(1)} %get-tuple-element.88.v_ref.v1_ref) | copy-start | bytes 1572868
  49.5 20.7 %copy-start.7 = (bf16[2,512,512]{2,1,0:T(8,128)(2,1)S(1)}, bf16[2,512,512]{2,1,0:T(8,128)(2,1)}, u32[]{:S(2)}) copy-start(bf16[2,512,512]{2,1,0:T(8,128)(2,1)} %wout_ref.5) | copy-start | bytes 3145732
  49.5 20.7 %copy-start.91 = (f32[2,1024]{1,0:T(2,128)S(1)}, f32[2,1024]{1,0:T(2,128)}, u32[]{:S(2)}) copy-start(f32[2,1024]{1,0:T(2,128)} %bglu_ref.3) | copy-start | bytes 24580
  61.1 22.8 %copy-start.73 = (f32[8,512]{1,0:T(8,128)}, f32[8,512]{1,0:T(8,128)S(1)}, u32[]{:S(2)}) copy-start(f32[8,512]{1,0:T(8,128)S(1)} %get-tuple-element.95.norm_ref.norm1_ref) | copy-start | bytes 49156
  74.8 9.9 %copy-start.53 = (bf16[256,512]{1,0:T(8,128)(2,1)}, bf16[256,512]{1,0:T(8,128)(2,1)S(1)}, u32[]{:S(2)}) copy-start(bf16[256,512]{1,0:T(8,128)(2,1)S(1)} %get-tuple-element.134.hlow_ref) | copy-start | bytes 786436
  74.8 9.9 %copy-start.55 = (bf16[256,512]{1,0:T(8,128)(2,1)}, bf16[256,512]{1,0:T(8,128)(2,1)S(1)}, u32[]{:S(2)}) copy-start(bf16[256,512]{1,0:T(8,128)(2,1)S(1)} %get-tuple-element.132.act_ref) | copy-start | bytes 786436
  74.8 9.9 %copy-start.57 = (bf16[256,512]{1,0:T(8,128)(2,1)}, bf16[256,512]{1,0:T(8,128)(2,1)S(1)}, u32[]{:S(2)}) copy-start(bf16[256,512]{1,0:T(8,128)(2,1)S(1)} %get-tuple-element.135.dylow_ref) | copy-start | bytes 786436
  74.8 9.9 %copy-start.95 = (f32[8,512]{1,0:T(8,128)}, f32[8,512]{1,0:T(8,128)S(1)}, u32[]{:S(2)}) copy-start(f32[8,512]{1,0:T(8,128)S(1)} %get-tuple-element.138) | copy-start | bytes 49156
  87.4 12.6 %all-to-all-start.5 = ((f32[32,8,128]{2,1,0:T(8,128)}), f32[32,8,128]{2,1,0:T(8,128)S(1)}, u32[]{:S(2)}, u32[]{:S(2)}) async-start(f32[32,8,128]{2,1,0:T(8,128)} %copy-done.80), calls=%async_computation.5 | async-start | bytes 262144 | tf_op jit(solution)/shard_map/all_to_all | solution.py:540
  90.0 1.0 copy-start.41
  94.5 1.0 copy-start.18
  95.5 1.3 copy-start.17
  99.0 1.0 copy-start.11
  100.0 1.0 copy-start.4
  101.1 1.2 copy-start.8
  102.3 1.0 copy-start.10
  103.3 1.0 copy-start.16
  104.4 1.0 copy-start.25
  105.4 1.0 copy-start.27
  106.5 1.0 copy-start.29
  107.5 1.0 copy-start.35
  119.9 15.7 %all-to-all-start.6 = ((f32[8,8,128]{2,1,0:T(8,128)}), f32[8,8,128]{2,1,0:T(8,128)S(1)}, u32[]{:S(2)}, u32[]{:S(2)}) async-start(f32[8,8,128]{2,1,0:T(8,128)} %copy-done.92), calls=%async_computation.6 | async-start | bytes 65536 | tf_op jit(solution)/shard_map/all_to_all | solution.py:540
  125.7 204.2 %all-reduce.4.cloned.1.call-start = ((), (), s32[]{:S(2)}) async-start(), calls=%async_computation.8 | async-start | bytes 16777216 | tf_op jit(solution)/shard_map/psum | solution.py:604
  125.7 1.0 copy-start.43
  130.2 1.0 copy-start.20
  131.2 4.3 %copy-start.5 = (f32[256,512]{1,0:T(8,128)S(1)}, f32[256,512]{1,0:T(8,128)}, u32[]{:S(2)}) copy-start(f32[256,512]{1,0:T(8,128)} %copy-done.3) | copy-start | bytes 1572868
  131.2 4.3 %copy-start.14 = (f32[256,512]{1,0:T(8,128)S(1)}, f32[256,512]{1,0:T(8,128)}, u32[]{:S(2)}) copy-start(f32[256,512]{1,0:T(8,128)} %copy-done.13) | copy-start | bytes 1572868
  131.2 4.3 %copy-start.46 = (f32[8,512]{1,0:T(8,128)S(1)}, f32[8,512]{1,0:T(8,128)}, u32[]{:S(2)}) copy-start(f32[8,512]{1,0:T(8,128)} %copy-done.44) | copy-start | bytes 49156
  131.2 4.3 %copy-start.48 = (f32[4,8,128]{2,1,0:T(8,128)S(1)}, f32[4,8,128]{2,1,0:T(8,128)}, u32[]{:S(2)}) copy-start(f32[4,8,128]{2,1,0:T(8,128)} %copy-done.47) | copy-start | bytes 49156
  131.2 4.3 %copy-start.76 = (f32[8,8,128]{2,1,0:T(8,128)S(1)}, f32[8,8,128]{2,1,0:T(8,128)}, u32[]{:S(2)}) copy-start(f32[8,8,128]{2,1,0:T(8,128)} %copy-done.75) | copy-start | bytes 98308
  131.2 4.3 %copy-start.79 = (f32[16,128]{1,0:T(8,128)S(1)}, f32[16,128]{1,0:T(8,128)}, u32[]{:S(2)}) copy-start(f32[16,128]{1,0:T(8,128)} %copy-done.77) | copy-start | bytes 24580
  131.3 4.3 %copy-start.85 = (f32[2,512]{1,0:T(2,128)S(1)}, f32[2,512]{1,0:T(2,128)}, u32[]{:S(2)}) copy-start(f32[2,512]{1,0:T(2,128)} %skip_ref.7) | copy-start | bytes 12292
  135.6 1.0 copy-start.23
  136.6 1.0 copy-start.31
  137.7 1.0 copy-start.33
  140.2 2.9 copy-start.12
  140.2 2.9 copy-start.19
  140.2 2.9 copy-start.21
  141.7 4.1 %copy-start.38 = (f32[256,512]{1,0:T(8,128)}, f32[256,512]{1,0:T(8,128)S(1)}, u32[]{:S(2)}) copy-start(f32[256,512]{1,0:T(8,128)S(1)} %get-tuple-element.116.dxn_ref) | copy-start | bytes 1572868
  141.7 1.1 copy-start.64
  145.8 6.7 %copy-start.100 = (f32[8,256]{1,0:T(8,128)S(1)}, f32[8,256]{1,0:T(8,128)}, u32[]{:S(2)}) copy-start(f32[8,256]{1,0:T(8,128)} %copy-done.99) | copy-start | bytes 24580
  145.8 51.2 %copy-start.37 = (f32[256,512]{1,0:T(8,128)S(1)}, f32[256,512]{1,0:T(8,128)}, u32[]{:S(2)}) copy-start(f32[256,512]{1,0:T(8,128)} %copy-done.36) | copy-start | bytes 1572868
  145.8 51.2 %copy-start.39 = (f32[256,512]{1,0:T(8,128)S(1)}, f32[256,512]{1,0:T(8,128)}, u32[]{:S(2)}) copy-start(f32[256,512]{1,0:T(8,128)} %copy-done.38) | copy-start | bytes 1572868
  145.8 51.2 %copy-start.72 = (f32[2,512]{1,0:T(2,128)S(1)}, f32[2,512]{1,0:T(2,128)}, u32[]{:S(2)}) copy-start(f32[2,512]{1,0:T(2,128)} %gain_ref.11) | copy-start | bytes 12292
  145.8 52.5 %copy-start.94 = (f32[8,512]{1,0:T(8,128)S(1)}, f32[8,512]{1,0:T(8,128)}, u32[]{:S(2)}) copy-start(f32[8,512]{1,0:T(8,128)} %copy-done.93) | copy-start | bytes 49156
  146.5 50.5 %all-to-all-start.7 = ((f32[32,8,128]{2,1,0:T(8,128)}), f32[32,8,128]{2,1,0:T(8,128)S(1)}, u32[]{:S(2)}, u32[]{:S(2)}) async-start(f32[32,8,128]{2,1,0:T(8,128)} %get-tuple-element.115), calls=%async_computation.7 | async-start | bytes 262144 | tf_op jit(solution)/shard_map/all_to_all | solution.py:540
  329.9 3.2 copy-start.105
  333.1 2.9 copy-start.104
  (46 other events, 34.7 us)
Sparse Core Ops, SparseCore 0:
  146.0 183.8 all-reduce.3

commit v2 on v1

--- a/solution.py
+++ b/solution.py
@@ -1,4 +1,5 @@
 import functools
+import math
 
 import jax
 import jax.numpy as jnp
@@ -29,6 +30,8 @@
         self.packed = rows * 2 * self.half
         self.stat = 2 * width // LANES
         self.tokens = self.T * self.all
+        self.bits = self.all.bit_length() - 1
+        self.extra = 0
 
 
 def dot(a, b):
@@ -58,12 +61,13 @@
     return lax.fori_loop(0, z.T // TILE, one, carry)
 
 
-def pack(ref, rows):
-    k = 0
+def pack(ref, rows, k=0):
+    w = ref.shape[1]
     for row in rows:
-        for i in range(row.shape[1] // LANES):
-            ref[k : k + 1, :] = row[:, i * LANES : (i + 1) * LANES]
+        for i in range(row.shape[1] // w):
+            ref[k : k + 1, :] = row[:, i * w : (i + 1) * w]
             k += 1
+    return k
 
 
 def unpack(ref, first, count):
@@ -222,9 +226,18 @@
     return full(0), full(1), full(2), row(3), row(4)
 
 
-def prepare(z, len_ref, x_ref, gout_ref, rate_ref, phase_ref, v_ref, up_ref, stat_ref, keep_f, keep_r, chunk_f, chunk_r, dev_f, dev_r, tab_ref, power_ref, tile_ref, natural_ref):
+def prepare(z, len_hbm, x_hbm, gout_hbm, rate_hbm, phase_hbm, gain_hbm, bias_hbm, skip_hbm, bglu_hbm, win_hbm, wout_hbm, wglu_hbm,
+            v_ref, up_ref, stat_ref, keep_f, keep_r, chunk_f, chunk_r, dev_f, dev_r, tab_ref, power_ref,
+            gain_ref, bias_ref, skip_ref, bglu_ref, win_ref, wout_ref, wglu_ref,
+            tile_ref, natural_ref, x_ref, gout_ref, rate_ref, phase_ref, len_ref, sem):
+    moves = [(x_hbm, x_ref), (len_hbm, len_ref), (rate_hbm, rate_ref), (phase_hbm, phase_ref), (gout_hbm, gout_ref),
+             (gain_hbm, gain_ref), (bias_hbm, bias_ref), (win_hbm, win_ref), (skip_hbm, skip_ref), (bglu_hbm, bglu_ref),
+             (wout_hbm, wout_ref), (wglu_hbm, wglu_ref)]
+    copies = [pltpu.make_async_copy(a, b, sem.at[i]) for i, (a, b) in enumerate(moves)]
+    for c in copies:
+        c.start()
+    copies[0].wait()
     to_steps(z, lambda rows: x_ref[rows, :].astype(F32), v_ref, natural_ref)
-    to_steps(z, lambda rows: gout_ref[rows, :].astype(F32), up_ref, natural_ref)
 
     def body(rows, c):
         v = v_ref[rows, :]
@@ -234,6 +247,9 @@
     s0, s1 = tiles(z, body, (zero, zero))
     pack(tile_ref, [jnp.sum(s0, 0, keepdims=True), jnp.sum(s1, 0, keepdims=True)])
     spread(stat_ref, tile_ref)
+    for c in copies[1:5]:
+        c.wait()
+    to_steps(z, lambda rows: gout_ref[rows, :].astype(F32), up_ref, natural_ref)
     base = lax.axis_index("tm") * z.S
     place = lax.broadcasted_iota(jnp.int32, (z.S, LANES), 0)
     at = base + (place % CHUNKS) * z.L + place // CHUNKS
@@ -284,6 +300,8 @@
             tab_ref[b * 8 + i : b * 8 + i + 1, :] = jnp.zeros_like(lr)
         pack(power_ref.at[2 * b], [device_power[0], device_power[0]] * z.R)
         pack(power_ref.at[2 * b + 1], [-device_power[1], device_power[1]] * z.R)
+    for c in copies[5:]:
+        c.wait()
 
 
 def enter(z, b, stat_ref, v_ref, gain_ref, bias_ref, win_ref, keep_ref, chunk_ref, tab_ref,
@@ -418,8 +436,8 @@
 
 
 def finish(z, b, recv_ref, dev_ref, power_ref, ends_ref, chunk_ref, dh_ref, keep_ref, tab_ref, proj_ref, h_ref, carry_ref,
-           fwd_keep_ref, dy_ref, v_ref, norm_ref, skip_ref, win_ref,
-           dplow_ref, dxn_ref, stat_ref, lam_ref, tile_ref, adj_carry_ref, stat_tile):
+           fwd_keep_ref, dy_ref, v_ref, norm_ref, skip_ref, win_ref, emit,
+           dplow_ref, dxn_ref, lam_ref, tile_ref, adj_carry_ref):
     lr, li, gamma, pr, pi = lam_rows(z, tab_ref, b)
     reverse = b == 0
     state = carries(z, recv_ref, dev_ref, power_ref, b, -1.0, ends_ref, chunk_ref, pr, -pi, tile_ref, adj_carry_ref, reverse)
@@ -459,14 +477,10 @@
 
     zero = jnp.zeros((8, z.D), F32)
     s0, s1 = tiles(z, body, (zero, zero))
-    pack(stat_tile, [jnp.sum(s0, 0, keepdims=True), jnp.sum(s1, 0, keepdims=True)])
-    spread(stat_ref, stat_tile)
-
-
-def norm_grad(z, b, stat_ref, stat_tile, norm_ref, gain_ref, total_ref):
-    bias_sum, gain_sum = two_sums(stat_ref, stat_tile, z)
-    total_ref[0:1, :] = bias_sum
-    total_ref[1:2, :] = gain_sum
+    emit(jnp.sum(s0, 0, keepdims=True), jnp.sum(s1, 0, keepdims=True))
+
+
+def norm_grad(z, b, bias_sum, gain_sum, norm_ref, gain_ref):
     mean, rstd = norm_ref[0:1, :], norm_ref[1:2, :]
     gain = gain_ref[b : b + 1, :]
     scale, shift, slope = rstd * gain, rstd * gain * bias_sum / z.tokens, rstd * gain * gain_sum / z.tokens
@@ -478,9 +492,12 @@
 
 
 def lower_block(z, stat_ref, dxn_ref, v1_ref, norm1_ref, gout_ref, sig_ref, gate_ref, slope_ref, v_ref, norm_ref, gain_ref, bias_ref,
-                wglu_ref, wout_ref, keep_ref, chunk_ref, tab_ref,
-                total_ref, e_ref, dz_ref, dy_ref, dylow_ref, dh_ref, ends_ref, send_ref, small_ref, tile_ref, stat_tile):
-    grad = norm_grad(z, 1, stat_ref, stat_tile, norm1_ref, gain_ref, total_ref)
+                wglu_ref, wout_ref, keep_ref, chunk_ref, tab_ref, act_ref, hlow_ref,
+                total_ref, e_ref, dy_ref, dylow_ref, dh_ref, ends_ref, send_ref, small_ref, half_keep, half_send, tile_ref, stat_tile, dz_ref):
+    bias_sum, gain_sum = two_sums(stat_ref, stat_tile, z)
+    grad = norm_grad(z, 1, bias_sum, gain_sum, norm1_ref, gain_ref)
+    total_ref[0:1, :] = bias_sum
+    total_ref[1:2, :] = gain_sum
     d = z.D
 
     def body(rows, c):
@@ -495,10 +512,71 @@
     s0, s1 = tiles(z, body, (zero, zero))
     descend(z, 0, jnp.concatenate([s0, s1], axis=1), dz_ref, slope_ref, v_ref, norm_ref, gain_ref, bias_ref, wglu_ref, wout_ref,
             keep_ref, chunk_ref, tab_ref, dy_ref, dylow_ref, dh_ref, ends_ref, send_ref, small_ref, tile_ref)
-
-
-def last(z, stat_ref, dxn_ref, v_ref, norm_ref, gain_ref, e_ref, total_ref, grad_ref, stat_tile, natural_ref, work_ref):
-    grad = norm_grad(z, 0, stat_ref, stat_tile, norm_ref, gain_ref, total_ref)
+    glu, out = units(act_ref, dz_ref, half_keep), units(hlow_ref, dylow_ref, half_keep)
+    cut = (len(glu) + len(out)) // 2
+    first_split(z, half_keep, half_send, glu[:cut], glu[cut:] + out)
+
+
+def units(a_ref, b_ref, like):
+    w = like.shape[1]
+
+    def strip(i):
+        return lambda: dot_0(a_ref[...], b_ref[:, i * w : (i + 1) * w])
+
+    return [strip(i) for i in range(b_ref.shape[1] // w)]
+
+
+def finish_upper(z, *refs):
+    ins, (act_ref, dz_ref, hlow_ref, dylow_ref, low_ref), outs = refs[:17], refs[17:22], refs[22:]
+    dxn_ref, stat_ref, lam_ref, keep_ref, send_ref, dplow_ref, tile_ref, carry_ref, stat_tile = outs
+
+    def emit(bias_sum, gain_sum):
+        pack(stat_tile, [bias_sum, gain_sum])
+        spread(stat_ref, stat_tile)
+
+    finish(z, 1, *ins, emit, dplow_ref, dxn_ref, lam_ref, tile_ref, carry_ref)
+    first_split(z, keep_ref, send_ref, units(act_ref, dz_ref, keep_ref),
+                units(hlow_ref, dylow_ref, keep_ref) + units(low_ref, dplow_ref, keep_ref))
+
+
+def finish_lower(z, *refs):
+    ins, (low_ref, small0_ref, small1_ref, lam1_ref), outs = refs[:17], refs[17:21], refs[21:]
+    dxn_ref, keep_ref, send_ref, dplow_ref, lam_ref, tile_ref, carry_ref = outs
+    first = keep_ref.shape[0] - z.extra
+
+    def emit(bias_sum, gain_sum):
+        sums = [bias_sum, gain_sum]
+        for small, lam in ((small0_ref, lam_ref), (small1_ref, lam1_ref)):
+            sums += [small[0:1, :], small[1:2, :], small[2:3, :], lam[0:1, :], lam[1:2, :]]
+        for ref in (keep_ref, send_ref):
+            k = pack(ref, sums, first)
+            if k < ref.shape[0]:
+                ref[k:, :] = jnp.zeros((ref.shape[0] - k, ref.shape[1]), F32)
+
+    finish(z, 0, *ins, emit, dplow_ref, dxn_ref, lam_ref, tile_ref, carry_ref)
+    strips = units(low_ref, dplow_ref, keep_ref)
+    first_split(z, keep_ref, send_ref, strips[: len(strips) // 2], strips[len(strips) // 2 :])
+
+
+def last(z, small_ref, dxn_ref, v_ref, norm_ref, gain_ref, e_ref, total1_ref, grad_ref, gain_out, bias_out, rate_out, phase_out, skip_out,
+         bglu_out, natural_ref, work_ref):
+    w = small_ref.shape[1]
+    at = [0]
+
+    def take(width):
+        row = unpack(small_ref, at[0], width // w)
+        at[0] += width // w
+        return row
+
+    bias_sum, gain_sum = take(z.D), take(z.D)
+    grad = norm_grad(z, 0, bias_sum, gain_sum, norm_ref, gain_ref)
+    bias_out[0:1, :] = bias_sum
+    gain_out[0:1, :] = gain_sum
+    bias_out[1:2, :] = total1_ref[0:1, :]
+    gain_out[1:2, :] = total1_ref[1:2, :]
+    for b in range(2):
+        for ref, width in ((skip_out, z.D), (bglu_out, 2 * z.D), (rate_out, z.N), (phase_out, z.N)):
+            ref[b : b + 1, :] = take(width)
 
     def body(rows, c):
         work_ref[rows, :] = grad(dxn_ref[rows, :], v_ref[rows, :], e_ref[rows, :])
@@ -508,24 +586,168 @@
     to_time(z, work_ref, grad_ref, natural_ref)
 
 
-def outer(z, act_ref, dz_ref, hlow_ref, dylow_ref, wglu_ref, wout_ref):
-    wglu_ref[...] = dot_0(act_ref[...], dz_ref[...])
-    wout_ref[...] = dot_0(hlow_ref[...], dylow_ref[...])
-
-
-def outer_in(z, low_ref, dplow_ref, win_ref):
-    win_ref[...] = dot_0(low_ref[...], dplow_ref[...])
-
-
-def run(kernel, name, outs, args, scratch=(), smem=0):
-    spaces = [pltpu.SMEM] * smem + [pltpu.VMEM] * (len(args) - smem)
+GRAD_TILE = 64
+STRIP = 256
+
+
+def own_bit(z, step):
+    me = lax.axis_index("tm") * z.rows + lax.axis_index("rows")
+    if step in (1, 2) and z.bits > 2:
+        odd = me % 2
+        bit = odd + 2 * (1 - odd) if step == 1 else 2 * odd + (1 - odd)
+        return (me >> bit) % 2
+    return (me >> step) % 2
+
+
+def pairs(z, step):
+    out = []
+    for i in range(z.all):
+        bit = step
+        if step in (1, 2) and z.bits > 2:
+            bit = (1 if i % 2 else 2) if step == 1 else (2 if i % 2 else 1)
+        out.append((i, i ^ (1 << bit)))
+    return out
+
+
+def first_split(z, keep_ref, send_ref, low, high):
+    bit = own_bit(z, 0)
+    n = z.D
+
+    def write(ref, products):
+        for i, product in enumerate(products):
+            ref[i * n : (i + 1) * n, :] = product()
+
+    @pl.when(bit == 0)
+    def _():
+        write(keep_ref, low)
+        write(send_ref, high)
+
+    @pl.when(bit == 1)
+    def _():
+        write(keep_ref, high)
+        write(send_ref, low)
+
+
+def strips_of(n):
+    size = math.gcd(GRAD_TILE, n)
+
+    def rows(part, i):
+        return pl.ds(pl.multiple_of(part * n + i * size, math.gcd(size, 8)), size)
+
+    return n // size, rows
+
+
+def halves(z, step, extra, keep_ref, recv_ref, next_ref, send_ref):
+    n = next_ref.shape[0] - extra
+    bit = own_bit(z, step)
+    count, rows = strips_of(n)
+
+    def one(i, c):
+        for ref, part in ((send_ref, 1 - bit), (next_ref, bit)):
+            ref[rows(0, i), :] = keep_ref[rows(part, i), :] + recv_ref[rows(part, i), :]
+        return c
+
+    lax.fori_loop(0, count, one, 0)
+    if extra:
+        both = keep_ref[2 * n :, :] + recv_ref[2 * n :, :]
+        next_ref[n:, :] = both
+        send_ref[n:, :] = both
+
+
+def total(extra, keep_ref, recv_ref, out_ref, *extra_ref):
+    n = out_ref.shape[0]
+    out_ref[...] = keep_ref[0:n, :] + recv_ref[0:n, :]
+    if extra:
+        extra_ref[0][...] = keep_ref[n:, :] + recv_ref[n:, :]
+
+
+def join(z, step, own_ref, recv_ref, out_ref):
+    n = own_ref.shape[0]
+    bit = own_bit(z, step)
+    count, rows = strips_of(n)
+
+    def one(i, c):
+        for ref, part in ((own_ref, bit), (recv_ref, 1 - bit)):
+            out_ref[rows(part, i), :] = ref[rows(0, i), :]
+        return c
+
+    lax.fori_loop(0, count, one, 0)
+
+
+class Exchange:
+    def __init__(self, z, keep, send, extra=0):
+        self.z, self.keep, self.send, self.extra = z, keep, send, extra
+        self.step, self.up, self.small = 0, False, None
+        self.width = keep.shape[1]
+
+    def go(self):
+        self.got = lax.ppermute(self.send, ("tm", "rows"), pairs(self.z, self.step))
+
+    def settle(self):
+        z, x = self.z, self.extra
+        n = self.keep.shape[0]
+        if self.up:
+            (self.keep,) = run(functools.partial(join, z, self.step), "join", [((2 * n, self.width), F32)], (self.keep, self.got))
+            self.send = self.keep
+            self.step -= 1
+            return
+        n -= x
+        self.step += 1
+        if self.step < z.bits:
+            half = ((n // 2 + x, self.width), F32)
+            self.keep, self.send = run(functools.partial(halves, z, self.step, x), "halves", [half, half], (self.keep, self.got))
+            return
+        outs = [((n, self.width), F32)] + ([((x, self.width), F32)] if x else [])
+        self.keep, *self.small = run(functools.partial(total, x), "total", outs, (self.keep, self.got))
+        self.send, self.up = self.keep, True
+        self.step = z.bits - 1
+
+    @property
+    def closing(self):
+        return self.up and self.step == 0
+
+
+def assemble(z, own1, got1, owna, gota, ownb, gotb, win_out, wout_out, wglu_out, sem):
+    bit = own_bit(z, 0)
+    w = own1.shape[1]
+
+    def strips(out, b):
+        return [out.at[b, :, i * w : (i + 1) * w] for i in range(out.shape[2] // w)]
+
+    places = [strips(wglu_out, 1) + strips(wout_out, 1) + strips(win_out, 1), strips(wglu_out, 0) + strips(wout_out, 0), strips(win_out, 0)]
+
+    def place(halves_of):
+        copies = []
+        for (low, high), outs in zip(halves_of, places):
+            cut = len(outs) // 2
+            for ref, part in ((low, outs[:cut]), (high, outs[cut:])):
+                for i, out in enumerate(part):
+                    copies.append(pltpu.make_async_copy(ref.at[i * z.D : (i + 1) * z.D, :], out, sem.at[len(copies)]))
+        for c in copies:
+            c.start()
+        for c in copies:
+            c.wait()
+
+    @pl.when(bit == 0)
+    def _():
+        place([(own1, got1), (owna, gota), (ownb, gotb)])
+
+    @pl.when(bit == 1)
+    def _():
+        place([(got1, own1), (gota, owna), (gotb, ownb)])
+
+
+def run(kernel, name, outs, args, scratch=(), sems=0, source=pltpu.VMEM, target=pltpu.VMEM):
+    if source is pltpu.HBM:
+        args = [pltpu.with_memory_space_constraint(a, source) for a in args]
+    shapes = [pltpu.VMEM(s, t) if t != jnp.int32 else pltpu.SMEM(s, t) for s, t in scratch]
     return pl.pallas_call(
         kernel,
         out_shape=[jax.ShapeDtypeStruct(s, t) for s, t in outs],
-        in_specs=[pl.BlockSpec(memory_space=m) for m in spaces],
-        out_specs=[pl.BlockSpec(memory_space=pltpu.VMEM)] * len(outs),
-        scratch_shapes=[pltpu.VMEM(s, t) for s, t in scratch],
-        compiler_params=pltpu.CompilerParams(vmem_limit_bytes=24 << 20),
+        in_specs=[pl.BlockSpec(memory_space=source)] * len(args),
+        out_specs=[pl.BlockSpec(memory_space=target)] * len(outs),
+        scratch_shapes=shapes + ([pltpu.SemaphoreType.DMA((sems,))] if sems else []),
+        compiler_params=pltpu.CompilerParams(vmem_limit_bytes=16 << 20),
         name=name,
     )(*args)
 
@@ -555,10 +777,13 @@
     bind = functools.partial
 
     natural = ((D // LANES, T, LANES), F32)
-    x, gout, stat0, keep_f, keep_r, chunk_f, chunk_r, dev_f, dev_r, tab, power = run(
+    (x, gout, stat0, keep_f, keep_r, chunk_f, chunk_r, dev_f, dev_r, tab, power,
+     bn_gain, bn_bias, skip_gain, b_glu, w_in, w_out, w_glu) = run(
         bind(prepare, z), "prepare",
-        [full, full, stat_shape, mask, mask, chunk_mask, chunk_mask, send_shape, send_shape, ((16, N), F32), ((4, z.packed, LANES), F32)],
-        (lengths, x_in.reshape(T, D), grad_out.reshape(T, D), decay_rate, phase), [stat_tile, natural], smem=1)
+        [full, full, stat_shape, mask, mask, chunk_mask, chunk_mask, send_shape, send_shape, ((16, N), F32), ((4, z.packed, LANES), F32)]
+        + [(a.shape, a.dtype) for a in (bn_gain, bn_bias, skip_gain, b_glu, w_in, w_out, w_glu)],
+        (lengths, x_in.reshape(T, D), grad_out.reshape(T, D), decay_rate, phase, bn_gain, bn_bias, skip_gain, b_glu, w_in, w_out, w_glu),
+        [stat_tile, natural, low, low, ((2, N), F32), ((2, N), F32), (lengths.shape, jnp.int32)], sems=12, source=pltpu.HBM)
     stat0 = swap(stat0, everyone)
     norm0, low0, proj0, ends0, send0 = run(
         bind(enter, z, 0), "enter0", [norm_shape, low, full_n, chunk, send_shape],
@@ -579,45 +804,73 @@
         (send1, dev_r, power, ends1, chunk_r, proj1, keep_r, tab, v1, norm1, bn_gain, bn_bias, skip_gain, w_out, w_glu, b_glu, gout,
          keep_f, chunk_f), [tile, wide_f, full, natural])
     adj1 = swap(adj1, "tm")
-    gwglu1, gwout1 = run(bind(outer, z), "outer1", [((D, 2 * D), F32), ((2 * N, D), F32)], (act1, dz1, hlow1, dylow1))
-    dplow1, dxn1, sum1, lam1 = run(
-        bind(finish, z, 1), "finish1", [low_n, full, stat_shape, lam_shape],
-        (adj1, dev_f, power, adj_ends1, chunk_f, dh1, keep_f, tab, proj1, h1, carry1, keep_r, dy1, v1, norm1, skip_gain, w_in),
-        [tile, chunk, stat_tile])
+    W = STRIP if D * D // STRIP % (8 * z.all) == 0 else LANES
+
+    def part(count):
+        return ((count * D // W * D // 2, W), F32)
+
+    dxn1, sum1, lam1, keep1, send1 = run(
+        bind(finish_upper, z), "finish1", [full, stat_shape, lam_shape, part(4), part(4)],
+        (adj1, dev_f, power, adj_ends1, chunk_f, dh1, keep_f, tab, proj1, h1, carry1, keep_r, dy1, v1, norm1, skip_gain, w_in,
+         act1, dz1, hlow1, dylow1, low1),
+        [low_n, tile, chunk, stat_tile])
+    one = Exchange(z, keep1, send1)
+    one.go()
     sum1 = swap(sum1, everyone)
-    (gwin1,) = run(bind(outer_in, z), "outer_in1", [((D, 2 * N), F32)], (low1, dplow1))
-    total1, e1, dz0, dy0, dylow0, dh0, adj_ends0, adj0, small0 = run(
+    one.got, sum1 = lax.optimization_barrier((one.got, sum1))
+    one.settle()
+    total1, e1, dy0, dylow0, dh0, adj_ends0, adj0, small0, keepa, senda = run(
         bind(lower_block, z), "lower_block",
-        [norm_shape, full, wide_b, full, low, full_n, chunk, send_shape, small_shape],
-        (sum1, dxn1, v1, norm1, gout, sig0, gate0, slope0, x, norm0, bn_gain, bn_bias, w_glu, w_out, keep_r, chunk_r, tab),
-        [tile, stat_tile])
+        [norm_shape, full, full, low, full_n, chunk, send_shape, small_shape, part(3), part(3)],
+        (sum1, dxn1, v1, norm1, gout, sig0, gate0, slope0, x, norm0, bn_gain, bn_bias, w_glu, w_out, keep_r, chunk_r, tab, act0, hlow0),
+        [tile, stat_tile, wide_b])
+    two = Exchange(z, keepa, senda)
+    one.send, two.send, adj0 = lax.optimization_barrier((one.send, two.send, adj0))
+    one.go()
+    two.go()
     adj0 = swap(adj0, "tm")
-    gwglu0, gwout0 = run(bind(outer, z), "outer0", [((D, 2 * D), F32), ((2 * N, D), F32)], (act0, dz0, hlow0, dylow0))
-    dplow0, dxn0, sum0, lam0 = run(
-        bind(finish, z, 0), "finish0", [low_n, full, stat_shape, lam_shape],
-        (adj0, dev_r, power, adj_ends0, chunk_r, dh0, keep_r, tab, proj0, h0, carry0, keep_f, dy0, x, norm0, skip_gain, w_in),
-        [tile, chunk, stat_tile])
-    sum0 = swap(sum0, everyone)
-    (gwin0,) = run(bind(outer_in, z), "outer_in0", [((D, 2 * N), F32)], (low0, dplow0))
-    total0, grad_x = run(
-        bind(last, z), "last", [norm_shape, full], (sum0, dxn0, x, norm0, bn_gain, e1), [stat_tile, natural, full])
-    summed = lax.psum(
-        (jnp.stack([gwin0, gwin1]), jnp.stack([gwout0, gwout1]), jnp.stack([gwglu0, gwglu1]),
-         jnp.stack([small0, small1]), jnp.stack([lam0, lam1])), everyone)
-    gwin, gwout, gwglu, small, lam = summed
-    totals = jnp.stack([total0, total1])
+    one.got, two.got, adj0 = lax.optimization_barrier((one.got, two.got, adj0))
+    rows_sum = (2 * D + 2 * (3 * D + 2 * N)) // W
+    z.extra = -(-rows_sum // 8) * 8
+    last_part = ((D // W * D // 2 + z.extra, W), F32)
+    dxn0, keepb, sendb = run(
+        bind(finish_lower, z), "finish0", [full, last_part, last_part],
+        (adj0, dev_r, power, adj_ends0, chunk_r, dh0, keep_r, tab, proj0, h0, carry0, keep_f, dy0, x, norm0, skip_gain, w_in,
+         low0, small0, small1, lam1),
+        [low_n, lam_shape, tile, chunk])
+    one.settle()
+    two.settle()
+    three = Exchange(z, keepb, sendb, z.extra)
+    one.send, two.send, three.send = lax.optimization_barrier((one.send, two.send, three.send))
+    for e in (one, two, three):
+        e.go()
+    sets = [one, two, three]
+    ahead = three.send
+    while not all(e.closing for e in sets):
+        for e in sets:
+            if not e.closing:
+                e.got, _ = lax.optimization_barrier((e.got, ahead))
+                e.settle()
+                e.go()
+                ahead = e.send
+    sums = (((2, D), F32), ((2, D), F32), ((2, N), F32), ((2, N), F32), ((2, D), F32), ((2, 2 * D), F32))
+    grad_x, gain_out, bias_out, rate_out, phase_out, skip_out, bglu_out = run(
+        bind(last, z), "last", [full, *sums], (three.small[0], dxn0, x, norm0, bn_gain, e1, total1), [natural, full])
+    gwin, gwout, gwglu = run(
+        bind(assemble, z), "assemble", [((2, D, 2 * N), F32), ((2, 2 * N, D), F32), ((2, D, 2 * D), F32)],
+        (one.keep, one.got, two.keep, two.got, three.keep, three.got), sems=16, target=pltpu.HBM)
     return (
         out.reshape(rows, steps, width),
         grad_x.reshape(rows, steps, width),
-        totals[:, 1],
-        totals[:, 0],
+        gain_out,
+        bias_out,
         gwin,
-        lam[:, 0],
-        lam[:, 1],
+        rate_out,
+        phase_out,
         gwout,
-        small[:, 0],
+        skip_out,
         gwglu,
-        small[:, 1:3].reshape(2, 2 * D),
+        bglu_out,
     )
 
 

time: 347 us -> 201 us (0.58)
  local copies, waits for them, and re-layouts: 67.2 us -> 0 us
  waiting for transfers between devices: 131 us -> 75 us
  blocking collectives: 95.6 us -> 77.3 us
  between operations: 14.6 us -> 1.1 us
  starting transfers between devices: 14.3 us -> 26.4 us
  other arithmetic: 6.87 us -> 0 us
  Pallas kernels: 15.3 us -> 21.4 us
    psum x1 -> x0, waiting for transfers between devices: 131 us -> none  [body(): lax.psum((jnp.stack([gwin0, gwin1]), jnp.stack([gwout0, gwout1]), jnp.sta...]
    ppermute x0 -> x30, waiting for transfers between devices: none -> 75 us  [go(): self.got = lax.ppermute(self.send, ('tm', 'rows'), pairs(self.z, self.step))]
    unnamed x220 -> x0, local copies, waits for them, and re-layouts: 67.2 us -> none
    psum x1 -> x0, blocking collectives: 42.7 us -> none  [body(): lax.psum((jnp.stack([gwin0, gwin1]), jnp.stack([gwout0, gwout1]), jnp.sta...]
    ppermute x0 -> x30, starting transfers between devices: none -> 26.4 us  [go(): self.got = lax.ppermute(self.send, ('tm', 'rows'), pairs(self.z, self.step))]
    all_to_all x5 -> x7, blocking collectives: 52.9 us -> 77.3 us  [swap(): return lax.all_to_all(a, axis, 0, 0)]
    all_to_all x3 -> x0, starting transfers between devices: 14.3 us -> none  [swap(): return lax.all_to_all(a, axis, 0, 0)]
    another operation x5 -> x0, other arithmetic: 6.87 us -> none  [the longest x1 4.27 us: body(): jnp.stack([gwglu0, gwglu1])]
  transfers between devices with their start and end apart: 4 -> 30, of which waited for: 1 -> 20; matrix products, arithmetic and copies ran while one was open for 2% -> 0% of each run, Pallas kernels for 1% -> 1%
where the time goes in v2:
time: 201 us
  blocking collectives  77.3 us (38%)
  waiting for transfers between devices  75 us (37%)
  starting transfers between devices  26.4 us (13%)
  Pallas kernels  21.4 us (11%)
    all_to_all x7, blocking collectives, swap(): return lax.all_to_all(a, axis, 0, 0)  77.3 us
    ppermute x30, waiting for transfers between devices, go(): self.got = lax.ppermute(self.send, ('tm', 'rows'), pairs(self.z, self.step))  75 us
    ppermute x30, starting transfers between devices, go(): self.got = lax.ppermute(self.send, ('tm', 'rows'), pairs(self.z, self.step))  26.4 us
    pallas_call x37, Pallas kernels, run(): pl.pallas_call(kernel, out_shape=[jax.ShapeDtypeStruct(s, t) for s, t in...  21.4 us
  transfers between devices with their start and end apart: 30, of which 20 were waited for; matrix products, arithmetic and copies ran while one was open for 0% of the time, Pallas kernels for 1%

profile of v2, /device:TPU:0, one launch (start us, length us, event | category | flops | bytes accessed | tf_op | source)
XLA Modules:
  0.0 201.2 jit_solution(36862950565159479)
XLA Ops:
  0.6 2.6 %prepare.1 = (f32[256,512]{1,0:T(8,128)S(1)}, f32[256,512]{1,0:T(8,128)S(1)}, f32[32,8,128]{2,1,0:T(8,128)S(1)}, f32[256,128]{1,0:T(8,128)S(1)}, f32[256,128]{1,...) custom-call(s32[2,16]{1,0:T(2,128)} %len_hbm.1, ...), custom_call_target="tpu_custom_call" | custom-call | tf_op jit(solution)/shard_map/prepare/pallas_call | solution.py:744
  3.3 15.3 %all_to_all.35.stat_ref = f32[32,8,128]{2,1,0:T(8,128)S(1)} all-to-all(f32[32,8,128]{2,1,0:T(8,128)S(1)} %get-tuple-element.148), channel_id=1, replica_groups=mesh['tm'=8,'rows'=4] {'tm','rows'}, dimensions={0} | all-to-all | bytes 262144 | tf_op jit(solution)/shard_map/all_to_all | solution.py:762
  18.6 0.6 enter0.1
  19.2 9.2 %all_to_all.36.recv_ref = f32[8,8,128]{2,1,0:T(8,128)S(1)} all-to-all(f32[8,8,128]{2,1,0:T(8,128)S(1)} %get-tuple-element.156), channel_id=1, replica_groups=mesh['tm'=8,'rows'=4] {'tm'}, dimensions={0} | all-to-all | bytes 65536 | tf_op jit(solution)/shard_map/all_to_all | solution.py:762
  28.4 1.6 middle.1
  30.0 9.9 %all_to_all.37.stat_ref = f32[32,8,128]{2,1,0:T(8,128)S(1)} all-to-all(f32[32,8,128]{2,1,0:T(8,128)S(1)} %get-tuple-element.166), channel_id=1, replica_groups=mesh['tm'=8,'rows'=4] {'tm','rows'}, dimensions={0} | all-to-all | bytes 262144 | tf_op jit(solution)/shard_map/all_to_all | solution.py:762
  39.9 0.7 enter1.1
  40.6 9.1 %all_to_all.38.recv_ref = f32[8,8,128]{2,1,0:T(8,128)S(1)} all-to-all(f32[8,8,128]{2,1,0:T(8,128)S(1)} %get-tuple-element.170), channel_id=1, replica_groups=mesh['tm'=8,'rows'=4] {'tm'}, dimensions={0} | all-to-all | bytes 65536 | tf_op jit(solution)/shard_map/all_to_all | solution.py:762
  49.7 3.7 %turn.1 = (f32[256,512]{1,0:T(8,128)S(1)}, bf16[256,512]{1,0:T(8,128)(2,1)S(1)}, f32[16,512]{1,0:T(8,128)S(1)}, bf16[256,512]{1,0:T(8,128)(2,1)S(1)}, bf16[256,5...) custom-call(f32[8,8,128]{2,1,0:T(8,128)S(1)} %all_to_all.38.recv_ref, ...), custom_call_target="tpu_custom_call" | custom-call | tf_op jit(solution)/shard_map/turn/pallas_call | solution.py:744
  53.4 9.0 %all_to_all.39.refs_0_ = f32[8,8,128]{2,1,0:T(8,128)S(1)} all-to-all(f32[8,8,128]{2,1,0:T(8,128)S(1)} %get-tuple-element.177), channel_id=1, replica_groups=mesh['tm'=8,'rows'=4] {'tm'}, dimensions={0} | all-to-all | bytes 65536 | tf_op jit(solution)/shard_map/all_to_all | solution.py:762
  62.5 1.5 finish1.1
  64.1 9.9 %all_to_all.40.stat_ref = f32[32,8,128]{2,1,0:T(8,128)S(1)} all-to-all(f32[32,8,128]{2,1,0:T(8,128)S(1)} %get-tuple-element.190), channel_id=1, replica_groups=mesh['tm'=8,'rows'=4] {'tm','rows'}, dimensions={0} | all-to-all | bytes 262144 | tf_op jit(solution)/shard_map/all_to_all | solution.py:762
  74.0 0.3 halves.12
  74.3 2.8 %lower_block.1 = (f32[8,512]{1,0:T(8,128)S(1)}, f32[256,512]{1,0:T(8,128)S(1)}, f32[256,512]{1,0:T(8,128)S(1)}, bf16[256,512]{1,0:T(8,128)(2,1)}, f32[256,512]{1...) custom-call(f32[32,8,128]{2,1,0:T(8,128)S(1)} %all_to_all.40.stat_re, ...), custom_call_target="tpu_custom_call" | custom-call | tf_op jit(solution)/shard_map/lower_block/pallas_call | solution.py:744
  77.1 0.3 collective-permute-start.2
  77.4 0.4 collective-permute-start.1
  77.8 14.7 %all_to_all.41.refs_0_ = f32[8,8,128]{2,1,0:T(8,128)S(1)} all-to-all(f32[8,8,128]{2,1,0:T(8,128)S(1)} %get-tuple-element.204), channel_id=1, replica_groups=mesh['tm'=8,'rows'=4] {'tm'}, dimensions={0} | all-to-all | bytes 65536 | tf_op jit(solution)/shard_map/all_to_all | solution.py:762
  92.5 0.1 halves.13
  92.7 0.2 halves.14
  92.9 1.4 finish0.1
  94.3 0.5 collective-permute-start.4
  94.8 0.8 collective-permute-start.5
  95.5 14.1 %collective-permute-done.5.recv_ref = f32[512,256]{1,0:T(8,128)S(1)} collective-permute-done((f32[512,256]{1,0:T(8,128)S(1)}, f32[512,256]{1,0:T(8,128)S(1)}, u32[]{:S(2)}, u32[]{:S(2)}) %collective-permute-start.5) | collective-permute-done | bytes 524320 | tf_op jit(solution)/shard_map/ppermute | solution.py:684
  109.7 0.5 collective-permute-done.4.recv_ref
  110.2 0.1 halves.16
  110.3 1.7 collective-permute-start.7
  112.0 0.6 collective-permute-start.8
  112.7 0.7 collective-permute-start.6
  113.4 5.2 %collective-permute-done.8.recv_ref = f32[256,256]{1,0:T(8,128)S(1)} collective-permute-done((f32[256,256]{1,0:T(8,128)S(1)}, f32[256,256]{1,0:T(8,128)S(1)}, u32[]{:S(2)}, u32[]{:S(2)}) %collective-permute-start.8) | collective-permute-done | bytes 262176 | tf_op jit(solution)/shard_map/ppermute | solution.py:684
  118.7 0.8 collective-permute-start.11
  119.5 1.3 collective-permute-done.7.recv_ref
  120.9 1.0 collective-permute-start.10
  122.0 1.4 collective-permute-start.9
  123.3 3.3 %collective-permute-done.11.recv_ref = f32[128,256]{1,0:T(8,128)S(1)} collective-permute-done((f32[128,256]{1,0:T(8,128)S(1)}, f32[128,256]{1,0:T(8,128)S(1)}, u32[]{:S(2)}, u32[]{:S(2)}) %collective-permute-start.11) | collective-permute-done | bytes 131104 | tf_op jit(solution)/shard_map/ppermute | solution.py:684
  126.7 2.4 %collective-permute-done.10.recv_ref = f32[192,256]{1,0:T(8,128)S(1)} collective-permute-done((f32[192,256]{1,0:T(8,128)S(1)}, f32[192,256]{1,0:T(8,128)S(1)}, u32[]{:S(2)}, u32[]{:S(2)}) %collective-permute-start.10) | collective-permute-done | bytes 196640 | tf_op jit(solution)/shard_map/ppermute | solution.py:684
  129.2 3.7 %collective-permute-done.14.recv_ref = f32[128,256]{1,0:T(8,128)S(1)} collective-permute-done((f32[128,256]{1,0:T(8,128)S(1)}, f32[128,256]{1,0:T(8,128)S(1)}, u32[]{:S(2)}, u32[]{:S(2)}) %collective-permute-start.14) | collective-permute-done | bytes 131104 | tf_op jit(solution)/shard_map/ppermute | solution.py:684
  133.0 3.4 %collective-permute-start.13 = (f32[96,256]{1,0:T(8,128)S(1)}, f32[96,256]{1,0:T(8,128)S(1)}, u32[]{:S(2)}, u32[]{:S(2)}) collective-permute-start(f32[96,256]{1,0:T(8,128)S(1)} %get-tuple-element.248), channel_id=1, source_target_pairs={{0,16},{1,17},{2,18},{3,19},{4,20},{5,21},{6,22},{7,23},{8,24},{9,... | collective-permute-start | bytes 294920 | tf_op jit(solution)/shard_map/ppermute | solution.py:684
  136.4 2.6 %collective-permute-done.13.recv_ref = f32[96,256]{1,0:T(8,128)S(1)} collective-permute-done((f32[96,256]{1,0:T(8,128)S(1)}, f32[96,256]{1,0:T(8,128)S(1)}, u32[]{:S(2)}, u32[]{:S(2)}) %collective-permute-start.13) | collective-permute-done | bytes 98336 | tf_op jit(solution)/shard_map/ppermute | solution.py:684
  139.0 3.2 %collective-permute-done.12.recv_ref = f32[88,256]{1,0:T(8,128)S(1)} collective-permute-done((f32[88,256]{1,0:T(8,128)S(1)}, f32[88,256]{1,0:T(8,128)S(1)}, u32[]{:S(2)}, u32[]{:S(2)}) %collective-permute-start.12) | collective-permute-done | bytes 90144 | tf_op jit(solution)/shard_map/ppermute | solution.py:684
  142.3 1.5 collective-permute-start.18
  143.8 0.1 collective-permute-start.16
  143.9 2.8 %collective-permute-start.15 = (f32[56,256]{1,0:T(8,128)S(1)}, f32[56,256]{1,0:T(8,128)S(1)}, u32[]{:S(2)}, u32[]{:S(2)}) collective-permute-start(f32[56,256]{1,0:T(8,128)S(1)} %get-tuple-element.257), channel_id=1, source_target_pairs={{0,16},{1,17},{2,18},{3,19},{4,20},{5,21},{6,22},{7,23},{8,24},{9,... | collective-permute-start | bytes 172040 | tf_op jit(solution)/shard_map/ppermute | solution.py:684
  146.7 4.0 %collective-permute-done.16.recv_ref = f32[96,256]{1,0:T(8,128)S(1)} collective-permute-done((f32[96,256]{1,0:T(8,128)S(1)}, f32[96,256]{1,0:T(8,128)S(1)}, u32[]{:S(2)}, u32[]{:S(2)}) %collective-permute-start.16) | collective-permute-done | bytes 98336 | tf_op jit(solution)/shard_map/ppermute | solution.py:684
  150.8 0.6 collective-permute-done.15.recv_ref
  151.4 0.4 collective-permute-done.18.recv_ref
  151.9 2.8 %collective-permute-start.19 = (f32[1024,256]{1,0:T(8,128)S(1)}, f32[1024,256]{1,0:T(8,128)S(1)}, u32[]{:S(2)}, u32[]{:S(2)}) collective-permute-start(f32[1024,256]{1,0:T(8,128)S(1)} %join.15.own_ref), channel_id=1, source_target_pairs={{0,4},{1,3},{2,6},{3,1},{4,0},{5,7},{6,2},{7,5},{8,12},{9,11},{10,... | collective-permute-start | bytes 3145736 | tf_op jit(solution)/shard_map/ppermute | solution.py:684
  154.6 6.0 %collective-permute-done.21.recv_ref = f32[192,256]{1,0:T(8,128)S(1)} collective-permute-done((f32[192,256]{1,0:T(8,128)S(1)}, f32[192,256]{1,0:T(8,128)S(1)}, u32[]{:S(2)}, u32[]{:S(2)}) %collective-permute-start.21) | collective-permute-done | bytes 196640 | tf_op jit(solution)/shard_map/ppermute | solution.py:684
  160.7 0.2 collective-permute-start.23
  160.9 1.5 collective-permute-start.20
  162.4 3.3 %collective-permute-done.20.recv_ref = f32[32,256]{1,0:T(8,128)S(1)} collective-permute-done((f32[32,256]{1,0:T(8,128)S(1)}, f32[32,256]{1,0:T(8,128)S(1)}, u32[]{:S(2)}, u32[]{:S(2)}) %collective-permute-start.20) | collective-permute-done | bytes 32800 | tf_op jit(solution)/shard_map/ppermute | solution.py:684
  165.7 5.8 %collective-permute-done.19.recv_ref = f32[1024,256]{1,0:T(8,128)S(1)} collective-permute-done((f32[1024,256]{1,0:T(8,128)S(1)}, f32[1024,256]{1,0:T(8,128)S(1)}, u32[]{:S(2)}, u32[]{:S(2)}) %collective-permute-start.19) | collective-permute-done | bytes 1048608 | tf_op jit(solution)/shard_map/ppermute | solution.py:684
  171.5 0.2 join.18.own1
  171.8 1.8 collective-permute-start.24
  173.6 0.1 collective-permute-start.25
  173.7 4.4 %collective-permute-done.25.recv_ref = f32[64,256]{1,0:T(8,128)S(1)} collective-permute-done((f32[64,256]{1,0:T(8,128)S(1)}, f32[64,256]{1,0:T(8,128)S(1)}, u32[]{:S(2)}, u32[]{:S(2)}) %collective-permute-start.25) | collective-permute-done | bytes 65568 | tf_op jit(solution)/shard_map/ppermute | solution.py:684
  178.1 5.7 %collective-permute-done.24.recv_ref = f32[768,256]{1,0:T(8,128)S(1)} collective-permute-done((f32[768,256]{1,0:T(8,128)S(1)}, f32[768,256]{1,0:T(8,128)S(1)}, u32[]{:S(2)}, u32[]{:S(2)}) %collective-permute-start.24) | collective-permute-done | bytes 786464 | tf_op jit(solution)/shard_map/ppermute | solution.py:684
  183.8 0.1 join.21.owna
  184.1 1.7 collective-permute-start.27
  185.8 3.3 %collective-permute-done.27.recv_ref = f32[128,256]{1,0:T(8,128)S(1)} collective-permute-done((f32[128,256]{1,0:T(8,128)S(1)}, f32[128,256]{1,0:T(8,128)S(1)}, u32[]{:S(2)}, u32[]{:S(2)}) %collective-permute-start.27) | collective-permute-done | bytes 131104 | tf_op jit(solution)/shard_map/ppermute | solution.py:684
  189.1 1.8 collective-permute-start.28
  190.9 4.6 %collective-permute-done.28.recv_ref = f32[256,256]{1,0:T(8,128)S(1)} collective-permute-done((f32[256,256]{1,0:T(8,128)S(1)}, f32[256,256]{1,0:T(8,128)S(1)}, u32[]{:S(2)}, u32[]{:S(2)}) %collective-permute-start.28) | collective-permute-done | bytes 262176 | tf_op jit(solution)/shard_map/ppermute | solution.py:684
  195.7 1.3 last.1
  197.0 0.6 collective-permute-done.29.gotb
  197.6 3.4 %assemble.1 = (f32[2,512,512]{2,1,0:T(8,128)}, f32[2,512,512]{2,1,0:T(8,128)}, f32[2,512,1024]{2,1,0:T(8,128)}) custom-call(f32[2048,256]{1,0:T(8,128)S(1)} %join.18.own1, f32[2048,256]{1,0:T(8,128)S(1)} %collective-permute-done.22.got1, f32[1536,256]{1,0:T(8,128)S(1)} %join.21.owna, f32[1536,256]{1,0:T(8,128)S(1)} %collective-permute-done.26.gota, ...), custom_call_target="tpu_custom_call" | custom-call | tf_op jit(solution)/shard_map/assemble/pallas_call | solution.py:744
  (40 shorter events, 1.2 us)
Async XLA Ops:
  64.0 10.0 %collective-permute-start = (f32[2048,256]{1,0:T(8,128)S(1)}, f32[2048,256]{1,0:T(8,128)S(1)}, u32[]{:S(2)}, u32[]{:S(2)}) collective-permute-start(f32[2048,256]{1,0:T(8,128)S(1)} %get-tuple-element.189), channel_id=1, source_target_pairs={{0,1},{1,0},{2,3},{3,2},{4,5},{5,4},{6,7},{7,6},{8,9},{9,8},{10,11... | collective-permute-start | bytes 6291464 | tf_op jit(solution)/shard_map/ppermute | solution.py:684
  77.1 15.4 %collective-permute-start.2 = (f32[1536,256]{1,0:T(8,128)S(1)}, f32[1536,256]{1,0:T(8,128)S(1)}, u32[]{:S(2)}, u32[]{:S(2)}) collective-permute-start(f32[1536,256]{1,0:T(8,128)S(1)} %get-tuple-element.203), channel_id=1, source_target_pairs={{0,1},{1,0},{2,3},{3,2},{4,5},{5,4},{6,7},{7,6},{8,9},{9,8},{10,11... | collective-permute-start | bytes 4718600 | tf_op jit(solution)/shard_map/ppermute | solution.py:684
  77.4 15.2 %collective-permute-start.1 = (f32[1024,256]{1,0:T(8,128)S(1)}, f32[1024,256]{1,0:T(8,128)S(1)}, u32[]{:S(2)}, u32[]{:S(2)}) collective-permute-start(f32[1024,256]{1,0:T(8,128)S(1)} %get-tuple-element.202), channel_id=1, source_target_pairs={{0,4},{1,3},{2,6},{3,1},{4,0},{5,7},{6,2},{7,5},{8,12},{9,11},{10,... | collective-permute-start | bytes 3145736 | tf_op jit(solution)/shard_map/ppermute | solution.py:684
  94.3 15.9 %collective-permute-start.4 = (f32[768,256]{1,0:T(8,128)S(1)}, f32[768,256]{1,0:T(8,128)S(1)}, u32[]{:S(2)}, u32[]{:S(2)}) collective-permute-start(f32[768,256]{1,0:T(8,128)S(1)} %get-tuple-element.225), channel_id=1, source_target_pairs={{0,4},{1,3},{2,6},{3,1},{4,0},{5,7},{6,2},{7,5},{8,12},{9,11},{10,... | collective-permute-start | bytes 2359304 | tf_op jit(solution)/shard_map/ppermute | solution.py:684
  94.8 14.9 %collective-permute-start.5 = (f32[512,256]{1,0:T(8,128)S(1)}, f32[512,256]{1,0:T(8,128)S(1)}, u32[]{:S(2)}, u32[]{:S(2)}) collective-permute-start(f32[512,256]{1,0:T(8,128)S(1)} %get-tuple-element.227), channel_id=1, source_target_pairs={{0,2},{1,5},{2,0},{3,7},{4,6},{5,1},{6,4},{7,3},{8,10},{9,13},{10,... | collective-permute-start | bytes 1572872 | tf_op jit(solution)/shard_map/ppermute | solution.py:684
  95.5 17.1 %collective-permute-start.3 = (f32[536,256]{1,0:T(8,128)S(1)}, f32[536,256]{1,0:T(8,128)S(1)}, u32[]{:S(2)}, u32[]{:S(2)}) collective-permute-start(f32[536,256]{1,0:T(8,128)S(1)} %get-tuple-element.223), channel_id=1, source_target_pairs={{0,1},{1,0},{2,3},{3,2},{4,5},{5,4},{6,7},{7,6},{8,9},{9,8},{10,11... | collective-permute-start | bytes 1646600 | tf_op jit(solution)/shard_map/ppermute | solution.py:684
  110.3 10.5 %collective-permute-start.7 = (f32[384,256]{1,0:T(8,128)S(1)}, f32[384,256]{1,0:T(8,128)S(1)}, u32[]{:S(2)}, u32[]{:S(2)}) collective-permute-start(f32[384,256]{1,0:T(8,128)S(1)} %get-tuple-element.231), channel_id=1, source_target_pairs={{0,2},{1,5},{2,0},{3,7},{4,6},{5,1},{6,4},{7,3},{8,10},{9,13},{10,... | collective-permute-start | bytes 1179656 | tf_op jit(solution)/shard_map/ppermute | solution.py:684
  112.0 6.6 %collective-permute-start.8 = (f32[256,256]{1,0:T(8,128)S(1)}, f32[256,256]{1,0:T(8,128)S(1)}, u32[]{:S(2)}, u32[]{:S(2)}) collective-permute-start(f32[256,256]{1,0:T(8,128)S(1)} %get-tuple-element.229), channel_id=1, source_target_pairs={{0,8},{1,9},{2,10},{3,11},{4,12},{5,13},{6,14},{7,15},{8,0},{9,1},... | collective-permute-start | bytes 786440 | tf_op jit(solution)/shard_map/ppermute | solution.py:684
  112.7 9.2 %collective-permute-start.6 = (f32[280,256]{1,0:T(8,128)S(1)}, f32[280,256]{1,0:T(8,128)S(1)}, u32[]{:S(2)}, u32[]{:S(2)}) collective-permute-start(f32[280,256]{1,0:T(8,128)S(1)} %get-tuple-element.234), channel_id=1, source_target_pairs={{0,4},{1,3},{2,6},{3,1},{4,0},{5,7},{6,2},{7,5},{8,12},{9,11},{10,... | collective-permute-start | bytes 860168 | tf_op jit(solution)/shard_map/ppermute | solution.py:684
  118.7 8.0 %collective-permute-start.11 = (f32[128,256]{1,0:T(8,128)S(1)}, f32[128,256]{1,0:T(8,128)S(1)}, u32[]{:S(2)}, u32[]{:S(2)}) collective-permute-start(f32[128,256]{1,0:T(8,128)S(1)} %get-tuple-element.238), channel_id=1, source_target_pairs={{0,16},{1,17},{2,18},{3,19},{4,20},{5,21},{6,22},{7,23},{8,24},{9,... | collective-permute-start | bytes 393224 | tf_op jit(solution)/shard_map/ppermute | solution.py:684
  120.9 8.2 %collective-permute-start.10 = (f32[192,256]{1,0:T(8,128)S(1)}, f32[192,256]{1,0:T(8,128)S(1)}, u32[]{:S(2)}, u32[]{:S(2)}) collective-permute-start(f32[192,256]{1,0:T(8,128)S(1)} %get-tuple-element.240), channel_id=1, source_target_pairs={{0,8},{1,9},{2,10},{3,11},{4,12},{5,13},{6,14},{7,15},{8,0},{9,1},... | collective-permute-start | bytes 589832 | tf_op jit(solution)/shard_map/ppermute | solution.py:684
  122.0 7.2 %collective-permute-start.9 = (f32[152,256]{1,0:T(8,128)S(1)}, f32[152,256]{1,0:T(8,128)S(1)}, u32[]{:S(2)}, u32[]{:S(2)}) collective-permute-start(f32[152,256]{1,0:T(8,128)S(1)} %get-tuple-element.243), channel_id=1, source_target_pairs={{0,2},{1,5},{2,0},{3,7},{4,6},{5,1},{6,4},{7,3},{8,10},{9,13},{10,... | collective-permute-start | bytes 466952 | tf_op jit(solution)/shard_map/ppermute | solution.py:684
  126.6 6.2 %collective-permute-start.14 = (f32[128,256]{1,0:T(8,128)S(1)}, f32[128,256]{1,0:T(8,128)S(1)}, u32[]{:S(2)}, u32[]{:S(2)}) collective-permute-start(f32[128,256]{1,0:T(8,128)S(1)} %total.3.own_ref), channel_id=1, source_target_pairs={{0,16},{1,17},{2,18},{3,19},{4,20},{5,21},{6,22},{7,23},{8,24},{9,... | collective-permute-start | bytes 393224 | tf_op jit(solution)/shard_map/ppermute | solution.py:684
  132.9 9.3 %collective-permute-start.17 = (f32[256,256]{1,0:T(8,128)S(1)}, f32[256,256]{1,0:T(8,128)S(1)}, u32[]{:S(2)}, u32[]{:S(2)}) collective-permute-start(f32[256,256]{1,0:T(8,128)S(1)} %join.12.own_ref), channel_id=1, source_target_pairs={{0,8},{1,9},{2,10},{3,11},{4,12},{5,13},{6,14},{7,15},{8,0},{9,1},... | collective-permute-start | bytes 786440 | tf_op jit(solution)/shard_map/ppermute | solution.py:684
  133.0 6.1 %collective-permute-start.13 = (f32[96,256]{1,0:T(8,128)S(1)}, f32[96,256]{1,0:T(8,128)S(1)}, u32[]{:S(2)}, u32[]{:S(2)}) collective-permute-start(f32[96,256]{1,0:T(8,128)S(1)} %get-tuple-element.248), channel_id=1, source_target_pairs={{0,16},{1,17},{2,18},{3,19},{4,20},{5,21},{6,22},{7,23},{8,24},{9,... | collective-permute-start | bytes 294920 | tf_op jit(solution)/shard_map/ppermute | solution.py:684
  136.3 5.9 %collective-permute-start.12 = (f32[88,256]{1,0:T(8,128)S(1)}, f32[88,256]{1,0:T(8,128)S(1)}, u32[]{:S(2)}, u32[]{:S(2)}) collective-permute-start(f32[88,256]{1,0:T(8,128)S(1)} %get-tuple-element.251), channel_id=1, source_target_pairs={{0,8},{1,9},{2,10},{3,11},{4,12},{5,13},{6,14},{7,15},{8,0},{9,1},... | collective-permute-start | bytes 270344 | tf_op jit(solution)/shard_map/ppermute | solution.py:684
  142.3 9.4 %collective-permute-start.18 = (f32[512,256]{1,0:T(8,128)S(1)}, f32[512,256]{1,0:T(8,128)S(1)}, u32[]{:S(2)}, u32[]{:S(2)}) collective-permute-start(f32[512,256]{1,0:T(8,128)S(1)} %join.13.own_ref), channel_id=1, source_target_pairs={{0,2},{1,5},{2,0},{3,7},{4,6},{5,1},{6,4},{7,3},{8,10},{9,13},{10,... | collective-permute-start | bytes 1572872 | tf_op jit(solution)/shard_map/ppermute | solution.py:684
  143.8 7.0 %collective-permute-start.16 = (f32[96,256]{1,0:T(8,128)S(1)}, f32[96,256]{1,0:T(8,128)S(1)}, u32[]{:S(2)}, u32[]{:S(2)}) collective-permute-start(f32[96,256]{1,0:T(8,128)S(1)} %total.4.own_ref), channel_id=1, source_target_pairs={{0,16},{1,17},{2,18},{3,19},{4,20},{5,21},{6,22},{7,23},{8,24},{9,... | collective-permute-start | bytes 294920 | tf_op jit(solution)/shard_map/ppermute | solution.py:684
  143.9 7.5 %collective-permute-start.15 = (f32[56,256]{1,0:T(8,128)S(1)}, f32[56,256]{1,0:T(8,128)S(1)}, u32[]{:S(2)}, u32[]{:S(2)}) collective-permute-start(f32[56,256]{1,0:T(8,128)S(1)} %get-tuple-element.257), channel_id=1, source_target_pairs={{0,16},{1,17},{2,18},{3,19},{4,20},{5,21},{6,22},{7,23},{8,24},{9,... | collective-permute-start | bytes 172040 | tf_op jit(solution)/shard_map/ppermute | solution.py:684
  151.9 19.6 %collective-permute-start.19 = (f32[1024,256]{1,0:T(8,128)S(1)}, f32[1024,256]{1,0:T(8,128)S(1)}, u32[]{:S(2)}, u32[]{:S(2)}) collective-permute-start(f32[1024,256]{1,0:T(8,128)S(1)} %join.15.own_ref), channel_id=1, source_target_pairs={{0,4},{1,3},{2,6},{3,1},{4,0},{5,7},{6,2},{7,5},{8,12},{9,11},{10,... | collective-permute-start | bytes 3145736 | tf_op jit(solution)/shard_map/ppermute | solution.py:684
  154.6 6.0 %collective-permute-start.21 = (f32[192,256]{1,0:T(8,128)S(1)}, f32[192,256]{1,0:T(8,128)S(1)}, u32[]{:S(2)}, u32[]{:S(2)}) collective-permute-start(f32[192,256]{1,0:T(8,128)S(1)} %join.14.own_ref), channel_id=1, source_target_pairs={{0,8},{1,9},{2,10},{3,11},{4,12},{5,13},{6,14},{7,15},{8,0},{9,1},... | collective-permute-start | bytes 589832 | tf_op jit(solution)/shard_map/ppermute | solution.py:684
  160.7 11.0 %collective-permute-start.23 = (f32[384,256]{1,0:T(8,128)S(1)}, f32[384,256]{1,0:T(8,128)S(1)}, u32[]{:S(2)}, u32[]{:S(2)}) collective-permute-start(f32[384,256]{1,0:T(8,128)S(1)} %join.16.own_ref), channel_id=1, source_target_pairs={{0,2},{1,5},{2,0},{3,7},{4,6},{5,1},{6,4},{7,3},{8,10},{9,13},{10,... | collective-permute-start | bytes 1179656 | tf_op jit(solution)/shard_map/ppermute | solution.py:684
  160.9 4.8 %collective-permute-start.20 = (f32[32,256]{1,0:T(8,128)S(1)}, f32[32,256]{1,0:T(8,128)S(1)}, u32[]{:S(2)}, u32[]{:S(2)}) collective-permute-start(f32[32,256]{1,0:T(8,128)S(1)} %get-tuple-element.268.own_ref), channel_id=1, source_target_pairs={{0,16},{1,17},{2,18},{3,19},{4,20},{5,21},{6,22},{7,23},{8,24},{9,... | collective-permute-start | bytes 98312 | tf_op jit(solution)/shard_map/ppermute | solution.py:684
  171.8 12.1 %collective-permute-start.24 = (f32[768,256]{1,0:T(8,128)S(1)}, f32[768,256]{1,0:T(8,128)S(1)}, u32[]{:S(2)}, u32[]{:S(2)}) collective-permute-start(f32[768,256]{1,0:T(8,128)S(1)} %join.19.own_ref), channel_id=1, source_target_pairs={{0,4},{1,3},{2,6},{3,1},{4,0},{5,7},{6,2},{7,5},{8,12},{9,11},{10,... | collective-permute-start | bytes 2359304 | tf_op jit(solution)/shard_map/ppermute | solution.py:684
  173.6 24.0 %collective-permute-start.22 = (f32[2048,256]{1,0:T(8,128)S(1)}, f32[2048,256]{1,0:T(8,128)S(1)}, u32[]{:S(2)}, u32[]{:S(2)}) collective-permute-start(f32[2048,256]{1,0:T(8,128)S(1)} %join.18.own1), channel_id=1, source_target_pairs={{0,1},{1,0},{2,3},{3,2},{4,5},{5,4},{6,7},{7,6},{8,9},{9,8},{10,11... | collective-permute-start | bytes 6291464 | tf_op jit(solution)/shard_map/ppermute | solution.py:684
  173.6 4.5 %collective-permute-start.25 = (f32[64,256]{1,0:T(8,128)S(1)}, f32[64,256]{1,0:T(8,128)S(1)}, u32[]{:S(2)}, u32[]{:S(2)}) collective-permute-start(f32[64,256]{1,0:T(8,128)S(1)} %join.17.own_ref), channel_id=1, source_target_pairs={{0,8},{1,9},{2,10},{3,11},{4,12},{5,13},{6,14},{7,15},{8,0},{9,1},... | collective-permute-start | bytes 196616 | tf_op jit(solution)/shard_map/ppermute | solution.py:684
  184.0 13.6 %collective-permute-start.26 = (f32[1536,256]{1,0:T(8,128)S(1)}, f32[1536,256]{1,0:T(8,128)S(1)}, u32[]{:S(2)}, u32[]{:S(2)}) collective-permute-start(f32[1536,256]{1,0:T(8,128)S(1)} %join.21.owna), channel_id=1, source_target_pairs={{0,1},{1,0},{2,3},{3,2},{4,5},{5,4},{6,7},{7,6},{8,9},{9,8},{10,11... | collective-permute-start | bytes 4718600 | tf_op jit(solution)/shard_map/ppermute | solution.py:684
  184.1 5.0 %collective-permute-start.27 = (f32[128,256]{1,0:T(8,128)S(1)}, f32[128,256]{1,0:T(8,128)S(1)}, u32[]{:S(2)}, u32[]{:S(2)}) collective-permute-start(f32[128,256]{1,0:T(8,128)S(1)} %join.20.own_ref), channel_id=1, source_target_pairs={{0,2},{1,5},{2,0},{3,7},{4,6},{5,1},{6,4},{7,3},{8,10},{9,13},{10,... | collective-permute-start | bytes 393224 | tf_op jit(solution)/shard_map/ppermute | solution.py:684
  189.1 6.4 %collective-permute-start.28 = (f32[256,256]{1,0:T(8,128)S(1)}, f32[256,256]{1,0:T(8,128)S(1)}, u32[]{:S(2)}, u32[]{:S(2)}) collective-permute-start(f32[256,256]{1,0:T(8,128)S(1)} %join.22.own_ref), channel_id=1, source_target_pairs={{0,4},{1,3},{2,6},{3,1},{4,0},{5,7},{6,2},{7,5},{8,12},{9,11},{10,... | collective-permute-start | bytes 786440 | tf_op jit(solution)/shard_map/ppermute | solution.py:684
  195.6 2.0 collective-permute-start.29

commit v3 on v2

--- a/solution.py
+++ b/solution.py
@@ -410,8 +410,8 @@
 
 def turn(z, recv_ref, dev_ref, power_ref, ends_ref, chunk_ref, proj_ref, keep_ref, tab_ref, v_ref, norm_ref, gain_ref,
          bias_ref, skip_ref, wout_ref, wglu_ref, bglu_ref, gout_ref, adj_keep_ref, adj_chunk_ref,
-         h_ref, hlow_ref, carry_ref, act_ref, out_ref, dz_ref, dy_ref, dylow_ref, dh_ref, adj_ends_ref, send_ref, small_ref,
-         tile_ref, wide_ref, slope_ref, natural_ref):
+         h_ref, carry_ref, out_ref, dy_ref, dh_ref, adj_ends_ref, send_ref, small_ref, half_keep, half_send,
+         tile_ref, wide_ref, slope_ref, natural_ref, hlow_ref, act_ref, dz_ref, dylow_ref):
     mix(z, 1, recv_ref, dev_ref, power_ref, ends_ref, chunk_ref, proj_ref, keep_ref, tab_ref, v_ref, norm_ref, gain_ref,
         bias_ref, skip_ref, wout_ref, wglu_ref, h_ref, hlow_ref, carry_ref, slope_ref, act_ref, tile_ref, wide_ref)
     d = z.D
@@ -433,6 +433,7 @@
     to_time(z, dy_ref, out_ref, natural_ref)
     descend(z, 1, jnp.concatenate([s0, s1], axis=1), dz_ref, slope_ref, v_ref, norm_ref, gain_ref, bias_ref, wglu_ref, wout_ref,
             adj_keep_ref, adj_chunk_ref, tab_ref, dy_ref, dylow_ref, dh_ref, adj_ends_ref, send_ref, small_ref, tile_ref)
+    split_strips(z, half_keep, half_send, units(act_ref, dz_ref, half_keep) + units(hlow_ref, dylow_ref, half_keep))
 
 
 def finish(z, b, recv_ref, dev_ref, power_ref, ends_ref, chunk_ref, dh_ref, keep_ref, tab_ref, proj_ref, h_ref, carry_ref,
@@ -493,7 +494,7 @@
 
 def lower_block(z, stat_ref, dxn_ref, v1_ref, norm1_ref, gout_ref, sig_ref, gate_ref, slope_ref, v_ref, norm_ref, gain_ref, bias_ref,
                 wglu_ref, wout_ref, keep_ref, chunk_ref, tab_ref, act_ref, hlow_ref,
-                total_ref, e_ref, dy_ref, dylow_ref, dh_ref, ends_ref, send_ref, small_ref, half_keep, half_send, tile_ref, stat_tile, dz_ref):
+                total_ref, e_ref, dy_ref, dh_ref, ends_ref, send_ref, small_ref, half_keep, half_send, tile_ref, stat_tile, dz_ref, dylow_ref):
     bias_sum, gain_sum = two_sums(stat_ref, stat_tile, z)
     grad = norm_grad(z, 1, bias_sum, gain_sum, norm1_ref, gain_ref)
     total_ref[0:1, :] = bias_sum
@@ -512,9 +513,7 @@
     s0, s1 = tiles(z, body, (zero, zero))
     descend(z, 0, jnp.concatenate([s0, s1], axis=1), dz_ref, slope_ref, v_ref, norm_ref, gain_ref, bias_ref, wglu_ref, wout_ref,
             keep_ref, chunk_ref, tab_ref, dy_ref, dylow_ref, dh_ref, ends_ref, send_ref, small_ref, tile_ref)
-    glu, out = units(act_ref, dz_ref, half_keep), units(hlow_ref, dylow_ref, half_keep)
-    cut = (len(glu) + len(out)) // 2
-    first_split(z, half_keep, half_send, glu[:cut], glu[cut:] + out)
+    split_strips(z, half_keep, half_send, units(act_ref, dz_ref, half_keep) + units(hlow_ref, dylow_ref, half_keep))
 
 
 def units(a_ref, b_ref, like):
@@ -527,20 +526,18 @@
 
 
 def finish_upper(z, *refs):
-    ins, (act_ref, dz_ref, hlow_ref, dylow_ref, low_ref), outs = refs[:17], refs[17:22], refs[22:]
-    dxn_ref, stat_ref, lam_ref, keep_ref, send_ref, dplow_ref, tile_ref, carry_ref, stat_tile = outs
+    ins, outs = refs[:17], refs[17:]
+    dxn_ref, dplow_ref, stat_ref, lam_ref, tile_ref, carry_ref, stat_tile = outs
 
     def emit(bias_sum, gain_sum):
         pack(stat_tile, [bias_sum, gain_sum])
         spread(stat_ref, stat_tile)
 
     finish(z, 1, *ins, emit, dplow_ref, dxn_ref, lam_ref, tile_ref, carry_ref)
-    first_split(z, keep_ref, send_ref, units(act_ref, dz_ref, keep_ref),
-                units(hlow_ref, dylow_ref, keep_ref) + units(low_ref, dplow_ref, keep_ref))
 
 
 def finish_lower(z, *refs):
-    ins, (low_ref, small0_ref, small1_ref, lam1_ref), outs = refs[:17], refs[17:21], refs[21:]
+    ins, (low_ref, low1_ref, dplow1_ref, small0_ref, small1_ref, lam1_ref), outs = refs[:17], refs[17:23], refs[23:]
     dxn_ref, keep_ref, send_ref, dplow_ref, lam_ref, tile_ref, carry_ref = outs
     first = keep_ref.shape[0] - z.extra
 
@@ -554,8 +551,7 @@
                 ref[k:, :] = jnp.zeros((ref.shape[0] - k, ref.shape[1]), F32)
 
     finish(z, 0, *ins, emit, dplow_ref, dxn_ref, lam_ref, tile_ref, carry_ref)
-    strips = units(low_ref, dplow_ref, keep_ref)
-    first_split(z, keep_ref, send_ref, strips[: len(strips) // 2], strips[len(strips) // 2 :])
+    split_strips(z, keep_ref, send_ref, units(low1_ref, dplow1_ref, keep_ref) + units(low_ref, dplow_ref, keep_ref))
 
 
 def last(z, small_ref, dxn_ref, v_ref, norm_ref, gain_ref, e_ref, total1_ref, grad_ref, gain_out, bias_out, rate_out, phase_out, skip_out,
@@ -587,45 +583,44 @@
 
 
 GRAD_TILE = 64
+SEQ = (2, 1, 0)
+ORDERS = ((0, 1, 2, 3, 4), (0, 1, 2, 3, 4), (0, 1, 2, 3, 4))
 STRIP = 256
 
 
-def own_bit(z, step):
+def bit_of(z, place, parity):
+    if place in (1, 2) and z.bits > 2:
+        return place if parity else 3 - place
+    return place
+
+
+def own_bit(z, place):
     me = lax.axis_index("tm") * z.rows + lax.axis_index("rows")
-    if step in (1, 2) and z.bits > 2:
-        odd = me % 2
-        bit = odd + 2 * (1 - odd) if step == 1 else 2 * odd + (1 - odd)
-        return (me >> bit) % 2
-    return (me >> step) % 2
-
-
-def pairs(z, step):
-    out = []
-    for i in range(z.all):
-        bit = step
-        if step in (1, 2) and z.bits > 2:
-            bit = (1 if i % 2 else 2) if step == 1 else (2 if i % 2 else 1)
-        out.append((i, i ^ (1 << bit)))
-    return out
-
-
-def first_split(z, keep_ref, send_ref, low, high):
+    odd = me % 2
+    return (me >> (odd * bit_of(z, place, 1) + (1 - odd) * bit_of(z, place, 0))) % 2
+
+
+def pairs(z, place):
+    return [(i, i ^ (1 << bit_of(z, place, i % 2))) for i in range(z.all)]
+
+
+def split_strips(z, keep_ref, send_ref, strips):
     bit = own_bit(z, 0)
-    n = z.D
+    cut = len(strips) // 2
 
     def write(ref, products):
         for i, product in enumerate(products):
-            ref[i * n : (i + 1) * n, :] = product()
+            ref[i * z.D : (i + 1) * z.D, :] = product()
 
     @pl.when(bit == 0)
     def _():
-        write(keep_ref, low)
-        write(send_ref, high)
+        write(keep_ref, strips[:cut])
+        write(send_ref, strips[cut:])
 
     @pl.when(bit == 1)
     def _():
-        write(keep_ref, high)
-        write(send_ref, low)
+        write(keep_ref, strips[cut:])
+        write(send_ref, strips[:cut])
 
 
 def strips_of(n):
@@ -675,19 +670,20 @@
 
 
 class Exchange:
-    def __init__(self, z, keep, send, extra=0):
+    def __init__(self, z, keep, send, extra=0, order=()):
         self.z, self.keep, self.send, self.extra = z, keep, send, extra
+        self.order = order if len(order) == z.bits else tuple(range(z.bits))
         self.step, self.up, self.small = 0, False, None
         self.width = keep.shape[1]
 
     def go(self):
-        self.got = lax.ppermute(self.send, ("tm", "rows"), pairs(self.z, self.step))
+        self.got = lax.ppermute(self.send, ("tm", "rows"), pairs(self.z, self.order[self.step]))
 
     def settle(self):
         z, x = self.z, self.extra
         n = self.keep.shape[0]
         if self.up:
-            (self.keep,) = run(functools.partial(join, z, self.step), "join", [((2 * n, self.width), F32)], (self.keep, self.got))
+            (self.keep,) = run(functools.partial(join, z, self.order[self.step]), "join", [((2 * n, self.width), F32)], (self.keep, self.got))
             self.send = self.keep
             self.step -= 1
             return
@@ -695,7 +691,7 @@
         self.step += 1
         if self.step < z.bits:
             half = ((n // 2 + x, self.width), F32)
-            self.keep, self.send = run(functools.partial(halves, z, self.step, x), "halves", [half, half], (self.keep, self.got))
+            self.keep, self.send = run(functools.partial(halves, z, self.order[self.step], x), "halves", [half, half], (self.keep, self.got))
             return
         outs = [((n, self.width), F32)] + ([((x, self.width), F32)] if x else [])
         self.keep, *self.small = run(functools.partial(total, x), "total", outs, (self.keep, self.got))
@@ -714,7 +710,7 @@
     def strips(out, b):
         return [out.at[b, :, i * w : (i + 1) * w] for i in range(out.shape[2] // w)]
 
-    places = [strips(wglu_out, 1) + strips(wout_out, 1) + strips(win_out, 1), strips(wglu_out, 0) + strips(wout_out, 0), strips(win_out, 0)]
+    places = [strips(wglu_out, 1) + strips(wout_out, 1), strips(wglu_out, 0) + strips(wout_out, 0), strips(win_out, 1) + strips(win_out, 0)]
 
     def place(halves_of):
         copies = []
@@ -798,58 +794,65 @@
         bind(enter, z, 1), "enter1", [norm_shape, low, full_n, chunk, send_shape],
         (stat1, v1, bn_gain, bn_bias, w_in, keep_r, chunk_r, tab), [stat_tile, tile])
     send1 = swap(send1, "tm")
-    h1, hlow1, carry1, act1, out, dz1, dy1, dylow1, dh1, adj_ends1, adj1, small1 = run(
+    W = STRIP if D * D // STRIP % (8 * z.all) == 0 else LANES
+
+    def part(count, extra=0):
+        return ((count * D // W * D // 2 + extra, W), F32)
+
+    def tie(*values):
+        return lax.optimization_barrier(values)
+
+    h1, carry1, out, dy1, dh1, adj_ends1, adj1, small1, keep1, send1 = run(
         bind(turn, z), "turn",
-        [full_n, low_n, chunk, low, low, wide_b, full, low, full_n, chunk, send_shape, small_shape],
+        [full_n, chunk, low, full, full_n, chunk, send_shape, small_shape, part(3), part(3)],
         (send1, dev_r, power, ends1, chunk_r, proj1, keep_r, tab, v1, norm1, bn_gain, bn_bias, skip_gain, w_out, w_glu, b_glu, gout,
-         keep_f, chunk_f), [tile, wide_f, full, natural])
+         keep_f, chunk_f), [tile, wide_f, full, natural, low_n, low, wide_b, low])
+    one = Exchange(z, keep1, send1, order=ORDERS[0])
+    one.send, adj1 = tie(one.send, adj1)
+    one.go()
     adj1 = swap(adj1, "tm")
-    W = STRIP if D * D // STRIP % (8 * z.all) == 0 else LANES
-
-    def part(count):
-        return ((count * D // W * D // 2, W), F32)
-
-    dxn1, sum1, lam1, keep1, send1 = run(
-        bind(finish_upper, z), "finish1", [full, stat_shape, lam_shape, part(4), part(4)],
-        (adj1, dev_f, power, adj_ends1, chunk_f, dh1, keep_f, tab, proj1, h1, carry1, keep_r, dy1, v1, norm1, skip_gain, w_in,
-         act1, dz1, hlow1, dylow1, low1),
-        [low_n, tile, chunk, stat_tile])
-    one = Exchange(z, keep1, send1)
+    one.got, adj1 = tie(one.got, adj1)
+    one.settle()
+    dxn1, dplow1, sum1, lam1 = run(
+        bind(finish_upper, z), "finish1", [full, low_n, stat_shape, lam_shape],
+        (adj1, dev_f, power, adj_ends1, chunk_f, dh1, keep_f, tab, proj1, h1, carry1, keep_r, dy1, v1, norm1, skip_gain, w_in),
+        [tile, chunk, stat_tile])
+    one.send, sum1 = tie(one.send, sum1)
     one.go()
     sum1 = swap(sum1, everyone)
-    one.got, sum1 = lax.optimization_barrier((one.got, sum1))
+    one.got, sum1 = tie(one.got, sum1)
     one.settle()
-    total1, e1, dy0, dylow0, dh0, adj_ends0, adj0, small0, keepa, senda = run(
+    total1, e1, dy0, dh0, adj_ends0, adj0, small0, keepa, senda = run(
         bind(lower_block, z), "lower_block",
-        [norm_shape, full, full, low, full_n, chunk, send_shape, small_shape, part(3), part(3)],
+        [norm_shape, full, full, full_n, chunk, send_shape, small_shape, part(3), part(3)],
         (sum1, dxn1, v1, norm1, gout, sig0, gate0, slope0, x, norm0, bn_gain, bn_bias, w_glu, w_out, keep_r, chunk_r, tab, act0, hlow0),
-        [tile, stat_tile, wide_b])
-    two = Exchange(z, keepa, senda)
-    one.send, two.send, adj0 = lax.optimization_barrier((one.send, two.send, adj0))
+        [tile, stat_tile, wide_b, low])
+    two = Exchange(z, keepa, senda, order=ORDERS[1])
+    one.send, two.send, adj0 = tie(one.send, two.send, adj0)
     one.go()
     two.go()
     adj0 = swap(adj0, "tm")
-    one.got, two.got, adj0 = lax.optimization_barrier((one.got, two.got, adj0))
+    one.got, two.got, adj0 = tie(one.got, two.got, adj0)
     rows_sum = (2 * D + 2 * (3 * D + 2 * N)) // W
     z.extra = -(-rows_sum // 8) * 8
-    last_part = ((D // W * D // 2 + z.extra, W), F32)
+    last_part = part(2, z.extra)
     dxn0, keepb, sendb = run(
         bind(finish_lower, z), "finish0", [full, last_part, last_part],
         (adj0, dev_r, power, adj_ends0, chunk_r, dh0, keep_r, tab, proj0, h0, carry0, keep_f, dy0, x, norm0, skip_gain, w_in,
-         low0, small0, small1, lam1),
+         low0, low1, dplow1, small0, small1, lam1),
         [low_n, lam_shape, tile, chunk])
     one.settle()
     two.settle()
-    three = Exchange(z, keepb, sendb, z.extra)
-    one.send, two.send, three.send = lax.optimization_barrier((one.send, two.send, three.send))
+    three = Exchange(z, keepb, sendb, z.extra, ORDERS[2])
+    one.send, two.send, three.send = tie(one.send, two.send, three.send)
     for e in (one, two, three):
         e.go()
-    sets = [one, two, three]
+    sets = [(one, two, three)[i] for i in SEQ]
     ahead = three.send
     while not all(e.closing for e in sets):
         for e in sets:
             if not e.closing:
-                e.got, _ = lax.optimization_barrier((e.got, ahead))
+                e.got, _ = tie(e.got, ahead)
                 e.settle()
                 e.go()
                 ahead = e.send

time: 201 us -> 192 us (0.955)
  waiting for transfers between devices: 75 us -> 68.8 us
  blocking collectives: 77.3 us -> 74.7 us
    ppermute x30, waiting for transfers between devices: 75 us -> 68.8 us  [go(): lax.ppermute(self.send, ('tm', 'rows'), pairs(self.z, self.order[self.ste...]
    all_to_all x7, blocking collectives: 77.3 us -> 74.7 us  [swap(): return lax.all_to_all(a, axis, 0, 0)]
  transfers between devices with their start and end apart: 30 -> 30, of which waited for: 20 -> 16; matrix products, arithmetic and copies ran while one was open for 0% -> 0% of each run, Pallas kernels for 1% -> 1%
where the time goes in v3:
time: 192 us
  blocking collectives  74.7 us (39%)
  waiting for transfers between devices  68.8 us (36%)
  starting transfers between devices  26.6 us (14%)
  Pallas kernels  20.9 us (11%)
    all_to_all x7, blocking collectives, swap(): return lax.all_to_all(a, axis, 0, 0)  74.7 us
    ppermute x30, waiting for transfers between devices, go(): lax.ppermute(self.send, ('tm', 'rows'), pairs(self.z, self.order[self.ste...  68.8 us
    ppermute x30, starting transfers between devices, go(): lax.ppermute(self.send, ('tm', 'rows'), pairs(self.z, self.order[self.ste...  26.6 us
    pallas_call x37, Pallas kernels, run(): pl.pallas_call(kernel, out_shape=[jax.ShapeDtypeStruct(s, t) for s, t in...  20.9 us
  transfers between devices with their start and end apart: 30, of which 16 were waited for; matrix products, arithmetic and copies ran while one was open for 0% of the time, Pallas kernels for 1%

profile of v3, /device:TPU:0, one launch (start us, length us, event | category | flops | bytes accessed | tf_op | source)
XLA Modules:
  0.0 192.2 jit_solution(4277963533420057858)
XLA Ops:
  0.6 2.6 %prepare.1 = (f32[256,512]{1,0:T(8,128)S(1)}, f32[256,512]{1,0:T(8,128)S(1)}, f32[32,8,128]{2,1,0:T(8,128)S(1)}, f32[256,128]{1,0:T(8,128)S(1)}, f32[256,128]{1,...) custom-call(s32[2,16]{1,0:T(2,128)} %len_hbm.1, ...), custom_call_target="tpu_custom_call" | custom-call | tf_op jit(solution)/shard_map/prepare/pallas_call | solution.py:740
  3.3 15.3 %all_to_all.35.stat_ref = f32[32,8,128]{2,1,0:T(8,128)S(1)} all-to-all(f32[32,8,128]{2,1,0:T(8,128)S(1)} %get-tuple-element.150), channel_id=1, replica_groups=mesh['tm'=8,'rows'=4] {'tm','rows'}, dimensions={0} | all-to-all | bytes 262144 | tf_op jit(solution)/shard_map/all_to_all | solution.py:758
  18.6 0.6 enter0.1
  19.2 9.2 %all_to_all.36.recv_ref = f32[8,8,128]{2,1,0:T(8,128)S(1)} all-to-all(f32[8,8,128]{2,1,0:T(8,128)S(1)} %get-tuple-element.158), channel_id=1, replica_groups=mesh['tm'=8,'rows'=4] {'tm'}, dimensions={0} | all-to-all | bytes 65536 | tf_op jit(solution)/shard_map/all_to_all | solution.py:758
  28.4 1.6 middle.1
  30.0 9.9 %all_to_all.37.stat_ref = f32[32,8,128]{2,1,0:T(8,128)S(1)} all-to-all(f32[32,8,128]{2,1,0:T(8,128)S(1)} %get-tuple-element.168), channel_id=1, replica_groups=mesh['tm'=8,'rows'=4] {'tm','rows'}, dimensions={0} | all-to-all | bytes 262144 | tf_op jit(solution)/shard_map/all_to_all | solution.py:758
  39.9 0.6 enter1.1
  40.6 9.1 %all_to_all.38.recv_ref = f32[8,8,128]{2,1,0:T(8,128)S(1)} all-to-all(f32[8,8,128]{2,1,0:T(8,128)S(1)} %get-tuple-element.172), channel_id=1, replica_groups=mesh['tm'=8,'rows'=4] {'tm'}, dimensions={0} | all-to-all | bytes 65536 | tf_op jit(solution)/shard_map/all_to_all | solution.py:758
  49.7 4.4 %turn.1 = (f32[256,512]{1,0:T(8,128)S(1)}, f32[16,512]{1,0:T(8,128)S(1)}, bf16[256,512]{1,0:T(8,128)(2,1)}, f32[256,512]{1,0:T(8,128)S(1)}, f32[256,512]{1,0:T(8...) custom-call(f32[8,8,128]{2,1,0:T(8,128)S(1)} %all_to_all.38.recv_ref, ...), custom_call_target="tpu_custom_call" | custom-call | tf_op jit(solution)/shard_map/turn/pallas_call | solution.py:740
  54.1 9.0 %all_to_all.39.refs_0_ = f32[8,8,128]{2,1,0:T(8,128)S(1)} all-to-all(f32[8,8,128]{2,1,0:T(8,128)S(1)} %get-tuple-element.183), channel_id=1, replica_groups=mesh['tm'=8,'rows'=4] {'tm'}, dimensions={0} | all-to-all | bytes 65536 | tf_op jit(solution)/shard_map/all_to_all | solution.py:758
  63.2 0.2 halves.12
  63.4 0.8 finish1.1
  64.2 0.6 collective-permute-start.1
  64.7 13.1 %all_to_all.40.stat_ref = f32[32,8,128]{2,1,0:T(8,128)S(1)} all-to-all(f32[32,8,128]{2,1,0:T(8,128)S(1)} %get-tuple-element.195), channel_id=1, replica_groups=mesh['tm'=8,'rows'=4] {'tm','rows'}, dimensions={0} | all-to-all | bytes 262144 | tf_op jit(solution)/shard_map/all_to_all | solution.py:758
  77.8 0.1 halves.13
  77.9 2.1 %lower_block.1 = (f32[8,512]{1,0:T(8,128)S(1)}, f32[256,512]{1,0:T(8,128)S(1)}, f32[256,512]{1,0:T(8,128)S(1)}, f32[256,512]{1,0:T(8,128)S(1)}, f32[16,512]{1,0:...) custom-call(f32[32,8,128]{2,1,0:T(8,128)S(1)} %all_to_all.40.stat_re, ...), custom_call_target="tpu_custom_call" | custom-call | tf_op jit(solution)/shard_map/lower_block/pallas_call | solution.py:740
  80.1 1.4 collective-permute-start.2
  81.5 9.0 %all_to_all.41.refs_0_ = f32[8,8,128]{2,1,0:T(8,128)S(1)} all-to-all(f32[8,8,128]{2,1,0:T(8,128)S(1)} %get-tuple-element.209), channel_id=1, replica_groups=mesh['tm'=8,'rows'=4] {'tm'}, dimensions={0} | all-to-all | bytes 65536 | tf_op jit(solution)/shard_map/all_to_all | solution.py:758
  90.6 0.2 halves.15
  90.8 1.5 finish0.1
  92.4 0.5 collective-permute-start.7
  93.0 2.2 %collective-permute-done.4.recv_ref = f32[1048,256]{1,0:T(8,128)S(1)} collective-permute-done((f32[1048,256]{1,0:T(8,128)S(1)}, f32[1048,256]{1,0:T(8,128)S(1)}, u32[]{:S(2)}, u32[]{:S(2)}) %collective-permute-start.4) | collective-permute-done | bytes 1073184 | tf_op jit(solution)/shard_map/ppermute | solution.py:680
  95.1 0.1 halves.16
  95.3 0.5 collective-permute-start.5
  95.8 8.7 %collective-permute-done.7.recv_ref = f32[768,256]{1,0:T(8,128)S(1)} collective-permute-done((f32[768,256]{1,0:T(8,128)S(1)}, f32[768,256]{1,0:T(8,128)S(1)}, u32[]{:S(2)}, u32[]{:S(2)}) %collective-permute-start.7) | collective-permute-done | bytes 786464 | tf_op jit(solution)/shard_map/ppermute | solution.py:680
  104.5 0.1 halves.17
  104.6 0.8 collective-permute-start.10
  105.4 0.4 collective-permute-start.6
  105.8 5.5 %collective-permute-done.6.recv_ref = f32[192,256]{1,0:T(8,128)S(1)} collective-permute-done((f32[192,256]{1,0:T(8,128)S(1)}, f32[192,256]{1,0:T(8,128)S(1)}, u32[]{:S(2)}, u32[]{:S(2)}) %collective-permute-start.6) | collective-permute-done | bytes 196640 | tf_op jit(solution)/shard_map/ppermute | solution.py:680
  111.3 2.6 %collective-permute-done.5.recv_ref = f32[536,256]{1,0:T(8,128)S(1)} collective-permute-done((f32[536,256]{1,0:T(8,128)S(1)}, f32[536,256]{1,0:T(8,128)S(1)}, u32[]{:S(2)}, u32[]{:S(2)}) %collective-permute-start.5) | collective-permute-done | bytes 548896 | tf_op jit(solution)/shard_map/ppermute | solution.py:680
  113.9 0.8 collective-permute-start.8
  114.8 0.4 collective-permute-start.13
  115.2 0.7 collective-permute-start.9
  115.9 5.6 %collective-permute-done.9.recv_ref = f32[96,256]{1,0:T(8,128)S(1)} collective-permute-done((f32[96,256]{1,0:T(8,128)S(1)}, f32[96,256]{1,0:T(8,128)S(1)}, u32[]{:S(2)}, u32[]{:S(2)}) %collective-permute-start.9) | collective-permute-done | bytes 98336 | tf_op jit(solution)/shard_map/ppermute | solution.py:680
  121.5 3.3 %collective-permute-start.12 = (f32[96,256]{1,0:T(8,128)S(1)}, f32[96,256]{1,0:T(8,128)S(1)}, u32[]{:S(2)}, u32[]{:S(2)}) collective-permute-start(f32[96,256]{1,0:T(8,128)S(1)} %total.3.own_ref), channel_id=1, source_target_pairs={{0,16},{1,17},{2,18},{3,19},{4,20},{5,21},{6,22},{7,23},{8,24},{9,... | collective-permute-start | bytes 294920 | tf_op jit(solution)/shard_map/ppermute | solution.py:680
  124.9 2.6 %collective-permute-done.12.recv_ref = f32[96,256]{1,0:T(8,128)S(1)} collective-permute-done((f32[96,256]{1,0:T(8,128)S(1)}, f32[96,256]{1,0:T(8,128)S(1)}, u32[]{:S(2)}, u32[]{:S(2)}) %collective-permute-start.12) | collective-permute-done | bytes 98336 | tf_op jit(solution)/shard_map/ppermute | solution.py:680
  127.6 2.0 %collective-permute-start.15 = (f32[192,256]{1,0:T(8,128)S(1)}, f32[192,256]{1,0:T(8,128)S(1)}, u32[]{:S(2)}, u32[]{:S(2)}) collective-permute-start(f32[192,256]{1,0:T(8,128)S(1)} %join.12.own_ref), channel_id=1, source_target_pairs={{0,8},{1,9},{2,10},{3,11},{4,12},{5,13},{6,14},{7,15},{8,0},{9,1},... | collective-permute-start | bytes 589832 | tf_op jit(solution)/shard_map/ppermute | solution.py:680
  129.7 2.7 %collective-permute-start.16 = (f32[96,256]{1,0:T(8,128)S(1)}, f32[96,256]{1,0:T(8,128)S(1)}, u32[]{:S(2)}, u32[]{:S(2)}) collective-permute-start(f32[96,256]{1,0:T(8,128)S(1)} %get-tuple-element.255), channel_id=1, source_target_pairs={{0,16},{1,17},{2,18},{3,19},{4,20},{5,21},{6,22},{7,23},{8,24},{9,... | collective-permute-start | bytes 294920 | tf_op jit(solution)/shard_map/ppermute | solution.py:680
  132.4 5.1 %collective-permute-done.11.recv_ref = f32[152,256]{1,0:T(8,128)S(1)} collective-permute-done((f32[152,256]{1,0:T(8,128)S(1)}, f32[152,256]{1,0:T(8,128)S(1)}, u32[]{:S(2)}, u32[]{:S(2)}) %collective-permute-start.11) | collective-permute-done | bytes 155680 | tf_op jit(solution)/shard_map/ppermute | solution.py:680
  137.6 0.6 collective-permute-start.17
  138.2 2.7 %collective-permute-start.18 = (f32[96,256]{1,0:T(8,128)S(1)}, f32[96,256]{1,0:T(8,128)S(1)}, u32[]{:S(2)}, u32[]{:S(2)}) collective-permute-start(f32[96,256]{1,0:T(8,128)S(1)} %total.4.own_ref), channel_id=1, source_target_pairs={{0,16},{1,17},{2,18},{3,19},{4,20},{5,21},{6,22},{7,23},{8,24},{9,... | collective-permute-start | bytes 294920 | tf_op jit(solution)/shard_map/ppermute | solution.py:680
  140.9 0.2 collective-permute-start.14
  141.1 7.2 %collective-permute-done.14.recv_ref = f32[88,256]{1,0:T(8,128)S(1)} collective-permute-done((f32[88,256]{1,0:T(8,128)S(1)}, f32[88,256]{1,0:T(8,128)S(1)}, u32[]{:S(2)}, u32[]{:S(2)}) %collective-permute-start.14) | collective-permute-done | bytes 90144 | tf_op jit(solution)/shard_map/ppermute | solution.py:680
  148.5 0.1 join.15.own_ref
  148.6 0.5 collective-permute-start.19
  149.1 2.3 %collective-permute-start.20 = (f32[192,256]{1,0:T(8,128)S(1)}, f32[192,256]{1,0:T(8,128)S(1)}, u32[]{:S(2)}, u32[]{:S(2)}) collective-permute-start(f32[192,256]{1,0:T(8,128)S(1)} %join.14.own_ref), channel_id=1, source_target_pairs={{0,8},{1,9},{2,10},{3,11},{4,12},{5,13},{6,14},{7,15},{8,0},{9,1},... | collective-permute-start | bytes 589832 | tf_op jit(solution)/shard_map/ppermute | solution.py:680
  151.4 5.3 %collective-permute-done.21.recv_ref = f32[64,256]{1,0:T(8,128)S(1)} collective-permute-done((f32[64,256]{1,0:T(8,128)S(1)}, f32[64,256]{1,0:T(8,128)S(1)}, u32[]{:S(2)}, u32[]{:S(2)}) %collective-permute-start.21) | collective-permute-done | bytes 65568 | tf_op jit(solution)/shard_map/ppermute | solution.py:680
  156.7 0.3 collective-permute-done.20.recv_ref
  157.0 1.7 collective-permute-start.23
  158.6 0.6 collective-permute-start.24
  159.2 5.6 %collective-permute-done.19.recv_ref = f32[768,256]{1,0:T(8,128)S(1)} collective-permute-done((f32[768,256]{1,0:T(8,128)S(1)}, f32[768,256]{1,0:T(8,128)S(1)}, u32[]{:S(2)}, u32[]{:S(2)}) %collective-permute-start.19) | collective-permute-done | bytes 786464 | tf_op jit(solution)/shard_map/ppermute | solution.py:680
  164.8 0.1 join.18.own1
  165.0 0.7 collective-permute-done.23.recv_ref
  165.8 1.4 collective-permute-start.25
  167.2 1.3 collective-permute-start.26
  168.5 7.9 %collective-permute-done.26.recv_ref = f32[256,256]{1,0:T(8,128)S(1)} collective-permute-done((f32[256,256]{1,0:T(8,128)S(1)}, f32[256,256]{1,0:T(8,128)S(1)}, u32[]{:S(2)}, u32[]{:S(2)}) %collective-permute-start.26) | collective-permute-done | bytes 262176 | tf_op jit(solution)/shard_map/ppermute | solution.py:680
  176.5 0.8 collective-permute-start.28
  177.3 0.6 collective-permute-done.25.recv_ref
  177.9 0.1 join.22.owna
  178.1 7.7 %collective-permute-done.28.recv_ref = f32[512,256]{1,0:T(8,128)S(1)} collective-permute-done((f32[512,256]{1,0:T(8,128)S(1)}, f32[512,256]{1,0:T(8,128)S(1)}, u32[]{:S(2)}, u32[]{:S(2)}) %collective-permute-start.28) | collective-permute-done | bytes 524320 | tf_op jit(solution)/shard_map/ppermute | solution.py:680
  185.8 0.1 join.23.ownb
  185.9 1.3 last.1
  187.2 1.4 collective-permute-done.29.gotb
  188.6 3.4 %assemble.1 = (f32[2,512,512]{2,1,0:T(8,128)}, f32[2,512,512]{2,1,0:T(8,128)}, f32[2,512,1024]{2,1,0:T(8,128)}) custom-call(f32[1536,256]{1,0:T(8,128)S(1)} %join.18.own1, f32[1536,256]{1,0:T(8,128)S(1)} %collective-permute-done.22.got1, f32[1536,256]{1,0:T(8,128)S(1)} %join.22.owna, f32[1536,256]{1,0:T(8,128)S(1)} %collective-permute-done.27.gota, ...), custom_call_target="tpu_custom_call" | custom-call | tf_op jit(solution)/shard_map/assemble/pallas_call | solution.py:740
  (40 shorter events, 1.1 us)
Async XLA Ops:
  54.1 9.1 %collective-permute-start = (f32[1536,256]{1,0:T(8,128)S(1)}, f32[1536,256]{1,0:T(8,128)S(1)}, u32[]{:S(2)}, u32[]{:S(2)}) collective-permute-start(f32[1536,256]{1,0:T(8,128)S(1)} %get-tuple-element.182), channel_id=1, source_target_pairs={{0,1},{1,0},{2,3},{3,2},{4,5},{5,4},{6,7},{7,6},{8,9},{9,8},{10,11... | collective-permute-start | bytes 4718600 | tf_op jit(solution)/shard_map/ppermute | solution.py:680
  64.2 13.6 %collective-permute-start.1 = (f32[768,256]{1,0:T(8,128)S(1)}, f32[768,256]{1,0:T(8,128)S(1)}, u32[]{:S(2)}, u32[]{:S(2)}) collective-permute-start(f32[768,256]{1,0:T(8,128)S(1)} %get-tuple-element.194), channel_id=1, source_target_pairs={{0,4},{1,3},{2,6},{3,1},{4,0},{5,7},{6,2},{7,5},{8,12},{9,11},{10,... | collective-permute-start | bytes 2359304 | tf_op jit(solution)/shard_map/ppermute | solution.py:680
  80.0 10.5 %collective-permute-start.3 = (f32[1536,256]{1,0:T(8,128)S(1)}, f32[1536,256]{1,0:T(8,128)S(1)}, u32[]{:S(2)}, u32[]{:S(2)}) collective-permute-start(f32[1536,256]{1,0:T(8,128)S(1)} %get-tuple-element.208), channel_id=1, source_target_pairs={{0,1},{1,0},{2,3},{3,2},{4,5},{5,4},{6,7},{7,6},{8,9},{9,8},{10,11... | collective-permute-start | bytes 4718600 | tf_op jit(solution)/shard_map/ppermute | solution.py:680
  80.1 10.4 %collective-permute-start.2 = (f32[384,256]{1,0:T(8,128)S(1)}, f32[384,256]{1,0:T(8,128)S(1)}, u32[]{:S(2)}, u32[]{:S(2)}) collective-permute-start(f32[384,256]{1,0:T(8,128)S(1)} %get-tuple-element.207), channel_id=1, source_target_pairs={{0,2},{1,5},{2,0},{3,7},{4,6},{5,1},{6,4},{7,3},{8,10},{9,13},{10,... | collective-permute-start | bytes 1179656 | tf_op jit(solution)/shard_map/ppermute | solution.py:680
  92.3 2.8 %collective-permute-start.4 = (f32[1048,256]{1,0:T(8,128)S(1)}, f32[1048,256]{1,0:T(8,128)S(1)}, u32[]{:S(2)}, u32[]{:S(2)}) collective-permute-start(f32[1048,256]{1,0:T(8,128)S(1)} %get-tuple-element.230), channel_id=1, source_target_pairs={{0,1},{1,0},{2,3},{3,2},{4,5},{5,4},{6,7},{7,6},{8,9},{9,8},{10,11... | collective-permute-start | bytes 3219464 | tf_op jit(solution)/shard_map/ppermute | solution.py:680
  92.4 12.1 %collective-permute-start.7 = (f32[768,256]{1,0:T(8,128)S(1)}, f32[768,256]{1,0:T(8,128)S(1)}, u32[]{:S(2)}, u32[]{:S(2)}) collective-permute-start(f32[768,256]{1,0:T(8,128)S(1)} %get-tuple-element.237), channel_id=1, source_target_pairs={{0,4},{1,3},{2,6},{3,1},{4,0},{5,7},{6,2},{7,5},{8,12},{9,11},{10,... | collective-permute-start | bytes 2359304 | tf_op jit(solution)/shard_map/ppermute | solution.py:680
  95.3 18.6 %collective-permute-start.5 = (f32[536,256]{1,0:T(8,128)S(1)}, f32[536,256]{1,0:T(8,128)S(1)}, u32[]{:S(2)}, u32[]{:S(2)}) collective-permute-start(f32[536,256]{1,0:T(8,128)S(1)} %get-tuple-element.233), channel_id=1, source_target_pairs={{0,4},{1,3},{2,6},{3,1},{4,0},{5,7},{6,2},{7,5},{8,12},{9,11},{10,... | collective-permute-start | bytes 1646600 | tf_op jit(solution)/shard_map/ppermute | solution.py:680
  104.6 10.1 %collective-permute-start.10 = (f32[384,256]{1,0:T(8,128)S(1)}, f32[384,256]{1,0:T(8,128)S(1)}, u32[]{:S(2)}, u32[]{:S(2)}) collective-permute-start(f32[384,256]{1,0:T(8,128)S(1)} %get-tuple-element.239), channel_id=1, source_target_pairs={{0,2},{1,5},{2,0},{3,7},{4,6},{5,1},{6,4},{7,3},{8,10},{9,13},{10,... | collective-permute-start | bytes 1179656 | tf_op jit(solution)/shard_map/ppermute | solution.py:680
  105.4 5.8 %collective-permute-start.6 = (f32[192,256]{1,0:T(8,128)S(1)}, f32[192,256]{1,0:T(8,128)S(1)}, u32[]{:S(2)}, u32[]{:S(2)}) collective-permute-start(f32[192,256]{1,0:T(8,128)S(1)} %get-tuple-element.235), channel_id=1, source_target_pairs={{0,8},{1,9},{2,10},{3,11},{4,12},{5,13},{6,14},{7,15},{8,0},{9,1},... | collective-permute-start | bytes 589832 | tf_op jit(solution)/shard_map/ppermute | solution.py:680
  113.9 10.9 %collective-permute-start.8 = (f32[280,256]{1,0:T(8,128)S(1)}, f32[280,256]{1,0:T(8,128)S(1)}, u32[]{:S(2)}, u32[]{:S(2)}) collective-permute-start(f32[280,256]{1,0:T(8,128)S(1)} %get-tuple-element.244), channel_id=1, source_target_pairs={{0,2},{1,5},{2,0},{3,7},{4,6},{5,1},{6,4},{7,3},{8,10},{9,13},{10,... | collective-permute-start | bytes 860168 | tf_op jit(solution)/shard_map/ppermute | solution.py:680
  114.8 10.1 %collective-permute-start.13 = (f32[192,256]{1,0:T(8,128)S(1)}, f32[192,256]{1,0:T(8,128)S(1)}, u32[]{:S(2)}, u32[]{:S(2)}) collective-permute-start(f32[192,256]{1,0:T(8,128)S(1)} %get-tuple-element.248), channel_id=1, source_target_pairs={{0,8},{1,9},{2,10},{3,11},{4,12},{5,13},{6,14},{7,15},{8,0},{9,1},... | collective-permute-start | bytes 589832 | tf_op jit(solution)/shard_map/ppermute | solution.py:680
  115.2 6.3 %collective-permute-start.9 = (f32[96,256]{1,0:T(8,128)S(1)}, f32[96,256]{1,0:T(8,128)S(1)}, u32[]{:S(2)}, u32[]{:S(2)}) collective-permute-start(f32[96,256]{1,0:T(8,128)S(1)} %get-tuple-element.241), channel_id=1, source_target_pairs={{0,16},{1,17},{2,18},{3,19},{4,20},{5,21},{6,22},{7,23},{8,24},{9,... | collective-permute-start | bytes 294920 | tf_op jit(solution)/shard_map/ppermute | solution.py:680
  121.5 6.0 %collective-permute-start.12 = (f32[96,256]{1,0:T(8,128)S(1)}, f32[96,256]{1,0:T(8,128)S(1)}, u32[]{:S(2)}, u32[]{:S(2)}) collective-permute-start(f32[96,256]{1,0:T(8,128)S(1)} %total.3.own_ref), channel_id=1, source_target_pairs={{0,16},{1,17},{2,18},{3,19},{4,20},{5,21},{6,22},{7,23},{8,24},{9,... | collective-permute-start | bytes 294920 | tf_op jit(solution)/shard_map/ppermute | solution.py:680
  127.6 10.0 %collective-permute-start.15 = (f32[192,256]{1,0:T(8,128)S(1)}, f32[192,256]{1,0:T(8,128)S(1)}, u32[]{:S(2)}, u32[]{:S(2)}) collective-permute-start(f32[192,256]{1,0:T(8,128)S(1)} %join.12.own_ref), channel_id=1, source_target_pairs={{0,8},{1,9},{2,10},{3,11},{4,12},{5,13},{6,14},{7,15},{8,0},{9,1},... | collective-permute-start | bytes 589832 | tf_op jit(solution)/shard_map/ppermute | solution.py:680
  129.6 7.9 %collective-permute-start.11 = (f32[152,256]{1,0:T(8,128)S(1)}, f32[152,256]{1,0:T(8,128)S(1)}, u32[]{:S(2)}, u32[]{:S(2)}) collective-permute-start(f32[152,256]{1,0:T(8,128)S(1)} %get-tuple-element.252), channel_id=1, source_target_pairs={{0,8},{1,9},{2,10},{3,11},{4,12},{5,13},{6,14},{7,15},{8,0},{9,1},... | collective-permute-start | bytes 466952 | tf_op jit(solution)/shard_map/ppermute | solution.py:680
  129.7 7.8 %collective-permute-start.16 = (f32[96,256]{1,0:T(8,128)S(1)}, f32[96,256]{1,0:T(8,128)S(1)}, u32[]{:S(2)}, u32[]{:S(2)}) collective-permute-start(f32[96,256]{1,0:T(8,128)S(1)} %get-tuple-element.255), channel_id=1, source_target_pairs={{0,16},{1,17},{2,18},{3,19},{4,20},{5,21},{6,22},{7,23},{8,24},{9,... | collective-permute-start | bytes 294920 | tf_op jit(solution)/shard_map/ppermute | solution.py:680
  137.6 10.8 %collective-permute-start.17 = (f32[384,256]{1,0:T(8,128)S(1)}, f32[384,256]{1,0:T(8,128)S(1)}, u32[]{:S(2)}, u32[]{:S(2)}) collective-permute-start(f32[384,256]{1,0:T(8,128)S(1)} %join.13.own_ref), channel_id=1, source_target_pairs={{0,2},{1,5},{2,0},{3,7},{4,6},{5,1},{6,4},{7,3},{8,10},{9,13},{10,... | collective-permute-start | bytes 1179656 | tf_op jit(solution)/shard_map/ppermute | solution.py:680
  138.2 10.2 %collective-permute-start.18 = (f32[96,256]{1,0:T(8,128)S(1)}, f32[96,256]{1,0:T(8,128)S(1)}, u32[]{:S(2)}, u32[]{:S(2)}) collective-permute-start(f32[96,256]{1,0:T(8,128)S(1)} %total.4.own_ref), channel_id=1, source_target_pairs={{0,16},{1,17},{2,18},{3,19},{4,20},{5,21},{6,22},{7,23},{8,24},{9,... | collective-permute-start | bytes 294920 | tf_op jit(solution)/shard_map/ppermute | solution.py:680
  140.9 7.4 %collective-permute-start.14 = (f32[88,256]{1,0:T(8,128)S(1)}, f32[88,256]{1,0:T(8,128)S(1)}, u32[]{:S(2)}, u32[]{:S(2)}) collective-permute-start(f32[88,256]{1,0:T(8,128)S(1)} %get-tuple-element.259), channel_id=1, source_target_pairs={{0,16},{1,17},{2,18},{3,19},{4,20},{5,21},{6,22},{7,23},{8,24},{9,... | collective-permute-start | bytes 270344 | tf_op jit(solution)/shard_map/ppermute | solution.py:680
  148.6 16.3 %collective-permute-start.19 = (f32[768,256]{1,0:T(8,128)S(1)}, f32[768,256]{1,0:T(8,128)S(1)}, u32[]{:S(2)}, u32[]{:S(2)}) collective-permute-start(f32[768,256]{1,0:T(8,128)S(1)} %join.15.own_ref), channel_id=1, source_target_pairs={{0,4},{1,3},{2,6},{3,1},{4,0},{5,7},{6,2},{7,5},{8,12},{9,11},{10,... | collective-permute-start | bytes 2359304 | tf_op jit(solution)/shard_map/ppermute | solution.py:680
  149.1 7.8 %collective-permute-start.20 = (f32[192,256]{1,0:T(8,128)S(1)}, f32[192,256]{1,0:T(8,128)S(1)}, u32[]{:S(2)}, u32[]{:S(2)}) collective-permute-start(f32[192,256]{1,0:T(8,128)S(1)} %join.14.own_ref), channel_id=1, source_target_pairs={{0,8},{1,9},{2,10},{3,11},{4,12},{5,13},{6,14},{7,15},{8,0},{9,1},... | collective-permute-start | bytes 589832 | tf_op jit(solution)/shard_map/ppermute | solution.py:680
  151.4 5.3 %collective-permute-start.21 = (f32[64,256]{1,0:T(8,128)S(1)}, f32[64,256]{1,0:T(8,128)S(1)}, u32[]{:S(2)}, u32[]{:S(2)}) collective-permute-start(f32[64,256]{1,0:T(8,128)S(1)} %get-tuple-element.271.own_ref), channel_id=1, source_target_pairs={{0,16},{1,17},{2,18},{3,19},{4,20},{5,21},{6,22},{7,23},{8,24},{9,... | collective-permute-start | bytes 196616 | tf_op jit(solution)/shard_map/ppermute | solution.py:680
  157.0 8.8 %collective-permute-start.23 = (f32[384,256]{1,0:T(8,128)S(1)}, f32[384,256]{1,0:T(8,128)S(1)}, u32[]{:S(2)}, u32[]{:S(2)}) collective-permute-start(f32[384,256]{1,0:T(8,128)S(1)} %join.17.own_ref), channel_id=1, source_target_pairs={{0,2},{1,5},{2,0},{3,7},{4,6},{5,1},{6,4},{7,3},{8,10},{9,13},{10,... | collective-permute-start | bytes 1179656 | tf_op jit(solution)/shard_map/ppermute | solution.py:680
  158.6 6.3 %collective-permute-start.24 = (f32[128,256]{1,0:T(8,128)S(1)}, f32[128,256]{1,0:T(8,128)S(1)}, u32[]{:S(2)}, u32[]{:S(2)}) collective-permute-start(f32[128,256]{1,0:T(8,128)S(1)} %join.16.own_ref), channel_id=1, source_target_pairs={{0,8},{1,9},{2,10},{3,11},{4,12},{5,13},{6,14},{7,15},{8,0},{9,1},... | collective-permute-start | bytes 393224 | tf_op jit(solution)/shard_map/ppermute | solution.py:680
  165.8 12.1 %collective-permute-start.25 = (f32[768,256]{1,0:T(8,128)S(1)}, f32[768,256]{1,0:T(8,128)S(1)}, u32[]{:S(2)}, u32[]{:S(2)}) collective-permute-start(f32[768,256]{1,0:T(8,128)S(1)} %join.20.own_ref), channel_id=1, source_target_pairs={{0,4},{1,3},{2,6},{3,1},{4,0},{5,7},{6,2},{7,5},{8,12},{9,11},{10,... | collective-permute-start | bytes 2359304 | tf_op jit(solution)/shard_map/ppermute | solution.py:680
  167.2 9.2 %collective-permute-start.26 = (f32[256,256]{1,0:T(8,128)S(1)}, f32[256,256]{1,0:T(8,128)S(1)}, u32[]{:S(2)}, u32[]{:S(2)}) collective-permute-start(f32[256,256]{1,0:T(8,128)S(1)} %join.19.own_ref), channel_id=1, source_target_pairs={{0,2},{1,5},{2,0},{3,7},{4,6},{5,1},{6,4},{7,3},{8,10},{9,13},{10,... | collective-permute-start | bytes 786440 | tf_op jit(solution)/shard_map/ppermute | solution.py:680
  168.5 18.7 %collective-permute-start.22 = (f32[1536,256]{1,0:T(8,128)S(1)}, f32[1536,256]{1,0:T(8,128)S(1)}, u32[]{:S(2)}, u32[]{:S(2)}) collective-permute-start(f32[1536,256]{1,0:T(8,128)S(1)} %join.18.own1), channel_id=1, source_target_pairs={{0,1},{1,0},{2,3},{3,2},{4,5},{5,4},{6,7},{7,6},{8,9},{9,8},{10,11... | collective-permute-start | bytes 4718600 | tf_op jit(solution)/shard_map/ppermute | solution.py:680
  176.5 9.2 %collective-permute-start.28 = (f32[512,256]{1,0:T(8,128)S(1)}, f32[512,256]{1,0:T(8,128)S(1)}, u32[]{:S(2)}, u32[]{:S(2)}) collective-permute-start(f32[512,256]{1,0:T(8,128)S(1)} %join.21.own_ref), channel_id=1, source_target_pairs={{0,4},{1,3},{2,6},{3,1},{4,0},{5,7},{6,2},{7,5},{8,12},{9,11},{10,... | collective-permute-start | bytes 1572872 | tf_op jit(solution)/shard_map/ppermute | solution.py:680
  178.0 10.6 %collective-permute-start.27 = (f32[1536,256]{1,0:T(8,128)S(1)}, f32[1536,256]{1,0:T(8,128)S(1)}, u32[]{:S(2)}, u32[]{:S(2)}) collective-permute-start(f32[1536,256]{1,0:T(8,128)S(1)} %join.22.owna), channel_id=1, source_target_pairs={{0,1},{1,0},{2,3},{3,2},{4,5},{5,4},{6,7},{7,6},{8,9},{9,8},{10,11... | collective-permute-start | bytes 4718600 | tf_op jit(solution)/shard_map/ppermute | solution.py:680
  185.9 2.7 %collective-permute-start.29 = (f32[1024,256]{1,0:T(8,128)S(1)}, f32[1024,256]{1,0:T(8,128)S(1)}, u32[]{:S(2)}, u32[]{:S(2)}) collective-permute-start(f32[1024,256]{1,0:T(8,128)S(1)} %join.23.ownb), channel_id=1, source_target_pairs={{0,1},{1,0},{2,3},{3,2},{4,5},{5,4},{6,7},{7,6},{8,9},{9,8},{10,11... | collective-permute-start | bytes 3145736 | tf_op jit(solution)/shard_map/ppermute | solution.py:680

commit v4 on v3

--- a/solution.py
+++ b/solution.py
@@ -410,8 +410,8 @@
 
 def turn(z, recv_ref, dev_ref, power_ref, ends_ref, chunk_ref, proj_ref, keep_ref, tab_ref, v_ref, norm_ref, gain_ref,
          bias_ref, skip_ref, wout_ref, wglu_ref, bglu_ref, gout_ref, adj_keep_ref, adj_chunk_ref,
-         h_ref, carry_ref, out_ref, dy_ref, dh_ref, adj_ends_ref, send_ref, small_ref, half_keep, half_send,
-         tile_ref, wide_ref, slope_ref, natural_ref, hlow_ref, act_ref, dz_ref, dylow_ref):
+         h_ref, carry_ref, final_ref, dy_ref, dh_ref, adj_ends_ref, send_ref, small_ref, half_keep, half_send,
+         tile_ref, wide_ref, slope_ref, hlow_ref, act_ref, dz_ref, dylow_ref):
     mix(z, 1, recv_ref, dev_ref, power_ref, ends_ref, chunk_ref, proj_ref, keep_ref, tab_ref, v_ref, norm_ref, gain_ref,
         bias_ref, skip_ref, wout_ref, wglu_ref, h_ref, hlow_ref, carry_ref, slope_ref, act_ref, tile_ref, wide_ref)
     d = z.D
@@ -421,7 +421,7 @@
         z1 = wide_ref[rows, 0:d] + b1
         sig = jax.nn.sigmoid(wide_ref[rows, d : 2 * d] + b2)
         prod = z1 * sig
-        dy_ref[rows, :] = v_ref[rows, :] + prod
+        final_ref[rows, :] = v_ref[rows, :] + prod
         e = gout_ref[rows, :]
         d1, d2 = e * sig, e * (prod * (1.0 - sig))
         dz_ref[rows, 0:d] = d1.astype(BF16)
@@ -430,7 +430,6 @@
 
     zero = jnp.zeros((8, d), F32)
     s0, s1 = tiles(z, body, (zero, zero))
-    to_time(z, dy_ref, out_ref, natural_ref)
     descend(z, 1, jnp.concatenate([s0, s1], axis=1), dz_ref, slope_ref, v_ref, norm_ref, gain_ref, bias_ref, wglu_ref, wout_ref,
             adj_keep_ref, adj_chunk_ref, tab_ref, dy_ref, dylow_ref, dh_ref, adj_ends_ref, send_ref, small_ref, tile_ref)
     split_strips(z, half_keep, half_send, units(act_ref, dz_ref, half_keep) + units(hlow_ref, dylow_ref, half_keep))
@@ -554,7 +553,7 @@
     split_strips(z, keep_ref, send_ref, units(low1_ref, dplow1_ref, keep_ref) + units(low_ref, dplow_ref, keep_ref))
 
 
-def last(z, small_ref, dxn_ref, v_ref, norm_ref, gain_ref, e_ref, total1_ref, grad_ref, gain_out, bias_out, rate_out, phase_out, skip_out,
+def last(z, small_ref, dxn_ref, v_ref, norm_ref, gain_ref, e_ref, total1_ref, final_ref, out_ref, grad_ref, gain_out, bias_out, rate_out, phase_out, skip_out,
          bglu_out, natural_ref, work_ref):
     w = small_ref.shape[1]
     at = [0]
@@ -580,10 +579,16 @@
 
     tiles(z, body, 0)
     to_time(z, work_ref, grad_ref, natural_ref)
+    to_time(z, final_ref, out_ref, natural_ref)
 
 
 GRAD_TILE = 64
-SEQ = (2, 1, 0)
+SEQ = (0, 2, 1)
+FIRST = ()
+COST = 1
+FLOPS = 20000000000
+TRANS = 0
+FLAT = (1, 1, 1)
 ORDERS = ((0, 1, 2, 3, 4), (0, 1, 2, 3, 4), (0, 1, 2, 3, 4))
 STRIP = 256
 
@@ -669,56 +674,60 @@
     lax.fori_loop(0, count, one, 0)
 
 
+def add(keep_ref, recv_ref, out_ref):
+    out_ref[...] = keep_ref[...] + recv_ref[...]
+
+
 class Exchange:
-    def __init__(self, z, keep, send, extra=0, order=()):
+    def __init__(self, z, keep, send, extra=0, order=(), flat=1):
         self.z, self.keep, self.send, self.extra = z, keep, send, extra
         self.order = order if len(order) == z.bits else tuple(range(z.bits))
-        self.step, self.up, self.small = 0, False, None
         self.width = keep.shape[1]
+        self.small = None
+        deep = z.bits - flat
+        self.plan = [("halve", i) for i in range(deep)] + [("sum", i) for i in range(deep, z.bits)] + [("double", i) for i in range(deep - 1, -1, -1)]
 
     def go(self):
-        self.got = lax.ppermute(self.send, ("tm", "rows"), pairs(self.z, self.order[self.step]))
+        self.got = lax.ppermute(self.send, ("tm", "rows"), pairs(self.z, self.order[self.plan[0][1]]))
 
     def settle(self):
         z, x = self.z, self.extra
+        (kind, i), (after, j) = self.plan.pop(0), self.plan[0]
         n = self.keep.shape[0]
-        if self.up:
-            (self.keep,) = run(functools.partial(join, z, self.order[self.step]), "join", [((2 * n, self.width), F32)], (self.keep, self.got))
-            self.send = self.keep
-            self.step -= 1
+        both = (self.keep, self.got)
+        if kind == "double":
+            (self.keep,) = run(functools.partial(join, z, self.order[i]), "join", [((2 * n, self.width), F32)], both)
+        elif after == "halve":
+            half = (((n - x) // 2 + x, self.width), F32)
+            self.keep, self.send = run(functools.partial(halves, z, self.order[j], x), "halves", [half, half], both)
             return
-        n -= x
-        self.step += 1
-        if self.step < z.bits:
-            half = ((n // 2 + x, self.width), F32)
-            self.keep, self.send = run(functools.partial(halves, z, self.order[self.step], x), "halves", [half, half], (self.keep, self.got))
-            return
-        outs = [((n, self.width), F32)] + ([((x, self.width), F32)] if x else [])
-        self.keep, *self.small = run(functools.partial(total, x), "total", outs, (self.keep, self.got))
-        self.send, self.up = self.keep, True
-        self.step = z.bits - 1
+        elif after == "double" and x:
+            self.keep, self.small = run(functools.partial(total, x), "total", [((n - x, self.width), F32), ((x, self.width), F32)], both)
+        else:
+            (self.keep,) = run(add, "add", [((n, self.width), F32)], both)
+        self.send = self.keep
 
     @property
     def closing(self):
-        return self.up and self.step == 0
-
-
-def assemble(z, own1, got1, owna, gota, ownb, gotb, win_out, wout_out, wglu_out, sem):
+        return len(self.plan) == 1
+
+
+def assemble(z, which, *refs):
+    own, got, (win_out, wout_out, wglu_out, sem) = refs[0], refs[1], refs[-4:]
     bit = own_bit(z, 0)
-    w = own1.shape[1]
+    w = own.shape[1]
 
     def strips(out, b):
         return [out.at[b, :, i * w : (i + 1) * w] for i in range(out.shape[2] // w)]
 
-    places = [strips(wglu_out, 1) + strips(wout_out, 1), strips(wglu_out, 0) + strips(wout_out, 0), strips(win_out, 1) + strips(win_out, 0)]
-
-    def place(halves_of):
+    outs = strips(win_out, 1) + strips(win_out, 0) if which == 2 else strips(wglu_out, 1 - which) + strips(wout_out, 1 - which)
+    cut = len(outs) // 2
+
+    def place(low, high):
         copies = []
-        for (low, high), outs in zip(halves_of, places):
-            cut = len(outs) // 2
-            for ref, part in ((low, outs[:cut]), (high, outs[cut:])):
-                for i, out in enumerate(part):
-                    copies.append(pltpu.make_async_copy(ref.at[i * z.D : (i + 1) * z.D, :], out, sem.at[len(copies)]))
+        for ref, part in ((low, outs[:cut]), (high, outs[cut:])):
+            for k, out in enumerate(part):
+                copies.append(pltpu.make_async_copy(ref.at[k * z.D : (k + 1) * z.D, :], out, sem.at[len(copies)]))
         for c in copies:
             c.start()
         for c in copies:
@@ -726,26 +735,28 @@
 
     @pl.when(bit == 0)
     def _():
-        place([(own1, got1), (owna, gota), (ownb, gotb)])
+        place(own, got)
 
     @pl.when(bit == 1)
     def _():
-        place([(got1, own1), (gota, owna), (gotb, ownb)])
-
-
-def run(kernel, name, outs, args, scratch=(), sems=0, source=pltpu.VMEM, target=pltpu.VMEM):
+        place(got, own)
+
+
+def run(kernel, name, outs, args, scratch=(), sems=0, source=pltpu.VMEM, target=pltpu.VMEM, onto=()):
     if source is pltpu.HBM:
         args = [pltpu.with_memory_space_constraint(a, source) for a in args]
     shapes = [pltpu.VMEM(s, t) if t != jnp.int32 else pltpu.SMEM(s, t) for s, t in scratch]
     return pl.pallas_call(
         kernel,
         out_shape=[jax.ShapeDtypeStruct(s, t) for s, t in outs],
-        in_specs=[pl.BlockSpec(memory_space=source)] * len(args),
+        in_specs=[pl.BlockSpec(memory_space=source)] * len(args) + [pl.BlockSpec(memory_space=target)] * len(onto),
         out_specs=[pl.BlockSpec(memory_space=target)] * len(outs),
         scratch_shapes=shapes + ([pltpu.SemaphoreType.DMA((sems,))] if sems else []),
         compiler_params=pltpu.CompilerParams(vmem_limit_bytes=16 << 20),
+        cost_estimate=pl.CostEstimate(flops=FLOPS, bytes_accessed=COST, transcendentals=TRANS) if name in ("halves", "join", "add", "total") else None,
+        input_output_aliases={len(args) + i: i for i in range(len(onto))},
         name=name,
-    )(*args)
+    )(*args, *onto)
 
 
 def body(x_in, lengths, bn_gain, bn_bias, w_in, decay_rate, phase, w_out, skip_gain, w_glu, b_glu, grad_out):
@@ -802,12 +813,12 @@
     def tie(*values):
         return lax.optimization_barrier(values)
 
-    h1, carry1, out, dy1, dh1, adj_ends1, adj1, small1, keep1, send1 = run(
+    h1, carry1, v2, dy1, dh1, adj_ends1, adj1, small1, keep1, send1 = run(
         bind(turn, z), "turn",
-        [full_n, chunk, low, full, full_n, chunk, send_shape, small_shape, part(3), part(3)],
+        [full_n, chunk, full, full, full_n, chunk, send_shape, small_shape, part(3), part(3)],
         (send1, dev_r, power, ends1, chunk_r, proj1, keep_r, tab, v1, norm1, bn_gain, bn_bias, skip_gain, w_out, w_glu, b_glu, gout,
-         keep_f, chunk_f), [tile, wide_f, full, natural, low_n, low, wide_b, low])
-    one = Exchange(z, keep1, send1, order=ORDERS[0])
+         keep_f, chunk_f), [tile, wide_f, full, low_n, low, wide_b, low])
+    one = Exchange(z, keep1, send1, order=ORDERS[0], flat=FLAT[0])
     one.send, adj1 = tie(one.send, adj1)
     one.go()
     adj1 = swap(adj1, "tm")
@@ -827,7 +838,7 @@
         [norm_shape, full, full, full_n, chunk, send_shape, small_shape, part(3), part(3)],
         (sum1, dxn1, v1, norm1, gout, sig0, gate0, slope0, x, norm0, bn_gain, bn_bias, w_glu, w_out, keep_r, chunk_r, tab, act0, hlow0),
         [tile, stat_tile, wide_b, low])
-    two = Exchange(z, keepa, senda, order=ORDERS[1])
+    two = Exchange(z, keepa, senda, order=ORDERS[1], flat=FLAT[1])
     one.send, two.send, adj0 = tie(one.send, two.send, adj0)
     one.go()
     two.go()
@@ -843,25 +854,34 @@
         [low_n, lam_shape, tile, chunk])
     one.settle()
     two.settle()
-    three = Exchange(z, keepb, sendb, z.extra, ORDERS[2])
+    three = Exchange(z, keepb, sendb, z.extra, ORDERS[2], FLAT[2])
     one.send, two.send, three.send = tie(one.send, two.send, three.send)
     for e in (one, two, three):
         e.go()
-    sets = [(one, two, three)[i] for i in SEQ]
+    sets = (one, two, three)
     ahead = three.send
-    while not all(e.closing for e in sets):
-        for e in sets:
-            if not e.closing:
-                e.got, _ = tie(e.got, ahead)
+    placed, done, queue = (), [], list(FIRST) if z.bits == 5 else []
+    while len(done) < len(sets):
+        for i in queue or SEQ:
+            e = sets[i]
+            if i in done:
+                continue
+            e.got, _ = tie(e.got, ahead)
+            if e.closing:
+                placed = run(
+                    bind(assemble, z, i), "assemble", [((2, D, 2 * N), F32), ((2, 2 * N, D), F32), ((2, D, 2 * D), F32)],
+                    (e.keep, e.got), sems=8 * (STRIP // W), target=pltpu.HBM, onto=placed)
+                ahead = placed[0]
+                done.append(i)
+            else:
                 e.settle()
                 e.go()
                 ahead = e.send
+        queue = []
     sums = (((2, D), F32), ((2, D), F32), ((2, N), F32), ((2, N), F32), ((2, D), F32), ((2, 2 * D), F32))
-    grad_x, gain_out, bias_out, rate_out, phase_out, skip_out, bglu_out = run(
-        bind(last, z), "last", [full, *sums], (three.small[0], dxn0, x, norm0, bn_gain, e1, total1), [natural, full])
-    gwin, gwout, gwglu = run(
-        bind(assemble, z), "assemble", [((2, D, 2 * N), F32), ((2, 2 * N, D), F32), ((2, D, 2 * D), F32)],
-        (one.keep, one.got, two.keep, two.got, three.keep, three.got), sems=16, target=pltpu.HBM)
+    out, grad_x, gain_out, bias_out, rate_out, phase_out, skip_out, bglu_out = run(
+        bind(last, z), "last", [low, full, *sums], (three.small, dxn0, x, norm0, bn_gain, e1, total1, v2), [natural, full])
+    gwin, gwout, gwglu = placed
     return (
         out.reshape(rows, steps, width),
         grad_x.reshape(rows, steps, width),

time: 192 us -> 175 us (0.911)
  waiting for transfers between devices: 68.8 us -> 58.9 us
  starting transfers between devices: 26.6 us -> 17.8 us
    ppermute x30 -> x27, waiting for transfers between devices: 68.8 us -> 58.9 us  [go(): lax.ppermute(self.send, ('tm', 'rows'), pairs(self.z, self.order[self.pla...]
    ppermute x30 -> x27, starting transfers between devices: 26.6 us -> 17.8 us  [go(): lax.ppermute(self.send, ('tm', 'rows'), pairs(self.z, self.order[self.pla...]
    pallas_call x37 -> x36, Pallas kernels: 20.9 us -> 21.5 us  [run(): pl.pallas_call(kernel, out_shape=[jax.ShapeDtypeStruct(s, t) for s, t in...]
  transfers between devices with their start and end apart: 30 -> 27, of which waited for: 16 -> 15; matrix products, arithmetic and copies ran while one was open for 0% -> 0% of each run, Pallas kernels for 1% -> 4%
where the time goes in v4:
time: 175 us; the launch traced here: 174 us
  blocking collectives  74.7 us (43%)
  waiting for transfers between devices  58.9 us (34%)
  Pallas kernels  21.5 us (12%)
  starting transfers between devices  17.8 us (10%)
    all_to_all x7, blocking collectives, swap(): return lax.all_to_all(a, axis, 0, 0)  74.7 us
    ppermute x27, waiting for transfers between devices, go(): lax.ppermute(self.send, ('tm', 'rows'), pairs(self.z, self.order[self.pla...  58.9 us
    pallas_call x36, Pallas kernels, run(): pl.pallas_call(kernel, out_shape=[jax.ShapeDtypeStruct(s, t) for s, t in...  21.5 us
    ppermute x27, starting transfers between devices, go(): lax.ppermute(self.send, ('tm', 'rows'), pairs(self.z, self.order[self.pla...  17.8 us
  transfers between devices with their start and end apart: 27, of which 15 were waited for; matrix products, arithmetic and copies ran while one was open for 0% of the time, Pallas kernels for 4%

profile of v4, /device:TPU:0, one launch (start us, length us, event | category | flops | bytes accessed | tf_op | source)
XLA Modules:
  0.0 174.2 jit_solution(5043968549916819844)
XLA Ops:
  0.6 2.6 %prepare.1 = (f32[256,512]{1,0:T(8,128)S(1)}, f32[256,512]{1,0:T(8,128)S(1)}, f32[32,8,128]{2,1,0:T(8,128)S(1)}, f32[256,128]{1,0:T(8,128)S(1)}, f32[256,128]{1,...) custom-call(s32[2,16]{1,0:T(2,128)} %len_hbm.1, ...), custom_call_target="tpu_custom_call" | custom-call | tf_op jit(solution)/shard_map/prepare/pallas_call | solution.py:749
  3.3 15.3 %all_to_all.35.stat_ref = f32[32,8,128]{2,1,0:T(8,128)S(1)} all-to-all(f32[32,8,128]{2,1,0:T(8,128)S(1)} %get-tuple-element.151), channel_id=1, replica_groups=mesh['tm'=8,'rows'=4] {'tm','rows'}, dimensions={0} | all-to-all | bytes 262144 | tf_op jit(solution)/shard_map/all_to_all | solution.py:769
  18.6 0.6 enter0.1
  19.2 9.2 %all_to_all.36.recv_ref = f32[8,8,128]{2,1,0:T(8,128)S(1)} all-to-all(f32[8,8,128]{2,1,0:T(8,128)S(1)} %get-tuple-element.159), channel_id=1, replica_groups=mesh['tm'=8,'rows'=4] {'tm'}, dimensions={0} | all-to-all | bytes 65536 | tf_op jit(solution)/shard_map/all_to_all | solution.py:769
  28.4 1.6 middle.1
  30.0 9.9 %all_to_all.37.stat_ref = f32[32,8,128]{2,1,0:T(8,128)S(1)} all-to-all(f32[32,8,128]{2,1,0:T(8,128)S(1)} %get-tuple-element.169), channel_id=1, replica_groups=mesh['tm'=8,'rows'=4] {'tm','rows'}, dimensions={0} | all-to-all | bytes 262144 | tf_op jit(solution)/shard_map/all_to_all | solution.py:769
  39.9 0.6 enter1.1
  40.6 9.1 %all_to_all.38.recv_ref = f32[8,8,128]{2,1,0:T(8,128)S(1)} all-to-all(f32[8,8,128]{2,1,0:T(8,128)S(1)} %get-tuple-element.173), channel_id=1, replica_groups=mesh['tm'=8,'rows'=4] {'tm'}, dimensions={0} | all-to-all | bytes 65536 | tf_op jit(solution)/shard_map/all_to_all | solution.py:769
  49.7 3.5 %turn.1 = (f32[256,512]{1,0:T(8,128)S(1)}, f32[16,512]{1,0:T(8,128)S(1)}, f32[256,512]{1,0:T(8,128)S(1)}, f32[256,512]{1,0:T(8,128)S(1)}, f32[256,512]{1,0:T(8,1...) custom-call(f32[8,8,128]{2,1,0:T(8,128)S(1)} %all_to_all.38.recv_ref, ...), custom_call_target="tpu_custom_call" | custom-call | tf_op jit(solution)/shard_map/turn/pallas_call | solution.py:749
  53.2 0.1 collective-permute-start
  53.2 9.1 %all_to_all.39.refs_0_ = f32[8,8,128]{2,1,0:T(8,128)S(1)} all-to-all(f32[8,8,128]{2,1,0:T(8,128)S(1)} %get-tuple-element.183), channel_id=1, replica_groups=mesh['tm'=8,'rows'=4] {'tm'}, dimensions={0} | all-to-all | bytes 65536 | tf_op jit(solution)/shard_map/all_to_all | solution.py:769
  62.3 0.2 halves.9
  62.5 0.8 finish1.1
  63.3 0.5 collective-permute-start.1
  63.9 13.1 %all_to_all.40.stat_ref = f32[32,8,128]{2,1,0:T(8,128)S(1)} all-to-all(f32[32,8,128]{2,1,0:T(8,128)S(1)} %get-tuple-element.195), channel_id=1, replica_groups=mesh['tm'=8,'rows'=4] {'tm','rows'}, dimensions={0} | all-to-all | bytes 262144 | tf_op jit(solution)/shard_map/all_to_all | solution.py:769
  76.9 0.1 halves.10
  77.0 2.1 %lower_block.1 = (f32[8,512]{1,0:T(8,128)S(1)}, f32[256,512]{1,0:T(8,128)S(1)}, f32[256,512]{1,0:T(8,128)S(1)}, f32[256,512]{1,0:T(8,128)S(1)}, f32[16,512]{1,0:...) custom-call(f32[32,8,128]{2,1,0:T(8,128)S(1)} %all_to_all.40.stat_re, ...), custom_call_target="tpu_custom_call" | custom-call | tf_op jit(solution)/shard_map/lower_block/pallas_call | solution.py:749
  79.1 0.1 collective-permute-start.3
  79.2 1.4 collective-permute-start.2
  80.6 9.0 %all_to_all.41.refs_0_ = f32[8,8,128]{2,1,0:T(8,128)S(1)} all-to-all(f32[8,8,128]{2,1,0:T(8,128)S(1)} %get-tuple-element.209), channel_id=1, replica_groups=mesh['tm'=8,'rows'=4] {'tm'}, dimensions={0} | all-to-all | bytes 65536 | tf_op jit(solution)/shard_map/all_to_all | solution.py:769
  89.7 0.2 halves.12
  89.9 1.5 finish0.1
  91.4 0.4 collective-permute-start.5
  91.9 0.8 collective-permute-start.8
  92.6 4.5 %collective-permute-done.5.recv_ref = f32[192,256]{1,0:T(8,128)S(1)} collective-permute-done((f32[192,256]{1,0:T(8,128)S(1)}, f32[192,256]{1,0:T(8,128)S(1)}, u32[]{:S(2)}, u32[]{:S(2)}) %collective-permute-start.5) | collective-permute-done | bytes 196640 | tf_op jit(solution)/shard_map/ppermute | solution.py:691
  97.2 0.6 collective-permute-start.7
  97.8 0.1 halves.13
  97.9 0.5 collective-permute-start.6
  98.4 5.5 %collective-permute-done.8.recv_ref = f32[768,256]{1,0:T(8,128)S(1)} collective-permute-done((f32[768,256]{1,0:T(8,128)S(1)}, f32[768,256]{1,0:T(8,128)S(1)}, u32[]{:S(2)}, u32[]{:S(2)}) %collective-permute-start.8) | collective-permute-done | bytes 786464 | tf_op jit(solution)/shard_map/ppermute | solution.py:691
  103.9 0.1 halves.14
  104.0 0.7 collective-permute-start.11
  104.8 1.3 collective-permute-done.7.recv_ref
  106.1 0.4 collective-permute-start.10
  106.5 9.2 %collective-permute-done.6.recv_ref = f32[536,256]{1,0:T(8,128)S(1)} collective-permute-done((f32[536,256]{1,0:T(8,128)S(1)}, f32[536,256]{1,0:T(8,128)S(1)}, u32[]{:S(2)}, u32[]{:S(2)}) %collective-permute-start.6) | collective-permute-done | bytes 548896 | tf_op jit(solution)/shard_map/ppermute | solution.py:691
  115.8 0.3 collective-permute-start.9
  116.1 1.7 collective-permute-start.14
  117.9 1.9 %collective-permute-start.13 = (f32[384,256]{1,0:T(8,128)S(1)}, f32[384,256]{1,0:T(8,128)S(1)}, u32[]{:S(2)}, u32[]{:S(2)}) collective-permute-start(f32[384,256]{1,0:T(8,128)S(1)} %join.9.own_ref), channel_id=1, source_target_pairs={{0,2},{1,5},{2,0},{3,7},{4,6},{5,1},{6,4},{7,3},{8,10},{9,13},{10,... | collective-permute-start | bytes 1179656 | tf_op jit(solution)/shard_map/ppermute | solution.py:691
  119.8 2.7 %collective-permute-done.9.recv_ref = f32[280,256]{1,0:T(8,128)S(1)} collective-permute-done((f32[280,256]{1,0:T(8,128)S(1)}, f32[280,256]{1,0:T(8,128)S(1)}, u32[]{:S(2)}, u32[]{:S(2)}) %collective-permute-start.9) | collective-permute-done | bytes 286752 | tf_op jit(solution)/shard_map/ppermute | solution.py:691
  122.5 1.7 collective-permute-start.12
  124.3 0.7 collective-permute-done.14.recv_ref
  125.0 0.2 collective-permute-start.17
  125.2 4.0 %collective-permute-done.13.recv_ref = f32[384,256]{1,0:T(8,128)S(1)} collective-permute-done((f32[384,256]{1,0:T(8,128)S(1)}, f32[384,256]{1,0:T(8,128)S(1)}, u32[]{:S(2)}, u32[]{:S(2)}) %collective-permute-start.13) | collective-permute-done | bytes 393248 | tf_op jit(solution)/shard_map/ppermute | solution.py:691
  129.3 0.9 collective-permute-start.16
  130.3 5.0 %collective-permute-done.17.recv_ref = f32[192,256]{1,0:T(8,128)S(1)} collective-permute-done((f32[192,256]{1,0:T(8,128)S(1)}, f32[192,256]{1,0:T(8,128)S(1)}, u32[]{:S(2)}, u32[]{:S(2)}) %collective-permute-start.17) | collective-permute-done | bytes 196640 | tf_op jit(solution)/shard_map/ppermute | solution.py:691
  135.4 0.7 collective-permute-start.20
  136.0 5.3 %collective-permute-done.16.recv_ref = f32[768,256]{1,0:T(8,128)S(1)} collective-permute-done((f32[768,256]{1,0:T(8,128)S(1)}, f32[768,256]{1,0:T(8,128)S(1)}, u32[]{:S(2)}, u32[]{:S(2)}) %collective-permute-start.16) | collective-permute-done | bytes 786464 | tf_op jit(solution)/shard_map/ppermute | solution.py:691
  141.3 0.1 join.11.refs_0_
  141.6 1.8 %collective-permute-start.18 = (f32[128,256]{1,0:T(8,128)S(1)}, f32[128,256]{1,0:T(8,128)S(1)}, u32[]{:S(2)}, u32[]{:S(2)}) collective-permute-start(f32[128,256]{1,0:T(8,128)S(1)} %get-tuple-element.268.own_ref), channel_id=1, source_target_pairs={{0,8},{1,9},{2,10},{3,11},{4,12},{5,13},{6,14},{7,15},{8,0},{9,1},... | collective-permute-start | bytes 393224 | tf_op jit(solution)/shard_map/ppermute | solution.py:691
  143.5 1.5 collective-permute-done.19.refs_1_
  145.0 1.7 assemble.3
  146.7 0.9 collective-permute-done.18.recv_ref
  147.6 1.1 collective-permute-start.21
  148.7 2.6 %collective-permute-done.22.recv_ref = f32[384,256]{1,0:T(8,128)S(1)} collective-permute-done((f32[384,256]{1,0:T(8,128)S(1)}, f32[384,256]{1,0:T(8,128)S(1)}, u32[]{:S(2)}, u32[]{:S(2)}) %collective-permute-start.22) | collective-permute-done | bytes 393248 | tf_op jit(solution)/shard_map/ppermute | solution.py:691
  151.3 0.5 collective-permute-start.24
  151.9 2.9 %collective-permute-done.21.recv_ref = f32[256,256]{1,0:T(8,128)S(1)} collective-permute-done((f32[256,256]{1,0:T(8,128)S(1)}, f32[256,256]{1,0:T(8,128)S(1)}, u32[]{:S(2)}, u32[]{:S(2)}) %collective-permute-start.21) | collective-permute-done | bytes 262176 | tf_op jit(solution)/shard_map/ppermute | solution.py:691
  154.8 1.2 collective-permute-start.23
  156.0 7.4 %collective-permute-done.24.recv_ref = f32[768,256]{1,0:T(8,128)S(1)} collective-permute-done((f32[768,256]{1,0:T(8,128)S(1)}, f32[768,256]{1,0:T(8,128)S(1)}, u32[]{:S(2)}, u32[]{:S(2)}) %collective-permute-start.24) | collective-permute-done | bytes 786464 | tf_op jit(solution)/shard_map/ppermute | solution.py:691
  163.4 0.1 join.16.refs_0_
  163.6 5.4 %collective-permute-done.23.recv_ref = f32[512,256]{1,0:T(8,128)S(1)} collective-permute-done((f32[512,256]{1,0:T(8,128)S(1)}, f32[512,256]{1,0:T(8,128)S(1)}, u32[]{:S(2)}, u32[]{:S(2)}) %collective-permute-start.23) | collective-permute-done | bytes 524320 | tf_op jit(solution)/shard_map/ppermute | solution.py:691
  169.0 0.1 join.17.refs_0_
  169.1 0.1 collective-permute-start.25
  169.2 1.6 last.1
  170.8 1.7 %assemble.4 = (f32[2,512,512]{2,1,0:T(8,128)}, f32[2,512,512]{2,1,0:T(8,128)}, f32[2,512,1024]{2,1,0:T(8,128)}) custom-call(f32[1536,256]{1,0:T(8,128)S(1)} %join.16.refs_0_, f32[1536,256]{1,0:T(8,128)S(1)} %collective-permute-done.26.refs_1_, f32[2,512,512]{2,1,0:T(8,128)} %get-tuple-element.271.refs_2_, ...), custom_call_target="tpu_custom_call", output_to_operand_aliasing={{0}: (2, {}), {1}: (3, {}), {2}: (4, {})} | custom-call | tf_op jit(solution)/shard_map/assemble/pallas_call | solution.py:749
  172.6 1.4 assemble.5
  (37 shorter events, 0.9 us)
Async XLA Ops:
  3.3 73.8 %copy-start = (f32[2,512]{1,0:T(2,128)}, f32[2,512]{1,0:T(2,128)S(1)}, u32[]{:S(2)}) copy-start(f32[2,512]{1,0:T(2,128)S(1)} %get-tuple-element.153.gain_ref) | copy-start | bytes 12292
  53.2 9.1 %collective-permute-start = (f32[1536,256]{1,0:T(8,128)S(1)}, f32[1536,256]{1,0:T(8,128)S(1)}, u32[]{:S(2)}, u32[]{:S(2)}) collective-permute-start(f32[1536,256]{1,0:T(8,128)S(1)} %get-tuple-element.182), channel_id=1, source_target_pairs={{0,1},{1,0},{2,3},{3,2},{4,5},{5,4},{6,7},{7,6},{8,9},{9,8},{10,11... | collective-permute-start | bytes 4718600 | tf_op jit(solution)/shard_map/ppermute | solution.py:691
  63.3 13.6 %collective-permute-start.1 = (f32[768,256]{1,0:T(8,128)S(1)}, f32[768,256]{1,0:T(8,128)S(1)}, u32[]{:S(2)}, u32[]{:S(2)}) collective-permute-start(f32[768,256]{1,0:T(8,128)S(1)} %get-tuple-element.194), channel_id=1, source_target_pairs={{0,4},{1,3},{2,6},{3,1},{4,0},{5,7},{6,2},{7,5},{8,12},{9,11},{10,... | collective-permute-start | bytes 2359304 | tf_op jit(solution)/shard_map/ppermute | solution.py:691
  79.1 10.5 %collective-permute-start.3 = (f32[1536,256]{1,0:T(8,128)S(1)}, f32[1536,256]{1,0:T(8,128)S(1)}, u32[]{:S(2)}, u32[]{:S(2)}) collective-permute-start(f32[1536,256]{1,0:T(8,128)S(1)} %get-tuple-element.208), channel_id=1, source_target_pairs={{0,1},{1,0},{2,3},{3,2},{4,5},{5,4},{6,7},{7,6},{8,9},{9,8},{10,11... | collective-permute-start | bytes 4718600 | tf_op jit(solution)/shard_map/ppermute | solution.py:691
  79.2 10.4 %collective-permute-start.2 = (f32[384,256]{1,0:T(8,128)S(1)}, f32[384,256]{1,0:T(8,128)S(1)}, u32[]{:S(2)}, u32[]{:S(2)}) collective-permute-start(f32[384,256]{1,0:T(8,128)S(1)} %get-tuple-element.207), channel_id=1, source_target_pairs={{0,2},{1,5},{2,0},{3,7},{4,6},{5,1},{6,4},{7,3},{8,10},{9,13},{10,... | collective-permute-start | bytes 1179656 | tf_op jit(solution)/shard_map/ppermute | solution.py:691
  91.4 5.7 %collective-permute-start.5 = (f32[192,256]{1,0:T(8,128)S(1)}, f32[192,256]{1,0:T(8,128)S(1)}, u32[]{:S(2)}, u32[]{:S(2)}) collective-permute-start(f32[192,256]{1,0:T(8,128)S(1)} %get-tuple-element.232), channel_id=1, source_target_pairs={{0,8},{1,9},{2,10},{3,11},{4,12},{5,13},{6,14},{7,15},{8,0},{9,1},... | collective-permute-start | bytes 589832 | tf_op jit(solution)/shard_map/ppermute | solution.py:691
  91.9 12.1 %collective-permute-start.8 = (f32[768,256]{1,0:T(8,128)S(1)}, f32[768,256]{1,0:T(8,128)S(1)}, u32[]{:S(2)}, u32[]{:S(2)}) collective-permute-start(f32[768,256]{1,0:T(8,128)S(1)} %get-tuple-element.238), channel_id=1, source_target_pairs={{0,4},{1,3},{2,6},{3,1},{4,0},{5,7},{6,2},{7,5},{8,12},{9,11},{10,... | collective-permute-start | bytes 2359304 | tf_op jit(solution)/shard_map/ppermute | solution.py:691
  92.6 5.1 %collective-permute-start.4 = (f32[1048,256]{1,0:T(8,128)S(1)}, f32[1048,256]{1,0:T(8,128)S(1)}, u32[]{:S(2)}, u32[]{:S(2)}) collective-permute-start(f32[1048,256]{1,0:T(8,128)S(1)} %get-tuple-element.230), channel_id=1, source_target_pairs={{0,1},{1,0},{2,3},{3,2},{4,5},{5,4},{6,7},{7,6},{8,9},{9,8},{10,11... | collective-permute-start | bytes 3219464 | tf_op jit(solution)/shard_map/ppermute | solution.py:691
  97.2 8.9 %collective-permute-start.7 = (f32[192,256]{1,0:T(8,128)S(1)}, f32[192,256]{1,0:T(8,128)S(1)}, u32[]{:S(2)}, u32[]{:S(2)}) collective-permute-start(f32[192,256]{1,0:T(8,128)S(1)} %add.5.keep_ref), channel_id=1, source_target_pairs={{0,16},{1,17},{2,18},{3,19},{4,20},{5,21},{6,22},{7,23},{8,24},{9,... | collective-permute-start | bytes 589832 | tf_op jit(solution)/shard_map/ppermute | solution.py:691
  97.9 17.8 %collective-permute-start.6 = (f32[536,256]{1,0:T(8,128)S(1)}, f32[536,256]{1,0:T(8,128)S(1)}, u32[]{:S(2)}, u32[]{:S(2)}) collective-permute-start(f32[536,256]{1,0:T(8,128)S(1)} %get-tuple-element.236), channel_id=1, source_target_pairs={{0,4},{1,3},{2,6},{3,1},{4,0},{5,7},{6,2},{7,5},{8,12},{9,11},{10,... | collective-permute-start | bytes 1646600 | tf_op jit(solution)/shard_map/ppermute | solution.py:691
  104.0 12.0 %collective-permute-start.11 = (f32[384,256]{1,0:T(8,128)S(1)}, f32[384,256]{1,0:T(8,128)S(1)}, u32[]{:S(2)}, u32[]{:S(2)}) collective-permute-start(f32[384,256]{1,0:T(8,128)S(1)} %get-tuple-element.240), channel_id=1, source_target_pairs={{0,2},{1,5},{2,0},{3,7},{4,6},{5,1},{6,4},{7,3},{8,10},{9,13},{10,... | collective-permute-start | bytes 1179656 | tf_op jit(solution)/shard_map/ppermute | solution.py:691
  106.1 11.8 %collective-permute-start.10 = (f32[192,256]{1,0:T(8,128)S(1)}, f32[192,256]{1,0:T(8,128)S(1)}, u32[]{:S(2)}, u32[]{:S(2)}) collective-permute-start(f32[192,256]{1,0:T(8,128)S(1)} %add.6.own_ref), channel_id=1, source_target_pairs={{0,8},{1,9},{2,10},{3,11},{4,12},{5,13},{6,14},{7,15},{8,0},{9,1},... | collective-permute-start | bytes 589832 | tf_op jit(solution)/shard_map/ppermute | solution.py:691
  115.8 6.7 %collective-permute-start.9 = (f32[280,256]{1,0:T(8,128)S(1)}, f32[280,256]{1,0:T(8,128)S(1)}, u32[]{:S(2)}, u32[]{:S(2)}) collective-permute-start(f32[280,256]{1,0:T(8,128)S(1)} %get-tuple-element.244), channel_id=1, source_target_pairs={{0,2},{1,5},{2,0},{3,7},{4,6},{5,1},{6,4},{7,3},{8,10},{9,13},{10,... | collective-permute-start | bytes 860168 | tf_op jit(solution)/shard_map/ppermute | solution.py:691
  116.1 8.8 %collective-permute-start.14 = (f32[192,256]{1,0:T(8,128)S(1)}, f32[192,256]{1,0:T(8,128)S(1)}, u32[]{:S(2)}, u32[]{:S(2)}) collective-permute-start(f32[192,256]{1,0:T(8,128)S(1)} %get-tuple-element.247), channel_id=1, source_target_pairs={{0,8},{1,9},{2,10},{3,11},{4,12},{5,13},{6,14},{7,15},{8,0},{9,1},... | collective-permute-start | bytes 589832 | tf_op jit(solution)/shard_map/ppermute | solution.py:691
  117.9 11.3 %collective-permute-start.13 = (f32[384,256]{1,0:T(8,128)S(1)}, f32[384,256]{1,0:T(8,128)S(1)}, u32[]{:S(2)}, u32[]{:S(2)}) collective-permute-start(f32[384,256]{1,0:T(8,128)S(1)} %join.9.own_ref), channel_id=1, source_target_pairs={{0,2},{1,5},{2,0},{3,7},{4,6},{5,1},{6,4},{7,3},{8,10},{9,13},{10,... | collective-permute-start | bytes 1179656 | tf_op jit(solution)/shard_map/ppermute | solution.py:691
  122.5 7.7 %collective-permute-start.12 = (f32[152,256]{1,0:T(8,128)S(1)}, f32[152,256]{1,0:T(8,128)S(1)}, u32[]{:S(2)}, u32[]{:S(2)}) collective-permute-start(f32[152,256]{1,0:T(8,128)S(1)} %get-tuple-element.251), channel_id=1, source_target_pairs={{0,8},{1,9},{2,10},{3,11},{4,12},{5,13},{6,14},{7,15},{8,0},{9,1},... | collective-permute-start | bytes 466952 | tf_op jit(solution)/shard_map/ppermute | solution.py:691
  125.0 10.4 %collective-permute-start.17 = (f32[192,256]{1,0:T(8,128)S(1)}, f32[192,256]{1,0:T(8,128)S(1)}, u32[]{:S(2)}, u32[]{:S(2)}) collective-permute-start(f32[192,256]{1,0:T(8,128)S(1)} %add.7.keep_ref), channel_id=1, source_target_pairs={{0,16},{1,17},{2,18},{3,19},{4,20},{5,21},{6,22},{7,23},{8,24},{9,... | collective-permute-start | bytes 589832 | tf_op jit(solution)/shard_map/ppermute | solution.py:691
  129.3 12.1 %collective-permute-start.16 = (f32[768,256]{1,0:T(8,128)S(1)}, f32[768,256]{1,0:T(8,128)S(1)}, u32[]{:S(2)}, u32[]{:S(2)}) collective-permute-start(f32[768,256]{1,0:T(8,128)S(1)} %join.10.own_ref), channel_id=1, source_target_pairs={{0,4},{1,3},{2,6},{3,1},{4,0},{5,7},{6,2},{7,5},{8,12},{9,11},{10,... | collective-permute-start | bytes 2359304 | tf_op jit(solution)/shard_map/ppermute | solution.py:691
  130.2 11.3 %collective-permute-start.15 = (f32[152,256]{1,0:T(8,128)S(1)}, f32[152,256]{1,0:T(8,128)S(1)}, u32[]{:S(2)}, u32[]{:S(2)}) collective-permute-start(f32[152,256]{1,0:T(8,128)S(1)} %add.8.keep_ref), channel_id=1, source_target_pairs={{0,16},{1,17},{2,18},{3,19},{4,20},{5,21},{6,22},{7,23},{8,24},{9,... | collective-permute-start | bytes 466952 | tf_op jit(solution)/shard_map/ppermute | solution.py:691
  135.4 8.0 %collective-permute-start.20 = (f32[192,256]{1,0:T(8,128)S(1)}, f32[192,256]{1,0:T(8,128)S(1)}, u32[]{:S(2)}, u32[]{:S(2)}) collective-permute-start(f32[192,256]{1,0:T(8,128)S(1)} %add.9.own_ref), channel_id=1, source_target_pairs={{0,8},{1,9},{2,10},{3,11},{4,12},{5,13},{6,14},{7,15},{8,0},{9,1},... | collective-permute-start | bytes 589832 | tf_op jit(solution)/shard_map/ppermute | solution.py:691
  141.5 3.5 %collective-permute-start.19 = (f32[1536,256]{1,0:T(8,128)S(1)}, f32[1536,256]{1,0:T(8,128)S(1)}, u32[]{:S(2)}, u32[]{:S(2)}) collective-permute-start(f32[1536,256]{1,0:T(8,128)S(1)} %join.11.refs_0_), channel_id=1, source_target_pairs={{0,1},{1,0},{2,3},{3,2},{4,5},{5,4},{6,7},{7,6},{8,9},{9,8},{10,11... | collective-permute-start | bytes 4718600 | tf_op jit(solution)/shard_map/ppermute | solution.py:691
  141.6 6.0 %collective-permute-start.18 = (f32[128,256]{1,0:T(8,128)S(1)}, f32[128,256]{1,0:T(8,128)S(1)}, u32[]{:S(2)}, u32[]{:S(2)}) collective-permute-start(f32[128,256]{1,0:T(8,128)S(1)} %get-tuple-element.268.own_ref), channel_id=1, source_target_pairs={{0,8},{1,9},{2,10},{3,11},{4,12},{5,13},{6,14},{7,15},{8,0},{9,1},... | collective-permute-start | bytes 393224 | tf_op jit(solution)/shard_map/ppermute | solution.py:691
  143.4 7.8 %collective-permute-start.22 = (f32[384,256]{1,0:T(8,128)S(1)}, f32[384,256]{1,0:T(8,128)S(1)}, u32[]{:S(2)}, u32[]{:S(2)}) collective-permute-start(f32[384,256]{1,0:T(8,128)S(1)} %join.12.own_ref), channel_id=1, source_target_pairs={{0,2},{1,5},{2,0},{3,7},{4,6},{5,1},{6,4},{7,3},{8,10},{9,13},{10,... | collective-permute-start | bytes 1179656 | tf_op jit(solution)/shard_map/ppermute | solution.py:691
  147.6 7.1 %collective-permute-start.21 = (f32[256,256]{1,0:T(8,128)S(1)}, f32[256,256]{1,0:T(8,128)S(1)}, u32[]{:S(2)}, u32[]{:S(2)}) collective-permute-start(f32[256,256]{1,0:T(8,128)S(1)} %join.13.own_ref), channel_id=1, source_target_pairs={{0,2},{1,5},{2,0},{3,7},{4,6},{5,1},{6,4},{7,3},{8,10},{9,13},{10,... | collective-permute-start | bytes 786440 | tf_op jit(solution)/shard_map/ppermute | solution.py:691
  151.3 12.1 %collective-permute-start.24 = (f32[768,256]{1,0:T(8,128)S(1)}, f32[768,256]{1,0:T(8,128)S(1)}, u32[]{:S(2)}, u32[]{:S(2)}) collective-permute-start(f32[768,256]{1,0:T(8,128)S(1)} %join.14.own_ref), channel_id=1, source_target_pairs={{0,4},{1,3},{2,6},{3,1},{4,0},{5,7},{6,2},{7,5},{8,12},{9,11},{10,... | collective-permute-start | bytes 2359304 | tf_op jit(solution)/shard_map/ppermute | solution.py:691
  154.8 14.2 %collective-permute-start.23 = (f32[512,256]{1,0:T(8,128)S(1)}, f32[512,256]{1,0:T(8,128)S(1)}, u32[]{:S(2)}, u32[]{:S(2)}) collective-permute-start(f32[512,256]{1,0:T(8,128)S(1)} %join.15.own_ref), channel_id=1, source_target_pairs={{0,4},{1,3},{2,6},{3,1},{4,0},{5,7},{6,2},{7,5},{8,12},{9,11},{10,... | collective-permute-start | bytes 1572872 | tf_op jit(solution)/shard_map/ppermute | solution.py:691
  163.5 5.7 %copy-start.1 = (f32[2,512]{1,0:T(2,128)S(1)}, f32[2,512]{1,0:T(2,128)}, u32[]{:S(2)}) copy-start(f32[2,512]{1,0:T(2,128)} %copy-done) | copy-start | bytes 12292
  163.5 7.3 %collective-permute-start.26 = (f32[1536,256]{1,0:T(8,128)S(1)}, f32[1536,256]{1,0:T(8,128)S(1)}, u32[]{:S(2)}, u32[]{:S(2)}) collective-permute-start(f32[1536,256]{1,0:T(8,128)S(1)} %join.16.refs_0_), channel_id=1, source_target_pairs={{0,1},{1,0},{2,3},{3,2},{4,5},{5,4},{6,7},{7,6},{8,9},{9,8},{10,11... | collective-permute-start | bytes 4718600 | tf_op jit(solution)/shard_map/ppermute | solution.py:691
  169.1 3.5 %collective-permute-start.25 = (f32[1024,256]{1,0:T(8,128)S(1)}, f32[1024,256]{1,0:T(8,128)S(1)}, u32[]{:S(2)}, u32[]{:S(2)}) collective-permute-start(f32[1024,256]{1,0:T(8,128)S(1)} %join.17.refs_0_), channel_id=1, source_target_pairs={{0,1},{1,0},{2,3},{3,2},{4,5},{5,4},{6,7},{7,6},{8,9},{9,8},{10,11... | collective-permute-start | bytes 3145736 | tf_op jit(solution)/shard_map/ppermute | solution.py:691

commit v5 on v4

--- a/solution.py
+++ b/solution.py
@@ -11,7 +11,7 @@
 EPS = 1e-05
 LANES = 128
 CHUNKS = 8
-TILE = 32
+TILE = 128
 F32 = jnp.float32
 BF16 = jnp.bfloat16
 ROOT_HALF = 0.7071067811865476
@@ -493,7 +493,8 @@
 
 def lower_block(z, stat_ref, dxn_ref, v1_ref, norm1_ref, gout_ref, sig_ref, gate_ref, slope_ref, v_ref, norm_ref, gain_ref, bias_ref,
                 wglu_ref, wout_ref, keep_ref, chunk_ref, tab_ref, act_ref, hlow_ref,
-                total_ref, e_ref, dy_ref, dh_ref, ends_ref, send_ref, small_ref, half_keep, half_send, tile_ref, stat_tile, dz_ref, dylow_ref):
+                total_ref, e_ref, dy_ref, dh_ref, ends_ref, send_ref, small_ref, glu_keep, glu_send, out_keep, out_send,
+                tile_ref, stat_tile, dz_ref, dylow_ref):
     bias_sum, gain_sum = two_sums(stat_ref, stat_tile, z)
     grad = norm_grad(z, 1, bias_sum, gain_sum, norm1_ref, gain_ref)
     total_ref[0:1, :] = bias_sum
@@ -512,7 +513,8 @@
     s0, s1 = tiles(z, body, (zero, zero))
     descend(z, 0, jnp.concatenate([s0, s1], axis=1), dz_ref, slope_ref, v_ref, norm_ref, gain_ref, bias_ref, wglu_ref, wout_ref,
             keep_ref, chunk_ref, tab_ref, dy_ref, dylow_ref, dh_ref, ends_ref, send_ref, small_ref, tile_ref)
-    split_strips(z, half_keep, half_send, units(act_ref, dz_ref, half_keep) + units(hlow_ref, dylow_ref, half_keep))
+    split_strips(z, glu_keep, glu_send, units(act_ref, dz_ref, glu_keep))
+    split_strips(z, out_keep, out_send, units(hlow_ref, dylow_ref, out_keep))
 
 
 def units(a_ref, b_ref, like):
@@ -583,13 +585,14 @@
 
 
 GRAD_TILE = 64
-SEQ = (0, 2, 1)
+SEQ = (0, 2, 1, 3)
 FIRST = ()
 COST = 1
 FLOPS = 20000000000
+HINTED = ("halves", "join", "add", "total", "finish1", "lower_block", "finish0")
 TRANS = 0
-FLAT = (1, 1, 1)
-ORDERS = ((0, 1, 2, 3, 4), (0, 1, 2, 3, 4), (0, 1, 2, 3, 4))
+FLAT = (1, 1, 1, 1)
+ORDERS = ((0, 1, 2, 3, 4), (0, 1, 2, 3, 4), (0, 1, 2, 3, 4), (0, 3, 1, 2, 4))
 STRIP = 256
 
 
@@ -720,7 +723,12 @@
     def strips(out, b):
         return [out.at[b, :, i * w : (i + 1) * w] for i in range(out.shape[2] // w)]
 
-    outs = strips(win_out, 1) + strips(win_out, 0) if which == 2 else strips(wglu_out, 1 - which) + strips(wout_out, 1 - which)
+    outs = (
+        lambda: strips(wglu_out, 1) + strips(wout_out, 1),
+        lambda: strips(wglu_out, 0),
+        lambda: strips(win_out, 1) + strips(win_out, 0),
+        lambda: strips(wout_out, 0),
+    )[which]()
     cut = len(outs) // 2
 
     def place(low, high):
@@ -753,7 +761,7 @@
         out_specs=[pl.BlockSpec(memory_space=target)] * len(outs),
         scratch_shapes=shapes + ([pltpu.SemaphoreType.DMA((sems,))] if sems else []),
         compiler_params=pltpu.CompilerParams(vmem_limit_bytes=16 << 20),
-        cost_estimate=pl.CostEstimate(flops=FLOPS, bytes_accessed=COST, transcendentals=TRANS) if name in ("halves", "join", "add", "total") else None,
+        cost_estimate=pl.CostEstimate(flops=FLOPS, bytes_accessed=COST, transcendentals=TRANS) if name in HINTED else None,
         input_output_aliases={len(args) + i: i for i in range(len(onto))},
         name=name,
     )(*args, *onto)
@@ -824,26 +832,30 @@
     adj1 = swap(adj1, "tm")
     one.got, adj1 = tie(one.got, adj1)
     one.settle()
+    _, adj1 = tie(one.send, adj1)
     dxn1, dplow1, sum1, lam1 = run(
         bind(finish_upper, z), "finish1", [full, low_n, stat_shape, lam_shape],
         (adj1, dev_f, power, adj_ends1, chunk_f, dh1, keep_f, tab, proj1, h1, carry1, keep_r, dy1, v1, norm1, skip_gain, w_in),
         [tile, chunk, stat_tile])
-    one.send, sum1 = tie(one.send, sum1)
+    _, sum1 = tie(one.send, sum1)
     one.go()
     sum1 = swap(sum1, everyone)
     one.got, sum1 = tie(one.got, sum1)
     one.settle()
-    total1, e1, dy0, dh0, adj_ends0, adj0, small0, keepa, senda = run(
+    _, sum1 = tie(one.send, sum1)
+    total1, e1, dy0, dh0, adj_ends0, adj0, small0, keepa, senda, keepo, sendo = run(
         bind(lower_block, z), "lower_block",
-        [norm_shape, full, full, full_n, chunk, send_shape, small_shape, part(3), part(3)],
+        [norm_shape, full, full, full_n, chunk, send_shape, small_shape, part(2), part(2), part(1), part(1)],
         (sum1, dxn1, v1, norm1, gout, sig0, gate0, slope0, x, norm0, bn_gain, bn_bias, w_glu, w_out, keep_r, chunk_r, tab, act0, hlow0),
         [tile, stat_tile, wide_b, low])
     two = Exchange(z, keepa, senda, order=ORDERS[1], flat=FLAT[1])
-    one.send, two.send, adj0 = tie(one.send, two.send, adj0)
+    four = Exchange(z, keepo, sendo, order=ORDERS[3], flat=FLAT[3])
+    *_, adj0 = tie(one.send, two.send, four.send, adj0)
     one.go()
     two.go()
+    four.go()
     adj0 = swap(adj0, "tm")
-    one.got, two.got, adj0 = tie(one.got, two.got, adj0)
+    one.got, two.got, four.got, adj0 = tie(one.got, two.got, four.got, adj0)
     rows_sum = (2 * D + 2 * (3 * D + 2 * N)) // W
     z.extra = -(-rows_sum // 8) * 8
     last_part = part(2, z.extra)
@@ -854,11 +866,11 @@
         [low_n, lam_shape, tile, chunk])
     one.settle()
     two.settle()
+    four.settle()
     three = Exchange(z, keepb, sendb, z.extra, ORDERS[2], FLAT[2])
-    one.send, two.send, three.send = tie(one.send, two.send, three.send)
-    for e in (one, two, three):
+    for e in (one, two, four, three):
         e.go()
-    sets = (one, two, three)
+    sets = (one, two, three, four)
     ahead = three.send
     placed, done, queue = (), [], list(FIRST) if z.bits == 5 else []
     while len(done) < len(sets):

time: 175 us -> 167 us (0.954)
  waiting for transfers between devices: 58.9 us -> 41.5 us
  starting transfers between devices: 17.8 us -> 27.8 us
    ppermute x27 -> x36, waiting for transfers between devices: 58.9 us -> 41.5 us  [go(): lax.ppermute(self.send, ('tm', 'rows'), pairs(self.z, self.order[self.pla...]
    ppermute x27 -> x36, starting transfers between devices: 17.8 us -> 27.8 us  [go(): lax.ppermute(self.send, ('tm', 'rows'), pairs(self.z, self.order[self.pla...]
    pallas_call x36 -> x45, Pallas kernels: 21.5 us -> 22 us  [run(): pl.pallas_call(kernel, out_shape=[jax.ShapeDtypeStruct(s, t) for s, t in...]
  transfers between devices with their start and end apart: 27 -> 36, of which waited for: 15 -> 17; matrix products, arithmetic and copies ran while one was open for 0% -> 0% of each run, Pallas kernels for 4% -> 6%
where the time goes in v5:
time: 167 us
  blocking collectives  74 us (44%)
  waiting for transfers between devices  41.5 us (25%)
  starting transfers between devices  27.8 us (17%)
  Pallas kernels  22 us (13%)
    all_to_all x7, blocking collectives, swap(): return lax.all_to_all(a, axis, 0, 0)  74 us
    ppermute x36, waiting for transfers between devices, go(): lax.ppermute(self.send, ('tm', 'rows'), pairs(self.z, self.order[self.pla...  41.5 us
    ppermute x36, starting transfers between devices, go(): lax.ppermute(self.send, ('tm', 'rows'), pairs(self.z, self.order[self.pla...  27.8 us
    pallas_call x45, Pallas kernels, run(): pl.pallas_call(kernel, out_shape=[jax.ShapeDtypeStruct(s, t) for s, t in...  22 us
  transfers between devices with their start and end apart: 36, of which 17 were waited for; matrix products, arithmetic and copies ran while one was open for 0% of the time, Pallas kernels for 6%

profile of v5, /device:TPU:0, one launch (start us, length us, event | category | flops | bytes accessed | tf_op | source)
XLA Modules:
  0.0 166.6 jit_solution(2501060984595749466)
XLA Ops:
  0.6 2.6 %prepare.1 = (f32[256,512]{1,0:T(8,128)S(1)}, f32[256,512]{1,0:T(8,128)S(1)}, f32[32,8,128]{2,1,0:T(8,128)S(1)}, f32[256,128]{1,0:T(8,128)S(1)}, f32[256,128]{1,...) custom-call(s32[2,16]{1,0:T(2,128)} %len_hbm.1, ...), custom_call_target="tpu_custom_call" | custom-call | tf_op jit(solution)/shard_map/prepare/pallas_call | solution.py:757
  3.3 15.3 %all_to_all.35.stat_ref = f32[32,8,128]{2,1,0:T(8,128)S(1)} all-to-all(f32[32,8,128]{2,1,0:T(8,128)S(1)} %get-tuple-element.167), channel_id=1, replica_groups=mesh['tm'=8,'rows'=4] {'tm','rows'}, dimensions={0} | all-to-all | bytes 262144 | tf_op jit(solution)/shard_map/all_to_all | solution.py:777
  18.6 0.6 enter0.1
  19.2 9.2 %all_to_all.36.recv_ref = f32[8,8,128]{2,1,0:T(8,128)S(1)} all-to-all(f32[8,8,128]{2,1,0:T(8,128)S(1)} %get-tuple-element.175), channel_id=1, replica_groups=mesh['tm'=8,'rows'=4] {'tm'}, dimensions={0} | all-to-all | bytes 65536 | tf_op jit(solution)/shard_map/all_to_all | solution.py:777
  28.4 1.5 middle.1
  29.8 9.9 %all_to_all.37.stat_ref = f32[32,8,128]{2,1,0:T(8,128)S(1)} all-to-all(f32[32,8,128]{2,1,0:T(8,128)S(1)} %get-tuple-element.185), channel_id=1, replica_groups=mesh['tm'=8,'rows'=4] {'tm','rows'}, dimensions={0} | all-to-all | bytes 262144 | tf_op jit(solution)/shard_map/all_to_all | solution.py:777
  39.8 0.6 enter1.1
  40.4 9.1 %all_to_all.38.recv_ref = f32[8,8,128]{2,1,0:T(8,128)S(1)} all-to-all(f32[8,8,128]{2,1,0:T(8,128)S(1)} %get-tuple-element.189), channel_id=1, replica_groups=mesh['tm'=8,'rows'=4] {'tm'}, dimensions={0} | all-to-all | bytes 65536 | tf_op jit(solution)/shard_map/all_to_all | solution.py:777
  49.5 3.3 %turn.1 = (f32[256,512]{1,0:T(8,128)S(1)}, f32[16,512]{1,0:T(8,128)S(1)}, f32[256,512]{1,0:T(8,128)S(1)}, f32[256,512]{1,0:T(8,128)S(1)}, f32[256,512]{1,0:T(8,1...) custom-call(f32[8,8,128]{2,1,0:T(8,128)S(1)} %all_to_all.38.recv_ref, ...), custom_call_target="tpu_custom_call" | custom-call | tf_op jit(solution)/shard_map/turn/pallas_call | solution.py:757
  52.9 9.1 %all_to_all.39.refs_0_ = f32[8,8,128]{2,1,0:T(8,128)S(1)} all-to-all(f32[8,8,128]{2,1,0:T(8,128)S(1)} %get-tuple-element.199), channel_id=1, replica_groups=mesh['tm'=8,'rows'=4] {'tm'}, dimensions={0} | all-to-all | bytes 65536 | tf_op jit(solution)/shard_map/all_to_all | solution.py:777
  62.0 0.2 halves.12
  62.2 0.5 collective-permute-start.1
  62.7 0.7 finish1.1
  63.5 12.4 %all_to_all.40.stat_ref = f32[32,8,128]{2,1,0:T(8,128)S(1)} all-to-all(f32[32,8,128]{2,1,0:T(8,128)S(1)} %get-tuple-element.211), channel_id=1, replica_groups=mesh['tm'=8,'rows'=4] {'tm','rows'}, dimensions={0} | all-to-all | bytes 262144 | tf_op jit(solution)/shard_map/all_to_all | solution.py:777
  75.9 2.3 %lower_block.1 = (f32[8,512]{1,0:T(8,128)S(1)}, f32[256,512]{1,0:T(8,128)S(1)}, f32[256,512]{1,0:T(8,128)S(1)}, f32[256,512]{1,0:T(8,128)S(1)}, f32[16,512]{1,0:...) custom-call(f32[32,8,128]{2,1,0:T(8,128)S(1)} %all_to_all.40.stat_re, ...), custom_call_target="tpu_custom_call" | custom-call | flops 20000000000 | bytes 1 | tf_op jit(solution)/shard_map/lower_block/pallas_call | solution.py:757
  78.3 0.5 collective-permute-start.4
  78.8 1.2 collective-permute-start.2
  80.0 9.0 %all_to_all.41.refs_0_ = f32[8,8,128]{2,1,0:T(8,128)S(1)} all-to-all(f32[8,8,128]{2,1,0:T(8,128)S(1)} %get-tuple-element.225), channel_id=1, replica_groups=mesh['tm'=8,'rows'=4] {'tm'}, dimensions={0} | all-to-all | bytes 65536 | tf_op jit(solution)/shard_map/all_to_all | solution.py:777
  89.2 0.5 collective-permute-start.10
  89.8 0.8 collective-permute-start.6
  90.6 1.4 finish0.1
  92.2 1.4 collective-permute-start.9
  93.6 2.1 %collective-permute-done.6.recv_ref = f32[192,256]{1,0:T(8,128)S(1)} collective-permute-done((f32[192,256]{1,0:T(8,128)S(1)}, f32[192,256]{1,0:T(8,128)S(1)}, u32[]{:S(2)}, u32[]{:S(2)}) %collective-permute-start.6) | collective-permute-done | bytes 196640 | tf_op jit(solution)/shard_map/ppermute | solution.py:694
  95.7 0.5 collective-permute-start.8
  96.4 1.8 %collective-permute-start.7 = (f32[536,256]{1,0:T(8,128)S(1)}, f32[536,256]{1,0:T(8,128)S(1)}, u32[]{:S(2)}, u32[]{:S(2)}) collective-permute-start(f32[536,256]{1,0:T(8,128)S(1)} %get-tuple-element.247), channel_id=1, source_target_pairs={{0,4},{1,3},{2,6},{3,1},{4,0},{5,7},{6,2},{7,5},{8,12},{9,11},{10,... | collective-permute-start | bytes 1646600 | tf_op jit(solution)/shard_map/ppermute | solution.py:694
  98.2 0.3 collective-permute-done.10.recv_ref
  98.6 0.9 collective-permute-start.14
  99.4 4.8 %collective-permute-done.9.recv_ref = f32[256,256]{1,0:T(8,128)S(1)} collective-permute-done((f32[256,256]{1,0:T(8,128)S(1)}, f32[256,256]{1,0:T(8,128)S(1)}, u32[]{:S(2)}, u32[]{:S(2)}) %collective-permute-start.9) | collective-permute-done | bytes 262176 | tf_op jit(solution)/shard_map/ppermute | solution.py:694
  104.3 1.3 collective-permute-start.13
  105.6 1.0 collective-permute-done.8.recv_ref
  106.7 0.5 collective-permute-done.7.recv_ref
  107.3 1.2 collective-permute-start.11
  108.5 1.4 collective-permute-start.18
  109.9 0.5 collective-permute-done.13.recv_ref
  110.5 0.9 collective-permute-start.17
  111.3 2.4 %collective-permute-done.12.recv_ref = f32[192,256]{1,0:T(8,128)S(1)} collective-permute-done((f32[192,256]{1,0:T(8,128)S(1)}, f32[192,256]{1,0:T(8,128)S(1)}, u32[]{:S(2)}, u32[]{:S(2)}) %collective-permute-start.12) | collective-permute-done | bytes 196640 | tf_op jit(solution)/shard_map/ppermute | solution.py:694
  113.8 0.9 collective-permute-start.16
  114.7 0.9 collective-permute-start.15
  115.6 1.5 collective-permute-start.22
  117.2 1.5 collective-permute-start.21
  118.7 4.6 %collective-permute-done.16.recv_ref = f32[384,256]{1,0:T(8,128)S(1)} collective-permute-done((f32[384,256]{1,0:T(8,128)S(1)}, f32[384,256]{1,0:T(8,128)S(1)}, u32[]{:S(2)}, u32[]{:S(2)}) %collective-permute-start.16) | collective-permute-done | bytes 393248 | tf_op jit(solution)/shard_map/ppermute | solution.py:694
  123.5 2.0 %collective-permute-start.19 = (f32[152,256]{1,0:T(8,128)S(1)}, f32[152,256]{1,0:T(8,128)S(1)}, u32[]{:S(2)}, u32[]{:S(2)}) collective-permute-start(f32[152,256]{1,0:T(8,128)S(1)} %add.11.keep_ref), channel_id=1, source_target_pairs={{0,16},{1,17},{2,18},{3,19},{4,20},{5,21},{6,22},{7,23},{8,24},{9,... | collective-permute-start | bytes 466952 | tf_op jit(solution)/shard_map/ppermute | solution.py:694
  125.5 1.6 collective-permute-done.22.recv_ref
  127.2 3.0 %collective-permute-done.21.recv_ref = f32[64,256]{1,0:T(8,128)S(1)} collective-permute-done((f32[64,256]{1,0:T(8,128)S(1)}, f32[64,256]{1,0:T(8,128)S(1)}, u32[]{:S(2)}, u32[]{:S(2)}) %collective-permute-start.21) | collective-permute-done | bytes 65568 | tf_op jit(solution)/shard_map/ppermute | solution.py:694
  130.2 0.8 collective-permute-start.25
  131.0 5.2 %collective-permute-done.20.recv_ref = f32[768,256]{1,0:T(8,128)S(1)} collective-permute-done((f32[768,256]{1,0:T(8,128)S(1)}, f32[768,256]{1,0:T(8,128)S(1)}, u32[]{:S(2)}, u32[]{:S(2)}) %collective-permute-start.20) | collective-permute-done | bytes 786464 | tf_op jit(solution)/shard_map/ppermute | solution.py:694
  136.5 0.9 collective-permute-start.29
  137.5 0.7 collective-permute-start.28
  138.2 1.6 collective-permute-done.24.refs_1_
  139.8 1.7 %assemble.4 = (f32[2,512,512]{2,1,0:T(8,128)}, f32[2,512,512]{2,1,0:T(8,128)}, f32[2,512,1024]{2,1,0:T(8,128)}) custom-call(f32[1536,256]{1,0:T(8,128)S(1)} %join.14.refs_0_, f32[1536,256]{1,0:T(8,128)S(1)} %collective-permute-done.24.refs_1_), custom_call_target="tpu_custom_call" | custom-call | tf_op jit(solution)/shard_map/assemble/pallas_call | solution.py:757
  141.5 0.9 collective-permute-done.23.recv_ref
  142.4 0.9 collective-permute-start.27
  143.3 0.8 collective-permute-done.29.recv_ref
  144.1 0.4 collective-permute-start.32
  144.5 2.0 %collective-permute-start.31 = (f32[256,256]{1,0:T(8,128)S(1)}, f32[256,256]{1,0:T(8,128)S(1)}, u32[]{:S(2)}, u32[]{:S(2)}) collective-permute-start(f32[256,256]{1,0:T(8,128)S(1)} %join.19.own_ref), channel_id=1, source_target_pairs={{0,8},{1,9},{2,10},{3,11},{4,12},{5,13},{6,14},{7,15},{8,0},{9,1},... | collective-permute-start | bytes 786440 | tf_op jit(solution)/shard_map/ppermute | solution.py:694
  146.6 4.4 %collective-permute-done.27.recv_ref = f32[256,256]{1,0:T(8,128)S(1)} collective-permute-done((f32[256,256]{1,0:T(8,128)S(1)}, f32[256,256]{1,0:T(8,128)S(1)}, u32[]{:S(2)}, u32[]{:S(2)}) %collective-permute-start.27) | collective-permute-done | bytes 262176 | tf_op jit(solution)/shard_map/ppermute | solution.py:694
  151.2 2.1 %collective-permute-done.32.recv_ref = f32[512,256]{1,0:T(8,128)S(1)} collective-permute-done((f32[512,256]{1,0:T(8,128)S(1)}, f32[512,256]{1,0:T(8,128)S(1)}, u32[]{:S(2)}, u32[]{:S(2)}) %collective-permute-start.32) | collective-permute-done | bytes 524320 | tf_op jit(solution)/shard_map/ppermute | solution.py:694
  153.4 1.0 collective-permute-start.35
  154.5 5.8 %collective-permute-done.30.recv_ref = f32[512,256]{1,0:T(8,128)S(1)} collective-permute-done((f32[512,256]{1,0:T(8,128)S(1)}, f32[512,256]{1,0:T(8,128)S(1)}, u32[]{:S(2)}, u32[]{:S(2)}) %collective-permute-start.30) | collective-permute-done | bytes 524320 | tf_op jit(solution)/shard_map/ppermute | solution.py:694
  160.5 0.5 collective-permute-start.34
  161.0 1.5 last.1
  162.5 1.4 assemble.5
  163.9 1.1 assemble.6
  165.0 1.4 assemble.7
  (60 shorter events, 2.5 us)
Async XLA Ops:
  52.8 9.1 %collective-permute-start = (f32[1536,256]{1,0:T(8,128)S(1)}, f32[1536,256]{1,0:T(8,128)S(1)}, u32[]{:S(2)}, u32[]{:S(2)}) collective-permute-start(f32[1536,256]{1,0:T(8,128)S(1)} %get-tuple-element.198), channel_id=1, source_target_pairs={{0,1},{1,0},{2,3},{3,2},{4,5},{5,4},{6,7},{7,6},{8,9},{9,8},{10,11... | collective-permute-start | bytes 4718600 | tf_op jit(solution)/shard_map/ppermute | solution.py:694
  62.2 13.6 %collective-permute-start.1 = (f32[768,256]{1,0:T(8,128)S(1)}, f32[768,256]{1,0:T(8,128)S(1)}, u32[]{:S(2)}, u32[]{:S(2)}) collective-permute-start(f32[768,256]{1,0:T(8,128)S(1)} %get-tuple-element.202), channel_id=1, source_target_pairs={{0,4},{1,3},{2,6},{3,1},{4,0},{5,7},{6,2},{7,5},{8,12},{9,11},{10,... | collective-permute-start | bytes 2359304 | tf_op jit(solution)/shard_map/ppermute | solution.py:694
  78.2 10.9 %collective-permute-start.3 = (f32[1024,256]{1,0:T(8,128)S(1)}, f32[1024,256]{1,0:T(8,128)S(1)}, u32[]{:S(2)}, u32[]{:S(2)}) collective-permute-start(f32[1024,256]{1,0:T(8,128)S(1)} %get-tuple-element.222), channel_id=1, source_target_pairs={{0,1},{1,0},{2,3},{3,2},{4,5},{5,4},{6,7},{7,6},{8,9},{9,8},{10,11... | collective-permute-start | bytes 3145736 | tf_op jit(solution)/shard_map/ppermute | solution.py:694
  78.3 10.8 %collective-permute-start.4 = (f32[512,256]{1,0:T(8,128)S(1)}, f32[512,256]{1,0:T(8,128)S(1)}, u32[]{:S(2)}, u32[]{:S(2)}) collective-permute-start(f32[512,256]{1,0:T(8,128)S(1)} %get-tuple-element.223), channel_id=1, source_target_pairs={{0,1},{1,0},{2,3},{3,2},{4,5},{5,4},{6,7},{7,6},{8,9},{9,8},{10,11... | collective-permute-start | bytes 1572872 | tf_op jit(solution)/shard_map/ppermute | solution.py:694
  78.8 10.3 %collective-permute-start.2 = (f32[384,256]{1,0:T(8,128)S(1)}, f32[384,256]{1,0:T(8,128)S(1)}, u32[]{:S(2)}, u32[]{:S(2)}) collective-permute-start(f32[384,256]{1,0:T(8,128)S(1)} %get-tuple-element.213), channel_id=1, source_target_pairs={{0,2},{1,5},{2,0},{3,7},{4,6},{5,1},{6,4},{7,3},{8,10},{9,13},{10,... | collective-permute-start | bytes 1179656 | tf_op jit(solution)/shard_map/ppermute | solution.py:694
  89.2 9.2 %collective-permute-start.10 = (f32[512,256]{1,0:T(8,128)S(1)}, f32[512,256]{1,0:T(8,128)S(1)}, u32[]{:S(2)}, u32[]{:S(2)}) collective-permute-start(f32[512,256]{1,0:T(8,128)S(1)} %get-tuple-element.255), channel_id=1, source_target_pairs={{0,4},{1,3},{2,6},{3,1},{4,0},{5,7},{6,2},{7,5},{8,12},{9,11},{10,... | collective-permute-start | bytes 1572872 | tf_op jit(solution)/shard_map/ppermute | solution.py:694
  89.8 5.9 %collective-permute-start.6 = (f32[192,256]{1,0:T(8,128)S(1)}, f32[192,256]{1,0:T(8,128)S(1)}, u32[]{:S(2)}, u32[]{:S(2)}) collective-permute-start(f32[192,256]{1,0:T(8,128)S(1)} %get-tuple-element.243), channel_id=1, source_target_pairs={{0,8},{1,9},{2,10},{3,11},{4,12},{5,13},{6,14},{7,15},{8,0},{9,1},... | collective-permute-start | bytes 589832 | tf_op jit(solution)/shard_map/ppermute | solution.py:694
  92.0 4.2 %collective-permute-start.5 = (f32[1048,256]{1,0:T(8,128)S(1)}, f32[1048,256]{1,0:T(8,128)S(1)}, u32[]{:S(2)}, u32[]{:S(2)}) collective-permute-start(f32[1048,256]{1,0:T(8,128)S(1)} %get-tuple-element.239), channel_id=1, source_target_pairs={{0,1},{1,0},{2,3},{3,2},{4,5},{5,4},{6,7},{7,6},{8,9},{9,8},{10,11... | collective-permute-start | bytes 3219464 | tf_op jit(solution)/shard_map/ppermute | solution.py:694
  92.2 12.0 %collective-permute-start.9 = (f32[256,256]{1,0:T(8,128)S(1)}, f32[256,256]{1,0:T(8,128)S(1)}, u32[]{:S(2)}, u32[]{:S(2)}) collective-permute-start(f32[256,256]{1,0:T(8,128)S(1)} %get-tuple-element.251), channel_id=1, source_target_pairs={{0,8},{1,9},{2,10},{3,11},{4,12},{5,13},{6,14},{7,15},{8,0},{9,1},... | collective-permute-start | bytes 786440 | tf_op jit(solution)/shard_map/ppermute | solution.py:694
  95.7 10.8 %collective-permute-start.8 = (f32[192,256]{1,0:T(8,128)S(1)}, f32[192,256]{1,0:T(8,128)S(1)}, u32[]{:S(2)}, u32[]{:S(2)}) collective-permute-start(f32[192,256]{1,0:T(8,128)S(1)} %add.7.keep_ref), channel_id=1, source_target_pairs={{0,16},{1,17},{2,18},{3,19},{4,20},{5,21},{6,22},{7,23},{8,24},{9,... | collective-permute-start | bytes 589832 | tf_op jit(solution)/shard_map/ppermute | solution.py:694
  96.4 10.8 %collective-permute-start.7 = (f32[536,256]{1,0:T(8,128)S(1)}, f32[536,256]{1,0:T(8,128)S(1)}, u32[]{:S(2)}, u32[]{:S(2)}) collective-permute-start(f32[536,256]{1,0:T(8,128)S(1)} %get-tuple-element.247), channel_id=1, source_target_pairs={{0,4},{1,3},{2,6},{3,1},{4,0},{5,7},{6,2},{7,5},{8,12},{9,11},{10,... | collective-permute-start | bytes 1646600 | tf_op jit(solution)/shard_map/ppermute | solution.py:694
  98.6 9.9 %collective-permute-start.14 = (f32[256,256]{1,0:T(8,128)S(1)}, f32[256,256]{1,0:T(8,128)S(1)}, u32[]{:S(2)}, u32[]{:S(2)}) collective-permute-start(f32[256,256]{1,0:T(8,128)S(1)} %get-tuple-element.257), channel_id=1, source_target_pairs={{0,2},{1,5},{2,0},{3,7},{4,6},{5,1},{6,4},{7,3},{8,10},{9,13},{10,... | collective-permute-start | bytes 786440 | tf_op jit(solution)/shard_map/ppermute | solution.py:694
  104.3 6.1 %collective-permute-start.13 = (f32[128,256]{1,0:T(8,128)S(1)}, f32[128,256]{1,0:T(8,128)S(1)}, u32[]{:S(2)}, u32[]{:S(2)}) collective-permute-start(f32[128,256]{1,0:T(8,128)S(1)} %get-tuple-element.259), channel_id=1, source_target_pairs={{0,4},{1,3},{2,6},{3,1},{4,0},{5,7},{6,2},{7,5},{8,12},{9,11},{10,... | collective-permute-start | bytes 393224 | tf_op jit(solution)/shard_map/ppermute | solution.py:694
  106.6 7.1 %collective-permute-start.12 = (f32[192,256]{1,0:T(8,128)S(1)}, f32[192,256]{1,0:T(8,128)S(1)}, u32[]{:S(2)}, u32[]{:S(2)}) collective-permute-start(f32[192,256]{1,0:T(8,128)S(1)} %add.8.own_ref), channel_id=1, source_target_pairs={{0,8},{1,9},{2,10},{3,11},{4,12},{5,13},{6,14},{7,15},{8,0},{9,1},... | collective-permute-start | bytes 589832 | tf_op jit(solution)/shard_map/ppermute | solution.py:694
  107.3 7.4 %collective-permute-start.11 = (f32[280,256]{1,0:T(8,128)S(1)}, f32[280,256]{1,0:T(8,128)S(1)}, u32[]{:S(2)}, u32[]{:S(2)}) collective-permute-start(f32[280,256]{1,0:T(8,128)S(1)} %get-tuple-element.263), channel_id=1, source_target_pairs={{0,2},{1,5},{2,0},{3,7},{4,6},{5,1},{6,4},{7,3},{8,10},{9,13},{10,... | collective-permute-start | bytes 860168 | tf_op jit(solution)/shard_map/ppermute | solution.py:694
  108.5 7.1 %collective-permute-start.18 = (f32[128,256]{1,0:T(8,128)S(1)}, f32[128,256]{1,0:T(8,128)S(1)}, u32[]{:S(2)}, u32[]{:S(2)}) collective-permute-start(f32[128,256]{1,0:T(8,128)S(1)} %get-tuple-element.267), channel_id=1, source_target_pairs={{0,8},{1,9},{2,10},{3,11},{4,12},{5,13},{6,14},{7,15},{8,0},{9,1},... | collective-permute-start | bytes 393224 | tf_op jit(solution)/shard_map/ppermute | solution.py:694
  110.5 6.7 %collective-permute-start.17 = (f32[64,256]{1,0:T(8,128)S(1)}, f32[64,256]{1,0:T(8,128)S(1)}, u32[]{:S(2)}, u32[]{:S(2)}) collective-permute-start(f32[64,256]{1,0:T(8,128)S(1)} %get-tuple-element.269), channel_id=1, source_target_pairs={{0,2},{1,5},{2,0},{3,7},{4,6},{5,1},{6,4},{7,3},{8,10},{9,13},{10,... | collective-permute-start | bytes 196616 | tf_op jit(solution)/shard_map/ppermute | solution.py:694
  113.8 9.5 %collective-permute-start.16 = (f32[384,256]{1,0:T(8,128)S(1)}, f32[384,256]{1,0:T(8,128)S(1)}, u32[]{:S(2)}, u32[]{:S(2)}) collective-permute-start(f32[384,256]{1,0:T(8,128)S(1)} %join.12.own_ref), channel_id=1, source_target_pairs={{0,2},{1,5},{2,0},{3,7},{4,6},{5,1},{6,4},{7,3},{8,10},{9,13},{10,... | collective-permute-start | bytes 1179656 | tf_op jit(solution)/shard_map/ppermute | solution.py:694
  114.7 8.8 %collective-permute-start.15 = (f32[152,256]{1,0:T(8,128)S(1)}, f32[152,256]{1,0:T(8,128)S(1)}, u32[]{:S(2)}, u32[]{:S(2)}) collective-permute-start(f32[152,256]{1,0:T(8,128)S(1)} %get-tuple-element.273), channel_id=1, source_target_pairs={{0,8},{1,9},{2,10},{3,11},{4,12},{5,13},{6,14},{7,15},{8,0},{9,1},... | collective-permute-start | bytes 466952 | tf_op jit(solution)/shard_map/ppermute | solution.py:694
  115.6 11.5 %collective-permute-start.22 = (f32[128,256]{1,0:T(8,128)S(1)}, f32[128,256]{1,0:T(8,128)S(1)}, u32[]{:S(2)}, u32[]{:S(2)}) collective-permute-start(f32[128,256]{1,0:T(8,128)S(1)} %add.9.keep_ref), channel_id=1, source_target_pairs={{0,16},{1,17},{2,18},{3,19},{4,20},{5,21},{6,22},{7,23},{8,24},{9,... | collective-permute-start | bytes 393224 | tf_op jit(solution)/shard_map/ppermute | solution.py:694
  117.2 13.0 %collective-permute-start.21 = (f32[64,256]{1,0:T(8,128)S(1)}, f32[64,256]{1,0:T(8,128)S(1)}, u32[]{:S(2)}, u32[]{:S(2)}) collective-permute-start(f32[64,256]{1,0:T(8,128)S(1)} %add.10.keep_ref), channel_id=1, source_target_pairs={{0,16},{1,17},{2,18},{3,19},{4,20},{5,21},{6,22},{7,23},{8,24},{9,... | collective-permute-start | bytes 196616 | tf_op jit(solution)/shard_map/ppermute | solution.py:694
  123.4 12.8 %collective-permute-start.20 = (f32[768,256]{1,0:T(8,128)S(1)}, f32[768,256]{1,0:T(8,128)S(1)}, u32[]{:S(2)}, u32[]{:S(2)}) collective-permute-start(f32[768,256]{1,0:T(8,128)S(1)} %join.13.own_ref), channel_id=1, source_target_pairs={{0,4},{1,3},{2,6},{3,1},{4,0},{5,7},{6,2},{7,5},{8,12},{9,11},{10,... | collective-permute-start | bytes 2359304 | tf_op jit(solution)/shard_map/ppermute | solution.py:694
  123.5 12.9 %collective-permute-start.19 = (f32[152,256]{1,0:T(8,128)S(1)}, f32[152,256]{1,0:T(8,128)S(1)}, u32[]{:S(2)}, u32[]{:S(2)}) collective-permute-start(f32[152,256]{1,0:T(8,128)S(1)} %add.11.keep_ref), channel_id=1, source_target_pairs={{0,16},{1,17},{2,18},{3,19},{4,20},{5,21},{6,22},{7,23},{8,24},{9,... | collective-permute-start | bytes 466952 | tf_op jit(solution)/shard_map/ppermute | solution.py:694
  127.1 9.3 %collective-permute-start.26 = (f32[128,256]{1,0:T(8,128)S(1)}, f32[128,256]{1,0:T(8,128)S(1)}, u32[]{:S(2)}, u32[]{:S(2)}) collective-permute-start(f32[128,256]{1,0:T(8,128)S(1)} %add.12.own_ref), channel_id=1, source_target_pairs={{0,8},{1,9},{2,10},{3,11},{4,12},{5,13},{6,14},{7,15},{8,0},{9,1},... | collective-permute-start | bytes 393224 | tf_op jit(solution)/shard_map/ppermute | solution.py:694
  130.2 7.2 %collective-permute-start.25 = (f32[64,256]{1,0:T(8,128)S(1)}, f32[64,256]{1,0:T(8,128)S(1)}, u32[]{:S(2)}, u32[]{:S(2)}) collective-permute-start(f32[64,256]{1,0:T(8,128)S(1)} %add.13.own_ref), channel_id=1, source_target_pairs={{0,2},{1,5},{2,0},{3,7},{4,6},{5,1},{6,4},{7,3},{8,10},{9,13},{10,... | collective-permute-start | bytes 196616 | tf_op jit(solution)/shard_map/ppermute | solution.py:694
  136.3 3.5 %collective-permute-start.24 = (f32[1536,256]{1,0:T(8,128)S(1)}, f32[1536,256]{1,0:T(8,128)S(1)}, u32[]{:S(2)}, u32[]{:S(2)}) collective-permute-start(f32[1536,256]{1,0:T(8,128)S(1)} %join.14.refs_0_), channel_id=1, source_target_pairs={{0,1},{1,0},{2,3},{3,2},{4,5},{5,4},{6,7},{7,6},{8,9},{9,8},{10,11... | collective-permute-start | bytes 4718600 | tf_op jit(solution)/shard_map/ppermute | solution.py:694
  136.4 6.0 %collective-permute-start.23 = (f32[128,256]{1,0:T(8,128)S(1)}, f32[128,256]{1,0:T(8,128)S(1)}, u32[]{:S(2)}, u32[]{:S(2)}) collective-permute-start(f32[128,256]{1,0:T(8,128)S(1)} %get-tuple-element.293.own_ref), channel_id=1, source_target_pairs={{0,8},{1,9},{2,10},{3,11},{4,12},{5,13},{6,14},{7,15},{8,0},{9,1},... | collective-permute-start | bytes 393224 | tf_op jit(solution)/shard_map/ppermute | solution.py:694
  136.5 7.5 %collective-permute-start.29 = (f32[256,256]{1,0:T(8,128)S(1)}, f32[256,256]{1,0:T(8,128)S(1)}, u32[]{:S(2)}, u32[]{:S(2)}) collective-permute-start(f32[256,256]{1,0:T(8,128)S(1)} %join.15.own_ref), channel_id=1, source_target_pairs={{0,2},{1,5},{2,0},{3,7},{4,6},{5,1},{6,4},{7,3},{8,10},{9,13},{10,... | collective-permute-start | bytes 786440 | tf_op jit(solution)/shard_map/ppermute | solution.py:694
  137.5 7.0 %collective-permute-start.28 = (f32[128,256]{1,0:T(8,128)S(1)}, f32[128,256]{1,0:T(8,128)S(1)}, u32[]{:S(2)}, u32[]{:S(2)}) collective-permute-start(f32[128,256]{1,0:T(8,128)S(1)} %join.16.own_ref), channel_id=1, source_target_pairs={{0,4},{1,3},{2,6},{3,1},{4,0},{5,7},{6,2},{7,5},{8,12},{9,11},{10,... | collective-permute-start | bytes 393224 | tf_op jit(solution)/shard_map/ppermute | solution.py:694
  142.4 8.6 %collective-permute-start.27 = (f32[256,256]{1,0:T(8,128)S(1)}, f32[256,256]{1,0:T(8,128)S(1)}, u32[]{:S(2)}, u32[]{:S(2)}) collective-permute-start(f32[256,256]{1,0:T(8,128)S(1)} %join.17.own_ref), channel_id=1, source_target_pairs={{0,2},{1,5},{2,0},{3,7},{4,6},{5,1},{6,4},{7,3},{8,10},{9,13},{10,... | collective-permute-start | bytes 786440 | tf_op jit(solution)/shard_map/ppermute | solution.py:694
  144.1 9.2 %collective-permute-start.32 = (f32[512,256]{1,0:T(8,128)S(1)}, f32[512,256]{1,0:T(8,128)S(1)}, u32[]{:S(2)}, u32[]{:S(2)}) collective-permute-start(f32[512,256]{1,0:T(8,128)S(1)} %join.18.own_ref), channel_id=1, source_target_pairs={{0,4},{1,3},{2,6},{3,1},{4,0},{5,7},{6,2},{7,5},{8,12},{9,11},{10,... | collective-permute-start | bytes 1572872 | tf_op jit(solution)/shard_map/ppermute | solution.py:694
  144.5 9.9 %collective-permute-start.31 = (f32[256,256]{1,0:T(8,128)S(1)}, f32[256,256]{1,0:T(8,128)S(1)}, u32[]{:S(2)}, u32[]{:S(2)}) collective-permute-start(f32[256,256]{1,0:T(8,128)S(1)} %join.19.own_ref), channel_id=1, source_target_pairs={{0,8},{1,9},{2,10},{3,11},{4,12},{5,13},{6,14},{7,15},{8,0},{9,1},... | collective-permute-start | bytes 786440 | tf_op jit(solution)/shard_map/ppermute | solution.py:694
  151.1 9.2 %collective-permute-start.30 = (f32[512,256]{1,0:T(8,128)S(1)}, f32[512,256]{1,0:T(8,128)S(1)}, u32[]{:S(2)}, u32[]{:S(2)}) collective-permute-start(f32[512,256]{1,0:T(8,128)S(1)} %join.20.own_ref), channel_id=1, source_target_pairs={{0,4},{1,3},{2,6},{3,1},{4,0},{5,7},{6,2},{7,5},{8,12},{9,11},{10,... | collective-permute-start | bytes 1572872 | tf_op jit(solution)/shard_map/ppermute | solution.py:694
  153.4 9.1 %collective-permute-start.35 = (f32[1024,256]{1,0:T(8,128)S(1)}, f32[1024,256]{1,0:T(8,128)S(1)}, u32[]{:S(2)}, u32[]{:S(2)}) collective-permute-start(f32[1024,256]{1,0:T(8,128)S(1)} %join.21.refs_0_), channel_id=1, source_target_pairs={{0,1},{1,0},{2,3},{3,2},{4,5},{5,4},{6,7},{7,6},{8,9},{9,8},{10,11... | collective-permute-start | bytes 3145736 | tf_op jit(solution)/shard_map/ppermute | solution.py:694
  160.4 4.6 %collective-permute-start.33 = (f32[1024,256]{1,0:T(8,128)S(1)}, f32[1024,256]{1,0:T(8,128)S(1)}, u32[]{:S(2)}, u32[]{:S(2)}) collective-permute-start(f32[1024,256]{1,0:T(8,128)S(1)} %join.23.refs_0_), channel_id=1, source_target_pairs={{0,1},{1,0},{2,3},{3,2},{4,5},{5,4},{6,7},{7,6},{8,9},{9,8},{10,11... | collective-permute-start | bytes 3145736 | tf_op jit(solution)/shard_map/ppermute | solution.py:694
  160.5 3.4 %collective-permute-start.34 = (f32[512,256]{1,0:T(8,128)S(1)}, f32[512,256]{1,0:T(8,128)S(1)}, u32[]{:S(2)}, u32[]{:S(2)}) collective-permute-start(f32[512,256]{1,0:T(8,128)S(1)} %join.22.refs_0_), channel_id=1, source_target_pairs={{0,1},{1,0},{2,3},{3,2},{4,5},{5,4},{6,7},{7,6},{8,9},{9,8},{10,11... | collective-permute-start | bytes 1572872 | tf_op jit(solution)/shard_map/ppermute | solution.py:694

commit v6 on v5

--- a/solution.py
+++ b/solution.py
@@ -527,18 +527,19 @@
 
 
 def finish_upper(z, *refs):
-    ins, outs = refs[:17], refs[17:]
-    dxn_ref, dplow_ref, stat_ref, lam_ref, tile_ref, carry_ref, stat_tile = outs
+    ins, low_ref, outs = refs[:17], refs[17], refs[18:]
+    dxn_ref, stat_ref, lam_ref, keep_ref, send_ref, dplow_ref, tile_ref, carry_ref, stat_tile = outs
 
     def emit(bias_sum, gain_sum):
         pack(stat_tile, [bias_sum, gain_sum])
         spread(stat_ref, stat_tile)
 
     finish(z, 1, *ins, emit, dplow_ref, dxn_ref, lam_ref, tile_ref, carry_ref)
+    split_strips(z, keep_ref, send_ref, units(low_ref, dplow_ref, keep_ref))
 
 
 def finish_lower(z, *refs):
-    ins, (low_ref, low1_ref, dplow1_ref, small0_ref, small1_ref, lam1_ref), outs = refs[:17], refs[17:23], refs[23:]
+    ins, (low_ref, small0_ref, small1_ref, lam1_ref), outs = refs[:17], refs[17:21], refs[21:]
     dxn_ref, keep_ref, send_ref, dplow_ref, lam_ref, tile_ref, carry_ref = outs
     first = keep_ref.shape[0] - z.extra
 
@@ -552,7 +553,7 @@
                 ref[k:, :] = jnp.zeros((ref.shape[0] - k, ref.shape[1]), F32)
 
     finish(z, 0, *ins, emit, dplow_ref, dxn_ref, lam_ref, tile_ref, carry_ref)
-    split_strips(z, keep_ref, send_ref, units(low1_ref, dplow1_ref, keep_ref) + units(low_ref, dplow_ref, keep_ref))
+    split_strips(z, keep_ref, send_ref, units(low_ref, dplow_ref, keep_ref))
 
 
 def last(z, small_ref, dxn_ref, v_ref, norm_ref, gain_ref, e_ref, total1_ref, final_ref, out_ref, grad_ref, gain_out, bias_out, rate_out, phase_out, skip_out,
@@ -585,14 +586,13 @@
 
 
 GRAD_TILE = 64
-SEQ = (0, 2, 1, 3)
+SEQ = (0, 2, 4, 1, 3)
 FIRST = ()
-COST = 1
 FLOPS = 20000000000
-HINTED = ("halves", "join", "add", "total", "finish1", "lower_block", "finish0")
-TRANS = 0
-FLAT = (1, 1, 1, 1)
-ORDERS = ((0, 1, 2, 3, 4), (0, 1, 2, 3, 4), (0, 1, 2, 3, 4), (0, 3, 1, 2, 4))
+HINTED = ("halves", "join", "add", "total", "finish1", "lower_block", "finish0", "last")
+WAIT = 3
+FLAT = (1, 1, 1, 2, 1)
+ORDERS = ((0, 1, 2, 3, 4), (0, 1, 2, 3, 4), (0, 1, 2, 3, 4), (0, 3, 1, 2, 4), (0, 3, 1, 2, 4))
 STRIP = 256
 
 
@@ -726,8 +726,9 @@
     outs = (
         lambda: strips(wglu_out, 1) + strips(wout_out, 1),
         lambda: strips(wglu_out, 0),
-        lambda: strips(win_out, 1) + strips(win_out, 0),
+        lambda: strips(win_out, 0),
         lambda: strips(wout_out, 0),
+        lambda: strips(win_out, 1),
     )[which]()
     cut = len(outs) // 2
 
@@ -761,7 +762,7 @@
         out_specs=[pl.BlockSpec(memory_space=target)] * len(outs),
         scratch_shapes=shapes + ([pltpu.SemaphoreType.DMA((sems,))] if sems else []),
         compiler_params=pltpu.CompilerParams(vmem_limit_bytes=16 << 20),
-        cost_estimate=pl.CostEstimate(flops=FLOPS, bytes_accessed=COST, transcendentals=TRANS) if name in HINTED else None,
+        cost_estimate=pl.CostEstimate(flops=FLOPS, bytes_accessed=1, transcendentals=0) if name in HINTED else None,
         input_output_aliases={len(args) + i: i for i in range(len(onto))},
         name=name,
     )(*args, *onto)
@@ -833,16 +834,19 @@
     one.got, adj1 = tie(one.got, adj1)
     one.settle()
     _, adj1 = tie(one.send, adj1)
-    dxn1, dplow1, sum1, lam1 = run(
-        bind(finish_upper, z), "finish1", [full, low_n, stat_shape, lam_shape],
-        (adj1, dev_f, power, adj_ends1, chunk_f, dh1, keep_f, tab, proj1, h1, carry1, keep_r, dy1, v1, norm1, skip_gain, w_in),
-        [tile, chunk, stat_tile])
-    _, sum1 = tie(one.send, sum1)
+    dxn1, sum1, lam1, keepi, sendi = run(
+        bind(finish_upper, z), "finish1", [full, stat_shape, lam_shape, part(1), part(1)],
+        (adj1, dev_f, power, adj_ends1, chunk_f, dh1, keep_f, tab, proj1, h1, carry1, keep_r, dy1, v1, norm1, skip_gain, w_in, low1),
+        [low_n, tile, chunk, stat_tile])
+    five = Exchange(z, keepi, sendi, order=ORDERS[4], flat=FLAT[4])
+    *_, sum1 = tie(one.send, five.send, sum1)
     one.go()
+    five.go()
     sum1 = swap(sum1, everyone)
-    one.got, sum1 = tie(one.got, sum1)
+    one.got, five.got, sum1 = tie(one.got, five.got, sum1)
     one.settle()
-    _, sum1 = tie(one.send, sum1)
+    five.settle()
+    *_, sum1 = tie(one.send, five.send, sum1)
     total1, e1, dy0, dh0, adj_ends0, adj0, small0, keepa, senda, keepo, sendo = run(
         bind(lower_block, z), "lower_block",
         [norm_shape, full, full, full_n, chunk, send_shape, small_shape, part(2), part(2), part(1), part(1)],
@@ -850,28 +854,32 @@
         [tile, stat_tile, wide_b, low])
     two = Exchange(z, keepa, senda, order=ORDERS[1], flat=FLAT[1])
     four = Exchange(z, keepo, sendo, order=ORDERS[3], flat=FLAT[3])
-    *_, adj0 = tie(one.send, two.send, four.send, adj0)
+    *_, adj0 = tie(one.send, two.send, four.send, five.send, adj0)
     one.go()
+    five.go()
     two.go()
     four.go()
     adj0 = swap(adj0, "tm")
-    one.got, two.got, four.got, adj0 = tie(one.got, two.got, four.got, adj0)
+    one.got, two.got, four.got, five.got, adj0 = tie(one.got, two.got, four.got, five.got, adj0)
     rows_sum = (2 * D + 2 * (3 * D + 2 * N)) // W
     z.extra = -(-rows_sum // 8) * 8
-    last_part = part(2, z.extra)
+    last_part = part(1, z.extra)
     dxn0, keepb, sendb = run(
         bind(finish_lower, z), "finish0", [full, last_part, last_part],
         (adj0, dev_r, power, adj_ends0, chunk_r, dh0, keep_r, tab, proj0, h0, carry0, keep_f, dy0, x, norm0, skip_gain, w_in,
-         low0, low1, dplow1, small0, small1, lam1),
+         low0, small0, small1, lam1),
         [low_n, lam_shape, tile, chunk])
     one.settle()
     two.settle()
     four.settle()
+    five.settle()
     three = Exchange(z, keepb, sendb, z.extra, ORDERS[2], FLAT[2])
-    for e in (one, two, four, three):
+    for e in (one, five, two, four, three):
         e.go()
-    sets = (one, two, three, four)
+    sets = (one, two, three, four, five)
     ahead = three.send
+    sums = (((2, D), F32), ((2, D), F32), ((2, N), F32), ((2, N), F32), ((2, D), F32), ((2, 2 * D), F32))
+    small_outs, wait = None, WAIT
     placed, done, queue = (), [], list(FIRST) if z.bits == 5 else []
     while len(done) < len(sets):
         for i in queue or SEQ:
@@ -889,11 +897,14 @@
                 e.settle()
                 e.go()
                 ahead = e.send
+                wait -= e.small is not None
+                if wait == 0 and small_outs is None:
+                    small_outs = run(
+                            bind(last, z), "last", [low, full, *sums], (three.small, dxn0, x, norm0, bn_gain, e1, total1, v2), [natural, full])
+                    ahead = small_outs[2]
         queue = []
-    sums = (((2, D), F32), ((2, D), F32), ((2, N), F32), ((2, N), F32), ((2, D), F32), ((2, 2 * D), F32))
-    out, grad_x, gain_out, bias_out, rate_out, phase_out, skip_out, bglu_out = run(
-        bind(last, z), "last", [low, full, *sums], (three.small, dxn0, x, norm0, bn_gain, e1, total1, v2), [natural, full])
     gwin, gwout, gwglu = placed
+    out, grad_x, gain_out, bias_out, rate_out, phase_out, skip_out, bglu_out = small_outs
     return (
         out.reshape(rows, steps, width),
         grad_x.reshape(rows, steps, width),

time: 167 us -> 164 us (0.982)
  waiting for transfers between devices: 41.5 us -> 29.3 us
  starting transfers between devices: 27.8 us -> 36 us
    ppermute x36 -> x44, waiting for transfers between devices: 41.5 us -> 29.3 us  [go(): lax.ppermute(self.send, ('tm', 'rows'), pairs(self.z, self.order[self.pla...]
    ppermute x36 -> x44, starting transfers between devices: 27.8 us -> 36 us  [go(): lax.ppermute(self.send, ('tm', 'rows'), pairs(self.z, self.order[self.pla...]
    pallas_call x45 -> x53, Pallas kernels: 22 us -> 23 us  [run(): pl.pallas_call(kernel, out_shape=[jax.ShapeDtypeStruct(s, t) for s, t in...]
  transfers between devices with their start and end apart: 36 -> 44, of which waited for: 17 -> 15; matrix products, arithmetic and copies ran while one was open for 0% -> 0% of each run, Pallas kernels for 6% -> 6%
where the time goes in v6:
time: 164 us
  blocking collectives  73.9 us (45%)
  starting transfers between devices  36 us (22%)
  waiting for transfers between devices  29.3 us (18%)
  Pallas kernels  23 us (14%)
    all_to_all x7, blocking collectives, swap(): return lax.all_to_all(a, axis, 0, 0)  73.9 us
    ppermute x44, starting transfers between devices, go(): lax.ppermute(self.send, ('tm', 'rows'), pairs(self.z, self.order[self.pla...  36 us
    ppermute x44, waiting for transfers between devices, go(): lax.ppermute(self.send, ('tm', 'rows'), pairs(self.z, self.order[self.pla...  29.3 us
    pallas_call x53, Pallas kernels, run(): pl.pallas_call(kernel, out_shape=[jax.ShapeDtypeStruct(s, t) for s, t in...  23 us
  transfers between devices with their start and end apart: 44, of which 15 were waited for; matrix products, arithmetic and copies ran while one was open for 0% of the time, Pallas kernels for 6%

profile of v6, /device:TPU:0, one launch (start us, length us, event | category | flops | bytes accessed | tf_op | source)
XLA Modules:
  0.0 163.6 jit_solution(3925165767937249062)
XLA Ops:
  0.6 2.6 %prepare.1 = (f32[256,512]{1,0:T(8,128)S(1)}, f32[256,512]{1,0:T(8,128)S(1)}, f32[32,8,128]{2,1,0:T(8,128)S(1)}, f32[256,128]{1,0:T(8,128)S(1)}, f32[256,128]{1,...) custom-call(s32[2,16]{1,0:T(2,128)} %len_hbm.1, ...), custom_call_target="tpu_custom_call" | custom-call | tf_op jit(solution)/shard_map/prepare/pallas_call | solution.py:758
  3.3 15.3 %all_to_all.35.stat_ref = f32[32,8,128]{2,1,0:T(8,128)S(1)} all-to-all(f32[32,8,128]{2,1,0:T(8,128)S(1)} %get-tuple-element.183), channel_id=1, replica_groups=mesh['tm'=8,'rows'=4] {'tm','rows'}, dimensions={0} | all-to-all | bytes 262144 | tf_op jit(solution)/shard_map/all_to_all | solution.py:778
  18.6 0.6 enter0.1
  19.2 9.2 %all_to_all.36.recv_ref = f32[8,8,128]{2,1,0:T(8,128)S(1)} all-to-all(f32[8,8,128]{2,1,0:T(8,128)S(1)} %get-tuple-element.191), channel_id=1, replica_groups=mesh['tm'=8,'rows'=4] {'tm'}, dimensions={0} | all-to-all | bytes 65536 | tf_op jit(solution)/shard_map/all_to_all | solution.py:778
  28.4 1.5 middle.1
  29.9 9.9 %all_to_all.37.stat_ref = f32[32,8,128]{2,1,0:T(8,128)S(1)} all-to-all(f32[32,8,128]{2,1,0:T(8,128)S(1)} %get-tuple-element.201), channel_id=1, replica_groups=mesh['tm'=8,'rows'=4] {'tm','rows'}, dimensions={0} | all-to-all | bytes 262144 | tf_op jit(solution)/shard_map/all_to_all | solution.py:778
  39.8 0.6 enter1.1
  40.4 9.1 %all_to_all.38.recv_ref = f32[8,8,128]{2,1,0:T(8,128)S(1)} all-to-all(f32[8,8,128]{2,1,0:T(8,128)S(1)} %get-tuple-element.205), channel_id=1, replica_groups=mesh['tm'=8,'rows'=4] {'tm'}, dimensions={0} | all-to-all | bytes 65536 | tf_op jit(solution)/shard_map/all_to_all | solution.py:778
  49.5 3.3 %turn.1 = (f32[256,512]{1,0:T(8,128)S(1)}, f32[16,512]{1,0:T(8,128)S(1)}, f32[256,512]{1,0:T(8,128)S(1)}, f32[256,512]{1,0:T(8,128)S(1)}, f32[256,512]{1,0:T(8,1...) custom-call(f32[8,8,128]{2,1,0:T(8,128)S(1)} %all_to_all.38.recv_ref, ...), custom_call_target="tpu_custom_call" | custom-call | tf_op jit(solution)/shard_map/turn/pallas_call | solution.py:758
  52.9 9.1 %all_to_all.39.refs_0_ = f32[8,8,128]{2,1,0:T(8,128)S(1)} all-to-all(f32[8,8,128]{2,1,0:T(8,128)S(1)} %get-tuple-element.215), channel_id=1, replica_groups=mesh['tm'=8,'rows'=4] {'tm'}, dimensions={0} | all-to-all | bytes 65536 | tf_op jit(solution)/shard_map/all_to_all | solution.py:778
  62.2 0.5 collective-permute-start.1
  62.8 1.1 finish1.1
  63.9 11.9 %all_to_all.40.stat_ref = f32[32,8,128]{2,1,0:T(8,128)S(1)} all-to-all(f32[32,8,128]{2,1,0:T(8,128)S(1)} %get-tuple-element.229), channel_id=1, replica_groups=mesh['tm'=8,'rows'=4] {'tm','rows'}, dimensions={0} | all-to-all | bytes 262144 | tf_op jit(solution)/shard_map/all_to_all | solution.py:778
  76.1 2.3 %lower_block.1 = (f32[8,512]{1,0:T(8,128)S(1)}, f32[256,512]{1,0:T(8,128)S(1)}, f32[256,512]{1,0:T(8,128)S(1)}, f32[256,512]{1,0:T(8,128)S(1)}, f32[16,512]{1,0:...) custom-call(f32[32,8,128]{2,1,0:T(8,128)S(1)} %all_to_all.40.stat_re, ...), custom_call_target="tpu_custom_call" | custom-call | flops 20000000000 | bytes 1 | tf_op jit(solution)/shard_map/lower_block/pallas_call | solution.py:758
  78.5 0.5 collective-permute-start.5
  78.9 1.2 collective-permute-start.3
  80.6 9.4 %all_to_all.41.refs_0_ = f32[8,8,128]{2,1,0:T(8,128)S(1)} all-to-all(f32[8,8,128]{2,1,0:T(8,128)S(1)} %get-tuple-element.246), channel_id=1, replica_groups=mesh['tm'=8,'rows'=4] {'tm'}, dimensions={0} | all-to-all | bytes 65536 | tf_op jit(solution)/shard_map/all_to_all | solution.py:778
  90.0 0.5 collective-permute-start.13
  90.6 0.8 collective-permute-start.8
  91.4 1.3 finish0.1
  93.0 1.3 collective-permute-start.12
  94.3 1.7 %collective-permute-start.11 = (f32[256,256]{1,0:T(8,128)S(1)}, f32[256,256]{1,0:T(8,128)S(1)}, u32[]{:S(2)}, u32[]{:S(2)}) collective-permute-start(f32[256,256]{1,0:T(8,128)S(1)} %get-tuple-element.270), channel_id=1, source_target_pairs={{0,8},{1,9},{2,10},{3,11},{4,12},{5,13},{6,14},{7,15},{8,0},{9,1},... | collective-permute-start | bytes 786440 | tf_op jit(solution)/shard_map/ppermute | solution.py:694
  96.0 0.6 collective-permute-done.8.recv_ref
  96.7 0.7 collective-permute-start.10
  97.4 1.3 collective-permute-start.9
  98.7 0.9 collective-permute-start.18
  99.6 3.3 %collective-permute-done.12.recv_ref = f32[512,256]{1,0:T(8,128)S(1)} collective-permute-done((f32[512,256]{1,0:T(8,128)S(1)}, f32[512,256]{1,0:T(8,128)S(1)}, u32[]{:S(2)}, u32[]{:S(2)}) %collective-permute-start.12) | collective-permute-done | bytes 524320 | tf_op jit(solution)/shard_map/ppermute | solution.py:694
  103.0 0.9 collective-permute-start.17
  103.9 2.7 %collective-permute-done.11.recv_ref = f32[256,256]{1,0:T(8,128)S(1)} collective-permute-done((f32[256,256]{1,0:T(8,128)S(1)}, f32[256,256]{1,0:T(8,128)S(1)}, u32[]{:S(2)}, u32[]{:S(2)}) %collective-permute-start.11) | collective-permute-done | bytes 262176 | tf_op jit(solution)/shard_map/ppermute | solution.py:694
  106.6 1.3 collective-permute-start.16
  108.3 0.9 collective-permute-start.14
  109.2 2.3 %collective-permute-start.23 = (f32[64,256]{1,0:T(8,128)S(1)}, f32[64,256]{1,0:T(8,128)S(1)}, u32[]{:S(2)}, u32[]{:S(2)}) collective-permute-start(f32[64,256]{1,0:T(8,128)S(1)} %add.12.keep_ref), channel_id=1, source_target_pairs={{0,16},{1,17},{2,18},{3,19},{4,20},{5,21},{6,22},{7,23},{8,24},{9,... | collective-permute-start | bytes 196616 | tf_op jit(solution)/shard_map/ppermute | solution.py:694
  111.6 0.8 collective-permute-start.22
  112.4 0.6 collective-permute-done.16.recv_ref
  113.0 0.8 collective-permute-start.21
  113.8 2.5 %collective-permute-done.15.recv_ref = f32[192,256]{1,0:T(8,128)S(1)} collective-permute-done((f32[192,256]{1,0:T(8,128)S(1)}, f32[192,256]{1,0:T(8,128)S(1)}, u32[]{:S(2)}, u32[]{:S(2)}) %collective-permute-start.15) | collective-permute-done | bytes 196640 | tf_op jit(solution)/shard_map/ppermute | solution.py:694
  116.3 1.2 collective-permute-start.20
  117.6 1.0 collective-permute-start.28
  118.6 1.3 collective-permute-start.27
  120.0 1.7 %collective-permute-start.26 = (f32[128,256]{1,0:T(8,128)S(1)}, f32[128,256]{1,0:T(8,128)S(1)}, u32[]{:S(2)}, u32[]{:S(2)}) collective-permute-start(f32[128,256]{1,0:T(8,128)S(1)} %add.16.keep_ref), channel_id=1, source_target_pairs={{0,16},{1,17},{2,18},{3,19},{4,20},{5,21},{6,22},{7,23},{8,24},{9,... | collective-permute-start | bytes 393224 | tf_op jit(solution)/shard_map/ppermute | solution.py:694
  121.7 3.4 %collective-permute-done.20.recv_ref = f32[384,256]{1,0:T(8,128)S(1)} collective-permute-done((f32[384,256]{1,0:T(8,128)S(1)}, f32[384,256]{1,0:T(8,128)S(1)}, u32[]{:S(2)}, u32[]{:S(2)}) %collective-permute-start.20) | collective-permute-done | bytes 393248 | tf_op jit(solution)/shard_map/ppermute | solution.py:694
  125.2 1.8 %collective-permute-start.25 = (f32[768,256]{1,0:T(8,128)S(1)}, f32[768,256]{1,0:T(8,128)S(1)}, u32[]{:S(2)}, u32[]{:S(2)}) collective-permute-start(f32[768,256]{1,0:T(8,128)S(1)} %join.15.own_ref), channel_id=1, source_target_pairs={{0,4},{1,3},{2,6},{3,1},{4,0},{5,7},{6,2},{7,5},{8,12},{9,11},{10,... | collective-permute-start | bytes 2359304 | tf_op jit(solution)/shard_map/ppermute | solution.py:694
  127.2 1.2 collective-permute-start.33
  128.4 2.4 %collective-permute-done.27.recv_ref = f32[128,256]{1,0:T(8,128)S(1)} collective-permute-done((f32[128,256]{1,0:T(8,128)S(1)}, f32[128,256]{1,0:T(8,128)S(1)}, u32[]{:S(2)}, u32[]{:S(2)}) %collective-permute-start.27) | collective-permute-done | bytes 131104 | tf_op jit(solution)/shard_map/ppermute | solution.py:694
  130.9 3.7 %collective-permute-done.26.recv_ref = f32[128,256]{1,0:T(8,128)S(1)} collective-permute-done((f32[128,256]{1,0:T(8,128)S(1)}, f32[128,256]{1,0:T(8,128)S(1)}, u32[]{:S(2)}, u32[]{:S(2)}) %collective-permute-start.26) | collective-permute-done | bytes 131104 | tf_op jit(solution)/shard_map/ppermute | solution.py:694
  134.6 1.8 %collective-permute-start.31 = (f32[128,256]{1,0:T(8,128)S(1)}, f32[128,256]{1,0:T(8,128)S(1)}, u32[]{:S(2)}, u32[]{:S(2)}) collective-permute-start(f32[128,256]{1,0:T(8,128)S(1)} %add.19.own_ref), channel_id=1, source_target_pairs={{0,4},{1,3},{2,6},{3,1},{4,0},{5,7},{6,2},{7,5},{8,12},{9,11},{10,... | collective-permute-start | bytes 393224 | tf_op jit(solution)/shard_map/ppermute | solution.py:694
  136.4 0.9 collective-permute-done.25.recv_ref
  137.6 1.1 collective-permute-done.33.recv_ref
  138.7 1.0 collective-permute-start.37
  139.7 1.8 %collective-permute-start.36 = (f32[256,256]{1,0:T(8,128)S(1)}, f32[256,256]{1,0:T(8,128)S(1)}, u32[]{:S(2)}, u32[]{:S(2)}) collective-permute-start(f32[256,256]{1,0:T(8,128)S(1)} %join.19.own_ref), channel_id=1, source_target_pairs={{0,2},{1,5},{2,0},{3,7},{4,6},{5,1},{6,4},{7,3},{8,10},{9,13},{10,... | collective-permute-start | bytes 786440 | tf_op jit(solution)/shard_map/ppermute | solution.py:694
  141.6 1.1 collective-permute-start.35
  142.7 1.5 last.1
  144.3 1.7 %assemble.5 = (f32[2,512,512]{2,1,0:T(8,128)}, f32[2,512,512]{2,1,0:T(8,128)}, f32[2,512,1024]{2,1,0:T(8,128)}) custom-call(f32[1536,256]{1,0:T(8,128)S(1)} %join.17.refs_0_, f32[1536,256]{1,0:T(8,128)S(1)} %collective-permute-done.30.refs_1_), custom_call_target="tpu_custom_call" | custom-call | tf_op jit(solution)/shard_map/assemble/pallas_call | solution.py:758
  146.4 1.7 %collective-permute-done.37.recv_ref = f32[256,256]{1,0:T(8,128)S(1)} collective-permute-done((f32[256,256]{1,0:T(8,128)S(1)}, f32[256,256]{1,0:T(8,128)S(1)}, u32[]{:S(2)}, u32[]{:S(2)}) %collective-permute-start.37) | collective-permute-done | bytes 262176 | tf_op jit(solution)/shard_map/ppermute | solution.py:694
  148.3 1.8 %collective-permute-start.40 = (f32[512,256]{1,0:T(8,128)S(1)}, f32[512,256]{1,0:T(8,128)S(1)}, u32[]{:S(2)}, u32[]{:S(2)}) collective-permute-start(f32[512,256]{1,0:T(8,128)S(1)} %join.23.own_ref), channel_id=1, source_target_pairs={{0,4},{1,3},{2,6},{3,1},{4,0},{5,7},{6,2},{7,5},{8,12},{9,11},{10,... | collective-permute-start | bytes 1572872 | tf_op jit(solution)/shard_map/ppermute | solution.py:694
  150.1 3.2 %collective-permute-done.35.recv_ref = f32[256,256]{1,0:T(8,128)S(1)} collective-permute-done((f32[256,256]{1,0:T(8,128)S(1)}, f32[256,256]{1,0:T(8,128)S(1)}, u32[]{:S(2)}, u32[]{:S(2)}) %collective-permute-start.35) | collective-permute-done | bytes 262176 | tf_op jit(solution)/shard_map/ppermute | solution.py:694
  153.5 1.8 %collective-permute-start.38 = (f32[256,256]{1,0:T(8,128)S(1)}, f32[256,256]{1,0:T(8,128)S(1)}, u32[]{:S(2)}, u32[]{:S(2)}) collective-permute-start(f32[256,256]{1,0:T(8,128)S(1)} %join.25.own_ref), channel_id=1, source_target_pairs={{0,4},{1,3},{2,6},{3,1},{4,0},{5,7},{6,2},{7,5},{8,12},{9,11},{10,... | collective-permute-start | bytes 786440 | tf_op jit(solution)/shard_map/ppermute | solution.py:694
  155.3 1.0 assemble.6
  156.4 1.2 collective-permute-done.40.recv_ref
  157.7 1.1 assemble.7
  158.8 1.6 collective-permute-done.38.recv_ref
  160.5 1.4 assemble.8
  161.9 0.5 collective-permute-done.42.refs_1_
  162.4 1.0 assemble.9
  (84 shorter events, 3.9 us)
Async XLA Ops:
  52.9 9.1 %collective-permute-start = (f32[1536,256]{1,0:T(8,128)S(1)}, f32[1536,256]{1,0:T(8,128)S(1)}, u32[]{:S(2)}, u32[]{:S(2)}) collective-permute-start(f32[1536,256]{1,0:T(8,128)S(1)} %get-tuple-element.214), channel_id=1, source_target_pairs={{0,1},{1,0},{2,3},{3,2},{4,5},{5,4},{6,7},{7,6},{8,9},{9,8},{10,11... | collective-permute-start | bytes 4718600 | tf_op jit(solution)/shard_map/ppermute | solution.py:694
  62.2 13.6 %collective-permute-start.1 = (f32[768,256]{1,0:T(8,128)S(1)}, f32[768,256]{1,0:T(8,128)S(1)}, u32[]{:S(2)}, u32[]{:S(2)}) collective-permute-start(f32[768,256]{1,0:T(8,128)S(1)} %get-tuple-element.218), channel_id=1, source_target_pairs={{0,4},{1,3},{2,6},{3,1},{4,0},{5,7},{6,2},{7,5},{8,12},{9,11},{10,... | collective-permute-start | bytes 2359304 | tf_op jit(solution)/shard_map/ppermute | solution.py:694
  63.9 12.0 %collective-permute-start.2 = (f32[512,256]{1,0:T(8,128)S(1)}, f32[512,256]{1,0:T(8,128)S(1)}, u32[]{:S(2)}, u32[]{:S(2)}) collective-permute-start(f32[512,256]{1,0:T(8,128)S(1)} %get-tuple-element.227), channel_id=1, source_target_pairs={{0,1},{1,0},{2,3},{3,2},{4,5},{5,4},{6,7},{7,6},{8,9},{9,8},{10,11... | collective-permute-start | bytes 1572872 | tf_op jit(solution)/shard_map/ppermute | solution.py:694
  78.4 11.6 %collective-permute-start.4 = (f32[1024,256]{1,0:T(8,128)S(1)}, f32[1024,256]{1,0:T(8,128)S(1)}, u32[]{:S(2)}, u32[]{:S(2)}) collective-permute-start(f32[1024,256]{1,0:T(8,128)S(1)} %get-tuple-element.243), channel_id=1, source_target_pairs={{0,1},{1,0},{2,3},{3,2},{4,5},{5,4},{6,7},{7,6},{8,9},{9,8},{10,11... | collective-permute-start | bytes 3145736 | tf_op jit(solution)/shard_map/ppermute | solution.py:694
  78.5 11.5 %collective-permute-start.5 = (f32[512,256]{1,0:T(8,128)S(1)}, f32[512,256]{1,0:T(8,128)S(1)}, u32[]{:S(2)}, u32[]{:S(2)}) collective-permute-start(f32[512,256]{1,0:T(8,128)S(1)} %get-tuple-element.244), channel_id=1, source_target_pairs={{0,1},{1,0},{2,3},{3,2},{4,5},{5,4},{6,7},{7,6},{8,9},{9,8},{10,11... | collective-permute-start | bytes 1572872 | tf_op jit(solution)/shard_map/ppermute | solution.py:694
  78.9 11.0 %collective-permute-start.3 = (f32[384,256]{1,0:T(8,128)S(1)}, f32[384,256]{1,0:T(8,128)S(1)}, u32[]{:S(2)}, u32[]{:S(2)}) collective-permute-start(f32[384,256]{1,0:T(8,128)S(1)} %get-tuple-element.231), channel_id=1, source_target_pairs={{0,2},{1,5},{2,0},{3,7},{4,6},{5,1},{6,4},{7,3},{8,10},{9,13},{10,... | collective-permute-start | bytes 1179656 | tf_op jit(solution)/shard_map/ppermute | solution.py:694
  80.2 9.8 %collective-permute-start.6 = (f32[256,256]{1,0:T(8,128)S(1)}, f32[256,256]{1,0:T(8,128)S(1)}, u32[]{:S(2)}, u32[]{:S(2)}) collective-permute-start(f32[256,256]{1,0:T(8,128)S(1)} %get-tuple-element.234), channel_id=1, source_target_pairs={{0,8},{1,9},{2,10},{3,11},{4,12},{5,13},{6,14},{7,15},{8,0},{9,1},... | collective-permute-start | bytes 786440 | tf_op jit(solution)/shard_map/ppermute | solution.py:694
  90.0 8.6 %collective-permute-start.13 = (f32[128,256]{1,0:T(8,128)S(1)}, f32[128,256]{1,0:T(8,128)S(1)}, u32[]{:S(2)}, u32[]{:S(2)}) collective-permute-start(f32[128,256]{1,0:T(8,128)S(1)} %get-tuple-element.278), channel_id=1, source_target_pairs={{0,4},{1,3},{2,6},{3,1},{4,0},{5,7},{6,2},{7,5},{8,12},{9,11},{10,... | collective-permute-start | bytes 393224 | tf_op jit(solution)/shard_map/ppermute | solution.py:694
  90.6 6.0 %collective-permute-start.8 = (f32[192,256]{1,0:T(8,128)S(1)}, f32[192,256]{1,0:T(8,128)S(1)}, u32[]{:S(2)}, u32[]{:S(2)}) collective-permute-start(f32[192,256]{1,0:T(8,128)S(1)} %get-tuple-element.262), channel_id=1, source_target_pairs={{0,8},{1,9},{2,10},{3,11},{4,12},{5,13},{6,14},{7,15},{8,0},{9,1},... | collective-permute-start | bytes 589832 | tf_op jit(solution)/shard_map/ppermute | solution.py:694
  92.7 4.6 %collective-permute-start.7 = (f32[536,256]{1,0:T(8,128)S(1)}, f32[536,256]{1,0:T(8,128)S(1)}, u32[]{:S(2)}, u32[]{:S(2)}) collective-permute-start(f32[536,256]{1,0:T(8,128)S(1)} %get-tuple-element.258), channel_id=1, source_target_pairs={{0,1},{1,0},{2,3},{3,2},{4,5},{5,4},{6,7},{7,6},{8,9},{9,8},{10,11... | collective-permute-start | bytes 1646600 | tf_op jit(solution)/shard_map/ppermute | solution.py:694
  93.0 9.9 %collective-permute-start.12 = (f32[512,256]{1,0:T(8,128)S(1)}, f32[512,256]{1,0:T(8,128)S(1)}, u32[]{:S(2)}, u32[]{:S(2)}) collective-permute-start(f32[512,256]{1,0:T(8,128)S(1)} %get-tuple-element.274), channel_id=1, source_target_pairs={{0,4},{1,3},{2,6},{3,1},{4,0},{5,7},{6,2},{7,5},{8,12},{9,11},{10,... | collective-permute-start | bytes 1572872 | tf_op jit(solution)/shard_map/ppermute | solution.py:694
  94.3 12.3 %collective-permute-start.11 = (f32[256,256]{1,0:T(8,128)S(1)}, f32[256,256]{1,0:T(8,128)S(1)}, u32[]{:S(2)}, u32[]{:S(2)}) collective-permute-start(f32[256,256]{1,0:T(8,128)S(1)} %get-tuple-element.270), channel_id=1, source_target_pairs={{0,8},{1,9},{2,10},{3,11},{4,12},{5,13},{6,14},{7,15},{8,0},{9,1},... | collective-permute-start | bytes 786440 | tf_op jit(solution)/shard_map/ppermute | solution.py:694
  96.7 11.3 %collective-permute-start.10 = (f32[192,256]{1,0:T(8,128)S(1)}, f32[192,256]{1,0:T(8,128)S(1)}, u32[]{:S(2)}, u32[]{:S(2)}) collective-permute-start(f32[192,256]{1,0:T(8,128)S(1)} %add.10.keep_ref), channel_id=1, source_target_pairs={{0,16},{1,17},{2,18},{3,19},{4,20},{5,21},{6,22},{7,23},{8,24},{9,... | collective-permute-start | bytes 589832 | tf_op jit(solution)/shard_map/ppermute | solution.py:694
  97.4 10.8 %collective-permute-start.9 = (f32[280,256]{1,0:T(8,128)S(1)}, f32[280,256]{1,0:T(8,128)S(1)}, u32[]{:S(2)}, u32[]{:S(2)}) collective-permute-start(f32[280,256]{1,0:T(8,128)S(1)} %get-tuple-element.266), channel_id=1, source_target_pairs={{0,4},{1,3},{2,6},{3,1},{4,0},{5,7},{6,2},{7,5},{8,12},{9,11},{10,... | collective-permute-start | bytes 860168 | tf_op jit(solution)/shard_map/ppermute | solution.py:694
  98.7 10.5 %collective-permute-start.18 = (f32[64,256]{1,0:T(8,128)S(1)}, f32[64,256]{1,0:T(8,128)S(1)}, u32[]{:S(2)}, u32[]{:S(2)}) collective-permute-start(f32[64,256]{1,0:T(8,128)S(1)} %get-tuple-element.280), channel_id=1, source_target_pairs={{0,2},{1,5},{2,0},{3,7},{4,6},{5,1},{6,4},{7,3},{8,10},{9,13},{10,... | collective-permute-start | bytes 196616 | tf_op jit(solution)/shard_map/ppermute | solution.py:694
  103.0 8.6 %collective-permute-start.17 = (f32[256,256]{1,0:T(8,128)S(1)}, f32[256,256]{1,0:T(8,128)S(1)}, u32[]{:S(2)}, u32[]{:S(2)}) collective-permute-start(f32[256,256]{1,0:T(8,128)S(1)} %get-tuple-element.282), channel_id=1, source_target_pairs={{0,2},{1,5},{2,0},{3,7},{4,6},{5,1},{6,4},{7,3},{8,10},{9,13},{10,... | collective-permute-start | bytes 786440 | tf_op jit(solution)/shard_map/ppermute | solution.py:694
  106.6 6.4 %collective-permute-start.16 = (f32[128,256]{1,0:T(8,128)S(1)}, f32[128,256]{1,0:T(8,128)S(1)}, u32[]{:S(2)}, u32[]{:S(2)}) collective-permute-start(f32[128,256]{1,0:T(8,128)S(1)} %get-tuple-element.284), channel_id=1, source_target_pairs={{0,4},{1,3},{2,6},{3,1},{4,0},{5,7},{6,2},{7,5},{8,12},{9,11},{10,... | collective-permute-start | bytes 393224 | tf_op jit(solution)/shard_map/ppermute | solution.py:694
  108.0 8.3 %collective-permute-start.15 = (f32[192,256]{1,0:T(8,128)S(1)}, f32[192,256]{1,0:T(8,128)S(1)}, u32[]{:S(2)}, u32[]{:S(2)}) collective-permute-start(f32[192,256]{1,0:T(8,128)S(1)} %add.11.own_ref), channel_id=1, source_target_pairs={{0,8},{1,9},{2,10},{3,11},{4,12},{5,13},{6,14},{7,15},{8,0},{9,1},... | collective-permute-start | bytes 589832 | tf_op jit(solution)/shard_map/ppermute | solution.py:694
  108.3 9.2 %collective-permute-start.14 = (f32[152,256]{1,0:T(8,128)S(1)}, f32[152,256]{1,0:T(8,128)S(1)}, u32[]{:S(2)}, u32[]{:S(2)}) collective-permute-start(f32[152,256]{1,0:T(8,128)S(1)} %get-tuple-element.288), channel_id=1, source_target_pairs={{0,2},{1,5},{2,0},{3,7},{4,6},{5,1},{6,4},{7,3},{8,10},{9,13},{10,... | collective-permute-start | bytes 466952 | tf_op jit(solution)/shard_map/ppermute | solution.py:694
  109.2 8.4 %collective-permute-start.23 = (f32[64,256]{1,0:T(8,128)S(1)}, f32[64,256]{1,0:T(8,128)S(1)}, u32[]{:S(2)}, u32[]{:S(2)}) collective-permute-start(f32[64,256]{1,0:T(8,128)S(1)} %add.12.keep_ref), channel_id=1, source_target_pairs={{0,16},{1,17},{2,18},{3,19},{4,20},{5,21},{6,22},{7,23},{8,24},{9,... | collective-permute-start | bytes 196616 | tf_op jit(solution)/shard_map/ppermute | solution.py:694
  111.6 7.0 %collective-permute-start.22 = (f32[128,256]{1,0:T(8,128)S(1)}, f32[128,256]{1,0:T(8,128)S(1)}, u32[]{:S(2)}, u32[]{:S(2)}) collective-permute-start(f32[128,256]{1,0:T(8,128)S(1)} %get-tuple-element.294), channel_id=1, source_target_pairs={{0,8},{1,9},{2,10},{3,11},{4,12},{5,13},{6,14},{7,15},{8,0},{9,1},... | collective-permute-start | bytes 393224 | tf_op jit(solution)/shard_map/ppermute | solution.py:694
  113.0 6.9 %collective-permute-start.21 = (f32[128,256]{1,0:T(8,128)S(1)}, f32[128,256]{1,0:T(8,128)S(1)}, u32[]{:S(2)}, u32[]{:S(2)}) collective-permute-start(f32[128,256]{1,0:T(8,128)S(1)} %add.13.keep_ref), channel_id=1, source_target_pairs={{0,2},{1,5},{2,0},{3,7},{4,6},{5,1},{6,4},{7,3},{8,10},{9,13},{10,... | collective-permute-start | bytes 393224 | tf_op jit(solution)/shard_map/ppermute | solution.py:694
  116.3 8.8 %collective-permute-start.20 = (f32[384,256]{1,0:T(8,128)S(1)}, f32[384,256]{1,0:T(8,128)S(1)}, u32[]{:S(2)}, u32[]{:S(2)}) collective-permute-start(f32[384,256]{1,0:T(8,128)S(1)} %join.14.own_ref), channel_id=1, source_target_pairs={{0,2},{1,5},{2,0},{3,7},{4,6},{5,1},{6,4},{7,3},{8,10},{9,13},{10,... | collective-permute-start | bytes 1179656 | tf_op jit(solution)/shard_map/ppermute | solution.py:694
  117.5 9.5 %collective-permute-start.19 = (f32[88,256]{1,0:T(8,128)S(1)}, f32[88,256]{1,0:T(8,128)S(1)}, u32[]{:S(2)}, u32[]{:S(2)}) collective-permute-start(f32[88,256]{1,0:T(8,128)S(1)} %get-tuple-element.299), channel_id=1, source_target_pairs={{0,8},{1,9},{2,10},{3,11},{4,12},{5,13},{6,14},{7,15},{8,0},{9,1},... | collective-permute-start | bytes 270344 | tf_op jit(solution)/shard_map/ppermute | solution.py:694
  117.6 9.5 %collective-permute-start.28 = (f32[64,256]{1,0:T(8,128)S(1)}, f32[64,256]{1,0:T(8,128)S(1)}, u32[]{:S(2)}, u32[]{:S(2)}) collective-permute-start(f32[64,256]{1,0:T(8,128)S(1)} %add.14.own_ref), channel_id=1, source_target_pairs={{0,2},{1,5},{2,0},{3,7},{4,6},{5,1},{6,4},{7,3},{8,10},{9,13},{10,... | collective-permute-start | bytes 196616 | tf_op jit(solution)/shard_map/ppermute | solution.py:694
  118.6 12.1 %collective-permute-start.27 = (f32[128,256]{1,0:T(8,128)S(1)}, f32[128,256]{1,0:T(8,128)S(1)}, u32[]{:S(2)}, u32[]{:S(2)}) collective-permute-start(f32[128,256]{1,0:T(8,128)S(1)} %add.15.keep_ref), channel_id=1, source_target_pairs={{0,16},{1,17},{2,18},{3,19},{4,20},{5,21},{6,22},{7,23},{8,24},{9,... | collective-permute-start | bytes 393224 | tf_op jit(solution)/shard_map/ppermute | solution.py:694
  120.0 14.6 %collective-permute-start.26 = (f32[128,256]{1,0:T(8,128)S(1)}, f32[128,256]{1,0:T(8,128)S(1)}, u32[]{:S(2)}, u32[]{:S(2)}) collective-permute-start(f32[128,256]{1,0:T(8,128)S(1)} %add.16.keep_ref), channel_id=1, source_target_pairs={{0,16},{1,17},{2,18},{3,19},{4,20},{5,21},{6,22},{7,23},{8,24},{9,... | collective-permute-start | bytes 393224 | tf_op jit(solution)/shard_map/ppermute | solution.py:694
  125.2 12.1 %collective-permute-start.25 = (f32[768,256]{1,0:T(8,128)S(1)}, f32[768,256]{1,0:T(8,128)S(1)}, u32[]{:S(2)}, u32[]{:S(2)}) collective-permute-start(f32[768,256]{1,0:T(8,128)S(1)} %join.15.own_ref), channel_id=1, source_target_pairs={{0,4},{1,3},{2,6},{3,1},{4,0},{5,7},{6,2},{7,5},{8,12},{9,11},{10,... | collective-permute-start | bytes 2359304 | tf_op jit(solution)/shard_map/ppermute | solution.py:694
  127.1 10.4 %collective-permute-start.24 = (f32[88,256]{1,0:T(8,128)S(1)}, f32[88,256]{1,0:T(8,128)S(1)}, u32[]{:S(2)}, u32[]{:S(2)}) collective-permute-start(f32[88,256]{1,0:T(8,128)S(1)} %add.17.keep_ref), channel_id=1, source_target_pairs={{0,16},{1,17},{2,18},{3,19},{4,20},{5,21},{6,22},{7,23},{8,24},{9,... | collective-permute-start | bytes 270344 | tf_op jit(solution)/shard_map/ppermute | solution.py:694
  127.2 11.5 %collective-permute-start.33 = (f32[128,256]{1,0:T(8,128)S(1)}, f32[128,256]{1,0:T(8,128)S(1)}, u32[]{:S(2)}, u32[]{:S(2)}) collective-permute-start(f32[128,256]{1,0:T(8,128)S(1)} %join.16.own_ref), channel_id=1, source_target_pairs={{0,4},{1,3},{2,6},{3,1},{4,0},{5,7},{6,2},{7,5},{8,12},{9,11},{10,... | collective-permute-start | bytes 393224 | tf_op jit(solution)/shard_map/ppermute | solution.py:694
  130.8 8.9 %collective-permute-start.32 = (f32[128,256]{1,0:T(8,128)S(1)}, f32[128,256]{1,0:T(8,128)S(1)}, u32[]{:S(2)}, u32[]{:S(2)}) collective-permute-start(f32[128,256]{1,0:T(8,128)S(1)} %add.18.own_ref), channel_id=1, source_target_pairs={{0,8},{1,9},{2,10},{3,11},{4,12},{5,13},{6,14},{7,15},{8,0},{9,1},... | collective-permute-start | bytes 393224 | tf_op jit(solution)/shard_map/ppermute | solution.py:694
  134.6 7.0 %collective-permute-start.31 = (f32[128,256]{1,0:T(8,128)S(1)}, f32[128,256]{1,0:T(8,128)S(1)}, u32[]{:S(2)}, u32[]{:S(2)}) collective-permute-start(f32[128,256]{1,0:T(8,128)S(1)} %add.19.own_ref), channel_id=1, source_target_pairs={{0,4},{1,3},{2,6},{3,1},{4,0},{5,7},{6,2},{7,5},{8,12},{9,11},{10,... | collective-permute-start | bytes 393224 | tf_op jit(solution)/shard_map/ppermute | solution.py:694
  137.4 6.9 %collective-permute-start.30 = (f32[1536,256]{1,0:T(8,128)S(1)}, f32[1536,256]{1,0:T(8,128)S(1)}, u32[]{:S(2)}, u32[]{:S(2)}) collective-permute-start(f32[1536,256]{1,0:T(8,128)S(1)} %join.17.refs_0_), channel_id=1, source_target_pairs={{0,1},{1,0},{2,3},{3,2},{4,5},{5,4},{6,7},{7,6},{8,9},{9,8},{10,11... | collective-permute-start | bytes 4718600 | tf_op jit(solution)/shard_map/ppermute | solution.py:694
  137.5 8.5 %collective-permute-start.29 = (f32[64,256]{1,0:T(8,128)S(1)}, f32[64,256]{1,0:T(8,128)S(1)}, u32[]{:S(2)}, u32[]{:S(2)}) collective-permute-start(f32[64,256]{1,0:T(8,128)S(1)} %get-tuple-element.320.own_ref), channel_id=1, source_target_pairs={{0,8},{1,9},{2,10},{3,11},{4,12},{5,13},{6,14},{7,15},{8,0},{9,1},... | collective-permute-start | bytes 196616 | tf_op jit(solution)/shard_map/ppermute | solution.py:694
  138.7 9.4 %collective-permute-start.37 = (f32[256,256]{1,0:T(8,128)S(1)}, f32[256,256]{1,0:T(8,128)S(1)}, u32[]{:S(2)}, u32[]{:S(2)}) collective-permute-start(f32[256,256]{1,0:T(8,128)S(1)} %join.18.own_ref), channel_id=1, source_target_pairs={{0,8},{1,9},{2,10},{3,11},{4,12},{5,13},{6,14},{7,15},{8,0},{9,1},... | collective-permute-start | bytes 786440 | tf_op jit(solution)/shard_map/ppermute | solution.py:694
  139.7 8.5 %collective-permute-start.36 = (f32[256,256]{1,0:T(8,128)S(1)}, f32[256,256]{1,0:T(8,128)S(1)}, u32[]{:S(2)}, u32[]{:S(2)}) collective-permute-start(f32[256,256]{1,0:T(8,128)S(1)} %join.19.own_ref), channel_id=1, source_target_pairs={{0,2},{1,5},{2,0},{3,7},{4,6},{5,1},{6,4},{7,3},{8,10},{9,13},{10,... | collective-permute-start | bytes 786440 | tf_op jit(solution)/shard_map/ppermute | solution.py:694
  141.6 11.7 %collective-permute-start.35 = (f32[256,256]{1,0:T(8,128)S(1)}, f32[256,256]{1,0:T(8,128)S(1)}, u32[]{:S(2)}, u32[]{:S(2)}) collective-permute-start(f32[256,256]{1,0:T(8,128)S(1)} %join.20.own_ref), channel_id=1, source_target_pairs={{0,8},{1,9},{2,10},{3,11},{4,12},{5,13},{6,14},{7,15},{8,0},{9,1},... | collective-permute-start | bytes 786440 | tf_op jit(solution)/shard_map/ppermute | solution.py:694
  146.1 7.4 %collective-permute-start.34 = (f32[128,256]{1,0:T(8,128)S(1)}, f32[128,256]{1,0:T(8,128)S(1)}, u32[]{:S(2)}, u32[]{:S(2)}) collective-permute-start(f32[128,256]{1,0:T(8,128)S(1)} %join.21.own_ref), channel_id=1, source_target_pairs={{0,2},{1,5},{2,0},{3,7},{4,6},{5,1},{6,4},{7,3},{8,10},{9,13},{10,... | collective-permute-start | bytes 393224 | tf_op jit(solution)/shard_map/ppermute | solution.py:694
  148.1 7.2 %collective-permute-start.41 = (f32[512,256]{1,0:T(8,128)S(1)}, f32[512,256]{1,0:T(8,128)S(1)}, u32[]{:S(2)}, u32[]{:S(2)}) collective-permute-start(f32[512,256]{1,0:T(8,128)S(1)} %join.22.refs_0_), channel_id=1, source_target_pairs={{0,1},{1,0},{2,3},{3,2},{4,5},{5,4},{6,7},{7,6},{8,9},{9,8},{10,11... | collective-permute-start | bytes 1572872 | tf_op jit(solution)/shard_map/ppermute | solution.py:694
  148.3 9.2 %collective-permute-start.40 = (f32[512,256]{1,0:T(8,128)S(1)}, f32[512,256]{1,0:T(8,128)S(1)}, u32[]{:S(2)}, u32[]{:S(2)}) collective-permute-start(f32[512,256]{1,0:T(8,128)S(1)} %join.23.own_ref), channel_id=1, source_target_pairs={{0,4},{1,3},{2,6},{3,1},{4,0},{5,7},{6,2},{7,5},{8,12},{9,11},{10,... | collective-permute-start | bytes 1572872 | tf_op jit(solution)/shard_map/ppermute | solution.py:694
  153.4 4.4 %collective-permute-start.39 = (f32[512,256]{1,0:T(8,128)S(1)}, f32[512,256]{1,0:T(8,128)S(1)}, u32[]{:S(2)}, u32[]{:S(2)}) collective-permute-start(f32[512,256]{1,0:T(8,128)S(1)} %join.24.refs_0_), channel_id=1, source_target_pairs={{0,1},{1,0},{2,3},{3,2},{4,5},{5,4},{6,7},{7,6},{8,9},{9,8},{10,11... | collective-permute-start | bytes 1572872 | tf_op jit(solution)/shard_map/ppermute | solution.py:694
  153.5 6.9 %collective-permute-start.38 = (f32[256,256]{1,0:T(8,128)S(1)}, f32[256,256]{1,0:T(8,128)S(1)}, u32[]{:S(2)}, u32[]{:S(2)}) collective-permute-start(f32[256,256]{1,0:T(8,128)S(1)} %join.25.own_ref), channel_id=1, source_target_pairs={{0,4},{1,3},{2,6},{3,1},{4,0},{5,7},{6,2},{7,5},{8,12},{9,11},{10,... | collective-permute-start | bytes 786440 | tf_op jit(solution)/shard_map/ppermute | solution.py:694
  157.6 2.8 %collective-permute-start.43 = (f32[1024,256]{1,0:T(8,128)S(1)}, f32[1024,256]{1,0:T(8,128)S(1)}, u32[]{:S(2)}, u32[]{:S(2)}) collective-permute-start(f32[1024,256]{1,0:T(8,128)S(1)} %join.26.refs_0_), channel_id=1, source_target_pairs={{0,1},{1,0},{2,3},{3,2},{4,5},{5,4},{6,7},{7,6},{8,9},{9,8},{10,11... | collective-permute-start | bytes 3145736 | tf_op jit(solution)/shard_map/ppermute | solution.py:694
  160.4 2.0 %collective-permute-start.42 = (f32[512,256]{1,0:T(8,128)S(1)}, f32[512,256]{1,0:T(8,128)S(1)}, u32[]{:S(2)}, u32[]{:S(2)}) collective-permute-start(f32[512,256]{1,0:T(8,128)S(1)} %join.27.refs_0_), channel_id=1, source_target_pairs={{0,1},{1,0},{2,3},{3,2},{4,5},{5,4},{6,7},{7,6},{8,9},{9,8},{10,11... | collective-permute-start | bytes 1572872 | tf_op jit(solution)/shard_map/ppermute | solution.py:694

commit v7 on v6

--- a/solution.py
+++ b/solution.py
@@ -11,7 +11,8 @@
 EPS = 1e-05
 LANES = 128
 CHUNKS = 8
-TILE = 128
+TILE = 64
+UNROLL = 4
 F32 = jnp.float32
 BF16 = jnp.bfloat16
 ROOT_HALF = 0.7071067811865476
@@ -58,7 +59,7 @@
     def one(i, c):
         return body(pl.ds(pl.multiple_of(i * TILE, TILE), TILE), c)
 
-    return lax.fori_loop(0, z.T // TILE, one, carry)
+    return lax.fori_loop(0, z.T // TILE, one, carry, unroll=UNROLL)
 
 
 def pack(ref, rows, k=0):

time: 164 us -> 162 us (0.988)
  Pallas kernels: 23 us -> 21 us
    pallas_call x53, Pallas kernels: 23 us -> 21 us  [run(): pl.pallas_call(kernel, out_shape=[jax.ShapeDtypeStruct(s, t) for s, t in...]
where the time goes in v7:
time: 162 us
  blocking collectives  74 us (46%)
  starting transfers between devices  36.1 us (22%)
  waiting for transfers between devices  29.2 us (18%)
  Pallas kernels  21 us (13%)
    all_to_all x7, blocking collectives, swap(): return lax.all_to_all(a, axis, 0, 0)  74 us
    ppermute x44, starting transfers between devices, go(): lax.ppermute(self.send, ('tm', 'rows'), pairs(self.z, self.order[self.pla...  36.1 us
    ppermute x44, waiting for transfers between devices, go(): lax.ppermute(self.send, ('tm', 'rows'), pairs(self.z, self.order[self.pla...  29.2 us
    pallas_call x53, Pallas kernels, run(): pl.pallas_call(kernel, out_shape=[jax.ShapeDtypeStruct(s, t) for s, t in...  21 us
  transfers between devices with their start and end apart: 44, of which 15 were waited for; matrix products, arithmetic and copies ran while one was open for 0% of the time, Pallas kernels for 6%

profile of v7, /device:TPU:0, one launch (start us, length us, event | category | flops | bytes accessed | tf_op | source)
XLA Modules:
  0.0 161.7 jit_solution(10532148624331265260)
XLA Ops:
  0.6 2.6 %prepare.1 = (f32[256,512]{1,0:T(8,128)S(1)}, f32[256,512]{1,0:T(8,128)S(1)}, f32[32,8,128]{2,1,0:T(8,128)S(1)}, f32[256,128]{1,0:T(8,128)S(1)}, f32[256,128]{1,...) custom-call(s32[2,16]{1,0:T(2,128)} %len_hbm.1, ...), custom_call_target="tpu_custom_call" | custom-call | tf_op jit(solution)/shard_map/prepare/pallas_call | solution.py:759
  3.3 15.3 %all_to_all.35.stat_ref = f32[32,8,128]{2,1,0:T(8,128)S(1)} all-to-all(f32[32,8,128]{2,1,0:T(8,128)S(1)} %get-tuple-element.183), channel_id=1, replica_groups=mesh['tm'=8,'rows'=4] {'tm','rows'}, dimensions={0} | all-to-all | bytes 262144 | tf_op jit(solution)/shard_map/all_to_all | solution.py:779
  18.6 0.5 enter0.1
  19.1 9.2 %all_to_all.36.recv_ref = f32[8,8,128]{2,1,0:T(8,128)S(1)} all-to-all(f32[8,8,128]{2,1,0:T(8,128)S(1)} %get-tuple-element.191), channel_id=1, replica_groups=mesh['tm'=8,'rows'=4] {'tm'}, dimensions={0} | all-to-all | bytes 65536 | tf_op jit(solution)/shard_map/all_to_all | solution.py:779
  28.3 1.2 middle.1
  29.4 9.9 %all_to_all.37.stat_ref = f32[32,8,128]{2,1,0:T(8,128)S(1)} all-to-all(f32[32,8,128]{2,1,0:T(8,128)S(1)} %get-tuple-element.201), channel_id=1, replica_groups=mesh['tm'=8,'rows'=4] {'tm','rows'}, dimensions={0} | all-to-all | bytes 262144 | tf_op jit(solution)/shard_map/all_to_all | solution.py:779
  39.4 0.5 enter1.1
  39.9 9.1 %all_to_all.38.recv_ref = f32[8,8,128]{2,1,0:T(8,128)S(1)} all-to-all(f32[8,8,128]{2,1,0:T(8,128)S(1)} %get-tuple-element.205), channel_id=1, replica_groups=mesh['tm'=8,'rows'=4] {'tm'}, dimensions={0} | all-to-all | bytes 65536 | tf_op jit(solution)/shard_map/all_to_all | solution.py:779
  49.0 2.6 %turn.1 = (f32[256,512]{1,0:T(8,128)S(1)}, f32[16,512]{1,0:T(8,128)S(1)}, f32[256,512]{1,0:T(8,128)S(1)}, f32[256,512]{1,0:T(8,128)S(1)}, f32[256,512]{1,0:T(8,1...) custom-call(f32[8,8,128]{2,1,0:T(8,128)S(1)} %all_to_all.38.recv_ref, ...), custom_call_target="tpu_custom_call" | custom-call | tf_op jit(solution)/shard_map/turn/pallas_call | solution.py:759
  51.7 9.1 %all_to_all.39.refs_0_ = f32[8,8,128]{2,1,0:T(8,128)S(1)} all-to-all(f32[8,8,128]{2,1,0:T(8,128)S(1)} %get-tuple-element.215), channel_id=1, replica_groups=mesh['tm'=8,'rows'=4] {'tm'}, dimensions={0} | all-to-all | bytes 65536 | tf_op jit(solution)/shard_map/all_to_all | solution.py:779
  61.0 0.5 collective-permute-start.1
  61.5 1.0 finish1.1
  62.5 12.0 %all_to_all.40.stat_ref = f32[32,8,128]{2,1,0:T(8,128)S(1)} all-to-all(f32[32,8,128]{2,1,0:T(8,128)S(1)} %get-tuple-element.229), channel_id=1, replica_groups=mesh['tm'=8,'rows'=4] {'tm','rows'}, dimensions={0} | all-to-all | bytes 262144 | tf_op jit(solution)/shard_map/all_to_all | solution.py:779
  74.8 1.9 %lower_block.1 = (f32[8,512]{1,0:T(8,128)S(1)}, f32[256,512]{1,0:T(8,128)S(1)}, f32[256,512]{1,0:T(8,128)S(1)}, f32[256,512]{1,0:T(8,128)S(1)}, f32[16,512]{1,0:...) custom-call(f32[32,8,128]{2,1,0:T(8,128)S(1)} %all_to_all.40.stat_re, ...), custom_call_target="tpu_custom_call" | custom-call | flops 20000000000 | bytes 1 | tf_op jit(solution)/shard_map/lower_block/pallas_call | solution.py:759
  76.7 0.5 collective-permute-start.5
  77.2 1.2 collective-permute-start.3
  78.9 9.4 %all_to_all.41.refs_0_ = f32[8,8,128]{2,1,0:T(8,128)S(1)} all-to-all(f32[8,8,128]{2,1,0:T(8,128)S(1)} %get-tuple-element.246), channel_id=1, replica_groups=mesh['tm'=8,'rows'=4] {'tm'}, dimensions={0} | all-to-all | bytes 65536 | tf_op jit(solution)/shard_map/all_to_all | solution.py:779
  88.3 0.5 collective-permute-start.13
  88.9 0.8 collective-permute-start.8
  89.7 1.2 finish0.1
  91.2 1.3 collective-permute-start.12
  92.5 1.7 %collective-permute-start.11 = (f32[256,256]{1,0:T(8,128)S(1)}, f32[256,256]{1,0:T(8,128)S(1)}, u32[]{:S(2)}, u32[]{:S(2)}) collective-permute-start(f32[256,256]{1,0:T(8,128)S(1)} %get-tuple-element.270), channel_id=1, source_target_pairs={{0,8},{1,9},{2,10},{3,11},{4,12},{5,13},{6,14},{7,15},{8,0},{9,1},... | collective-permute-start | bytes 786440 | tf_op jit(solution)/shard_map/ppermute | solution.py:695
  94.2 0.7 collective-permute-done.8.recv_ref
  94.9 0.7 collective-permute-start.10
  95.7 1.3 collective-permute-start.9
  97.0 0.9 collective-permute-start.18
  97.9 3.2 %collective-permute-done.12.recv_ref = f32[512,256]{1,0:T(8,128)S(1)} collective-permute-done((f32[512,256]{1,0:T(8,128)S(1)}, f32[512,256]{1,0:T(8,128)S(1)}, u32[]{:S(2)}, u32[]{:S(2)}) %collective-permute-start.12) | collective-permute-done | bytes 524320 | tf_op jit(solution)/shard_map/ppermute | solution.py:695
  101.2 0.9 collective-permute-start.17
  102.0 2.7 %collective-permute-done.11.recv_ref = f32[256,256]{1,0:T(8,128)S(1)} collective-permute-done((f32[256,256]{1,0:T(8,128)S(1)}, f32[256,256]{1,0:T(8,128)S(1)}, u32[]{:S(2)}, u32[]{:S(2)}) %collective-permute-start.11) | collective-permute-done | bytes 262176 | tf_op jit(solution)/shard_map/ppermute | solution.py:695
  104.8 1.4 collective-permute-start.16
  106.5 0.9 collective-permute-start.14
  107.4 2.3 %collective-permute-start.23 = (f32[64,256]{1,0:T(8,128)S(1)}, f32[64,256]{1,0:T(8,128)S(1)}, u32[]{:S(2)}, u32[]{:S(2)}) collective-permute-start(f32[64,256]{1,0:T(8,128)S(1)} %add.12.keep_ref), channel_id=1, source_target_pairs={{0,16},{1,17},{2,18},{3,19},{4,20},{5,21},{6,22},{7,23},{8,24},{9,... | collective-permute-start | bytes 196616 | tf_op jit(solution)/shard_map/ppermute | solution.py:695
  109.8 0.8 collective-permute-start.22
  110.6 0.6 collective-permute-done.16.recv_ref
  111.2 0.8 collective-permute-start.21
  112.0 2.4 %collective-permute-done.15.recv_ref = f32[192,256]{1,0:T(8,128)S(1)} collective-permute-done((f32[192,256]{1,0:T(8,128)S(1)}, f32[192,256]{1,0:T(8,128)S(1)}, u32[]{:S(2)}, u32[]{:S(2)}) %collective-permute-start.15) | collective-permute-done | bytes 196640 | tf_op jit(solution)/shard_map/ppermute | solution.py:695
  114.5 1.2 collective-permute-start.20
  115.8 1.0 collective-permute-start.28
  116.8 1.4 collective-permute-start.27
  118.2 1.7 %collective-permute-start.26 = (f32[128,256]{1,0:T(8,128)S(1)}, f32[128,256]{1,0:T(8,128)S(1)}, u32[]{:S(2)}, u32[]{:S(2)}) collective-permute-start(f32[128,256]{1,0:T(8,128)S(1)} %add.16.keep_ref), channel_id=1, source_target_pairs={{0,16},{1,17},{2,18},{3,19},{4,20},{5,21},{6,22},{7,23},{8,24},{9,... | collective-permute-start | bytes 393224 | tf_op jit(solution)/shard_map/ppermute | solution.py:695
  119.9 3.4 %collective-permute-done.20.recv_ref = f32[384,256]{1,0:T(8,128)S(1)} collective-permute-done((f32[384,256]{1,0:T(8,128)S(1)}, f32[384,256]{1,0:T(8,128)S(1)}, u32[]{:S(2)}, u32[]{:S(2)}) %collective-permute-start.20) | collective-permute-done | bytes 393248 | tf_op jit(solution)/shard_map/ppermute | solution.py:695
  123.3 1.8 %collective-permute-start.25 = (f32[768,256]{1,0:T(8,128)S(1)}, f32[768,256]{1,0:T(8,128)S(1)}, u32[]{:S(2)}, u32[]{:S(2)}) collective-permute-start(f32[768,256]{1,0:T(8,128)S(1)} %join.15.own_ref), channel_id=1, source_target_pairs={{0,4},{1,3},{2,6},{3,1},{4,0},{5,7},{6,2},{7,5},{8,12},{9,11},{10,... | collective-permute-start | bytes 2359304 | tf_op jit(solution)/shard_map/ppermute | solution.py:695
  125.3 1.2 collective-permute-start.33
  126.5 3.5 %collective-permute-done.27.recv_ref = f32[128,256]{1,0:T(8,128)S(1)} collective-permute-done((f32[128,256]{1,0:T(8,128)S(1)}, f32[128,256]{1,0:T(8,128)S(1)}, u32[]{:S(2)}, u32[]{:S(2)}) %collective-permute-start.27) | collective-permute-done | bytes 131104 | tf_op jit(solution)/shard_map/ppermute | solution.py:695
  130.1 2.7 %collective-permute-done.26.recv_ref = f32[128,256]{1,0:T(8,128)S(1)} collective-permute-done((f32[128,256]{1,0:T(8,128)S(1)}, f32[128,256]{1,0:T(8,128)S(1)}, u32[]{:S(2)}, u32[]{:S(2)}) %collective-permute-start.26) | collective-permute-done | bytes 131104 | tf_op jit(solution)/shard_map/ppermute | solution.py:695
  132.8 1.8 %collective-permute-start.31 = (f32[128,256]{1,0:T(8,128)S(1)}, f32[128,256]{1,0:T(8,128)S(1)}, u32[]{:S(2)}, u32[]{:S(2)}) collective-permute-start(f32[128,256]{1,0:T(8,128)S(1)} %add.19.own_ref), channel_id=1, source_target_pairs={{0,4},{1,3},{2,6},{3,1},{4,0},{5,7},{6,2},{7,5},{8,12},{9,11},{10,... | collective-permute-start | bytes 393224 | tf_op jit(solution)/shard_map/ppermute | solution.py:695
  134.6 0.8 collective-permute-done.25.recv_ref
  135.7 1.1 collective-permute-done.33.recv_ref
  136.8 1.0 collective-permute-start.37
  137.9 1.9 %collective-permute-start.36 = (f32[256,256]{1,0:T(8,128)S(1)}, f32[256,256]{1,0:T(8,128)S(1)}, u32[]{:S(2)}, u32[]{:S(2)}) collective-permute-start(f32[256,256]{1,0:T(8,128)S(1)} %join.19.own_ref), channel_id=1, source_target_pairs={{0,2},{1,5},{2,0},{3,7},{4,6},{5,1},{6,4},{7,3},{8,10},{9,13},{10,... | collective-permute-start | bytes 786440 | tf_op jit(solution)/shard_map/ppermute | solution.py:695
  139.7 1.1 collective-permute-start.35
  140.9 1.5 last.1
  142.4 1.7 %assemble.5 = (f32[2,512,512]{2,1,0:T(8,128)}, f32[2,512,512]{2,1,0:T(8,128)}, f32[2,512,1024]{2,1,0:T(8,128)}) custom-call(f32[1536,256]{1,0:T(8,128)S(1)} %join.17.refs_0_, f32[1536,256]{1,0:T(8,128)S(1)} %collective-permute-done.30.refs_1_), custom_call_target="tpu_custom_call" | custom-call | tf_op jit(solution)/shard_map/assemble/pallas_call | solution.py:759
  144.5 1.7 %collective-permute-done.37.recv_ref = f32[256,256]{1,0:T(8,128)S(1)} collective-permute-done((f32[256,256]{1,0:T(8,128)S(1)}, f32[256,256]{1,0:T(8,128)S(1)}, u32[]{:S(2)}, u32[]{:S(2)}) %collective-permute-start.37) | collective-permute-done | bytes 262176 | tf_op jit(solution)/shard_map/ppermute | solution.py:695
  146.4 1.8 %collective-permute-start.40 = (f32[512,256]{1,0:T(8,128)S(1)}, f32[512,256]{1,0:T(8,128)S(1)}, u32[]{:S(2)}, u32[]{:S(2)}) collective-permute-start(f32[512,256]{1,0:T(8,128)S(1)} %join.23.own_ref), channel_id=1, source_target_pairs={{0,4},{1,3},{2,6},{3,1},{4,0},{5,7},{6,2},{7,5},{8,12},{9,11},{10,... | collective-permute-start | bytes 1572872 | tf_op jit(solution)/shard_map/ppermute | solution.py:695
  148.3 3.2 %collective-permute-done.35.recv_ref = f32[256,256]{1,0:T(8,128)S(1)} collective-permute-done((f32[256,256]{1,0:T(8,128)S(1)}, f32[256,256]{1,0:T(8,128)S(1)}, u32[]{:S(2)}, u32[]{:S(2)}) %collective-permute-start.35) | collective-permute-done | bytes 262176 | tf_op jit(solution)/shard_map/ppermute | solution.py:695
  151.6 1.8 %collective-permute-start.38 = (f32[256,256]{1,0:T(8,128)S(1)}, f32[256,256]{1,0:T(8,128)S(1)}, u32[]{:S(2)}, u32[]{:S(2)}) collective-permute-start(f32[256,256]{1,0:T(8,128)S(1)} %join.25.own_ref), channel_id=1, source_target_pairs={{0,4},{1,3},{2,6},{3,1},{4,0},{5,7},{6,2},{7,5},{8,12},{9,11},{10,... | collective-permute-start | bytes 786440 | tf_op jit(solution)/shard_map/ppermute | solution.py:695
  153.5 1.0 assemble.6
  154.5 1.2 collective-permute-done.40.recv_ref
  155.9 1.1 assemble.7
  156.9 1.6 collective-permute-done.38.recv_ref
  158.6 1.4 assemble.8
  160.0 0.5 collective-permute-done.42.refs_1_
  160.5 1.0 assemble.9
  (84 shorter events, 3.8 us)
Async XLA Ops:
  51.6 9.1 %collective-permute-start = (f32[1536,256]{1,0:T(8,128)S(1)}, f32[1536,256]{1,0:T(8,128)S(1)}, u32[]{:S(2)}, u32[]{:S(2)}) collective-permute-start(f32[1536,256]{1,0:T(8,128)S(1)} %get-tuple-element.214), channel_id=1, source_target_pairs={{0,1},{1,0},{2,3},{3,2},{4,5},{5,4},{6,7},{7,6},{8,9},{9,8},{10,11... | collective-permute-start | bytes 4718600 | tf_op jit(solution)/shard_map/ppermute | solution.py:695
  61.0 13.6 %collective-permute-start.1 = (f32[768,256]{1,0:T(8,128)S(1)}, f32[768,256]{1,0:T(8,128)S(1)}, u32[]{:S(2)}, u32[]{:S(2)}) collective-permute-start(f32[768,256]{1,0:T(8,128)S(1)} %get-tuple-element.218), channel_id=1, source_target_pairs={{0,4},{1,3},{2,6},{3,1},{4,0},{5,7},{6,2},{7,5},{8,12},{9,11},{10,... | collective-permute-start | bytes 2359304 | tf_op jit(solution)/shard_map/ppermute | solution.py:695
  62.5 12.1 %collective-permute-start.2 = (f32[512,256]{1,0:T(8,128)S(1)}, f32[512,256]{1,0:T(8,128)S(1)}, u32[]{:S(2)}, u32[]{:S(2)}) collective-permute-start(f32[512,256]{1,0:T(8,128)S(1)} %get-tuple-element.227), channel_id=1, source_target_pairs={{0,1},{1,0},{2,3},{3,2},{4,5},{5,4},{6,7},{7,6},{8,9},{9,8},{10,11... | collective-permute-start | bytes 1572872 | tf_op jit(solution)/shard_map/ppermute | solution.py:695
  76.7 11.6 %collective-permute-start.4 = (f32[1024,256]{1,0:T(8,128)S(1)}, f32[1024,256]{1,0:T(8,128)S(1)}, u32[]{:S(2)}, u32[]{:S(2)}) collective-permute-start(f32[1024,256]{1,0:T(8,128)S(1)} %get-tuple-element.243), channel_id=1, source_target_pairs={{0,1},{1,0},{2,3},{3,2},{4,5},{5,4},{6,7},{7,6},{8,9},{9,8},{10,11... | collective-permute-start | bytes 3145736 | tf_op jit(solution)/shard_map/ppermute | solution.py:695
  76.7 11.5 %collective-permute-start.5 = (f32[512,256]{1,0:T(8,128)S(1)}, f32[512,256]{1,0:T(8,128)S(1)}, u32[]{:S(2)}, u32[]{:S(2)}) collective-permute-start(f32[512,256]{1,0:T(8,128)S(1)} %get-tuple-element.244), channel_id=1, source_target_pairs={{0,1},{1,0},{2,3},{3,2},{4,5},{5,4},{6,7},{7,6},{8,9},{9,8},{10,11... | collective-permute-start | bytes 1572872 | tf_op jit(solution)/shard_map/ppermute | solution.py:695
  77.2 11.0 %collective-permute-start.3 = (f32[384,256]{1,0:T(8,128)S(1)}, f32[384,256]{1,0:T(8,128)S(1)}, u32[]{:S(2)}, u32[]{:S(2)}) collective-permute-start(f32[384,256]{1,0:T(8,128)S(1)} %get-tuple-element.231), channel_id=1, source_target_pairs={{0,2},{1,5},{2,0},{3,7},{4,6},{5,1},{6,4},{7,3},{8,10},{9,13},{10,... | collective-permute-start | bytes 1179656 | tf_op jit(solution)/shard_map/ppermute | solution.py:695
  78.5 9.8 %collective-permute-start.6 = (f32[256,256]{1,0:T(8,128)S(1)}, f32[256,256]{1,0:T(8,128)S(1)}, u32[]{:S(2)}, u32[]{:S(2)}) collective-permute-start(f32[256,256]{1,0:T(8,128)S(1)} %get-tuple-element.234), channel_id=1, source_target_pairs={{0,8},{1,9},{2,10},{3,11},{4,12},{5,13},{6,14},{7,15},{8,0},{9,1},... | collective-permute-start | bytes 786440 | tf_op jit(solution)/shard_map/ppermute | solution.py:695
  88.3 8.6 %collective-permute-start.13 = (f32[128,256]{1,0:T(8,128)S(1)}, f32[128,256]{1,0:T(8,128)S(1)}, u32[]{:S(2)}, u32[]{:S(2)}) collective-permute-start(f32[128,256]{1,0:T(8,128)S(1)} %get-tuple-element.278), channel_id=1, source_target_pairs={{0,4},{1,3},{2,6},{3,1},{4,0},{5,7},{6,2},{7,5},{8,12},{9,11},{10,... | collective-permute-start | bytes 393224 | tf_op jit(solution)/shard_map/ppermute | solution.py:695
  88.9 6.0 %collective-permute-start.8 = (f32[192,256]{1,0:T(8,128)S(1)}, f32[192,256]{1,0:T(8,128)S(1)}, u32[]{:S(2)}, u32[]{:S(2)}) collective-permute-start(f32[192,256]{1,0:T(8,128)S(1)} %get-tuple-element.262), channel_id=1, source_target_pairs={{0,8},{1,9},{2,10},{3,11},{4,12},{5,13},{6,14},{7,15},{8,0},{9,1},... | collective-permute-start | bytes 589832 | tf_op jit(solution)/shard_map/ppermute | solution.py:695
  90.9 4.7 %collective-permute-start.7 = (f32[536,256]{1,0:T(8,128)S(1)}, f32[536,256]{1,0:T(8,128)S(1)}, u32[]{:S(2)}, u32[]{:S(2)}) collective-permute-start(f32[536,256]{1,0:T(8,128)S(1)} %get-tuple-element.258), channel_id=1, source_target_pairs={{0,1},{1,0},{2,3},{3,2},{4,5},{5,4},{6,7},{7,6},{8,9},{9,8},{10,11... | collective-permute-start | bytes 1646600 | tf_op jit(solution)/shard_map/ppermute | solution.py:695
  91.2 9.9 %collective-permute-start.12 = (f32[512,256]{1,0:T(8,128)S(1)}, f32[512,256]{1,0:T(8,128)S(1)}, u32[]{:S(2)}, u32[]{:S(2)}) collective-permute-start(f32[512,256]{1,0:T(8,128)S(1)} %get-tuple-element.274), channel_id=1, source_target_pairs={{0,4},{1,3},{2,6},{3,1},{4,0},{5,7},{6,2},{7,5},{8,12},{9,11},{10,... | collective-permute-start | bytes 1572872 | tf_op jit(solution)/shard_map/ppermute | solution.py:695
  92.5 12.2 %collective-permute-start.11 = (f32[256,256]{1,0:T(8,128)S(1)}, f32[256,256]{1,0:T(8,128)S(1)}, u32[]{:S(2)}, u32[]{:S(2)}) collective-permute-start(f32[256,256]{1,0:T(8,128)S(1)} %get-tuple-element.270), channel_id=1, source_target_pairs={{0,8},{1,9},{2,10},{3,11},{4,12},{5,13},{6,14},{7,15},{8,0},{9,1},... | collective-permute-start | bytes 786440 | tf_op jit(solution)/shard_map/ppermute | solution.py:695
  94.9 11.2 %collective-permute-start.10 = (f32[192,256]{1,0:T(8,128)S(1)}, f32[192,256]{1,0:T(8,128)S(1)}, u32[]{:S(2)}, u32[]{:S(2)}) collective-permute-start(f32[192,256]{1,0:T(8,128)S(1)} %add.10.keep_ref), channel_id=1, source_target_pairs={{0,16},{1,17},{2,18},{3,19},{4,20},{5,21},{6,22},{7,23},{8,24},{9,... | collective-permute-start | bytes 589832 | tf_op jit(solution)/shard_map/ppermute | solution.py:695
  95.7 10.7 %collective-permute-start.9 = (f32[280,256]{1,0:T(8,128)S(1)}, f32[280,256]{1,0:T(8,128)S(1)}, u32[]{:S(2)}, u32[]{:S(2)}) collective-permute-start(f32[280,256]{1,0:T(8,128)S(1)} %get-tuple-element.266), channel_id=1, source_target_pairs={{0,4},{1,3},{2,6},{3,1},{4,0},{5,7},{6,2},{7,5},{8,12},{9,11},{10,... | collective-permute-start | bytes 860168 | tf_op jit(solution)/shard_map/ppermute | solution.py:695
  97.0 10.4 %collective-permute-start.18 = (f32[64,256]{1,0:T(8,128)S(1)}, f32[64,256]{1,0:T(8,128)S(1)}, u32[]{:S(2)}, u32[]{:S(2)}) collective-permute-start(f32[64,256]{1,0:T(8,128)S(1)} %get-tuple-element.280), channel_id=1, source_target_pairs={{0,2},{1,5},{2,0},{3,7},{4,6},{5,1},{6,4},{7,3},{8,10},{9,13},{10,... | collective-permute-start | bytes 196616 | tf_op jit(solution)/shard_map/ppermute | solution.py:695
  101.2 8.6 %collective-permute-start.17 = (f32[256,256]{1,0:T(8,128)S(1)}, f32[256,256]{1,0:T(8,128)S(1)}, u32[]{:S(2)}, u32[]{:S(2)}) collective-permute-start(f32[256,256]{1,0:T(8,128)S(1)} %get-tuple-element.282), channel_id=1, source_target_pairs={{0,2},{1,5},{2,0},{3,7},{4,6},{5,1},{6,4},{7,3},{8,10},{9,13},{10,... | collective-permute-start | bytes 786440 | tf_op jit(solution)/shard_map/ppermute | solution.py:695
  104.8 6.4 %collective-permute-start.16 = (f32[128,256]{1,0:T(8,128)S(1)}, f32[128,256]{1,0:T(8,128)S(1)}, u32[]{:S(2)}, u32[]{:S(2)}) collective-permute-start(f32[128,256]{1,0:T(8,128)S(1)} %get-tuple-element.284), channel_id=1, source_target_pairs={{0,4},{1,3},{2,6},{3,1},{4,0},{5,7},{6,2},{7,5},{8,12},{9,11},{10,... | collective-permute-start | bytes 393224 | tf_op jit(solution)/shard_map/ppermute | solution.py:695
  106.2 8.2 %collective-permute-start.15 = (f32[192,256]{1,0:T(8,128)S(1)}, f32[192,256]{1,0:T(8,128)S(1)}, u32[]{:S(2)}, u32[]{:S(2)}) collective-permute-start(f32[192,256]{1,0:T(8,128)S(1)} %add.11.own_ref), channel_id=1, source_target_pairs={{0,8},{1,9},{2,10},{3,11},{4,12},{5,13},{6,14},{7,15},{8,0},{9,1},... | collective-permute-start | bytes 589832 | tf_op jit(solution)/shard_map/ppermute | solution.py:695
  106.5 9.2 %collective-permute-start.14 = (f32[152,256]{1,0:T(8,128)S(1)}, f32[152,256]{1,0:T(8,128)S(1)}, u32[]{:S(2)}, u32[]{:S(2)}) collective-permute-start(f32[152,256]{1,0:T(8,128)S(1)} %get-tuple-element.288), channel_id=1, source_target_pairs={{0,2},{1,5},{2,0},{3,7},{4,6},{5,1},{6,4},{7,3},{8,10},{9,13},{10,... | collective-permute-start | bytes 466952 | tf_op jit(solution)/shard_map/ppermute | solution.py:695
  107.4 8.4 %collective-permute-start.23 = (f32[64,256]{1,0:T(8,128)S(1)}, f32[64,256]{1,0:T(8,128)S(1)}, u32[]{:S(2)}, u32[]{:S(2)}) collective-permute-start(f32[64,256]{1,0:T(8,128)S(1)} %add.12.keep_ref), channel_id=1, source_target_pairs={{0,16},{1,17},{2,18},{3,19},{4,20},{5,21},{6,22},{7,23},{8,24},{9,... | collective-permute-start | bytes 196616 | tf_op jit(solution)/shard_map/ppermute | solution.py:695
  109.8 7.0 %collective-permute-start.22 = (f32[128,256]{1,0:T(8,128)S(1)}, f32[128,256]{1,0:T(8,128)S(1)}, u32[]{:S(2)}, u32[]{:S(2)}) collective-permute-start(f32[128,256]{1,0:T(8,128)S(1)} %get-tuple-element.294), channel_id=1, source_target_pairs={{0,8},{1,9},{2,10},{3,11},{4,12},{5,13},{6,14},{7,15},{8,0},{9,1},... | collective-permute-start | bytes 393224 | tf_op jit(solution)/shard_map/ppermute | solution.py:695
  111.2 7.0 %collective-permute-start.21 = (f32[128,256]{1,0:T(8,128)S(1)}, f32[128,256]{1,0:T(8,128)S(1)}, u32[]{:S(2)}, u32[]{:S(2)}) collective-permute-start(f32[128,256]{1,0:T(8,128)S(1)} %add.13.keep_ref), channel_id=1, source_target_pairs={{0,2},{1,5},{2,0},{3,7},{4,6},{5,1},{6,4},{7,3},{8,10},{9,13},{10,... | collective-permute-start | bytes 393224 | tf_op jit(solution)/shard_map/ppermute | solution.py:695
  114.5 8.8 %collective-permute-start.20 = (f32[384,256]{1,0:T(8,128)S(1)}, f32[384,256]{1,0:T(8,128)S(1)}, u32[]{:S(2)}, u32[]{:S(2)}) collective-permute-start(f32[384,256]{1,0:T(8,128)S(1)} %join.14.own_ref), channel_id=1, source_target_pairs={{0,2},{1,5},{2,0},{3,7},{4,6},{5,1},{6,4},{7,3},{8,10},{9,13},{10,... | collective-permute-start | bytes 1179656 | tf_op jit(solution)/shard_map/ppermute | solution.py:695
  115.7 9.5 %collective-permute-start.19 = (f32[88,256]{1,0:T(8,128)S(1)}, f32[88,256]{1,0:T(8,128)S(1)}, u32[]{:S(2)}, u32[]{:S(2)}) collective-permute-start(f32[88,256]{1,0:T(8,128)S(1)} %get-tuple-element.299), channel_id=1, source_target_pairs={{0,8},{1,9},{2,10},{3,11},{4,12},{5,13},{6,14},{7,15},{8,0},{9,1},... | collective-permute-start | bytes 270344 | tf_op jit(solution)/shard_map/ppermute | solution.py:695
  115.8 9.5 %collective-permute-start.28 = (f32[64,256]{1,0:T(8,128)S(1)}, f32[64,256]{1,0:T(8,128)S(1)}, u32[]{:S(2)}, u32[]{:S(2)}) collective-permute-start(f32[64,256]{1,0:T(8,128)S(1)} %add.14.own_ref), channel_id=1, source_target_pairs={{0,2},{1,5},{2,0},{3,7},{4,6},{5,1},{6,4},{7,3},{8,10},{9,13},{10,... | collective-permute-start | bytes 196616 | tf_op jit(solution)/shard_map/ppermute | solution.py:695
  116.8 13.2 %collective-permute-start.27 = (f32[128,256]{1,0:T(8,128)S(1)}, f32[128,256]{1,0:T(8,128)S(1)}, u32[]{:S(2)}, u32[]{:S(2)}) collective-permute-start(f32[128,256]{1,0:T(8,128)S(1)} %add.15.keep_ref), channel_id=1, source_target_pairs={{0,16},{1,17},{2,18},{3,19},{4,20},{5,21},{6,22},{7,23},{8,24},{9,... | collective-permute-start | bytes 393224 | tf_op jit(solution)/shard_map/ppermute | solution.py:695
  118.2 14.6 %collective-permute-start.26 = (f32[128,256]{1,0:T(8,128)S(1)}, f32[128,256]{1,0:T(8,128)S(1)}, u32[]{:S(2)}, u32[]{:S(2)}) collective-permute-start(f32[128,256]{1,0:T(8,128)S(1)} %add.16.keep_ref), channel_id=1, source_target_pairs={{0,16},{1,17},{2,18},{3,19},{4,20},{5,21},{6,22},{7,23},{8,24},{9,... | collective-permute-start | bytes 393224 | tf_op jit(solution)/shard_map/ppermute | solution.py:695
  123.3 12.1 %collective-permute-start.25 = (f32[768,256]{1,0:T(8,128)S(1)}, f32[768,256]{1,0:T(8,128)S(1)}, u32[]{:S(2)}, u32[]{:S(2)}) collective-permute-start(f32[768,256]{1,0:T(8,128)S(1)} %join.15.own_ref), channel_id=1, source_target_pairs={{0,4},{1,3},{2,6},{3,1},{4,0},{5,7},{6,2},{7,5},{8,12},{9,11},{10,... | collective-permute-start | bytes 2359304 | tf_op jit(solution)/shard_map/ppermute | solution.py:695
  125.2 10.4 %collective-permute-start.24 = (f32[88,256]{1,0:T(8,128)S(1)}, f32[88,256]{1,0:T(8,128)S(1)}, u32[]{:S(2)}, u32[]{:S(2)}) collective-permute-start(f32[88,256]{1,0:T(8,128)S(1)} %add.17.keep_ref), channel_id=1, source_target_pairs={{0,16},{1,17},{2,18},{3,19},{4,20},{5,21},{6,22},{7,23},{8,24},{9,... | collective-permute-start | bytes 270344 | tf_op jit(solution)/shard_map/ppermute | solution.py:695
  125.3 11.5 %collective-permute-start.33 = (f32[128,256]{1,0:T(8,128)S(1)}, f32[128,256]{1,0:T(8,128)S(1)}, u32[]{:S(2)}, u32[]{:S(2)}) collective-permute-start(f32[128,256]{1,0:T(8,128)S(1)} %join.16.own_ref), channel_id=1, source_target_pairs={{0,4},{1,3},{2,6},{3,1},{4,0},{5,7},{6,2},{7,5},{8,12},{9,11},{10,... | collective-permute-start | bytes 393224 | tf_op jit(solution)/shard_map/ppermute | solution.py:695
  130.0 7.8 %collective-permute-start.32 = (f32[128,256]{1,0:T(8,128)S(1)}, f32[128,256]{1,0:T(8,128)S(1)}, u32[]{:S(2)}, u32[]{:S(2)}) collective-permute-start(f32[128,256]{1,0:T(8,128)S(1)} %add.18.own_ref), channel_id=1, source_target_pairs={{0,8},{1,9},{2,10},{3,11},{4,12},{5,13},{6,14},{7,15},{8,0},{9,1},... | collective-permute-start | bytes 393224 | tf_op jit(solution)/shard_map/ppermute | solution.py:695
  132.8 6.9 %collective-permute-start.31 = (f32[128,256]{1,0:T(8,128)S(1)}, f32[128,256]{1,0:T(8,128)S(1)}, u32[]{:S(2)}, u32[]{:S(2)}) collective-permute-start(f32[128,256]{1,0:T(8,128)S(1)} %add.19.own_ref), channel_id=1, source_target_pairs={{0,4},{1,3},{2,6},{3,1},{4,0},{5,7},{6,2},{7,5},{8,12},{9,11},{10,... | collective-permute-start | bytes 393224 | tf_op jit(solution)/shard_map/ppermute | solution.py:695
  135.5 6.9 %collective-permute-start.30 = (f32[1536,256]{1,0:T(8,128)S(1)}, f32[1536,256]{1,0:T(8,128)S(1)}, u32[]{:S(2)}, u32[]{:S(2)}) collective-permute-start(f32[1536,256]{1,0:T(8,128)S(1)} %join.17.refs_0_), channel_id=1, source_target_pairs={{0,1},{1,0},{2,3},{3,2},{4,5},{5,4},{6,7},{7,6},{8,9},{9,8},{10,11... | collective-permute-start | bytes 4718600 | tf_op jit(solution)/shard_map/ppermute | solution.py:695
  135.6 8.5 %collective-permute-start.29 = (f32[64,256]{1,0:T(8,128)S(1)}, f32[64,256]{1,0:T(8,128)S(1)}, u32[]{:S(2)}, u32[]{:S(2)}) collective-permute-start(f32[64,256]{1,0:T(8,128)S(1)} %get-tuple-element.320.own_ref), channel_id=1, source_target_pairs={{0,8},{1,9},{2,10},{3,11},{4,12},{5,13},{6,14},{7,15},{8,0},{9,1},... | collective-permute-start | bytes 196616 | tf_op jit(solution)/shard_map/ppermute | solution.py:695
  136.8 9.4 %collective-permute-start.37 = (f32[256,256]{1,0:T(8,128)S(1)}, f32[256,256]{1,0:T(8,128)S(1)}, u32[]{:S(2)}, u32[]{:S(2)}) collective-permute-start(f32[256,256]{1,0:T(8,128)S(1)} %join.18.own_ref), channel_id=1, source_target_pairs={{0,8},{1,9},{2,10},{3,11},{4,12},{5,13},{6,14},{7,15},{8,0},{9,1},... | collective-permute-start | bytes 786440 | tf_op jit(solution)/shard_map/ppermute | solution.py:695
  137.9 8.5 %collective-permute-start.36 = (f32[256,256]{1,0:T(8,128)S(1)}, f32[256,256]{1,0:T(8,128)S(1)}, u32[]{:S(2)}, u32[]{:S(2)}) collective-permute-start(f32[256,256]{1,0:T(8,128)S(1)} %join.19.own_ref), channel_id=1, source_target_pairs={{0,2},{1,5},{2,0},{3,7},{4,6},{5,1},{6,4},{7,3},{8,10},{9,13},{10,... | collective-permute-start | bytes 786440 | tf_op jit(solution)/shard_map/ppermute | solution.py:695
  139.7 11.7 %collective-permute-start.35 = (f32[256,256]{1,0:T(8,128)S(1)}, f32[256,256]{1,0:T(8,128)S(1)}, u32[]{:S(2)}, u32[]{:S(2)}) collective-permute-start(f32[256,256]{1,0:T(8,128)S(1)} %join.20.own_ref), channel_id=1, source_target_pairs={{0,8},{1,9},{2,10},{3,11},{4,12},{5,13},{6,14},{7,15},{8,0},{9,1},... | collective-permute-start | bytes 786440 | tf_op jit(solution)/shard_map/ppermute | solution.py:695
  144.2 7.4 %collective-permute-start.34 = (f32[128,256]{1,0:T(8,128)S(1)}, f32[128,256]{1,0:T(8,128)S(1)}, u32[]{:S(2)}, u32[]{:S(2)}) collective-permute-start(f32[128,256]{1,0:T(8,128)S(1)} %join.21.own_ref), channel_id=1, source_target_pairs={{0,2},{1,5},{2,0},{3,7},{4,6},{5,1},{6,4},{7,3},{8,10},{9,13},{10,... | collective-permute-start | bytes 393224 | tf_op jit(solution)/shard_map/ppermute | solution.py:695
  146.3 7.2 %collective-permute-start.41 = (f32[512,256]{1,0:T(8,128)S(1)}, f32[512,256]{1,0:T(8,128)S(1)}, u32[]{:S(2)}, u32[]{:S(2)}) collective-permute-start(f32[512,256]{1,0:T(8,128)S(1)} %join.22.refs_0_), channel_id=1, source_target_pairs={{0,1},{1,0},{2,3},{3,2},{4,5},{5,4},{6,7},{7,6},{8,9},{9,8},{10,11... | collective-permute-start | bytes 1572872 | tf_op jit(solution)/shard_map/ppermute | solution.py:695
  146.4 9.2 %collective-permute-start.40 = (f32[512,256]{1,0:T(8,128)S(1)}, f32[512,256]{1,0:T(8,128)S(1)}, u32[]{:S(2)}, u32[]{:S(2)}) collective-permute-start(f32[512,256]{1,0:T(8,128)S(1)} %join.23.own_ref), channel_id=1, source_target_pairs={{0,4},{1,3},{2,6},{3,1},{4,0},{5,7},{6,2},{7,5},{8,12},{9,11},{10,... | collective-permute-start | bytes 1572872 | tf_op jit(solution)/shard_map/ppermute | solution.py:695
  151.5 4.4 %collective-permute-start.39 = (f32[512,256]{1,0:T(8,128)S(1)}, f32[512,256]{1,0:T(8,128)S(1)}, u32[]{:S(2)}, u32[]{:S(2)}) collective-permute-start(f32[512,256]{1,0:T(8,128)S(1)} %join.24.refs_0_), channel_id=1, source_target_pairs={{0,1},{1,0},{2,3},{3,2},{4,5},{5,4},{6,7},{7,6},{8,9},{9,8},{10,11... | collective-permute-start | bytes 1572872 | tf_op jit(solution)/shard_map/ppermute | solution.py:695
  151.6 6.9 %collective-permute-start.38 = (f32[256,256]{1,0:T(8,128)S(1)}, f32[256,256]{1,0:T(8,128)S(1)}, u32[]{:S(2)}, u32[]{:S(2)}) collective-permute-start(f32[256,256]{1,0:T(8,128)S(1)} %join.25.own_ref), channel_id=1, source_target_pairs={{0,4},{1,3},{2,6},{3,1},{4,0},{5,7},{6,2},{7,5},{8,12},{9,11},{10,... | collective-permute-start | bytes 786440 | tf_op jit(solution)/shard_map/ppermute | solution.py:695
  155.8 2.8 %collective-permute-start.43 = (f32[1024,256]{1,0:T(8,128)S(1)}, f32[1024,256]{1,0:T(8,128)S(1)}, u32[]{:S(2)}, u32[]{:S(2)}) collective-permute-start(f32[1024,256]{1,0:T(8,128)S(1)} %join.26.refs_0_), channel_id=1, source_target_pairs={{0,1},{1,0},{2,3},{3,2},{4,5},{5,4},{6,7},{7,6},{8,9},{9,8},{10,11... | collective-permute-start | bytes 3145736 | tf_op jit(solution)/shard_map/ppermute | solution.py:695
  158.5 2.0 %collective-permute-start.42 = (f32[512,256]{1,0:T(8,128)S(1)}, f32[512,256]{1,0:T(8,128)S(1)}, u32[]{:S(2)}, u32[]{:S(2)}) collective-permute-start(f32[512,256]{1,0:T(8,128)S(1)} %join.27.refs_0_), channel_id=1, source_target_pairs={{0,1},{1,0},{2,3},{3,2},{4,5},{5,4},{6,7},{7,6},{8,9},{9,8},{10,11... | collective-permute-start | bytes 1572872 | tf_op jit(solution)/shard_map/ppermute | solution.py:695
